TPU v7x, 32 devices: a whole 2x2x4 slice. The times are simulated.
32 devices in a mesh: mesh: 8 (over y, x, core), band: 4 (over z).
Axes of the slice: x: 2, y: 2, z: 4, core: 2. Of those that a mesh axis runs over, the one named last changes fastest.
Arguments:
- states: float32 [2, 64, 8192], P(None, 'band', 'mesh'), may hold values from -6 to 6
- frozen: float32 [2, 32, 8192], P(None, 'band', 'mesh'), may hold values from -0.125 to 0.125
- weights: float32 [8, 8192], P(None, 'mesh'), may hold values from 0.1 to 1
- potential: float32 [8192], P('mesh'), may hold values from -2 to 2
- send_list: int32 [8, 8, 256], P('mesh'), may hold values from 0 to 1023
- neighbours: int32 [8, 8192], P(None, 'mesh'), may hold values from 0 to 3071, as said below
Outputs:
- evolved: float32 [2, 64, 8192], P(None, 'band', 'mesh')
Inputs may be any that keep to these rules, and one draw needn't show every extreme that they name: `neighbours`: an entry below 1024 names a point of the same part; an entry 1024 + s * 256 + c names ghost slot c from part s, where part s is at most 3 parts away in the cyclic order of parts or exactly half the number of parts away, and every part names ghost slots from all those parts. Slots of send_list[s, i] that part i never names hold arbitrary points of part s.
All inputs are finite; a program needn't handle non-finite values.
Results may differ from a plain program's by a relative error of at most 0.0001.
Values sent between devices are 32-bit elements; how exact they have to be, the bound alone decides.
No kernel may reach another device: no remote copies, remote signals or barrier semaphores. Data moves between devices by JAX's collectives and lax.ppermute only.
A program may use at most 128 MiB of HBM per device.

v0:
```python
import jax
import jax.numpy as jnp
from jax import lax
from jax.sharding import PartitionSpec as P

NBRS = 8
TERMS = 4


time_step = 0.3


def rotate(field):
    return jnp.stack([field[1], -field[0]])


def body(states, frozen, weights, potential, send_list, neighbours):
    parts = lax.axis_size("mesh")
    rows = states.shape[1]
    capacity = send_list.shape[2]
    routes = send_list[0]
    full_frozen = lax.all_gather(frozen, "band", axis=1, tiled=True)
    total = states
    term = states
    for order in range(1, TERMS + 1):
        paired = jnp.stack([term, rotate(term)])
        partial_intersection = jnp.einsum(
            "cmp,ocjp->omj", full_frozen, paired, precision=lax.Precision.HIGHEST
        )
        intersection = lax.psum(partial_intersection, "mesh")
        packed = jnp.take(term, routes.reshape(-1), axis=2).reshape(2, rows, parts, capacity)
        arrived = lax.all_to_all(packed, "mesh", split_axis=2, concat_axis=2, tiled=True)
        extended = jnp.concatenate([term, arrived.reshape(2, rows, parts * capacity)], axis=2)
        stencil = jnp.zeros_like(term)
        for apply_order in range(NBRS):
            stencil = stencil + weights[apply_order] * (
                jnp.take(extended, neighbours[apply_order], axis=2) - term
            )
        blocks = jnp.stack(
            [
                jnp.stack([intersection[0], -intersection[1]]),
                jnp.stack([intersection[1], intersection[0]]),
            ]
        )
        exchange = jnp.einsum("dmp,cdmj->cjp", full_frozen, blocks, precision=lax.Precision.HIGHEST)
        image = -0.5 * stencil + potential * term - exchange
        term = time_step / order * rotate(image)
        total = total + term
    return total


def solution(mesh):
    return jax.shard_map(
        body,
        mesh=mesh,
        in_specs=(
            P(None, "band", "mesh"),
            P(None, "band", "mesh"),
            P(None, "mesh"),
            P("mesh"),
            P("mesh", None, None),
            P(None, "mesh"),
        ),
        out_specs=P(None, "band", "mesh"),
        check_vma=False,
    )
```

profile of v0, /device:TPU:0, one launch (start us, length us, event | category | flops | bytes accessed | tf_op | source)
XLA Modules:
  0.0 581.9 jit_solution(13586005560089532101)
XLA Ops:
  2.1 14.4 %gather_fusion = f32[2048,2,16]{2,1,0:T(2,128)} fusion(f32[2,16,1024]{1,0,2:T(2,128)S(1)} %copy.119, s32[2048]{0:T(1024)S(1)} %fusion.108), kind=kCustom, calls=%fused_computation.clone | custom fusion | bytes 532480 | tf_op jit(solution)/shard_map/jit(_take)/gather | solution.py:31
  16.5 10.0 %broadcast_select_fusion.3 = f32[2048,2,16]{2,1,0:T(2,128)S(1)} fusion(f32[2048,2,16]{2,1,0:T(2,128)} %gather_fusion, pred[2048]{0:T(1024)(128)(4,1)S(1)} %compare_and_fusion), kind=kLoop, calls=%fused_computation.39 | loop fusion | flops 65536 | bytes 526336 | tf_op jit(solution)/shard_map/jit(_take)/select_n | solution.py:31
  28.4 5.2 all-to-all-start
  39.6 14.2 %all_gather.3 = f32[2,32,1024]{2,1,0:T(8,128)S(1)} all-gather(f32[2,8,1024]{2,1,0:T(8,128)S(1)} %copy-done.34), channel_id=1, replica_groups=mesh['mesh'=8,'band'=4] {'band'}, dimensions={1}, use_global_device_ids=true | all-gather | bytes 327680 | tf_op jit(solution)/shard_map/all_gather | solution.py:22
  54.2 23.0 %psum.28 = f32[2,32,16]{1,2,0:T(8,128)S(1)} all-reduce(f32[2,32,16]{1,2,0:T(8,128)S(1)} %convolution_bitcast_fusion.7), channel_id=1, replica_groups=mesh['mesh'=8,'band'=4] {'mesh'}, use_global_device_ids=true, to_apply=%region_0.3 | all-reduce | flops 1024 | bytes 8192 | tf_op jit(solution)/shard_map/psum | solution.py:30
  79.9 4.1 copy.122
  84.0 7.6 %gather_fusion.1 = f32[1024,2,16]{2,1,0:T(2,128)} fusion(f32[2,16,3072]{1,0,2:T(2,128)S(1)} %copy.122, s32[1024]{0:T(1024)} %fusion.109), kind=kCustom, calls=%fused_computation.1.clone | custom fusion | bytes 266240 | tf_op jit(solution)/shard_map/jit(_take)/gather | solution.py:37
  93.6 7.6 %gather_fusion.2 = f32[1024,2,16]{2,1,0:T(2,128)} fusion(f32[2,16,3072]{1,0,2:T(2,128)S(1)} %copy.122, s32[1024]{0:T(1024)} %fusion.110), kind=kCustom, calls=%fused_computation.5.clone | custom fusion | bytes 266240 | tf_op jit(solution)/shard_map/jit(_take)/gather | solution.py:37
  103.3 7.6 %gather_fusion.3 = f32[1024,2,16]{2,1,0:T(2,128)} fusion(f32[2,16,3072]{1,0,2:T(2,128)S(1)} %copy.122, s32[1024]{0:T(1024)} %fusion.111), kind=kCustom, calls=%fused_computation.6.clone | custom fusion | bytes 266240 | tf_op jit(solution)/shard_map/jit(_take)/gather | solution.py:37
  110.9 2.0 copy.127
  112.9 7.6 %gather_fusion.4 = f32[1024,2,16]{2,1,0:T(2,128)} fusion(f32[2,16,3072]{1,0,2:T(2,128)S(1)} %copy.122, s32[1024]{0:T(1024)} %fusion.112), kind=kCustom, calls=%fused_computation.7.clone | custom fusion | bytes 266240 | tf_op jit(solution)/shard_map/jit(_take)/gather | solution.py:37
  122.5 7.6 %gather_fusion.5 = f32[1024,2,16]{2,1,0:T(2,128)} fusion(f32[2,16,3072]{1,0,2:T(2,128)S(1)} %copy.122, s32[1024]{0:T(1024)} %fusion.113), kind=kCustom, calls=%fused_computation.8.clone | custom fusion | bytes 266240 | tf_op jit(solution)/shard_map/jit(_take)/gather | solution.py:37
  132.1 7.6 %gather_fusion.6 = f32[1024,2,16]{2,1,0:T(2,128)} fusion(f32[2,16,3072]{1,0,2:T(2,128)S(1)} %copy.122, s32[1024]{0:T(1024)} %fusion.114), kind=kCustom, calls=%fused_computation.9.clone | custom fusion | bytes 266240 | tf_op jit(solution)/shard_map/jit(_take)/gather | solution.py:37
  141.7 7.5 %gather_fusion.7 = f32[1024,2,16]{2,1,0:T(2,128)} fusion(f32[2,16,3072]{1,0,2:T(2,128)S(1)} %copy.122, s32[1024]{0:T(1024)S(1)} %fusion.115), kind=kCustom, calls=%fused_computation.10.clone | custom fusion | bytes 266240 | tf_op jit(solution)/shard_map/jit(_take)/gather | solution.py:37
  151.2 7.5 %gather_fusion.8 = f32[1024,2,16]{2,1,0:T(2,128)} fusion(f32[2,16,3072]{1,0,2:T(2,128)S(1)} %copy.122, s32[1024]{0:T(1024)S(1)} %fusion.116), kind=kCustom, calls=%fused_computation.11.clone | custom fusion | bytes 266240 | tf_op jit(solution)/shard_map/jit(_take)/gather | solution.py:37
  163.5 22.3 %psum.29 = f32[2,32,16]{1,2,0:T(8,128)S(1)} all-reduce(f32[2,32,16]{1,2,0:T(8,128)S(1)} %convolution_bitcast_fusion.6), channel_id=1, replica_groups=mesh['mesh'=8,'band'=4] {'mesh'}, use_global_device_ids=true, to_apply=%region_1.4 | all-reduce | flops 1024 | bytes 8192 | tf_op jit(solution)/shard_map/psum | solution.py:30
  185.8 14.4 %gather_fusion.9 = f32[2048,2,16]{2,1,0:T(2,128)} fusion(f32[2,16,1024]{1,0,2:T(2,128)S(1)} %copy.138, s32[2048]{0:T(1024)S(1)} %fusion.108), kind=kCustom, calls=%fused_computation.2.clone | custom fusion | bytes 532480 | tf_op jit(solution)/shard_map/jit(_take)/gather | solution.py:31
  200.2 10.0 %broadcast_select_fusion.2 = f32[2048,2,16]{2,1,0:T(2,128)S(1)} fusion(f32[2048,2,16]{2,1,0:T(2,128)} %gather_fusion.9, pred[2048]{0:T(1024)(128)(4,1)S(1)} %copy-done.36), kind=kLoop, calls=%fused_computation.38 | loop fusion | flops 65536 | bytes 526336 | tf_op jit(solution)/shard_map/jit(_take)/select_n | solution.py:31
  212.1 3.6 all-to-all-start.1
  216.3 6.1 %all-to-all-done.1 = f32[2,16,8,256]{3,1,0,2:T(8,128)S(1)} async-done(((f32[2,16,8,256]{3,1,0,2:T(8,128)}), f32[2,16,8,256]{3,1,0,2:T(8,128)S(1)}, u32[]{:S(2)}, u32[]{:S(2)}) %all-to-all-start.1) | async-done | bytes 262176 | tf_op jit(solution)/shard_map/all_to_all | solution.py:32
  223.2 4.1 copy.141
  227.3 7.7 %gather_fusion.10 = f32[1024,2,16]{2,1,0:T(2,128)} fusion(f32[2,16,3072]{1,0,2:T(2,128)S(1)} %copy.141, s32[1024]{0:T(1024)} %fusion.109), kind=kCustom, calls=%fused_computation.12.clone | custom fusion | bytes 266240 | tf_op jit(solution)/shard_map/jit(_take)/gather | solution.py:37
  235.0 7.6 %gather_fusion.11 = f32[1024,2,16]{2,1,0:T(2,128)} fusion(f32[2,16,3072]{1,0,2:T(2,128)S(1)} %copy.141, s32[1024]{0:T(1024)} %fusion.110), kind=kCustom, calls=%fused_computation.13.clone | custom fusion | bytes 266240 | tf_op jit(solution)/shard_map/jit(_take)/gather | solution.py:37
  242.6 7.6 %gather_fusion.12 = f32[1024,2,16]{2,1,0:T(2,128)} fusion(f32[2,16,3072]{1,0,2:T(2,128)S(1)} %copy.141, s32[1024]{0:T(1024)} %fusion.111), kind=kCustom, calls=%fused_computation.14.clone | custom fusion | bytes 266240 | tf_op jit(solution)/shard_map/jit(_take)/gather | solution.py:37
  250.2 7.6 %gather_fusion.13 = f32[1024,2,16]{2,1,0:T(2,128)} fusion(f32[2,16,3072]{1,0,2:T(2,128)S(1)} %copy.141, s32[1024]{0:T(1024)} %fusion.112), kind=kCustom, calls=%fused_computation.15.clone | custom fusion | bytes 266240 | tf_op jit(solution)/shard_map/jit(_take)/gather | solution.py:37
  257.8 7.6 %gather_fusion.14 = f32[1024,2,16]{2,1,0:T(2,128)} fusion(f32[2,16,3072]{1,0,2:T(2,128)S(1)} %copy.141, s32[1024]{0:T(1024)} %fusion.113), kind=kCustom, calls=%fused_computation.16.clone | custom fusion | bytes 266240 | tf_op jit(solution)/shard_map/jit(_take)/gather | solution.py:37
  265.4 7.6 %gather_fusion.15 = f32[1024,2,16]{2,1,0:T(2,128)} fusion(f32[2,16,3072]{1,0,2:T(2,128)S(1)} %copy.141, s32[1024]{0:T(1024)} %fusion.114), kind=kCustom, calls=%fused_computation.17.clone | custom fusion | bytes 266240 | tf_op jit(solution)/shard_map/jit(_take)/gather | solution.py:37
  273.0 7.5 %gather_fusion.16 = f32[1024,2,16]{2,1,0:T(2,128)} fusion(f32[2,16,3072]{1,0,2:T(2,128)S(1)} %copy.141, s32[1024]{0:T(1024)S(1)} %fusion.115), kind=kCustom, calls=%fused_computation.18.clone | custom fusion | bytes 266240 | tf_op jit(solution)/shard_map/jit(_take)/gather | solution.py:37
  280.5 7.5 %gather_fusion.17 = f32[1024,2,16]{2,1,0:T(2,128)} fusion(f32[2,16,3072]{1,0,2:T(2,128)S(1)} %copy.141, s32[1024]{0:T(1024)S(1)} %fusion.116), kind=kCustom, calls=%fused_computation.19.clone | custom fusion | bytes 266240 | tf_op jit(solution)/shard_map/jit(_take)/gather | solution.py:37
  287.9 2.1 copy.142
  290.0 2.1 copy.144
  292.2 2.1 copy.146
  303.7 22.3 %psum.30 = f32[2,32,16]{1,2,0:T(8,128)S(1)} all-reduce(f32[2,32,16]{1,2,0:T(8,128)S(1)} %convolution_bitcast_fusion.5), channel_id=1, replica_groups=mesh['mesh'=8,'band'=4] {'mesh'}, use_global_device_ids=true, to_apply=%region_2.5 | all-reduce | flops 1024 | bytes 8192 | tf_op jit(solution)/shard_map/psum | solution.py:30
  326.0 14.4 %gather_fusion.18 = f32[2048,2,16]{2,1,0:T(2,128)} fusion(f32[2,16,1024]{1,0,2:T(2,128)S(1)} %copy.157, s32[2048]{0:T(1024)S(1)} %fusion.108), kind=kCustom, calls=%fused_computation.3.clone | custom fusion | bytes 532480 | tf_op jit(solution)/shard_map/jit(_take)/gather | solution.py:31
  340.4 10.0 %broadcast_select_fusion.1 = f32[2048,2,16]{2,1,0:T(2,128)S(1)} fusion(f32[2048,2,16]{2,1,0:T(2,128)} %gather_fusion.18, pred[2048]{0:T(1024)(128)(4,1)S(1)} %copy-done.37), kind=kLoop, calls=%fused_computation.37 | loop fusion | flops 65536 | bytes 526336 | tf_op jit(solution)/shard_map/jit(_take)/select_n | solution.py:31
  352.2 3.4 all-to-all-start.2
  356.3 6.2 %all-to-all-done.2 = f32[2,16,8,256]{3,1,0,2:T(8,128)S(1)} async-done(((f32[2,16,8,256]{3,1,0,2:T(8,128)}), f32[2,16,8,256]{3,1,0,2:T(8,128)S(1)}, u32[]{:S(2)}, u32[]{:S(2)}) %all-to-all-start.2) | async-done | bytes 262176 | tf_op jit(solution)/shard_map/all_to_all | solution.py:32
  363.3 4.1 copy.160
  367.5 7.7 %gather_fusion.19 = f32[1024,2,16]{2,1,0:T(2,128)} fusion(f32[2,16,3072]{1,0,2:T(2,128)S(1)} %copy.160, s32[1024]{0:T(1024)} %fusion.109), kind=kCustom, calls=%fused_computation.20.clone | custom fusion | bytes 266240 | tf_op jit(solution)/shard_map/jit(_take)/gather | solution.py:37
  375.1 7.6 %gather_fusion.20 = f32[1024,2,16]{2,1,0:T(2,128)} fusion(f32[2,16,3072]{1,0,2:T(2,128)S(1)} %copy.160, s32[1024]{0:T(1024)} %fusion.110), kind=kCustom, calls=%fused_computation.21.clone | custom fusion | bytes 266240 | tf_op jit(solution)/shard_map/jit(_take)/gather | solution.py:37
  382.8 7.6 %gather_fusion.21 = f32[1024,2,16]{2,1,0:T(2,128)} fusion(f32[2,16,3072]{1,0,2:T(2,128)S(1)} %copy.160, s32[1024]{0:T(1024)} %fusion.111), kind=kCustom, calls=%fused_computation.22.clone | custom fusion | bytes 266240 | tf_op jit(solution)/shard_map/jit(_take)/gather | solution.py:37
  390.4 7.6 %gather_fusion.22 = f32[1024,2,16]{2,1,0:T(2,128)} fusion(f32[2,16,3072]{1,0,2:T(2,128)S(1)} %copy.160, s32[1024]{0:T(1024)} %fusion.112), kind=kCustom, calls=%fused_computation.23.clone | custom fusion | bytes 266240 | tf_op jit(solution)/shard_map/jit(_take)/gather | solution.py:37
  398.0 7.6 %gather_fusion.23 = f32[1024,2,16]{2,1,0:T(2,128)} fusion(f32[2,16,3072]{1,0,2:T(2,128)S(1)} %copy.160, s32[1024]{0:T(1024)} %fusion.113), kind=kCustom, calls=%fused_computation.24.clone | custom fusion | bytes 266240 | tf_op jit(solution)/shard_map/jit(_take)/gather | solution.py:37
  405.6 7.6 %gather_fusion.24 = f32[1024,2,16]{2,1,0:T(2,128)} fusion(f32[2,16,3072]{1,0,2:T(2,128)S(1)} %copy.160, s32[1024]{0:T(1024)} %fusion.114), kind=kCustom, calls=%fused_computation.25.clone | custom fusion | bytes 266240 | tf_op jit(solution)/shard_map/jit(_take)/gather | solution.py:37
  413.2 7.5 %gather_fusion.25 = f32[1024,2,16]{2,1,0:T(2,128)} fusion(f32[2,16,3072]{1,0,2:T(2,128)S(1)} %copy.160, s32[1024]{0:T(1024)S(1)} %fusion.115), kind=kCustom, calls=%fused_computation.26.clone | custom fusion | bytes 266240 | tf_op jit(solution)/shard_map/jit(_take)/gather | solution.py:37
  420.7 7.5 %gather_fusion.26 = f32[1024,2,16]{2,1,0:T(2,128)} fusion(f32[2,16,3072]{1,0,2:T(2,128)S(1)} %copy.160, s32[1024]{0:T(1024)S(1)} %fusion.116), kind=kCustom, calls=%fused_computation.27.clone | custom fusion | bytes 266240 | tf_op jit(solution)/shard_map/jit(_take)/gather | solution.py:37
  428.1 2.1 copy.161
  430.2 2.1 copy.163
  432.4 2.1 copy.165
  443.8 22.3 %psum.31 = f32[2,32,16]{1,2,0:T(8,128)S(1)} all-reduce(f32[2,32,16]{1,2,0:T(8,128)S(1)} %convolution_bitcast_fusion.4), channel_id=1, replica_groups=mesh['mesh'=8,'band'=4] {'mesh'}, use_global_device_ids=true, to_apply=%region_3.6 | all-reduce | flops 1024 | bytes 8192 | tf_op jit(solution)/shard_map/psum | solution.py:30
  466.1 14.4 %gather_fusion.27 = f32[2048,2,16]{2,1,0:T(2,128)} fusion(f32[2,16,1024]{1,0,2:T(2,128)S(1)} %copy.176, s32[2048]{0:T(1024)S(1)} %fusion.108), kind=kCustom, calls=%fused_computation.4.clone | custom fusion | bytes 532480 | tf_op jit(solution)/shard_map/jit(_take)/gather | solution.py:31
  480.6 10.0 %broadcast_select_fusion = f32[2048,2,16]{2,1,0:T(2,128)S(1)} fusion(f32[2048,2,16]{2,1,0:T(2,128)} %gather_fusion.27, pred[2048]{0:T(1024)(128)(4,1)S(1)} %copy-done.38), kind=kLoop, calls=%fused_computation.36 | loop fusion | flops 65536 | bytes 526336 | tf_op jit(solution)/shard_map/jit(_take)/select_n | solution.py:31
  492.4 3.8 all-to-all-start.3
  496.8 6.0 %all-to-all-done.3 = f32[2,16,8,256]{3,1,0,2:T(8,128)S(1)} async-done(((f32[2,16,8,256]{3,1,0,2:T(8,128)}), f32[2,16,8,256]{3,1,0,2:T(8,128)S(1)}, u32[]{:S(2)}, u32[]{:S(2)}) %all-to-all-start.3) | async-done | bytes 262176 | tf_op jit(solution)/shard_map/all_to_all | solution.py:32
  503.6 4.1 copy.179
  507.8 7.6 %gather_fusion.28 = f32[1024,2,16]{2,1,0:T(2,128)} fusion(f32[2,16,3072]{1,0,2:T(2,128)S(1)} %copy.179, s32[1024]{0:T(1024)} %fusion.109), kind=kCustom, calls=%fused_computation.28.clone | custom fusion | bytes 266240 | tf_op jit(solution)/shard_map/jit(_take)/gather | solution.py:37
  515.4 7.6 %gather_fusion.29 = f32[1024,2,16]{2,1,0:T(2,128)} fusion(f32[2,16,3072]{1,0,2:T(2,128)S(1)} %copy.179, s32[1024]{0:T(1024)} %fusion.110), kind=kCustom, calls=%fused_computation.29.clone | custom fusion | bytes 266240 | tf_op jit(solution)/shard_map/jit(_take)/gather | solution.py:37
  523.0 7.6 %gather_fusion.30 = f32[1024,2,16]{2,1,0:T(2,128)} fusion(f32[2,16,3072]{1,0,2:T(2,128)S(1)} %copy.179, s32[1024]{0:T(1024)} %fusion.111), kind=kCustom, calls=%fused_computation.30.clone | custom fusion | bytes 266240 | tf_op jit(solution)/shard_map/jit(_take)/gather | solution.py:37
  530.6 7.6 %gather_fusion.31 = f32[1024,2,16]{2,1,0:T(2,128)} fusion(f32[2,16,3072]{1,0,2:T(2,128)S(1)} %copy.179, s32[1024]{0:T(1024)} %fusion.112), kind=kCustom, calls=%fused_computation.31.clone | custom fusion | bytes 266240 | tf_op jit(solution)/shard_map/jit(_take)/gather | solution.py:37
  538.2 7.5 %gather_fusion.32 = f32[1024,2,16]{2,1,0:T(2,128)} fusion(f32[2,16,3072]{1,0,2:T(2,128)S(1)} %copy.179, s32[1024]{0:T(1024)S(1)} %copy-done.29), kind=kCustom, calls=%fused_computation.32.clone | custom fusion | bytes 266240 | tf_op jit(solution)/shard_map/jit(_take)/gather | solution.py:37
  545.7 7.5 %gather_fusion.33 = f32[1024,2,16]{2,1,0:T(2,128)} fusion(f32[2,16,3072]{1,0,2:T(2,128)S(1)} %copy.179, s32[1024]{0:T(1024)S(1)} %copy-done.28), kind=kCustom, calls=%fused_computation.33.clone | custom fusion | bytes 266240 | tf_op jit(solution)/shard_map/jit(_take)/gather | solution.py:37
  553.2 7.5 %gather_fusion.34 = f32[1024,2,16]{2,1,0:T(2,128)} fusion(f32[2,16,3072]{1,0,2:T(2,128)S(1)} %copy.179, s32[1024]{0:T(1024)S(1)} %fusion.115), kind=kCustom, calls=%fused_computation.34.clone | custom fusion | bytes 266240 | tf_op jit(solution)/shard_map/jit(_take)/gather | solution.py:37
  560.7 7.5 %gather_fusion.35 = f32[1024,2,16]{2,1,0:T(2,128)} fusion(f32[2,16,3072]{1,0,2:T(2,128)S(1)} %copy.179, s32[1024]{0:T(1024)S(1)} %fusion.116), kind=kCustom, calls=%fused_computation.35.clone | custom fusion | bytes 266240 | tf_op jit(solution)/shard_map/jit(_take)/gather | solution.py:37
  568.2 2.2 copy.180
  (178 shorter events, 69.4 us)
Async XLA Ops:
  0.7 27.7 %copy-start.35 = (pred[2048]{0:T(1024)(128)(4,1)}, pred[2048]{0:T(1024)(128)(4,1)S(1)}, u32[]{:S(2)}) copy-start(pred[2048]{0:T(1024)(128)(4,1)S(1)} %compare_and_fusion) | copy-start | bytes 6148
  16.5 17.1 %copy-start = (f32[2,16,1024]{2,1,0:T(8,128)S(1)}, f32[2,16,1024]{2,1,0:T(8,128)}, u32[]{:S(2)}) copy-start(f32[2,16,1024]{2,1,0:T(8,128)} %param.10) | copy-start | bytes 393220
  16.5 17.1 %copy-start.39 = (s32[8,1024]{1,0:T(8,128)S(1)}, s32[8,1024]{1,0:T(8,128)}, u32[]{:S(2)}) copy-start(s32[8,1024]{1,0:T(8,128)} %param.15) | copy-start | bytes 98308
  16.5 23.1 %copy-start.34 = (f32[2,8,1024]{2,1,0:T(8,128)S(1)}, f32[2,8,1024]{2,1,0:T(8,128)}, u32[]{:S(2)}) copy-start(f32[2,8,1024]{2,1,0:T(8,128)} %param.11) | copy-start | bytes 196612
  26.5 50.7 %copy-start.41 = (f32[1024]{0:T(1024)S(1)}, f32[1024]{0:T(1024)}, u32[]{:S(2)}) copy-start(f32[1024]{0:T(1024)} %param.13) | copy-start | bytes 12292
  26.5 51.9 %copy-start.40 = (f32[8,1024]{1,0:T(8,128)S(1)}, f32[8,1024]{1,0:T(8,128)}, u32[]{:S(2)}) copy-start(f32[8,1024]{1,0:T(8,128)} %param.12) | copy-start | bytes 98308
  28.4 50.6 %all-to-all-start = ((f32[2,16,8,256]{3,1,0,2:T(8,128)}), f32[2,16,8,256]{3,1,0,2:T(8,128)S(1)}, u32[]{:S(2)}, u32[]{:S(2)}) async-start(f32[2,16,8,256]{3,1,0,2:T(8,128)} %copy.120), calls=%async_computation | async-start | bytes 524288 | tf_op jit(solution)/shard_map/all_to_all | solution.py:32
  158.7 41.5 %copy-start.36 = (pred[2048]{0:T(1024)(128)(4,1)S(1)}, pred[2048]{0:T(1024)(128)(4,1)}, u32[]{:S(2)}) copy-start(pred[2048]{0:T(1024)(128)(4,1)} %copy-done.35) | copy-start | bytes 6148
  161.9 0.6 copy-start.11
  161.9 0.6 copy-start.13
  212.1 10.3 %all-to-all-start.1 = ((f32[2,16,8,256]{3,1,0,2:T(8,128)}), f32[2,16,8,256]{3,1,0,2:T(8,128)S(1)}, u32[]{:S(2)}, u32[]{:S(2)}) async-start(f32[2,16,8,256]{3,1,0,2:T(8,128)} %copy.139), calls=%async_computation.1 | async-start | bytes 524288 | tf_op jit(solution)/shard_map/all_to_all | solution.py:32
  287.9 10.4 %copy-start.9 = (f32[1024,2,16]{2,1,0:T(2,128)S(1)}, f32[1024,2,16]{2,1,0:T(2,128)}, u32[]{:S(2)}) copy-start(f32[1024,2,16]{2,1,0:T(2,128)} %gather_fusion.15) | copy-start | bytes 393220
  290.0 9.3 %copy-start.7 = (f32[1024,2,16]{2,1,0:T(2,128)S(1)}, f32[1024,2,16]{2,1,0:T(2,128)}, u32[]{:S(2)}) copy-start(f32[1024,2,16]{2,1,0:T(2,128)} %gather_fusion.16) | copy-start | bytes 393220
  292.2 7.6 %copy-start.5 = (f32[1024,2,16]{2,1,0:T(2,128)S(1)}, f32[1024,2,16]{2,1,0:T(2,128)}, u32[]{:S(2)}) copy-start(f32[1024,2,16]{2,1,0:T(2,128)} %gather_fusion.17) | copy-start | bytes 393220
  299.8 40.6 %copy-start.37 = (pred[2048]{0:T(1024)(128)(4,1)S(1)}, pred[2048]{0:T(1024)(128)(4,1)}, u32[]{:S(2)}) copy-start(pred[2048]{0:T(1024)(128)(4,1)} %copy-done.35) | copy-start | bytes 6148
  302.1 0.6 copy-start.15
  302.1 0.6 copy-start.17
  352.2 10.3 %all-to-all-start.2 = ((f32[2,16,8,256]{3,1,0,2:T(8,128)}), f32[2,16,8,256]{3,1,0,2:T(8,128)S(1)}, u32[]{:S(2)}, u32[]{:S(2)}) async-start(f32[2,16,8,256]{3,1,0,2:T(8,128)} %copy.158), calls=%async_computation.2 | async-start | bytes 524288 | tf_op jit(solution)/shard_map/all_to_all | solution.py:32
  428.1 10.4 %copy-start.10 = (f32[1024,2,16]{2,1,0:T(2,128)S(1)}, f32[1024,2,16]{2,1,0:T(2,128)}, u32[]{:S(2)}) copy-start(f32[1024,2,16]{2,1,0:T(2,128)} %gather_fusion.24) | copy-start | bytes 393220
  430.2 9.3 %copy-start.8 = (f32[1024,2,16]{2,1,0:T(2,128)S(1)}, f32[1024,2,16]{2,1,0:T(2,128)}, u32[]{:S(2)}) copy-start(f32[1024,2,16]{2,1,0:T(2,128)} %gather_fusion.25) | copy-start | bytes 393220
  432.4 7.6 %copy-start.6 = (f32[1024,2,16]{2,1,0:T(2,128)S(1)}, f32[1024,2,16]{2,1,0:T(2,128)}, u32[]{:S(2)}) copy-start(f32[1024,2,16]{2,1,0:T(2,128)} %gather_fusion.26) | copy-start | bytes 393220
  440.0 40.6 %copy-start.38 = (pred[2048]{0:T(1024)(128)(4,1)S(1)}, pred[2048]{0:T(1024)(128)(4,1)}, u32[]{:S(2)}) copy-start(pred[2048]{0:T(1024)(128)(4,1)} %copy-done.35) | copy-start | bytes 6148
  442.2 0.6 copy-start.19
  442.2 0.6 copy-start.21
  492.4 45.8 %copy-start.29 = (s32[1024]{0:T(1024)S(1)}, s32[1024]{0:T(1024)}, u32[]{:S(2)}) copy-start(s32[1024]{0:T(1024)} %fusion.113) | copy-start | bytes 12292
  492.4 10.4 %all-to-all-start.3 = ((f32[2,16,8,256]{3,1,0,2:T(8,128)}), f32[2,16,8,256]{3,1,0,2:T(8,128)S(1)}, u32[]{:S(2)}, u32[]{:S(2)}) async-start(f32[2,16,8,256]{3,1,0,2:T(8,128)} %copy.177), calls=%async_computation.3 | async-start | bytes 524288 | tf_op jit(solution)/shard_map/all_to_all | solution.py:32
  496.2 49.5 %copy-start.28 = (s32[1024]{0:T(1024)S(1)}, s32[1024]{0:T(1024)}, u32[]{:S(2)}) copy-start(s32[1024]{0:T(1024)} %fusion.114) | copy-start | bytes 12292
  568.2 6.2 %copy-start.1 = (f32[1024,2,16]{2,1,0:T(2,128)S(1)}, f32[1024,2,16]{2,1,0:T(2,128)}, u32[]{:S(2)}) copy-start(f32[1024,2,16]{2,1,0:T(2,128)} %gather_fusion.31) | copy-start | bytes 393220
  568.2 7.3 %copy-start.2 = (f32[1024,2,16]{2,1,0:T(2,128)S(1)}, f32[1024,2,16]{2,1,0:T(2,128)}, u32[]{:S(2)}) copy-start(f32[1024,2,16]{2,1,0:T(2,128)} %gather_fusion.32) | copy-start | bytes 393220
  568.2 8.4 %copy-start.3 = (f32[1024,2,16]{2,1,0:T(2,128)S(1)}, f32[1024,2,16]{2,1,0:T(2,128)}, u32[]{:S(2)}) copy-start(f32[1024,2,16]{2,1,0:T(2,128)} %gather_fusion.33) | copy-start | bytes 393220
  574.4 5.2 copy-start.30
  574.4 5.2 copy-start.31
  574.4 5.2 copy-start.32
  574.4 5.2 copy-start.33
  575.5 3.6 copy-start.4
  576.6 3.0 copy-start.20
  576.6 3.0 copy-start.22
  576.6 3.0 copy-start.23
  576.6 3.0 copy-start.24
  576.6 3.0 copy-start.25
  576.6 3.0 copy-start.26
  576.6 3.0 copy-start.27
  576.6 4.5 copy-start.12
  576.6 4.5 copy-start.14
  576.7 4.5 copy-start.16
  576.7 4.5 copy-start.18
where the time goes:
time: 585 us; the launch traced here: 582 us
  local copies, waits for them, and re-layouts  382 us (65%)
  blocking collectives  104 us (18%)
  other arithmetic  53 us (9%)
  waiting for transfers between devices  18.3 us (3%)
  starting transfers between devices  15.9 us (3%)
  matrix products  8.07 us (1%)
    gather x64, local copies, waits for them, and re-layouts, body(): jnp.take(extended, neighbours[apply_order], axis=2) - term  293 us
    psum x4, blocking collectives, body(): intersection = lax.psum(partial_intersection, 'mesh')  89.9 us
    gather x4, local copies, waits for them, and re-layouts, body(): jnp.take(term, routes.reshape(-1), axis=2).reshape(2, rows, parts, capacity)  57.6 us
    select_n x4, other arithmetic, body(): jnp.take(term, routes.reshape(-1), axis=2).reshape(2, rows, parts, capacity)  39.9 us
    all_to_all x4, waiting for transfers between devices, body(): lax.all_to_all(packed, 'mesh', split_axis=2, concat_axis=2, tiled=True)  18.3 us
    concatenate x4, local copies, waits for them, and re-layouts, body(): jnp.concatenate([term, arrived.reshape(2, rows, parts * capacity)], axis=2)  16.6 us
    all_to_all x4, starting transfers between devices, body(): lax.all_to_all(packed, 'mesh', split_axis=2, concat_axis=2, tiled=True)  15.9 us
    all_gather x1, blocking collectives, body(): full_frozen = lax.all_gather(frozen, 'band', axis=1, tiled=True)  14.2 us
  transfers between devices with their start and end apart: 4, of which 3 were waited for; matrix products, arithmetic and copies ran while one was open for 2% of the time, Pallas kernels for 0%

commit v1 on v0

v1 whole, which is shorter than its diff:
```python
import functools

import jax
import jax.numpy as jnp
from jax import lax
from jax.experimental import pallas as pl
from jax.experimental.pallas import tpu as pltpu
from jax.sharding import PartitionSpec as P

TERMS = 4
REACH = 3
LANES = 128
TILE = 256

time_step = 0.3

F32, BF16 = jnp.float32, jnp.bfloat16
VMEM_LIMIT = 48 << 20


def split(value):
    high = value.astype(BF16)
    return high, (value - high.astype(F32)).astype(BF16)


def stacked(value):
    high, low = split(value)
    return jnp.concatenate([high, low], axis=0), high


def matmul(left, right):
    return lax.dot_general(left, right, (((1,), (0,)), ((), ())), preferred_element_type=F32)


def matmul_transposed(left, right):
    return lax.dot_general(left, right, (((1,), (1,)), ((), ())), preferred_element_type=F32)


def blocks_of(parts):
    if parts == 8:
        return list(range(8))
    relative = [0]
    for offset in [*range(1, REACH + 1), *range(-REACH, 0), parts // 2]:
        if offset % parts not in relative:
            relative.append(offset % parts)
    return relative


def receiver_of(me, block, parts):
    return me ^ block if parts == 8 else lax.rem(me + block, parts)


def block_of(sender, me, parts):
    if parts == 8:
        return sender ^ me
    relative = lax.rem(me - sender + parts, parts)
    result = jnp.zeros_like(relative)
    for place, block in enumerate(blocks_of(parts)):
        result = jnp.where(relative == block, place, result)
    return result


def call(kernel, out_shape, cost, *args, scalars=0):
    spaces = [pl.BlockSpec(memory_space=pltpu.SMEM if at < scalars else pltpu.VMEM) for at in range(len(args))]
    outs = [pl.BlockSpec(memory_space=pltpu.VMEM)] * len(out_shape)
    return pl.pallas_call(
        kernel,
        out_shape=[jax.ShapeDtypeStruct(shape, dtype) for shape, dtype in out_shape],
        in_specs=spaces,
        out_specs=outs,
        compiler_params=pltpu.CompilerParams(vmem_limit_bytes=VMEM_LIMIT),
        cost_estimate=pl.CostEstimate(flops=cost[0], bytes_accessed=cost[1], transcendentals=0),
    )(*args)


def pack_kernel(parts, me_ref, states_ref, routes_ref, select_ref, payload_ref):
    points = states_ref.shape[1]
    capacity = routes_ref.shape[1]
    rows = states_ref.shape[0]
    both, _ = stacked(states_ref[...])
    me = me_ref[0]
    row_id = lax.broadcasted_iota(jnp.int32, (points, capacity), 0)
    for place, block in enumerate(blocks_of(parts)):
        route = routes_ref[pl.ds(receiver_of(me, block, parts), 1), :]
        one_hot = jnp.where(row_id == route, 1.0, 0.0).astype(BF16)
        select_ref[:, pl.ds(place * capacity, capacity)] = one_hot
        if place:
            packed = matmul(both, one_hot)
            payload_ref[place - 1] = packed[:rows] + packed[rows:]


def stencil_kernel(parts, capacity, me_ref, neighbours_ref, weights_ref, potential_ref, near_high, near_low, far_high, far_low, diagonal_ref):
    count, points = neighbours_ref.shape
    me = me_ref[0]
    named = neighbours_ref[...]
    ghost = jnp.maximum(named - points, 0)
    sender = ghost // capacity
    place = block_of(sender, me, parts)
    named = jnp.where(named < points, named, points + place * capacity + (ghost - sender * capacity))
    half = 0.5 * weights_ref[...]
    diagonal_ref[...] = jnp.sum(half, axis=0, keepdims=True) + potential_ref[...]
    targets = [named[k : k + 1] for k in range(count)]
    values = [half[k : k + 1] for k in range(count)]
    for k in range(count):
        for later in range(k + 1, count):
            same = targets[k] == targets[later]
            values[k] = jnp.where(same, values[k] + values[later], values[k])
            targets[later] = jnp.where(same, -1, targets[later])
    tall = 16
    near_tiles = near_high.shape[0] // TILE
    tiles = near_tiles + far_high.shape[0] // TILE
    row_id = lax.broadcasted_iota(jnp.int32, (tall, LANES), 0).astype(F32).astype(BF16)
    zero = jnp.zeros((tall, LANES), BF16)
    for lane in range(0, points, LANES):
        at = [jnp.broadcast_to(t[:, lane : lane + LANES], (tall, LANES)) for t in targets]
        pieces = [split(jnp.broadcast_to(v[:, lane : lane + LANES], (tall, LANES))) for v in values]

        def tile_rows(high_ref, low_ref, first, tile):
            local = [
                jnp.where(a // TILE == tile, a - tile * TILE, -1).astype(F32).astype(BF16)
                for a in at
            ]
            for row in range(0, TILE, tall):
                here = row_id + jnp.asarray(row, BF16)
                high, low = zero, zero
                for k in range(count):
                    hit = local[k] == here
                    high = jnp.where(hit, pieces[k][0], high)
                    low = jnp.where(hit, pieces[k][1], low)
                start = pl.multiple_of((tile - first) * TILE + row, tall)
                high_ref[pl.ds(start, tall), lane : lane + LANES] = high
                low_ref[pl.ds(start, tall), lane : lane + LANES] = low

        @pl.loop(0, near_tiles)
        def _(tile):
            tile_rows(near_high, near_low, 0, tile)

        @pl.loop(near_tiles, tiles)
        def _(tile):
            tile_rows(far_high, far_low, near_tiles, tile)


def frozen_kernel(frozen_ref, states_ref, wide_high, wide_low, partial_ref):
    groups, _, vectors, points = frozen_ref.shape
    real = jnp.concatenate([frozen_ref[g, 0] for g in range(groups)], axis=0)
    imag = jnp.concatenate([frozen_ref[g, 1] for g in range(groups)], axis=0)
    wide = jnp.concatenate(
        [jnp.concatenate([real, imag], axis=1), jnp.concatenate([-imag, real], axis=1)], axis=0
    )
    high, low = split(wide)
    wide_high[...] = high
    wide_low[...] = low
    partial_ref[...] = intersect(states_ref[...], high, low)


def intersect(term, wide_high, wide_low):
    half = term.shape[0] // 2
    line = jnp.concatenate([term[:half], term[half:]], axis=1)
    both, high = stacked(line)
    result = matmul_transposed(both, wide_high)
    result = result[:half] + result[half:] + matmul_transposed(high, wide_low)
    columns = result.shape[1]
    if columns >= LANES:
        return result
    fold = LANES // columns
    tall = half // fold
    return jnp.concatenate([result[i * tall : (i + 1) * tall] for i in range(fold)], axis=1)


def unfold(folded, half, columns):
    if columns >= LANES:
        return folded
    fold = LANES // columns
    return jnp.concatenate([folded[:, i * columns : (i + 1) * columns] for i in range(fold)], axis=0)


def apply_exchange(total, half, wide_high, wide_low):
    both, high = stacked(unfold(total, half, wide_high.shape[0]))
    result = matmul(both, wide_high)
    result = result[:half] + result[half:] + matmul(high, wide_low)
    points = result.shape[1] // 2
    return jnp.concatenate([result[:, :points], result[:, points:]], axis=0)


def near_kernel(term_ref, select_ref, near_high, near_low, diagonal_ref, base_ref):
    rows, points = term_ref.shape
    term = term_ref[...]
    both, high = stacked(term)
    own = matmul(both, select_ref[:, : near_high.shape[0] - points])
    own_both, own_high = stacked(own[:rows] + own[rows:])
    value = matmul(both, near_high[:points]) + matmul(own_both, near_high[points:])
    low = matmul(high, near_low[:points]) + matmul(own_high, near_low[points:])
    base_ref[...] = term * diagonal_ref[...] - (value[:rows] + value[rows:] + low)


def far_kernel(order, last, first, *refs):
    if first:
        ghosts_ref, sums_ref, base_ref, total_ref, select_ref, far_high, far_low, wide_high, wide_low = refs[:9]
        outs = refs[9:]
    else:
        ghosts_ref, sums_ref, base_ref, total_ref, select_ref, far_high, far_low, wide_high, wide_low = refs[:9]
        outs = refs[9:]
    rows = base_ref.shape[0]
    half = rows // 2
    blocks = ghosts_ref.shape[0]
    capacity = ghosts_ref.shape[2]
    if first:
        sums = sums_ref[...]
    else:
        width = sums_ref.shape[1]
        sums = sums_ref[...]
        for block in range(blocks):
            sums = sums + ghosts_ref[block, rows:, :width]
    image = base_ref[...] - apply_exchange(sums, half, wide_high[...], wide_low[...])
    pieces = [stacked(ghosts_ref[block, :rows, :]) for block in range(blocks)]
    both = jnp.concatenate([piece[0] for piece in pieces], axis=1)
    high = jnp.concatenate([piece[1] for piece in pieces], axis=1)
    far = matmul(both, far_high[...])
    image = image - (far[:rows] + far[rows:] + matmul(high, far_low[...]))
    scale = time_step / order
    term = jnp.concatenate([scale * image[half:], -scale * image[:half]], axis=0)
    outs[0][...] = total_ref[...] + term
    if last:
        return
    _, term_ref, payload_ref, partial_ref = outs
    term_ref[...] = term
    both, _ = stacked(term)
    partial = intersect(term, wide_high[...], wide_low[...])
    partial_ref[...] = partial
    tall, width = partial.shape
    if width < capacity:
        partial = jnp.concatenate([partial, jnp.zeros((tall, capacity - width), F32)], axis=1)
    for block in range(blocks):
        packed = matmul(both, select_ref[:, pl.ds((block + 1) * capacity, capacity)])
        payload_ref[block, :rows, :] = packed[:rows] + packed[rows:]
        payload_ref[block, rows:, :] = partial


def swap(value, bits, parts):
    return lax.ppermute(value, "mesh", [(part, part ^ bits) for part in range(parts)])


def exchange(payload, parts):
    if parts == 8:
        across = [
            swap(payload[2 * chip - 1 : 2 * chip + 1], 2 * chip, parts) for chip in range(1, 4)
        ]
        passed = jnp.concatenate([payload[:1]] + [block[1:] for block in across], axis=0)
        passed = swap(passed, 1, parts)
        order = [passed[:1]]
        for chip in range(3):
            order += [across[chip][:1], passed[chip + 1 : chip + 2]]
        return jnp.concatenate(order, axis=0)
    arrived = [
        lax.ppermute(payload[at], "mesh", [(part, (part + block) % parts) for part in range(parts)])
        for at, block in enumerate(blocks_of(parts)[1:])
    ]
    return jnp.stack(arrived)


def add_up(partial, parts):
    if parts == 8:
        pair = partial + swap(partial, 1, parts)
        return pair + swap(pair, 2, parts) + swap(pair, 4, parts) + swap(pair, 6, parts)
    return lax.psum(partial, "mesh")


def gather_frozen(frozen):
    bands = lax.axis_size("band")
    if bands <= 4:
        pieces = [frozen]
        for step in range(1, bands):
            pieces.append(lax.ppermute(frozen, "band", [(at, (at + step) % bands) for at in range(bands)]))
        return jnp.stack(pieces)
    return lax.all_gather(frozen, "band", axis=0, tiled=False)


def body(states, frozen, weights, potential, send_list, neighbours):
    parts = lax.axis_size("mesh")
    points = states.shape[2]
    rows = 2 * states.shape[1]
    capacity = send_list.shape[2]
    places = len(blocks_of(parts))
    me = lax.axis_index("mesh").astype(jnp.int32).reshape(1)
    field = states.reshape(rows, points)
    routes = send_list[0]

    select, payload = call(
        functools.partial(pack_kernel, parts),
        [((points, places * capacity), BF16), ((places - 1, rows, capacity), F32)],
        (4 * rows * points * places * capacity, 4 << 20),
        me, field, routes, scalars=1,
    )
    ghosts = exchange(payload, parts)
    full_frozen = gather_frozen(frozen)
    near_rows, far_rows = points + capacity, (places - 1) * capacity
    near_high, near_low, far_high, far_low, diagonal = call(
        functools.partial(stencil_kernel, parts, capacity),
        [((near_rows, points), BF16)] * 2 + [((far_rows, points), BF16)] * 2 + [((1, points), F32)],
        (6 * (near_rows + far_rows) * points, 12 << 20),
        me, neighbours, weights, potential.reshape(1, points), scalars=1,
    )
    vectors = full_frozen.shape[0] * full_frozen.shape[2]
    columns = 2 * vectors
    half = rows // 2
    sum_shape = (half, columns) if columns >= LANES else (half * columns // LANES, LANES)
    wide_high, wide_low, partial = call(
        frozen_kernel,
        [((columns, 2 * points), BF16)] * 2 + [(sum_shape, F32)],
        (6 * columns * points * rows, 2 << 20),
        full_frozen, field,
    )
    sums = add_up(partial, parts)
    total, term = field, field
    for order in range(1, TERMS + 1):
        (base,) = call(
            near_kernel,
            [((rows, points), F32)],
            (6 * rows * points * near_rows, 8 << 20),
            term, select, near_high, near_low, diagonal,
        )
        last = order == TERMS
        shapes = [((rows, points), F32)]
        if not last:
            shapes += [
                ((rows, points), F32),
                ((places - 1, rows + sum_shape[0], capacity), F32),
                (sum_shape, F32),
            ]
        outs = call(
            functools.partial(far_kernel, order, last, order == 1),
            shapes,
            (6 * rows * points * far_rows, 12 << 20),
            ghosts, sums, base, total, select, far_high, far_low, wide_high, wide_low,
        )
        total = outs[0]
        if not last:
            _, term, payload, sums = outs
            ghosts = exchange(payload, parts)
    return total.reshape(states.shape)


def solution(mesh):
    return jax.shard_map(
        body,
        mesh=mesh,
        in_specs=(
            P(None, "band", "mesh"),
            P(None, "band", "mesh"),
            P(None, "mesh"),
            P("mesh"),
            P("mesh", None, None),
            P(None, "mesh"),
        ),
        out_specs=P(None, "band", "mesh"),
        check_vma=False,
    )
```

time: 585 us -> 99.3 us (0.17)
  local copies, waits for them, and re-layouts: 382 us -> 7.03 us
  blocking collectives: 104 us -> 0 us
  other arithmetic: 53 us -> 0.92 us
  Pallas kernels: 0 us -> 49.3 us
  starting transfers between devices: 15.9 us -> 24.1 us
  matrix products: 8.07 us -> 0 us
    gather x68 -> x0, local copies, waits for them, and re-layouts: 351 us -> none  [the longest x64 293 us: body(): jnp.take(extended, neighbours[apply_order], axis=2) - term]
    psum x4 -> x0, blocking collectives: 89.9 us -> none  [body(): intersection = lax.psum(partial_intersection, 'mesh')]
    pallas_call x0 -> x11, Pallas kernels: none -> 49.3 us  [call(): pl.pallas_call(kernel, out_shape=[jax.ShapeDtypeStruct(shape, dtype) for...]
    select_n x4 -> x0, other arithmetic: 39.9 us -> none  [body(): jnp.take(term, routes.reshape(-1), axis=2).reshape(2, rows, parts, capacity)]
    ppermute x0 -> x23, starting transfers between devices: none -> 24.1 us  [the longest x20 18.1 us: swap(): lax.ppermute(value, 'mesh', [(part, part ^ bits) for part in range(parts)])]
    all_to_all x4 -> x0, waiting for transfers between devices: 18.3 us -> none  [body(): lax.all_to_all(packed, 'mesh', split_axis=2, concat_axis=2, tiled=True)]
    ppermute x0 -> x23, waiting for transfers between devices: none -> 16.8 us  [the longest x20 16.8 us: swap(): lax.ppermute(value, 'mesh', [(part, part ^ bits) for part in range(parts)])]
    concatenate x4, local copies, waits for them, and re-layouts: 16.6 us -> 0.02 us  [exchange(): return jnp.concatenate(order, axis=0)]
  transfers between devices with their start and end apart: 4 -> 23, of which waited for: 3 -> 12; matrix products, arithmetic and copies ran while one was open for 2% -> 1% of each run, Pallas kernels for 0% -> 27%
where the time goes in v1:
time: 99.3 us; the launch traced here: 98.8 us
  Pallas kernels  49.3 us (50%)
  starting transfers between devices  24.1 us (24%)
  waiting for transfers between devices  16.8 us (17%)
  local copies, waits for them, and re-layouts  7.03 us (7%)
    pallas_call x11, Pallas kernels, call(): pl.pallas_call(kernel, out_shape=[jax.ShapeDtypeStruct(shape, dtype) for...  49.3 us
    ppermute x20, starting transfers between devices, swap(): lax.ppermute(value, 'mesh', [(part, part ^ bits) for part in range(parts)])  18.1 us
    ppermute x20, waiting for transfers between devices, swap(): lax.ppermute(value, 'mesh', [(part, part ^ bits) for part in range(parts)])  16.8 us
    unnamed x40, local copies, waits for them, and re-layouts  6.83 us
    ppermute x3, starting transfers between devices, gather_frozen(): lax.ppermute(frozen, 'band', [(at, (at + step) % bands) for at in range(b...  6.06 us
  transfers between devices with their start and end apart: 23, of which 12 were waited for; matrix products, arithmetic and copies ran while one was open for 1% of the time, Pallas kernels for 27%

profile of v1, /device:TPU:0, one launch (start us, length us, event | category | flops | bytes accessed | tf_op | source)
XLA Modules:
  0.0 98.8 jit_solution(870877500112268753)
XLA Ops:
  0.0 3.0 %collective-permute-start.4 = (f32[2,8,1024]{2,1,0:T(8,128)}, f32[2,8,1024]{2,1,0:T(8,128)S(1)}, u32[]{:S(2)}, u32[]{:S(2)}) collective-permute-start(f32[2,8,1024]{2,1,0:T(8,128)} %param.7), channel_id=1, source_target_pairs={{0,1},{1,2},{2,3},{3,0},{4,5},{5,6},{6,7},{7,4},{8,9},{9,10},{10,1... | collective-permute-start | bytes 196616 | tf_op jit(solution)/shard_map/ppermute | solution.py:273
  3.0 2.0 %collective-permute-start.6 = (f32[2,8,1024]{2,1,0:T(8,128)}, f32[2,8,1024]{2,1,0:T(8,128)S(1)}, u32[]{:S(2)}, u32[]{:S(2)}) collective-permute-start(f32[2,8,1024]{2,1,0:T(8,128)} %param.7), channel_id=1, source_target_pairs={{0,3},{1,0},{2,1},{3,2},{4,7},{5,4},{6,5},{7,6},{8,11},{9,8},{10,9... | collective-permute-start | bytes 196616 | tf_op jit(solution)/shard_map/ppermute | solution.py:273
  5.1 1.0 %collective-permute-start.5 = (f32[2,8,1024]{2,1,0:T(8,128)}, f32[2,8,1024]{2,1,0:T(8,128)S(1)}, u32[]{:S(2)}, u32[]{:S(2)}) collective-permute-start(f32[2,8,1024]{2,1,0:T(8,128)} %param.7), channel_id=1, source_target_pairs={{0,2},{1,3},{2,0},{3,1},{4,6},{5,7},{6,4},{7,5},{8,10},{9,11},{10,... | collective-permute-start | bytes 196616 | tf_op jit(solution)/shard_map/ppermute | solution.py:273
  6.1 0.9 copy-done.2
  7.0 0.7 copy-done.7
  7.7 1.2 %shard_map.64 = (bf16[1024,2048]{1,0:T(8,128)(2,1)S(1)}, f32[7,32,256]{2,1,0:T(8,128)S(1)}) custom-call(s32[1]{0:T(128)} %bitcast.me_ref, f32[32,1024]{1,0:T(8,128)S(1)} %bitcast.9, s32[8,256]{1,0:T(8,128)S(1)} %bitcast.14), custom_call_target="tpu_custom_call" | custom-call | flops 268435456 | bytes 4194304 | tf_op jit(solution)/shard_map/pallas_call | solution.py:66
  8.8 2.0 %copy-done = bf16[1024,2048]{1,0:T(8,128)(2,1)} copy-done((bf16[1024,2048]{1,0:T(8,128)(2,1)}, bf16[1024,2048]{1,0:T(8,128)(2,1)S(1)}, u32[]{:S(2)}) %copy-start) | copy-done | bytes 4194328
  10.9 1.6 %collective-permute-start = (f32[2,32,256]{2,1,0:T(8,128)S(1)}, f32[2,32,256]{2,1,0:T(8,128)S(1)}, u32[]{:S(2)}, u32[]{:S(2)}) collective-permute-start(f32[2,32,256]{2,1,0:T(8,128)S(1)} %get-tuple-element.58), channel_id=1, source_target_pairs={{0,8},{4,12},{8,0},{12,4},{16,24},{20,28},{24,16},{28,20},{1,9},{5... | collective-permute-start | bytes 196616 | tf_op jit(solution)/shard_map/ppermute | solution.py:240
  12.4 1.5 %collective-permute-start.2 = (f32[2,32,256]{2,1,0:T(8,128)S(1)}, f32[2,32,256]{2,1,0:T(8,128)S(1)}, u32[]{:S(2)}, u32[]{:S(2)}) collective-permute-start(f32[2,32,256]{2,1,0:T(8,128)S(1)} %get-tuple-element.59), channel_id=1, source_target_pairs={{0,24},{4,28},{8,16},{12,20},{16,8},{20,12},{24,0},{28,4},{1,25},{... | collective-permute-start | bytes 196616 | tf_op jit(solution)/shard_map/ppermute | solution.py:240
  13.9 0.8 copy-done.4
  14.7 0.8 copy-done.5
  15.4 0.7 copy-done.6
  16.1 11.6 %shard_map.66 = (bf16[1280,1024]{1,0:T(8,128)(2,1)S(1)}, bf16[1280,1024]{1,0:T(8,128)(2,1)S(1)}, bf16[1792,1024]{1,0:T(8,128)(2,1)}, bf16[1792,1024]{1,0:T(8,128)(2,1)}, f32[1,1024]{1,0:T(1,128)S(1)}) custom-call(s32[1]{0:T(128)} %bitcast.me_ref, s32[8,1024]{1,0:T(8,128)S(1)} %copy-done.4, f32[8,1024]{1,0:T(8,128)S(1)} %copy-done.5, f32[1,1024]{1,0:T(1,128)S(1)} %bitcast.13), custom_call_target="tpu_custom_call" | custom-call | flops 18874368 | bytes 12582912 | tf_op jit(solution)/shard_map/pallas_call | solution.py:66
  27.7 0.0 collective-permute-done.4
  27.7 0.5 collective-permute-start.1
  28.2 0.0 collective-permute-done.6
  28.2 0.0 collective-permute-done.5
  28.2 0.9 pad_maximum_fusion.frozen_ref
  29.1 0.0 copy-start.3
  29.1 0.9 copy-done.3
  30.0 0.3 shard_map.65
  30.3 0.0 collective-permute-start.7
  30.3 3.5 %shard_map.67.refs_2_ = f32[32,1024]{1,0:T(8,128)S(1)} custom-call(f32[32,1024]{1,0:T(8,128)S(1)} %bitcast.11, bf16[1024,2048]{1,0:T(8,128)(2,1)} %copy-done, bf16[1280,1024]{1,0:T(8,128)(2,1)S(1)} %get-tuple-element.30.near_high, bf16[1280,1024]{1,0:T(8,128)(2,1)S(1)} %get-tuple-element.31.near_low, f32[1,1024]{1,0:T(1,128)S(1)} %get-tuple-element.32.diagonal_ref), custom_call_target="tpu_custom_call" | custom-call | flops 251658240 | bytes 8388608 | tf_op jit(solution)/shard_map/pallas_call | solution.py:66
  33.9 0.0 collective-permute-done
  33.9 0.0 collective-permute-done.1
  33.9 0.0 collective-permute-done.7
  34.0 2.5 %collective-permute-start.10 = (f32[8,128]{1,0:T(8,128)S(1)}, f32[8,128]{1,0:T(8,128)S(1)}, u32[]{:S(2)}, u32[]{:S(2)}) collective-permute-start(f32[8,128]{1,0:T(8,128)S(1)} %add.12), channel_id=1, source_target_pairs={{0,24},{4,28},{8,16},{12,20},{16,8},{20,12},{24,0},{28,4},{1,25},{... | collective-permute-start | bytes 12296 | tf_op jit(solution)/shard_map/ppermute | solution.py:240
  36.5 0.5 collective-permute-start.9
  37.0 0.5 collective-permute-start.8
  37.5 0.1 collective-permute-start.3
  37.6 0.9 collective-permute-done.10
  38.5 1.6 %collective-permute-done.9 = f32[8,128]{1,0:T(8,128)S(1)} collective-permute-done((f32[8,128]{1,0:T(8,128)S(1)}, f32[8,128]{1,0:T(8,128)S(1)}, u32[]{:S(2)}, u32[]{:S(2)}) %collective-permute-start.9) | collective-permute-done | bytes 4128 | tf_op jit(solution)/shard_map/ppermute | solution.py:240
  40.1 0.5 collective-permute-done.8
  40.7 5.7 %shard_map.68 = (f32[32,1024]{1,0:T(8,128)S(1)}, f32[32,1024]{1,0:T(8,128)S(1)}, f32[7,40,256]{2,1,0:T(8,128)S(1)}, f32[8,128]{1,0:T(8,128)S(1)}) custom-call(f32[7,32,256]{2,1,0:T(8,128)S(1)} %constant_dynamic-update-slice_fusion.refs_0_, f32[8,128]{1,0:T(8,128)S(1)} %add_add_fusion.refs_1_, f32[32,1024]{1,0:T(8,128)S(1)} %shard_map.67.refs_2_, ...), custom_call_target="tpu_custom_call" | custom-call | flops 352321536 | bytes 12582912 | tf_op jit(solution)/shard_map/pallas_call | solution.py:66
  46.5 0.6 collective-permute-start.11
  47.1 2.4 %collective-permute-start.13 = (f32[2,40,256]{2,1,0:T(8,128)S(1)}, f32[2,40,256]{2,1,0:T(8,128)S(1)}, u32[]{:S(2)}, u32[]{:S(2)}) collective-permute-start(f32[2,40,256]{2,1,0:T(8,128)S(1)} %get-tuple-element.56), channel_id=1, source_target_pairs={{0,24},{4,28},{8,16},{12,20},{16,8},{20,12},{24,0},{28,4},{1,25},{... | collective-permute-start | bytes 245768 | tf_op jit(solution)/shard_map/ppermute | solution.py:240
  49.5 0.5 collective-permute-start.12
  50.0 1.5 %collective-permute-done.11 = f32[2,40,256]{2,1,0:T(8,128)S(1)} collective-permute-done((f32[2,40,256]{2,1,0:T(8,128)S(1)}, f32[2,40,256]{2,1,0:T(8,128)S(1)}, u32[]{:S(2)}, u32[]{:S(2)}) %collective-permute-start.11) | collective-permute-done | bytes 81952 | tf_op jit(solution)/shard_map/ppermute | solution.py:240
  51.5 1.3 %collective-permute-done.13 = f32[2,40,256]{2,1,0:T(8,128)S(1)} collective-permute-done((f32[2,40,256]{2,1,0:T(8,128)S(1)}, f32[2,40,256]{2,1,0:T(8,128)S(1)}, u32[]{:S(2)}, u32[]{:S(2)}) %collective-permute-start.13) | collective-permute-done | bytes 81952 | tf_op jit(solution)/shard_map/ppermute | solution.py:240
  52.8 1.1 %collective-permute-done.12 = f32[2,40,256]{2,1,0:T(8,128)S(1)} collective-permute-done((f32[2,40,256]{2,1,0:T(8,128)S(1)}, f32[2,40,256]{2,1,0:T(8,128)S(1)}, u32[]{:S(2)}, u32[]{:S(2)}) %collective-permute-start.12) | collective-permute-done | bytes 81952 | tf_op jit(solution)/shard_map/ppermute | solution.py:240
  54.0 0.1 collective-permute-start.14
  54.0 3.4 %shard_map.69.refs_2_ = f32[32,1024]{1,0:T(8,128)S(1)} custom-call(f32[32,1024]{1,0:T(8,128)S(1)} %get-tuple-element.39.term_ref, bf16[1024,2048]{1,0:T(8,128)(2,1)} %copy-done, bf16[1280,1024]{1,0:T(8,128)(2,1)S(1)} %get-tuple-element.30.near_high, bf16[1280,1024]{1,0:T(8,128)(2,1)S(1)} %get-tuple-element.31.near_low, ...), custom_call_target="tpu_custom_call" | custom-call | flops 251658240 | bytes 8388608 | tf_op jit(solution)/shard_map/pallas_call | solution.py:66
  57.4 0.0 collective-permute-done.14
  57.5 5.7 %shard_map.70 = (f32[32,1024]{1,0:T(8,128)S(1)}, f32[32,1024]{1,0:T(8,128)S(1)}, f32[7,40,256]{2,1,0:T(8,128)S(1)}, f32[8,128]{1,0:T(8,128)S(1)}) custom-call(f32[7,40,256]{2,1,0:T(8,128)S(1)} %constant_dynamic-update-slice_fusion.7.refs_0_, f32[8,128]{1,0:T(8,128)S(1)} %get-tuple-element.38.refs_1_, f32[32,1024]{1,0:T(8,128)S(1)} %shard_map.69.refs_2_, ...), custom_call_target="tpu_custom_call" | custom-call | flops 352321536 | bytes 12582912 | tf_op jit(solution)/shard_map/pallas_call | solution.py:66
  63.3 0.9 collective-permute-start.15
  64.2 1.5 %collective-permute-start.17 = (f32[2,40,256]{2,1,0:T(8,128)S(1)}, f32[2,40,256]{2,1,0:T(8,128)S(1)}, u32[]{:S(2)}, u32[]{:S(2)}) collective-permute-start(f32[2,40,256]{2,1,0:T(8,128)S(1)} %get-tuple-element.53), channel_id=1, source_target_pairs={{0,24},{4,28},{8,16},{12,20},{16,8},{20,12},{24,0},{28,4},{1,25},{... | collective-permute-start | bytes 245768 | tf_op jit(solution)/shard_map/ppermute | solution.py:240
  65.7 1.2 %collective-permute-start.16 = (f32[2,40,256]{2,1,0:T(8,128)S(1)}, f32[2,40,256]{2,1,0:T(8,128)S(1)}, u32[]{:S(2)}, u32[]{:S(2)}) collective-permute-start(f32[2,40,256]{2,1,0:T(8,128)S(1)} %get-tuple-element.54), channel_id=1, source_target_pairs={{0,16},{4,20},{8,24},{12,28},{16,0},{20,4},{24,8},{28,12},{1,17},{... | collective-permute-start | bytes 245768 | tf_op jit(solution)/shard_map/ppermute | solution.py:240
  66.8 1.7 %collective-permute-done.15 = f32[2,40,256]{2,1,0:T(8,128)S(1)} collective-permute-done((f32[2,40,256]{2,1,0:T(8,128)S(1)}, f32[2,40,256]{2,1,0:T(8,128)S(1)}, u32[]{:S(2)}, u32[]{:S(2)}) %collective-permute-start.15) | collective-permute-done | bytes 81952 | tf_op jit(solution)/shard_map/ppermute | solution.py:240
  68.6 1.8 %collective-permute-done.17 = f32[2,40,256]{2,1,0:T(8,128)S(1)} collective-permute-done((f32[2,40,256]{2,1,0:T(8,128)S(1)}, f32[2,40,256]{2,1,0:T(8,128)S(1)}, u32[]{:S(2)}, u32[]{:S(2)}) %collective-permute-start.17) | collective-permute-done | bytes 81952 | tf_op jit(solution)/shard_map/ppermute | solution.py:240
  70.4 1.3 %collective-permute-done.16 = f32[2,40,256]{2,1,0:T(8,128)S(1)} collective-permute-done((f32[2,40,256]{2,1,0:T(8,128)S(1)}, f32[2,40,256]{2,1,0:T(8,128)S(1)}, u32[]{:S(2)}, u32[]{:S(2)}) %collective-permute-start.16) | collective-permute-done | bytes 81952 | tf_op jit(solution)/shard_map/ppermute | solution.py:240
  71.7 0.1 collective-permute-start.18
  71.8 3.3 %shard_map.71.refs_2_ = f32[32,1024]{1,0:T(8,128)S(1)} custom-call(f32[32,1024]{1,0:T(8,128)S(1)} %get-tuple-element.43.term_ref, bf16[1024,2048]{1,0:T(8,128)(2,1)} %copy-done, bf16[1280,1024]{1,0:T(8,128)(2,1)S(1)} %get-tuple-element.30.near_high, bf16[1280,1024]{1,0:T(8,128)(2,1)S(1)} %get-tuple-element.31.near_low, ...), custom_call_target="tpu_custom_call" | custom-call | flops 251658240 | bytes 8388608 | tf_op jit(solution)/shard_map/pallas_call | solution.py:66
  75.1 0.0 collective-permute-done.18
  75.2 5.7 %shard_map.72 = (f32[32,1024]{1,0:T(8,128)S(1)}, f32[32,1024]{1,0:T(8,128)S(1)}, f32[7,40,256]{2,1,0:T(8,128)S(1)}, f32[8,128]{1,0:T(8,128)S(1)}) custom-call(f32[7,40,256]{2,1,0:T(8,128)S(1)} %constant_dynamic-update-slice_fusion.14.refs_0_, f32[8,128]{1,0:T(8,128)S(1)} %get-tuple-element.42.refs_1_, f32[32,1024]{1,0:T(8,128)S(1)} %shard_map.71.refs_2_, ...), custom_call_target="tpu_custom_call" | custom-call | flops 352321536 | bytes 12582912 | tf_op jit(solution)/shard_map/pallas_call | solution.py:66
  81.0 1.1 %collective-permute-start.19 = (f32[2,40,256]{2,1,0:T(8,128)S(1)}, f32[2,40,256]{2,1,0:T(8,128)S(1)}, u32[]{:S(2)}, u32[]{:S(2)}) collective-permute-start(f32[2,40,256]{2,1,0:T(8,128)S(1)} %get-tuple-element.49), channel_id=1, source_target_pairs={{0,8},{4,12},{8,0},{12,4},{16,24},{20,28},{24,16},{28,20},{1,9},{5... | collective-permute-start | bytes 245768 | tf_op jit(solution)/shard_map/ppermute | solution.py:240
  82.1 1.6 %collective-permute-start.21 = (f32[2,40,256]{2,1,0:T(8,128)S(1)}, f32[2,40,256]{2,1,0:T(8,128)S(1)}, u32[]{:S(2)}, u32[]{:S(2)}) collective-permute-start(f32[2,40,256]{2,1,0:T(8,128)S(1)} %get-tuple-element.50), channel_id=1, source_target_pairs={{0,24},{4,28},{8,16},{12,20},{16,8},{20,12},{24,0},{28,4},{1,25},{... | collective-permute-start | bytes 245768 | tf_op jit(solution)/shard_map/ppermute | solution.py:240
  83.7 0.9 collective-permute-start.20
  84.6 1.7 %collective-permute-done.19 = f32[2,40,256]{2,1,0:T(8,128)S(1)} collective-permute-done((f32[2,40,256]{2,1,0:T(8,128)S(1)}, f32[2,40,256]{2,1,0:T(8,128)S(1)}, u32[]{:S(2)}, u32[]{:S(2)}) %collective-permute-start.19) | collective-permute-done | bytes 81952 | tf_op jit(solution)/shard_map/ppermute | solution.py:240
  86.3 2.1 %collective-permute-done.21 = f32[2,40,256]{2,1,0:T(8,128)S(1)} collective-permute-done((f32[2,40,256]{2,1,0:T(8,128)S(1)}, f32[2,40,256]{2,1,0:T(8,128)S(1)}, u32[]{:S(2)}, u32[]{:S(2)}) %collective-permute-start.21) | collective-permute-done | bytes 81952 | tf_op jit(solution)/shard_map/ppermute | solution.py:240
  88.4 1.3 %collective-permute-done.20 = f32[2,40,256]{2,1,0:T(8,128)S(1)} collective-permute-done((f32[2,40,256]{2,1,0:T(8,128)S(1)}, f32[2,40,256]{2,1,0:T(8,128)S(1)}, u32[]{:S(2)}, u32[]{:S(2)}) %collective-permute-start.20) | collective-permute-done | bytes 81952 | tf_op jit(solution)/shard_map/ppermute | solution.py:240
  89.7 0.1 collective-permute-start.22
  89.8 3.3 %shard_map.73.refs_2_ = f32[32,1024]{1,0:T(8,128)S(1)} custom-call(f32[32,1024]{1,0:T(8,128)S(1)} %get-tuple-element.47.term_ref, bf16[1024,2048]{1,0:T(8,128)(2,1)} %copy-done, bf16[1280,1024]{1,0:T(8,128)(2,1)S(1)} %get-tuple-element.30.near_high, bf16[1280,1024]{1,0:T(8,128)(2,1)S(1)} %get-tuple-element.31.near_low, ...), custom_call_target="tpu_custom_call" | custom-call | flops 251658240 | bytes 8388608 | tf_op jit(solution)/shard_map/pallas_call | solution.py:66
  93.1 0.0 collective-permute-done.22
  93.3 5.5 %shard_map.74 = f32[32,1024]{1,0:T(8,128)} custom-call(f32[7,40,256]{2,1,0:T(8,128)S(1)} %constant_dynamic-update-slice_fusion.21.refs_0_, f32[8,128]{1,0:T(8,128)S(1)} %get-tuple-element.46.refs_1_, f32[32,1024]{1,0:T(8,128)S(1)} %shard_map.73.refs_2_, f32[32,1024]{1,0:T(8,128)S(1)} %get-tuple-element.48.refs_3_, bf16[1024,2048]{1,0:T(8,128)(2,1)} %copy-done, ...), custom_call_target="tpu_custom_call" | custom-call | flops 352321536 | bytes 12582912 | tf_op jit(solution)/shard_map/pallas_call | solution.py:66
  (64 shorter events, 0.4 us)
Async XLA Ops:
  0.0 27.7 %collective-permute-start.4 = (f32[2,8,1024]{2,1,0:T(8,128)}, f32[2,8,1024]{2,1,0:T(8,128)S(1)}, u32[]{:S(2)}, u32[]{:S(2)}) collective-permute-start(f32[2,8,1024]{2,1,0:T(8,128)} %param.7), channel_id=1, source_target_pairs={{0,1},{1,2},{2,3},{3,0},{4,5},{5,6},{6,7},{7,4},{8,9},{9,10},{10,1... | collective-permute-start | bytes 196616 | tf_op jit(solution)/shard_map/ppermute | solution.py:273
  3.0 25.2 %collective-permute-start.6 = (f32[2,8,1024]{2,1,0:T(8,128)}, f32[2,8,1024]{2,1,0:T(8,128)S(1)}, u32[]{:S(2)}, u32[]{:S(2)}) collective-permute-start(f32[2,8,1024]{2,1,0:T(8,128)} %param.7), channel_id=1, source_target_pairs={{0,3},{1,0},{2,1},{3,2},{4,7},{5,4},{6,5},{7,6},{8,11},{9,8},{10,9... | collective-permute-start | bytes 196616 | tf_op jit(solution)/shard_map/ppermute | solution.py:273
  5.1 23.2 %collective-permute-start.5 = (f32[2,8,1024]{2,1,0:T(8,128)}, f32[2,8,1024]{2,1,0:T(8,128)S(1)}, u32[]{:S(2)}, u32[]{:S(2)}) collective-permute-start(f32[2,8,1024]{2,1,0:T(8,128)} %param.7), channel_id=1, source_target_pairs={{0,2},{1,3},{2,0},{3,1},{4,6},{5,7},{6,4},{7,5},{8,10},{9,11},{10,... | collective-permute-start | bytes 196616 | tf_op jit(solution)/shard_map/ppermute | solution.py:273
  6.1 0.9 copy-start.2
  7.0 0.7 copy-start.7
  8.8 2.0 %copy-start = (bf16[1024,2048]{1,0:T(8,128)(2,1)}, bf16[1024,2048]{1,0:T(8,128)(2,1)S(1)}, u32[]{:S(2)}) copy-start(bf16[1024,2048]{1,0:T(8,128)(2,1)S(1)} %get-tuple-element.29.select_ref.refs_4_) | copy-start | bytes 12582916
  10.9 23.0 %collective-permute-start = (f32[2,32,256]{2,1,0:T(8,128)S(1)}, f32[2,32,256]{2,1,0:T(8,128)S(1)}, u32[]{:S(2)}, u32[]{:S(2)}) collective-permute-start(f32[2,32,256]{2,1,0:T(8,128)S(1)} %get-tuple-element.58), channel_id=1, source_target_pairs={{0,8},{4,12},{8,0},{12,4},{16,24},{20,28},{24,16},{28,20},{1,9},{5... | collective-permute-start | bytes 196616 | tf_op jit(solution)/shard_map/ppermute | solution.py:240
  12.4 21.5 %collective-permute-start.2 = (f32[2,32,256]{2,1,0:T(8,128)S(1)}, f32[2,32,256]{2,1,0:T(8,128)S(1)}, u32[]{:S(2)}, u32[]{:S(2)}) collective-permute-start(f32[2,32,256]{2,1,0:T(8,128)S(1)} %get-tuple-element.59), channel_id=1, source_target_pairs={{0,24},{4,28},{8,16},{12,20},{16,8},{20,12},{24,0},{28,4},{1,25},{... | collective-permute-start | bytes 196616 | tf_op jit(solution)/shard_map/ppermute | solution.py:240
  13.9 0.8 copy-start.4
  14.7 0.8 copy-start.5
  15.4 0.7 copy-start.6
  27.7 6.2 %collective-permute-start.1 = (f32[2,32,256]{2,1,0:T(8,128)S(1)}, f32[2,32,256]{2,1,0:T(8,128)S(1)}, u32[]{:S(2)}, u32[]{:S(2)}) collective-permute-start(f32[2,32,256]{2,1,0:T(8,128)S(1)} %get-tuple-element.60), channel_id=1, source_target_pairs={{0,16},{4,20},{8,24},{12,28},{16,0},{20,4},{24,8},{28,12},{1,17},{... | collective-permute-start | bytes 196616 | tf_op jit(solution)/shard_map/ppermute | solution.py:240
  29.1 0.9 copy-start.3
  30.3 3.6 %collective-permute-start.7 = (f32[8,128]{1,0:T(8,128)S(1)}, f32[8,128]{1,0:T(8,128)S(1)}, u32[]{:S(2)}, u32[]{:S(2)}) collective-permute-start(f32[8,128]{1,0:T(8,128)S(1)} %get-tuple-element.28), channel_id=1, source_target_pairs={{0,4},{4,0},{8,12},{12,8},{16,20},{20,16},{24,28},{28,24},{1,5},{5... | collective-permute-start | bytes 12296 | tf_op jit(solution)/shard_map/ppermute | solution.py:240
  30.3 10.4 %copy-start.1 = (bf16[1792,1024]{1,0:T(8,128)(2,1)S(1)}, bf16[1792,1024]{1,0:T(8,128)(2,1)}, u32[]{:S(2)}) copy-start(bf16[1792,1024]{1,0:T(8,128)(2,1)} %get-tuple-element.33.refs_5_) | copy-start | bytes 11010052
  34.0 4.6 %collective-permute-start.10 = (f32[8,128]{1,0:T(8,128)S(1)}, f32[8,128]{1,0:T(8,128)S(1)}, u32[]{:S(2)}, u32[]{:S(2)}) collective-permute-start(f32[8,128]{1,0:T(8,128)S(1)} %add.12), channel_id=1, source_target_pairs={{0,24},{4,28},{8,16},{12,20},{16,8},{20,12},{24,0},{28,4},{1,25},{... | collective-permute-start | bytes 12296 | tf_op jit(solution)/shard_map/ppermute | solution.py:240
  36.5 3.6 %collective-permute-start.9 = (f32[8,128]{1,0:T(8,128)S(1)}, f32[8,128]{1,0:T(8,128)S(1)}, u32[]{:S(2)}, u32[]{:S(2)}) collective-permute-start(f32[8,128]{1,0:T(8,128)S(1)} %add.12), channel_id=1, source_target_pairs={{0,16},{4,20},{8,24},{12,28},{16,0},{20,4},{24,8},{28,12},{1,17},{... | collective-permute-start | bytes 12296 | tf_op jit(solution)/shard_map/ppermute | solution.py:240
  37.0 3.6 %collective-permute-start.8 = (f32[8,128]{1,0:T(8,128)S(1)}, f32[8,128]{1,0:T(8,128)S(1)}, u32[]{:S(2)}, u32[]{:S(2)}) collective-permute-start(f32[8,128]{1,0:T(8,128)S(1)} %add.12), channel_id=1, source_target_pairs={{0,8},{4,12},{8,0},{12,4},{16,24},{20,28},{24,16},{28,20},{1,9},{5... | collective-permute-start | bytes 12296 | tf_op jit(solution)/shard_map/ppermute | solution.py:240
  37.5 3.1 %collective-permute-start.3 = (f32[4,32,256]{2,1,0:T(8,128)S(1)}, f32[4,32,256]{2,1,0:T(8,128)S(1)}, u32[]{:S(2)}, u32[]{:S(2)}) collective-permute-start(f32[4,32,256]{2,1,0:T(8,128)S(1)} %pad_maximum_fusion.4), channel_id=1, source_target_pairs={{0,4},{4,0},{8,12},{12,8},{16,20},{20,16},{24,28},{28,24},{1,5},{5... | collective-permute-start | bytes 393224 | tf_op jit(solution)/shard_map/ppermute | solution.py:240
  46.5 5.1 %collective-permute-start.11 = (f32[2,40,256]{2,1,0:T(8,128)S(1)}, f32[2,40,256]{2,1,0:T(8,128)S(1)}, u32[]{:S(2)}, u32[]{:S(2)}) collective-permute-start(f32[2,40,256]{2,1,0:T(8,128)S(1)} %get-tuple-element.55), channel_id=1, source_target_pairs={{0,8},{4,12},{8,0},{12,4},{16,24},{20,28},{24,16},{28,20},{1,9},{5... | collective-permute-start | bytes 245768 | tf_op jit(solution)/shard_map/ppermute | solution.py:240
  47.1 5.7 %collective-permute-start.13 = (f32[2,40,256]{2,1,0:T(8,128)S(1)}, f32[2,40,256]{2,1,0:T(8,128)S(1)}, u32[]{:S(2)}, u32[]{:S(2)}) collective-permute-start(f32[2,40,256]{2,1,0:T(8,128)S(1)} %get-tuple-element.56), channel_id=1, source_target_pairs={{0,24},{4,28},{8,16},{12,20},{16,8},{20,12},{24,0},{28,4},{1,25},{... | collective-permute-start | bytes 245768 | tf_op jit(solution)/shard_map/ppermute | solution.py:240
  49.5 4.4 %collective-permute-start.12 = (f32[2,40,256]{2,1,0:T(8,128)S(1)}, f32[2,40,256]{2,1,0:T(8,128)S(1)}, u32[]{:S(2)}, u32[]{:S(2)}) collective-permute-start(f32[2,40,256]{2,1,0:T(8,128)S(1)} %get-tuple-element.57), channel_id=1, source_target_pairs={{0,16},{4,20},{8,24},{12,28},{16,0},{20,4},{24,8},{28,12},{1,17},{... | collective-permute-start | bytes 245768 | tf_op jit(solution)/shard_map/ppermute | solution.py:240
  54.0 3.5 %collective-permute-start.14 = (f32[4,40,256]{2,1,0:T(8,128)S(1)}, f32[4,40,256]{2,1,0:T(8,128)S(1)}, u32[]{:S(2)}, u32[]{:S(2)}) collective-permute-start(f32[4,40,256]{2,1,0:T(8,128)S(1)} %pad_maximum_fusion.1), channel_id=1, source_target_pairs={{0,4},{4,0},{8,12},{12,8},{16,20},{20,16},{24,28},{28,24},{1,5},{5... | collective-permute-start | bytes 491528 | tf_op jit(solution)/shard_map/ppermute | solution.py:240
  63.3 5.3 %collective-permute-start.15 = (f32[2,40,256]{2,1,0:T(8,128)S(1)}, f32[2,40,256]{2,1,0:T(8,128)S(1)}, u32[]{:S(2)}, u32[]{:S(2)}) collective-permute-start(f32[2,40,256]{2,1,0:T(8,128)S(1)} %get-tuple-element.52), channel_id=1, source_target_pairs={{0,8},{4,12},{8,0},{12,4},{16,24},{20,28},{24,16},{28,20},{1,9},{5... | collective-permute-start | bytes 245768 | tf_op jit(solution)/shard_map/ppermute | solution.py:240
  64.2 6.2 %collective-permute-start.17 = (f32[2,40,256]{2,1,0:T(8,128)S(1)}, f32[2,40,256]{2,1,0:T(8,128)S(1)}, u32[]{:S(2)}, u32[]{:S(2)}) collective-permute-start(f32[2,40,256]{2,1,0:T(8,128)S(1)} %get-tuple-element.53), channel_id=1, source_target_pairs={{0,24},{4,28},{8,16},{12,20},{16,8},{20,12},{24,0},{28,4},{1,25},{... | collective-permute-start | bytes 245768 | tf_op jit(solution)/shard_map/ppermute | solution.py:240
  65.7 6.0 %collective-permute-start.16 = (f32[2,40,256]{2,1,0:T(8,128)S(1)}, f32[2,40,256]{2,1,0:T(8,128)S(1)}, u32[]{:S(2)}, u32[]{:S(2)}) collective-permute-start(f32[2,40,256]{2,1,0:T(8,128)S(1)} %get-tuple-element.54), channel_id=1, source_target_pairs={{0,16},{4,20},{8,24},{12,28},{16,0},{20,4},{24,8},{28,12},{1,17},{... | collective-permute-start | bytes 245768 | tf_op jit(solution)/shard_map/ppermute | solution.py:240
  71.7 3.5 %collective-permute-start.18 = (f32[4,40,256]{2,1,0:T(8,128)S(1)}, f32[4,40,256]{2,1,0:T(8,128)S(1)}, u32[]{:S(2)}, u32[]{:S(2)}) collective-permute-start(f32[4,40,256]{2,1,0:T(8,128)S(1)} %pad_maximum_fusion.2), channel_id=1, source_target_pairs={{0,4},{4,0},{8,12},{12,8},{16,20},{20,16},{24,28},{28,24},{1,5},{5... | collective-permute-start | bytes 491528 | tf_op jit(solution)/shard_map/ppermute | solution.py:240
  81.0 5.3 %collective-permute-start.19 = (f32[2,40,256]{2,1,0:T(8,128)S(1)}, f32[2,40,256]{2,1,0:T(8,128)S(1)}, u32[]{:S(2)}, u32[]{:S(2)}) collective-permute-start(f32[2,40,256]{2,1,0:T(8,128)S(1)} %get-tuple-element.49), channel_id=1, source_target_pairs={{0,8},{4,12},{8,0},{12,4},{16,24},{20,28},{24,16},{28,20},{1,9},{5... | collective-permute-start | bytes 245768 | tf_op jit(solution)/shard_map/ppermute | solution.py:240
  82.1 6.2 %collective-permute-start.21 = (f32[2,40,256]{2,1,0:T(8,128)S(1)}, f32[2,40,256]{2,1,0:T(8,128)S(1)}, u32[]{:S(2)}, u32[]{:S(2)}) collective-permute-start(f32[2,40,256]{2,1,0:T(8,128)S(1)} %get-tuple-element.50), channel_id=1, source_target_pairs={{0,24},{4,28},{8,16},{12,20},{16,8},{20,12},{24,0},{28,4},{1,25},{... | collective-permute-start | bytes 245768 | tf_op jit(solution)/shard_map/ppermute | solution.py:240
  83.7 6.0 %collective-permute-start.20 = (f32[2,40,256]{2,1,0:T(8,128)S(1)}, f32[2,40,256]{2,1,0:T(8,128)S(1)}, u32[]{:S(2)}, u32[]{:S(2)}) collective-permute-start(f32[2,40,256]{2,1,0:T(8,128)S(1)} %get-tuple-element.51), channel_id=1, source_target_pairs={{0,16},{4,20},{8,24},{12,28},{16,0},{20,4},{24,8},{28,12},{1,17},{... | collective-permute-start | bytes 245768 | tf_op jit(solution)/shard_map/ppermute | solution.py:240
  89.7 3.5 %collective-permute-start.22 = (f32[4,40,256]{2,1,0:T(8,128)S(1)}, f32[4,40,256]{2,1,0:T(8,128)S(1)}, u32[]{:S(2)}, u32[]{:S(2)}) collective-permute-start(f32[4,40,256]{2,1,0:T(8,128)S(1)} %pad_maximum_fusion.3), channel_id=1, source_target_pairs={{0,4},{4,0},{8,12},{12,8},{16,20},{20,16},{24,28},{28,24},{1,5},{5... | collective-permute-start | bytes 491528 | tf_op jit(solution)/shard_map/ppermute | solution.py:240

commit v2 on v0

v2 whole, which is shorter than its diff:
```python
import functools

import jax
import jax.numpy as jnp
from jax import lax
from jax.experimental import pallas as pl
from jax.experimental.pallas import tpu as pltpu
from jax.sharding import PartitionSpec as P

TERMS = 4
REACH = 3
LANES = 128
TILE = 256

time_step = 0.3

F32, BF16 = jnp.float32, jnp.bfloat16
VMEM_LIMIT = 24 << 20


def split(value):
    high = value.astype(BF16)
    return high, (value - high.astype(F32)).astype(BF16)


def stacked(value):
    high, low = split(value)
    return jnp.concatenate([high, low], axis=0), high


def dot(left, right):
    return lax.dot_general(left, right, (((1,), (0,)), ((), ())), preferred_element_type=F32)


def product(both, high, right_high, right_low):
    rows = high.shape[0]
    result = dot(both, right_high)
    return result[:rows] + result[rows:] + dot(high, right_low)


def blocks_of(parts):
    if parts == 8:
        return [0, 2, 4, 6, 1, 3, 5, 7]
    relative = [0]
    for offset in [*range(1, REACH + 1), *range(-REACH, 0), parts // 2]:
        if offset % parts not in relative:
            relative.append(offset % parts)
    return relative


EARLY = 3


def receiver_of(me, block, parts):
    return me ^ block if parts == 8 else lax.rem(me + block, parts)


def place_of(sender, me, parts):
    relative = sender ^ me if parts == 8 else lax.rem(me - sender + parts, parts)
    result = jnp.zeros_like(relative)
    for place, block in enumerate(blocks_of(parts)):
        result = jnp.where(relative == block, place, result)
    return result


def call(kernel, out_shape, cost, *args, scalars=0):
    spaces = [pl.BlockSpec(memory_space=pltpu.SMEM if at < scalars else pltpu.VMEM) for at in range(len(args))]
    outs = [pl.BlockSpec(memory_space=pltpu.VMEM)] * len(out_shape)
    return pl.pallas_call(
        kernel,
        out_shape=[jax.ShapeDtypeStruct(shape, dtype) for shape, dtype in out_shape],
        in_specs=spaces,
        out_specs=outs,
        compiler_params=pltpu.CompilerParams(vmem_limit_bytes=VMEM_LIMIT),
        cost_estimate=pl.CostEstimate(flops=cost[0], bytes_accessed=cost[1], transcendentals=0),
    )(*args)


def stencil_rows(targets, values, outs, first):
    tall = 16
    points = targets[0].shape[1]
    row_id = lax.broadcasted_iota(jnp.int32, (tall, LANES), 0).astype(jnp.int16)
    zero = jnp.zeros((tall, LANES), BF16)
    for lane in range(0, points, LANES):
        at = [jnp.broadcast_to(t[:, lane : lane + LANES], (tall, LANES)) for t in targets]
        pieces = [split(jnp.broadcast_to(v[:, lane : lane + LANES], (tall, LANES))) for v in values]
        base = first
        for high_ref, low_ref in outs:

            @pl.loop(0, high_ref.shape[0] // TILE)
            def _(tile, base=base, high_ref=high_ref, low_ref=low_ref):
                local = [(a - (base + tile * TILE)).astype(jnp.int16) for a in at]
                for row in range(0, TILE, tall):
                    here = row_id + jnp.int16(row)
                    high, low = zero, zero
                    for target, (value_high, value_low) in zip(local, pieces, strict=True):
                        hit = target == here
                        high = jnp.where(hit, value_high, high)
                        low = jnp.where(hit, value_low, low)
                    start = pl.multiple_of(tile * TILE + row, tall)
                    high_ref[pl.ds(start, tall), lane : lane + LANES] = high
                    low_ref[pl.ds(start, tall), lane : lane + LANES] = low

            base = base + high_ref.shape[0]


def plan_kernel(parts, capacity, me_ref, neighbours_ref, weights_ref, potential_ref, routes_ref, targets_ref, values_ref, diagonal_ref, select_ref, near_high, near_low):
    count, points = neighbours_ref.shape
    me = me_ref[0]
    named = neighbours_ref[...]
    ghost = jnp.maximum(named - points, 0)
    sender = ghost // capacity
    place = place_of(sender, me, parts)
    named = jnp.where(named < points, named, points + place * capacity + (ghost - sender * capacity))
    half = 0.5 * weights_ref[...]
    diagonal_ref[...] = jnp.sum(half, axis=0, keepdims=True) + potential_ref[...]
    targets = [named[k : k + 1] for k in range(count)]
    values = [half[k : k + 1] for k in range(count)]
    for k in range(count):
        for later in range(k + 1, count):
            same = targets[k] == targets[later]
            values[k] = jnp.where(same, values[k] + values[later], values[k])
            targets[later] = jnp.where(same, -1, targets[later])
    for k in range(count):
        targets_ref[k : k + 1] = targets[k]
        values_ref[k : k + 1] = values[k]
    row_id = lax.broadcasted_iota(jnp.int32, (points, capacity), 0)
    for place, block in enumerate(blocks_of(parts)):
        route = routes_ref[pl.ds(receiver_of(me, block, parts), 1), :]
        select_ref[:, pl.ds(place * capacity, capacity)] = jnp.where(row_id == route, 1.0, 0.0).astype(BF16)
    stencil_rows(targets, values, [(near_high, near_low)], 0)


def ghost_kernel(first, targets_ref, values_ref, *outs):
    count = targets_ref.shape[0]
    targets = [targets_ref[k : k + 1] for k in range(count)]
    values = [values_ref[k : k + 1] for k in range(count)]
    stencil_rows(targets, values, list(zip(outs[::2], outs[1::2], strict=True)), first)


def intersect(both, high, turned_high, turned_low):
    half = high.shape[0] // 2
    columns = turned_high.shape[1] // 2
    result = product(both, high, turned_high, turned_low)
    if columns >= LANES:
        return result[:half, :columns] + result[half:, columns:]
    result = result[:half] + pltpu.roll(result[half:], columns, 1)
    lane = lax.broadcasted_iota(jnp.int32, (half // 2, LANES), 1)
    return jnp.where(lane < columns, result[: half // 2], pltpu.roll(result[half // 2 :], columns, 1))


def exchange_term(sums, half, wide_high, wide_low):
    columns = wide_high.shape[0] // 2
    if columns >= LANES:
        zero = jnp.zeros_like(sums)
        left = jnp.concatenate([jnp.concatenate([sums, zero], axis=1), jnp.concatenate([zero, sums], axis=1)], axis=0)
    else:
        lower = lax.broadcasted_iota(jnp.int32, sums.shape, 1) < columns
        rolled = pltpu.roll(sums, columns, 1)
        left = jnp.concatenate(
            [
                jnp.where(lower, sums, 0.0),
                jnp.where(lower, rolled, 0.0),
                jnp.where(lower, 0.0, rolled),
                jnp.where(lower, 0.0, sums),
            ],
            axis=0,
        )
    both, high = stacked(left)
    return product(both, high, wide_high, wide_low)


def send(term, select_ref, turned_high, turned_low, early_refs, late_ref, partial_ref, paired):
    rows = term.shape[0]
    both, high = stacked(term)
    partial = intersect(both, high, turned_high, turned_low)
    partial_ref[...] = partial
    tall, width = partial.shape
    capacity = late_ref.shape[2]
    if width < capacity:
        partial = jnp.concatenate([partial, jnp.zeros((tall, capacity - width), F32)], axis=1)
    late = late_ref.shape[0]
    places = [(ref, 0) for ref in early_refs]
    if paired:
        places += [(late_ref, 0)] + [(ref, 1) for ref in early_refs]
    else:
        places += [(late_ref, at) for at in range(late)]
    for place, (ref, at) in enumerate(places):
        packed = dot(both, select_ref[:, pl.ds((place + 1) * capacity, capacity)])
        ref[at, :rows, :] = packed[:rows] + packed[rows:]
        ref[at, rows:, :] = partial


def start_kernel(paired, frozen_ref, field_ref, select_ref, wide_high, wide_low, turned_high, turned_low, partial_ref, late_ref, *early_refs):
    groups = frozen_ref.shape[0]
    real = jnp.concatenate([frozen_ref[g, 0] for g in range(groups)], axis=0)
    imag = jnp.concatenate([frozen_ref[g, 1] for g in range(groups)], axis=0)
    wide = jnp.concatenate([real, -imag, imag, real], axis=0)
    wide_high[...], wide_low[...] = split(wide)
    high, low = split(wide.T)
    turned_high[...] = high
    turned_low[...] = low
    send(field_ref[...], select_ref, high, low, early_refs, late_ref, partial_ref, paired)


def near_kernel(term_ref, select_ref, near_high, near_low, diagonal_ref, base_ref):
    rows, points = term_ref.shape
    term = term_ref[...]
    both, high = stacked(term)
    own = dot(both, select_ref[:, : near_high.shape[0] - points])
    own_both, own_high = stacked(own[:rows] + own[rows:])
    value = product(both, high, near_high[:points], near_low[:points])
    value = value + product(own_both, own_high, near_high[points:], near_low[points:])
    base_ref[...] = term * diagonal_ref[...] - value


def ghost_values(blocks, high, low):
    pieces = [stacked(block) for block in blocks]
    both = jnp.concatenate([piece[0] for piece in pieces], axis=1)
    return product(both, jnp.concatenate([piece[1] for piece in pieces], axis=1), high, low)


def early_kernel(base_ref, partial_ref, early_high, early_low, *refs):
    early_refs, (base_out, sums_out) = refs[:-2], refs[-2:]
    rows = base_ref.shape[0]
    sums = partial_ref[...]
    for ref in early_refs:
        sums = sums + ref[0, rows:, : sums.shape[1]]
    sums_out[...] = sums
    base_out[...] = base_ref[...] - ghost_values([ref[0, :rows, :] for ref in early_refs], early_high[...], early_low[...])


def late_kernel(order, last, paired, late_ref, base_ref, sums_ref, total_ref, select_ref, late_high, late_low, wide_high, wide_low, turned_high, turned_low, *outs):
    rows = base_ref.shape[0]
    half = rows // 2
    blocks = late_ref.shape[0]
    sums = sums_ref[...]
    for block in range(blocks):
        sums = sums + late_ref[block, rows:, : sums.shape[1]]
    image = base_ref[...] - exchange_term(sums, half, wide_high[...], wide_low[...])
    image = image - ghost_values([late_ref[block, :rows, :] for block in range(blocks)], late_high[...], late_low[...])
    scale = time_step / order
    term = jnp.concatenate([scale * image[half:], -scale * image[:half]], axis=0)
    outs[0][...] = total_ref[...] + term
    if last:
        return
    _, term_ref, partial_ref, late_out, *early_outs = outs
    term_ref[...] = term
    send(term, select_ref, turned_high[...], turned_low[...], early_outs, late_out, partial_ref, paired)


def swap(value, bits, parts):
    return lax.ppermute(value, "mesh", [(part, part ^ bits) for part in range(parts)])


def move(value, offset, parts):
    return lax.ppermute(value, "mesh", [(part, (part + offset) % parts) for part in range(parts)])


def gather_frozen(frozen):
    bands = lax.axis_size("band")
    if bands <= 4:
        pieces = [frozen]
        for step in range(1, bands):
            pieces.append(lax.ppermute(frozen, "band", [(at, (at + step) % bands) for at in range(bands)]))
        return jnp.stack(pieces)
    return lax.all_gather(frozen, "band", axis=0, tiled=False)


def body(states, frozen, weights, potential, send_list, neighbours):
    parts = lax.axis_size("mesh")
    points = states.shape[2]
    rows = 2 * states.shape[1]
    half = rows // 2
    capacity = send_list.shape[2]
    relations = blocks_of(parts)
    places = len(relations)
    paired = parts == 8
    me = lax.axis_index("mesh").astype(jnp.int32).reshape(1)
    field = states.reshape(rows, points)
    count = neighbours.shape[0]

    full_frozen = gather_frozen(frozen)
    near_rows, early_rows, late_rows = points + capacity, EARLY * capacity, (places - 1 - EARLY) * capacity
    targets, values, diagonal, select, near_high, near_low = call(
        functools.partial(plan_kernel, parts, capacity),
        [((count, points), jnp.int32), ((count, points), F32), ((1, points), F32), ((points, places * capacity), BF16)]
        + [((near_rows, points), BF16)] * 2,
        (6 * near_rows * points, 12 << 20),
        me, neighbours, weights, potential.reshape(1, points), send_list[0], scalars=1,
    )
    vectors = full_frozen.shape[0] * full_frozen.shape[2]
    columns = 2 * vectors
    sum_shape = (half, columns) if columns >= LANES else (half * columns // LANES, LANES)
    tall = rows + sum_shape[0]
    outgoing = [(sum_shape, F32), ((1 if paired else places - 1 - EARLY, tall, capacity), F32)]
    outgoing += [((2 if paired else 1, tall, capacity), F32)] * EARLY
    wide_high, wide_low, turned_high, turned_low, partial, late, *early = call(
        functools.partial(start_kernel, paired),
        [((2 * columns, points), BF16)] * 2 + [((points, 2 * columns), BF16)] * 2 + outgoing,
        (6 * rows * points * places * capacity, 4 << 20),
        full_frozen, field, select,
    )
    total, term = field, field
    ghost_matrices = None
    for order in range(1, TERMS + 1):
        if paired:
            early = [swap(block, bits, parts) for block, bits in zip(early, relations[1 : 1 + EARLY], strict=True)]
        else:
            early = [move(block, offset, parts) for block, offset in zip(early, relations[1:], strict=False)]
        if ghost_matrices is None:
            ghost_matrices = call(
                functools.partial(ghost_kernel, near_rows),
                [((early_rows, points), BF16)] * 2 + [((late_rows, points), BF16)] * 2,
                (6 * (early_rows + late_rows) * points, 24 << 20),
                targets, values,
            )
            early_high, early_low, late_high, late_low = ghost_matrices
        (base,) = call(
            near_kernel,
            [((rows, points), F32)],
            (6 * rows * points * near_rows, 16 << 20),
            term, select, near_high, near_low, diagonal,
        )
        if paired:
            late = jnp.concatenate([late] + [block[1:] for block in early], axis=0)
            late, base = lax.optimization_barrier((late, base))
            late = swap(late, 1, parts)
        else:
            late = jnp.stack(
                [move(late[at], offset, parts) for at, offset in enumerate(relations[1 + EARLY :])]
            )
        base, sums = call(
            early_kernel,
            [((rows, points), F32), (sum_shape, F32)],
            (6 * rows * points * early_rows, 4 << 20),
            base, partial, early_high, early_low, *early,
        )
        last = order == TERMS
        shapes = [((rows, points), F32)]
        if not last:
            shapes += [((rows, points), F32)] + outgoing
        outs = call(
            functools.partial(late_kernel, order, last, paired),
            shapes,
            (6 * rows * points * late_rows, 12 << 20),
            late, base, sums, total, select, late_high, late_low, wide_high, wide_low, turned_high, turned_low,
        )
        total = outs[0]
        if not last:
            _, term, partial, late, *early = outs
    return total.reshape(states.shape)


def solution(mesh):
    return jax.shard_map(
        body,
        mesh=mesh,
        in_specs=(
            P(None, "band", "mesh"),
            P(None, "band", "mesh"),
            P(None, "mesh"),
            P("mesh"),
            P("mesh", None, None),
            P(None, "mesh"),
        ),
        out_specs=P(None, "band", "mesh"),
        check_vma=False,
    )
```

time: 585 us -> 62.8 us (0.11)
  local copies, waits for them, and re-layouts: 382 us -> 3.84 us
  blocking collectives: 104 us -> 0 us
  other arithmetic: 53 us -> 0.92 us
  Pallas kernels: 0 us -> 23.3 us
  matrix products: 8.07 us -> 0 us
    gather x68 -> x0, local copies, waits for them, and re-layouts: 351 us -> none  [the longest x64 293 us: body(): jnp.take(extended, neighbours[apply_order], axis=2) - term]
    psum x4 -> x0, blocking collectives: 89.9 us -> none  [body(): intersection = lax.psum(partial_intersection, 'mesh')]
    select_n x4 -> x0, other arithmetic: 39.9 us -> none  [body(): jnp.take(term, routes.reshape(-1), axis=2).reshape(2, rows, parts, capacity)]
    pallas_call x0 -> x15, Pallas kernels: none -> 23.3 us  [call(): pl.pallas_call(kernel, out_shape=[jax.ShapeDtypeStruct(shape, dtype) for...]
    ppermute x0 -> x19, starting transfers between devices: none -> 20.4 us  [the longest x16 14.3 us: swap(): lax.ppermute(value, 'mesh', [(part, part ^ bits) for part in range(parts)])]
    all_to_all x4 -> x0, waiting for transfers between devices: 18.3 us -> none  [body(): lax.all_to_all(packed, 'mesh', split_axis=2, concat_axis=2, tiled=True)]
    concatenate x4 -> x0, local copies, waits for them, and re-layouts: 16.6 us -> none  [body(): jnp.concatenate([term, arrived.reshape(2, rows, parts * capacity)], axis=2)]
    all_to_all x4 -> x0, starting transfers between devices: 15.9 us -> none  [body(): lax.all_to_all(packed, 'mesh', split_axis=2, concat_axis=2, tiled=True)]
  transfers between devices with their start and end apart: 4 -> 19, of which waited for: 3 -> 13; matrix products, arithmetic and copies ran while one was open for 2% -> 0% of each run, Pallas kernels for 0% -> 25%
where the time goes in v2:
time: 62.8 us; the launch traced here: 62.4 us
  Pallas kernels  23.3 us (37%)
  starting transfers between devices  20.4 us (32%)
  waiting for transfers between devices  13.8 us (22%)
  local copies, waits for them, and re-layouts  3.84 us (6%)
  other arithmetic  0.92 us (1%)
    pallas_call x15, Pallas kernels, call(): pl.pallas_call(kernel, out_shape=[jax.ShapeDtypeStruct(shape, dtype) for...  23.3 us
    ppermute x16, starting transfers between devices, swap(): lax.ppermute(value, 'mesh', [(part, part ^ bits) for part in range(parts)])  14.3 us
    ppermute x16, waiting for transfers between devices, swap(): lax.ppermute(value, 'mesh', [(part, part ^ bits) for part in range(parts)])  13.8 us
    ppermute x3, starting transfers between devices, gather_frozen(): lax.ppermute(frozen, 'band', [(at, (at + step) % bands) for at in range(b...  6.06 us
    unnamed x10, local copies, waits for them, and re-layouts  3.8 us
  transfers between devices with their start and end apart: 19, of which 13 were waited for; matrix products, arithmetic and copies ran while one was open for 0% of the time, Pallas kernels for 25%

profile of v2, /device:TPU:0, one launch (start us, length us, event | category | flops | bytes accessed | tf_op | source)
XLA Modules:
  0.0 62.4 jit_solution(13832121395939909120)
XLA Ops:
  0.0 3.0 %collective-permute-start = (f32[2,8,1024]{2,1,0:T(8,128)}, f32[2,8,1024]{2,1,0:T(8,128)S(1)}, u32[]{:S(2)}, u32[]{:S(2)}) collective-permute-start(f32[2,8,1024]{2,1,0:T(8,128)} %param.7), channel_id=1, source_target_pairs={{0,1},{1,2},{2,3},{3,0},{4,5},{5,6},{6,7},{7,4},{8,9},{9,10},{10,1... | collective-permute-start | bytes 196616 | tf_op jit(solution)/shard_map/ppermute | solution.py:265
  3.0 2.0 %collective-permute-start.2 = (f32[2,8,1024]{2,1,0:T(8,128)}, f32[2,8,1024]{2,1,0:T(8,128)S(1)}, u32[]{:S(2)}, u32[]{:S(2)}) collective-permute-start(f32[2,8,1024]{2,1,0:T(8,128)} %param.7), channel_id=1, source_target_pairs={{0,3},{1,0},{2,1},{3,2},{4,7},{5,4},{6,5},{7,6},{8,11},{9,8},{10,9... | collective-permute-start | bytes 196616 | tf_op jit(solution)/shard_map/ppermute | solution.py:265
  5.1 1.0 %collective-permute-start.1 = (f32[2,8,1024]{2,1,0:T(8,128)}, f32[2,8,1024]{2,1,0:T(8,128)S(1)}, u32[]{:S(2)}, u32[]{:S(2)}) collective-permute-start(f32[2,8,1024]{2,1,0:T(8,128)} %param.7), channel_id=1, source_target_pairs={{0,2},{1,3},{2,0},{3,1},{4,6},{5,7},{6,4},{7,5},{8,10},{9,11},{10,... | collective-permute-start | bytes 196616 | tf_op jit(solution)/shard_map/ppermute | solution.py:265
  6.1 0.0 copy-start.1
  6.1 0.8 %copy-done.1 = s32[8,1024]{1,0:T(8,128)S(1)} copy-done((s32[8,1024]{1,0:T(8,128)S(1)}, s32[8,1024]{1,0:T(8,128)}, u32[]{:S(2)}) %copy-start.1) | copy-done | bytes 32792
  6.8 0.0 copy-start.2
  6.8 0.8 %copy-done.2 = f32[8,1024]{1,0:T(8,128)S(1)} copy-done((f32[8,1024]{1,0:T(8,128)S(1)}, f32[8,1024]{1,0:T(8,128)}, u32[]{:S(2)}) %copy-start.2) | copy-done | bytes 32792
  7.6 0.0 copy-start.3
  7.6 0.7 %copy-done.3 = s32[1,8,256]{2,1,0:T(8,128)S(1)} copy-done((s32[1,8,256]{2,1,0:T(8,128)S(1)}, s32[1,8,256]{2,1,0:T(8,128)}, u32[]{:S(2)}) %copy-start.3) | copy-done | bytes 8216
  8.3 0.0 copy-start.4
  8.3 0.7 %copy-done.4 = f32[1024]{0:T(1024)S(1)} copy-done((f32[1024]{0:T(1024)S(1)}, f32[1024]{0:T(1024)}, u32[]{:S(2)}) %copy-start.4) | copy-done | bytes 4120
  9.0 4.2 %shard_map.64 = (s32[8,1024]{1,0:T(8,128)S(1)}, f32[8,1024]{1,0:T(8,128)S(1)}, f32[1,1024]{1,0:T(1,128)S(1)}, bf16[1024,2048]{1,0:T(8,128)(2,1)S(1)}, bf16[1280,...) custom-call(s32[1]{0:T(128)} %bitcast.5.me_ref, s32[8,1024]{1,0:T(8,128)S(1)} %copy-done.1, f32[8,1024]{1,0:T(8,128)S(1)} %copy-done.2, ...), custom_call_target="tpu_custom_call" | custom-call | flops 7864320 | bytes 12582912 | tf_op jit(solution)/shard_map/pallas_call | solution.py:69
  13.1 0.0 collective-permute-done
  13.2 0.0 collective-permute-done.2
  13.2 0.0 collective-permute-done.1
  13.2 0.9 %pad_maximum_fusion.frozen_ref = f32[4,2,8,1024]{3,2,1,0:T(8,128)S(1)} fusion(f32[1,2,8,1024]{3,2,1,0:T(8,128)S(1)} %bitcast.16, f32[1,2,8,1024]{3,2,1,0:T(8,128)S(1)} %bitcast.17, f32[1,2,8,1024]{3,2,1,0:T(8,128)S(1)} %bitcast.15, f32[1,2,8,1024]{3,2,1,0:T(8,128)} %bitcast.14), kind=kLoop, calls=%fused_computation | loop fusion | flops 196608 | bytes 524288 | tf_op jit(solution)/shard_map/stack | solution.py:266
  14.0 0.0 copy-start
  14.1 0.9 %copy-done = f32[2,16,1024]{2,1,0:T(8,128)S(1)} copy-done((f32[2,16,1024]{2,1,0:T(8,128)S(1)}, f32[2,16,1024]{2,1,0:T(8,128)}, u32[]{:S(2)}) %copy-start) | copy-done | bytes 131096
  14.9 1.0 %shard_map.65 = (bf16[128,1024]{1,0:T(8,128)(2,1)S(1)}, bf16[128,1024]{1,0:T(8,128)(2,1)S(1)}, bf16[1024,128]{1,0:T(8,128)(2,1)S(1)}, bf16[1024,128]{1,0:T(8,128...) custom-call(f32[4,2,8,1024]{3,2,1,0:T(8,128)S(1)} %pad_maximum_fusio, ...), custom_call_target="tpu_custom_call" | custom-call | flops 402653184 | bytes 4194304 | tf_op jit(solution)/shard_map/pallas_call | solution.py:69
  16.0 1.5 %collective-permute-start.3 = (f32[2,40,256]{2,1,0:T(8,128)S(1)}, f32[2,40,256]{2,1,0:T(8,128)S(1)}, u32[]{:S(2)}, u32[]{:S(2)}) collective-permute-start(f32[2,40,256]{2,1,0:T(8,128)S(1)} %get-tuple-element.63), channel_id=1, source_target_pairs={{0,8},{4,12},{8,0},{12,4},{16,24},{20,28},{24,16},{28,20},{1,9},{5... | collective-permute-start | bytes 245768 | tf_op jit(solution)/shard_map/ppermute | solution.py:253
  17.5 1.5 %collective-permute-start.4 = (f32[2,40,256]{2,1,0:T(8,128)S(1)}, f32[2,40,256]{2,1,0:T(8,128)S(1)}, u32[]{:S(2)}, u32[]{:S(2)}) collective-permute-start(f32[2,40,256]{2,1,0:T(8,128)S(1)} %get-tuple-element.64), channel_id=1, source_target_pairs={{0,16},{4,20},{8,24},{12,28},{16,0},{20,4},{24,8},{28,12},{1,17},{... | collective-permute-start | bytes 245768 | tf_op jit(solution)/shard_map/ppermute | solution.py:253
  19.0 0.5 collective-permute-start.5
  19.5 1.1 %shard_map.66.base_ref = f32[32,1024]{1,0:T(8,128)S(1)} custom-call(f32[32,1024]{1,0:T(8,128)S(1)} %bitcast.10, bf16[1024,2048]{1,0:T(8,128)(2,1)S(1)} %get-tuple-element.61.select_ref, bf16[1280,1024]{1,0:T(8,128)(2,1)S(1)} %get-tuple-element.66.near_high, bf16[1280,1024]{1,0:T(8,128)(2,1)S(1)} %get-tuple-element.67.near_low, ...), custom_call_target="tpu_custom_call" | custom-call | flops 251658240 | bytes 16777216 | tf_op jit(solution)/shard_map/pallas_call | solution.py:69
  20.6 0.4 collective-permute-done.3.refs_0_
  21.0 1.7 %collective-permute-done.4.refs_1_ = f32[2,40,256]{2,1,0:T(8,128)S(1)} collective-permute-done((f32[2,40,256]{2,1,0:T(8,128)S(1)}, f32[2,40,256]{2,1,0:T(8,128)S(1)}, u32[]{:S(2)}, u32[]{:S(2)}) %collective-permute-start.4) | collective-permute-done | bytes 81952 | tf_op jit(solution)/shard_map/ppermute | solution.py:253
  22.7 1.6 %collective-permute-done.5.refs_2_ = f32[2,40,256]{2,1,0:T(8,128)S(1)} collective-permute-done((f32[2,40,256]{2,1,0:T(8,128)S(1)}, f32[2,40,256]{2,1,0:T(8,128)S(1)}, u32[]{:S(2)}, u32[]{:S(2)}) %collective-permute-start.5) | collective-permute-done | bytes 81952 | tf_op jit(solution)/shard_map/ppermute | solution.py:253
  24.3 0.1 collective-permute-start.6
  24.4 4.3 %shard_map.67 = (bf16[768,1024]{1,0:T(8,128)(2,1)S(1)}, bf16[768,1024]{1,0:T(8,128)(2,1)S(1)}, bf16[1024,1024]{1,0:T(8,128)(2,1)S(1)}, bf16[1024,1024]{1,0:T(8,128)(2,1)S(1)}) custom-call(s32[8,1024]{1,0:T(8,128)S(1)} %get-tuple-element.72.targets_ref, f32[8,1024]{1,0:T(8,128)S(1)} %get-tuple-element.73.values_ref), custom_call_target="tpu_custom_call" | custom-call | flops 11010048 | bytes 25165824 | tf_op jit(solution)/shard_map/pallas_call | solution.py:69
  28.7 0.6 %shard_map.68 = (f32[32,1024]{1,0:T(8,128)S(1)}, f32[8,128]{1,0:T(8,128)S(1)}) custom-call(f32[32,1024]{1,0:T(8,128)S(1)} %shard_map.66.base_ref, f32[8,128]{1,0:T(8,128)S(1)} %get-tuple-element.71.partial_ref, bf16[768,1024]{1,0:T(8,128)(2,1)S(1)} %get-tuple-element.74.early_high, bf16[768,1024]{1,0:T(8,128)(2,1)S(1)} %get-tuple-element.75.early_low, ...), custom_call_target="tpu_custom_call" | custom-call | flops 150994944 | bytes 4194304 | tf_op jit(solution)/shard_map/pallas_call | solution.py:69
  29.3 0.0 collective-permute-done.6.late_ref
  29.4 1.8 %shard_map.69 = (f32[32,1024]{1,0:T(8,128)S(1)}, f32[32,1024]{1,0:T(8,128)S(1)}, f32[8,128]{1,0:T(8,128)S(1)}, f32[1,40,256]{2,1,0:T(8,128)S(1)}, f32[2,40,256]{...) custom-call(f32[4,40,256]{2,1,0:T(8,128)S(1)} %collective-permute-done.6.late_ref, ...), custom_call_target="tpu_custom_call" | custom-call | flops 201326592 | bytes 12582912 | tf_op jit(solution)/shard_map/pallas_call | solution.py:69
  31.1 0.6 collective-permute-start.7
  31.7 0.5 collective-permute-start.8
  32.2 2.4 %collective-permute-start.9 = (f32[2,40,256]{2,1,0:T(8,128)S(1)}, f32[2,40,256]{2,1,0:T(8,128)S(1)}, u32[]{:S(2)}, u32[]{:S(2)}) collective-permute-start(f32[2,40,256]{2,1,0:T(8,128)S(1)} %get-tuple-element.87), channel_id=1, source_target_pairs={{0,24},{4,28},{8,16},{12,20},{16,8},{20,12},{24,0},{28,4},{1,25},{... | collective-permute-start | bytes 245768 | tf_op jit(solution)/shard_map/ppermute | solution.py:253
  34.6 1.1 %shard_map.70.base_ref = f32[32,1024]{1,0:T(8,128)S(1)} custom-call(f32[32,1024]{1,0:T(8,128)S(1)} %get-tuple-element.88.term_ref, bf16[1024,2048]{1,0:T(8,128)(2,1)S(1)} %get-tuple-element.61.select_ref, bf16[1280,1024]{1,0:T(8,128)(2,1)S(1)} %get-tuple-element.66.near_high, bf16[1280,1024]{1,0:T(8,128)(2,1)S(1)} %get-tuple-element.67.near_low, ...), custom_call_target="tpu_custom_call" | custom-call | flops 251658240 | bytes 16777216 | tf_op jit(solution)/shard_map/pallas_call | solution.py:69
  35.7 0.6 collective-permute-done.7.refs_0_
  36.3 1.7 %collective-permute-done.8.refs_1_ = f32[2,40,256]{2,1,0:T(8,128)S(1)} collective-permute-done((f32[2,40,256]{2,1,0:T(8,128)S(1)}, f32[2,40,256]{2,1,0:T(8,128)S(1)}, u32[]{:S(2)}, u32[]{:S(2)}) %collective-permute-start.8) | collective-permute-done | bytes 81952 | tf_op jit(solution)/shard_map/ppermute | solution.py:253
  38.0 0.0 collective-permute-done.9.refs_2_
  38.0 0.1 collective-permute-start.10
  38.1 0.6 %shard_map.71 = (f32[32,1024]{1,0:T(8,128)S(1)}, f32[8,128]{1,0:T(8,128)S(1)}) custom-call(f32[32,1024]{1,0:T(8,128)S(1)} %shard_map.70.base_ref, f32[8,128]{1,0:T(8,128)S(1)} %get-tuple-element.91.partial_ref, bf16[768,1024]{1,0:T(8,128)(2,1)S(1)} %get-tuple-element.74.early_high, bf16[768,1024]{1,0:T(8,128)(2,1)S(1)} %get-tuple-element.75.early_low, ...), custom_call_target="tpu_custom_call" | custom-call | flops 150994944 | bytes 4194304 | tf_op jit(solution)/shard_map/pallas_call | solution.py:69
  38.8 0.7 %collective-permute-done.10.late_ref = f32[4,40,256]{2,1,0:T(8,128)S(1)} collective-permute-done((f32[4,40,256]{2,1,0:T(8,128)S(1)}, f32[4,40,256]{2,1,0:T(8,128)S(1)}, u32[]{:S(2)}, u32[]{:S(2)}) %collective-permute-start.10) | collective-permute-done | bytes 163872 | tf_op jit(solution)/shard_map/ppermute | solution.py:253
  39.5 1.8 %shard_map.72 = (f32[32,1024]{1,0:T(8,128)S(1)}, f32[32,1024]{1,0:T(8,128)S(1)}, f32[8,128]{1,0:T(8,128)S(1)}, f32[1,40,256]{2,1,0:T(8,128)S(1)}, f32[2,40,256]{...) custom-call(f32[4,40,256]{2,1,0:T(8,128)S(1)} %collective-permute-done.10.late_ref, ...), custom_call_target="tpu_custom_call" | custom-call | flops 201326592 | bytes 12582912 | tf_op jit(solution)/shard_map/pallas_call | solution.py:69
  41.3 1.5 %collective-permute-start.11 = (f32[2,40,256]{2,1,0:T(8,128)S(1)}, f32[2,40,256]{2,1,0:T(8,128)S(1)}, u32[]{:S(2)}, u32[]{:S(2)}) collective-permute-start(f32[2,40,256]{2,1,0:T(8,128)S(1)} %get-tuple-element.96), channel_id=1, source_target_pairs={{0,8},{4,12},{8,0},{12,4},{16,24},{20,28},{24,16},{28,20},{1,9},{5... | collective-permute-start | bytes 245768 | tf_op jit(solution)/shard_map/ppermute | solution.py:253
  42.8 1.0 %collective-permute-start.12 = (f32[2,40,256]{2,1,0:T(8,128)S(1)}, f32[2,40,256]{2,1,0:T(8,128)S(1)}, u32[]{:S(2)}, u32[]{:S(2)}) collective-permute-start(f32[2,40,256]{2,1,0:T(8,128)S(1)} %get-tuple-element.97), channel_id=1, source_target_pairs={{0,16},{4,20},{8,24},{12,28},{16,0},{20,4},{24,8},{28,12},{1,17},{... | collective-permute-start | bytes 245768 | tf_op jit(solution)/shard_map/ppermute | solution.py:253
  43.8 1.0 %collective-permute-start.13 = (f32[2,40,256]{2,1,0:T(8,128)S(1)}, f32[2,40,256]{2,1,0:T(8,128)S(1)}, u32[]{:S(2)}, u32[]{:S(2)}) collective-permute-start(f32[2,40,256]{2,1,0:T(8,128)S(1)} %get-tuple-element.98), channel_id=1, source_target_pairs={{0,24},{4,28},{8,16},{12,20},{16,8},{20,12},{24,0},{28,4},{1,25},{... | collective-permute-start | bytes 245768 | tf_op jit(solution)/shard_map/ppermute | solution.py:253
  44.8 1.1 %shard_map.73.base_ref = f32[32,1024]{1,0:T(8,128)S(1)} custom-call(f32[32,1024]{1,0:T(8,128)S(1)} %get-tuple-element.99.term_ref, bf16[1024,2048]{1,0:T(8,128)(2,1)S(1)} %get-tuple-element.61.select_ref, bf16[1280,1024]{1,0:T(8,128)(2,1)S(1)} %get-tuple-element.66.near_high, bf16[1280,1024]{1,0:T(8,128)(2,1)S(1)} %get-tuple-element.67.near_low, ...), custom_call_target="tpu_custom_call" | custom-call | flops 251658240 | bytes 16777216 | tf_op jit(solution)/shard_map/pallas_call | solution.py:69
  45.9 0.0 collective-permute-done.11.refs_0_
  45.9 2.2 %collective-permute-done.12.refs_1_ = f32[2,40,256]{2,1,0:T(8,128)S(1)} collective-permute-done((f32[2,40,256]{2,1,0:T(8,128)S(1)}, f32[2,40,256]{2,1,0:T(8,128)S(1)}, u32[]{:S(2)}, u32[]{:S(2)}) %collective-permute-start.12) | collective-permute-done | bytes 81952 | tf_op jit(solution)/shard_map/ppermute | solution.py:253
  48.1 1.0 %collective-permute-done.13.refs_2_ = f32[2,40,256]{2,1,0:T(8,128)S(1)} collective-permute-done((f32[2,40,256]{2,1,0:T(8,128)S(1)}, f32[2,40,256]{2,1,0:T(8,128)S(1)}, u32[]{:S(2)}, u32[]{:S(2)}) %collective-permute-start.13) | collective-permute-done | bytes 81952 | tf_op jit(solution)/shard_map/ppermute | solution.py:253
  49.1 0.1 collective-permute-start.14
  49.2 0.6 %shard_map.74 = (f32[32,1024]{1,0:T(8,128)S(1)}, f32[8,128]{1,0:T(8,128)S(1)}) custom-call(f32[32,1024]{1,0:T(8,128)S(1)} %shard_map.73.base_ref, f32[8,128]{1,0:T(8,128)S(1)} %get-tuple-element.102.partial_ref, bf16[768,1024]{1,0:T(8,128)(2,1)S(1)} %get-tuple-element.74.early_high, bf16[768,1024]{1,0:T(8,128)(2,1)S(1)} %get-tuple-element.75.early_low, ...), custom_call_target="tpu_custom_call" | custom-call | flops 150994944 | bytes 4194304 | tf_op jit(solution)/shard_map/pallas_call | solution.py:69
  49.9 0.7 %collective-permute-done.14.late_ref = f32[4,40,256]{2,1,0:T(8,128)S(1)} collective-permute-done((f32[4,40,256]{2,1,0:T(8,128)S(1)}, f32[4,40,256]{2,1,0:T(8,128)S(1)}, u32[]{:S(2)}, u32[]{:S(2)}) %collective-permute-start.14) | collective-permute-done | bytes 163872 | tf_op jit(solution)/shard_map/ppermute | solution.py:253
  50.6 1.8 %shard_map.75 = (f32[32,1024]{1,0:T(8,128)S(1)}, f32[32,1024]{1,0:T(8,128)S(1)}, f32[8,128]{1,0:T(8,128)S(1)}, f32[1,40,256]{2,1,0:T(8,128)S(1)}, f32[2,40,256]{...) custom-call(f32[4,40,256]{2,1,0:T(8,128)S(1)} %collective-permute-done.14.late_ref, ...), custom_call_target="tpu_custom_call" | custom-call | flops 201326592 | bytes 12582912 | tf_op jit(solution)/shard_map/pallas_call | solution.py:69
  52.4 0.7 %collective-permute-start.15 = (f32[2,40,256]{2,1,0:T(8,128)S(1)}, f32[2,40,256]{2,1,0:T(8,128)S(1)}, u32[]{:S(2)}, u32[]{:S(2)}) collective-permute-start(f32[2,40,256]{2,1,0:T(8,128)S(1)} %get-tuple-element.107), channel_id=1, source_target_pairs={{0,8},{4,12},{8,0},{12,4},{16,24},{20,28},{24,16},{28,20},{1,9},{5... | collective-permute-start | bytes 245768 | tf_op jit(solution)/shard_map/ppermute | solution.py:253
  53.1 0.9 %collective-permute-start.16 = (f32[2,40,256]{2,1,0:T(8,128)S(1)}, f32[2,40,256]{2,1,0:T(8,128)S(1)}, u32[]{:S(2)}, u32[]{:S(2)}) collective-permute-start(f32[2,40,256]{2,1,0:T(8,128)S(1)} %get-tuple-element.108), channel_id=1, source_target_pairs={{0,16},{4,20},{8,24},{12,28},{16,0},{20,4},{24,8},{28,12},{1,17},{... | collective-permute-start | bytes 245768 | tf_op jit(solution)/shard_map/ppermute | solution.py:253
  54.0 1.9 %collective-permute-start.17 = (f32[2,40,256]{2,1,0:T(8,128)S(1)}, f32[2,40,256]{2,1,0:T(8,128)S(1)}, u32[]{:S(2)}, u32[]{:S(2)}) collective-permute-start(f32[2,40,256]{2,1,0:T(8,128)S(1)} %get-tuple-element.109), channel_id=1, source_target_pairs={{0,24},{4,28},{8,16},{12,20},{16,8},{20,12},{24,0},{28,4},{1,25},{... | collective-permute-start | bytes 245768 | tf_op jit(solution)/shard_map/ppermute | solution.py:253
  55.9 1.1 %shard_map.76.base_ref = f32[32,1024]{1,0:T(8,128)S(1)} custom-call(f32[32,1024]{1,0:T(8,128)S(1)} %get-tuple-element.110.term_ref, bf16[1024,2048]{1,0:T(8,128)(2,1)S(1)} %get-tuple-element.61.select_ref, bf16[1280,1024]{1,0:T(8,128)(2,1)S(1)} %get-tuple-element.66.near_high, bf16[1280,1024]{1,0:T(8,128)(2,1)S(1)} %get-tuple-element.67.near_low, ...), custom_call_target="tpu_custom_call" | custom-call | flops 251658240 | bytes 16777216 | tf_op jit(solution)/shard_map/pallas_call | solution.py:69
  57.0 0.1 collective-permute-done.15.refs_0_
  57.1 1.4 %collective-permute-done.16.refs_1_ = f32[2,40,256]{2,1,0:T(8,128)S(1)} collective-permute-done((f32[2,40,256]{2,1,0:T(8,128)S(1)}, f32[2,40,256]{2,1,0:T(8,128)S(1)}, u32[]{:S(2)}, u32[]{:S(2)}) %collective-permute-start.16) | collective-permute-done | bytes 81952 | tf_op jit(solution)/shard_map/ppermute | solution.py:253
  58.4 0.9 %collective-permute-done.17.refs_2_ = f32[2,40,256]{2,1,0:T(8,128)S(1)} collective-permute-done((f32[2,40,256]{2,1,0:T(8,128)S(1)}, f32[2,40,256]{2,1,0:T(8,128)S(1)}, u32[]{:S(2)}, u32[]{:S(2)}) %collective-permute-start.17) | collective-permute-done | bytes 81952 | tf_op jit(solution)/shard_map/ppermute | solution.py:253
  59.3 0.1 collective-permute-start.18
  59.4 0.6 %shard_map.77 = (f32[32,1024]{1,0:T(8,128)S(1)}, f32[8,128]{1,0:T(8,128)S(1)}) custom-call(f32[32,1024]{1,0:T(8,128)S(1)} %shard_map.76.base_ref, f32[8,128]{1,0:T(8,128)S(1)} %get-tuple-element.113.partial_ref, bf16[768,1024]{1,0:T(8,128)(2,1)S(1)} %get-tuple-element.74.early_high, bf16[768,1024]{1,0:T(8,128)(2,1)S(1)} %get-tuple-element.75.early_low, ...), custom_call_target="tpu_custom_call" | custom-call | flops 150994944 | bytes 4194304 | tf_op jit(solution)/shard_map/pallas_call | solution.py:69
  60.0 0.7 %collective-permute-done.18.late_ref = f32[4,40,256]{2,1,0:T(8,128)S(1)} collective-permute-done((f32[4,40,256]{2,1,0:T(8,128)S(1)}, f32[4,40,256]{2,1,0:T(8,128)S(1)}, u32[]{:S(2)}, u32[]{:S(2)}) %collective-permute-start.18) | collective-permute-done | bytes 163872 | tf_op jit(solution)/shard_map/ppermute | solution.py:253
  60.8 1.6 %shard_map.78 = f32[32,1024]{1,0:T(8,128)} custom-call(f32[4,40,256]{2,1,0:T(8,128)S(1)} %collective-permute-done.18.late_ref, f32[32,1024]{1,0:T(8,128)S(1)} %get-tuple-element.114.base_ref, f32[8,128]{1,0:T(8,128)S(1)} %get-tuple-element.115.sums_ref, f32[32,1024]{1,0:T(8,128)S(1)} %get-tuple-element.116.total_ref, ...), custom_call_target="tpu_custom_call" | custom-call | flops 201326592 | bytes 12582912 | tf_op jit(solution)/shard_map/pallas_call | solution.py:69
  (16 shorter events, 0.1 us)
Async XLA Ops:
  0.0 13.1 %collective-permute-start = (f32[2,8,1024]{2,1,0:T(8,128)}, f32[2,8,1024]{2,1,0:T(8,128)S(1)}, u32[]{:S(2)}, u32[]{:S(2)}) collective-permute-start(f32[2,8,1024]{2,1,0:T(8,128)} %param.7), channel_id=1, source_target_pairs={{0,1},{1,2},{2,3},{3,0},{4,5},{5,6},{6,7},{7,4},{8,9},{9,10},{10,1... | collective-permute-start | bytes 196616 | tf_op jit(solution)/shard_map/ppermute | solution.py:265
  3.0 10.1 %collective-permute-start.2 = (f32[2,8,1024]{2,1,0:T(8,128)}, f32[2,8,1024]{2,1,0:T(8,128)S(1)}, u32[]{:S(2)}, u32[]{:S(2)}) collective-permute-start(f32[2,8,1024]{2,1,0:T(8,128)} %param.7), channel_id=1, source_target_pairs={{0,3},{1,0},{2,1},{3,2},{4,7},{5,4},{6,5},{7,6},{8,11},{9,8},{10,9... | collective-permute-start | bytes 196616 | tf_op jit(solution)/shard_map/ppermute | solution.py:265
  5.1 8.1 %collective-permute-start.1 = (f32[2,8,1024]{2,1,0:T(8,128)}, f32[2,8,1024]{2,1,0:T(8,128)S(1)}, u32[]{:S(2)}, u32[]{:S(2)}) collective-permute-start(f32[2,8,1024]{2,1,0:T(8,128)} %param.7), channel_id=1, source_target_pairs={{0,2},{1,3},{2,0},{3,1},{4,6},{5,7},{6,4},{7,5},{8,10},{9,11},{10,... | collective-permute-start | bytes 196616 | tf_op jit(solution)/shard_map/ppermute | solution.py:265
  6.1 0.8 %copy-start.1 = (s32[8,1024]{1,0:T(8,128)S(1)}, s32[8,1024]{1,0:T(8,128)}, u32[]{:S(2)}) copy-start(s32[8,1024]{1,0:T(8,128)} %neighbours_ref.1) | copy-start | bytes 98308
  6.8 0.8 %copy-start.2 = (f32[8,1024]{1,0:T(8,128)S(1)}, f32[8,1024]{1,0:T(8,128)}, u32[]{:S(2)}) copy-start(f32[8,1024]{1,0:T(8,128)} %weights_ref.1) | copy-start | bytes 98308
  7.6 0.7 %copy-start.3 = (s32[1,8,256]{2,1,0:T(8,128)S(1)}, s32[1,8,256]{2,1,0:T(8,128)}, u32[]{:S(2)}) copy-start(s32[1,8,256]{2,1,0:T(8,128)} %param.10) | copy-start | bytes 24580
  8.3 0.7 %copy-start.4 = (f32[1024]{0:T(1024)S(1)}, f32[1024]{0:T(1024)}, u32[]{:S(2)}) copy-start(f32[1024]{0:T(1024)} %param.9) | copy-start | bytes 12292
  14.0 0.9 %copy-start = (f32[2,16,1024]{2,1,0:T(8,128)S(1)}, f32[2,16,1024]{2,1,0:T(8,128)}, u32[]{:S(2)}) copy-start(f32[2,16,1024]{2,1,0:T(8,128)} %param.6) | copy-start | bytes 393220
  16.0 5.0 %collective-permute-start.3 = (f32[2,40,256]{2,1,0:T(8,128)S(1)}, f32[2,40,256]{2,1,0:T(8,128)S(1)}, u32[]{:S(2)}, u32[]{:S(2)}) collective-permute-start(f32[2,40,256]{2,1,0:T(8,128)S(1)} %get-tuple-element.63), channel_id=1, source_target_pairs={{0,8},{4,12},{8,0},{12,4},{16,24},{20,28},{24,16},{28,20},{1,9},{5... | collective-permute-start | bytes 245768 | tf_op jit(solution)/shard_map/ppermute | solution.py:253
  17.5 5.2 %collective-permute-start.4 = (f32[2,40,256]{2,1,0:T(8,128)S(1)}, f32[2,40,256]{2,1,0:T(8,128)S(1)}, u32[]{:S(2)}, u32[]{:S(2)}) collective-permute-start(f32[2,40,256]{2,1,0:T(8,128)S(1)} %get-tuple-element.64), channel_id=1, source_target_pairs={{0,16},{4,20},{8,24},{12,28},{16,0},{20,4},{24,8},{28,12},{1,17},{... | collective-permute-start | bytes 245768 | tf_op jit(solution)/shard_map/ppermute | solution.py:253
  19.0 5.3 %collective-permute-start.5 = (f32[2,40,256]{2,1,0:T(8,128)S(1)}, f32[2,40,256]{2,1,0:T(8,128)S(1)}, u32[]{:S(2)}, u32[]{:S(2)}) collective-permute-start(f32[2,40,256]{2,1,0:T(8,128)S(1)} %get-tuple-element.65), channel_id=1, source_target_pairs={{0,24},{4,28},{8,16},{12,20},{16,8},{20,12},{24,0},{28,4},{1,25},{... | collective-permute-start | bytes 245768 | tf_op jit(solution)/shard_map/ppermute | solution.py:253
  24.3 5.0 %collective-permute-start.6 = (f32[4,40,256]{2,1,0:T(8,128)S(1)}, f32[4,40,256]{2,1,0:T(8,128)S(1)}, u32[]{:S(2)}, u32[]{:S(2)}) collective-permute-start(f32[4,40,256]{2,1,0:T(8,128)S(1)} %pad_maximum_fusion.1), channel_id=1, source_target_pairs={{0,4},{4,0},{8,12},{12,8},{16,20},{20,16},{24,28},{28,24},{1,5},{5... | collective-permute-start | bytes 491528 | tf_op jit(solution)/shard_map/ppermute | solution.py:253
  31.1 5.2 %collective-permute-start.7 = (f32[2,40,256]{2,1,0:T(8,128)S(1)}, f32[2,40,256]{2,1,0:T(8,128)S(1)}, u32[]{:S(2)}, u32[]{:S(2)}) collective-permute-start(f32[2,40,256]{2,1,0:T(8,128)S(1)} %get-tuple-element.85), channel_id=1, source_target_pairs={{0,8},{4,12},{8,0},{12,4},{16,24},{20,28},{24,16},{28,20},{1,9},{5... | collective-permute-start | bytes 245768 | tf_op jit(solution)/shard_map/ppermute | solution.py:253
  31.7 6.3 %collective-permute-start.8 = (f32[2,40,256]{2,1,0:T(8,128)S(1)}, f32[2,40,256]{2,1,0:T(8,128)S(1)}, u32[]{:S(2)}, u32[]{:S(2)}) collective-permute-start(f32[2,40,256]{2,1,0:T(8,128)S(1)} %get-tuple-element.86), channel_id=1, source_target_pairs={{0,16},{4,20},{8,24},{12,28},{16,0},{20,4},{24,8},{28,12},{1,17},{... | collective-permute-start | bytes 245768 | tf_op jit(solution)/shard_map/ppermute | solution.py:253
  32.2 5.8 %collective-permute-start.9 = (f32[2,40,256]{2,1,0:T(8,128)S(1)}, f32[2,40,256]{2,1,0:T(8,128)S(1)}, u32[]{:S(2)}, u32[]{:S(2)}) collective-permute-start(f32[2,40,256]{2,1,0:T(8,128)S(1)} %get-tuple-element.87), channel_id=1, source_target_pairs={{0,24},{4,28},{8,16},{12,20},{16,8},{20,12},{24,0},{28,4},{1,25},{... | collective-permute-start | bytes 245768 | tf_op jit(solution)/shard_map/ppermute | solution.py:253
  38.0 1.5 %collective-permute-start.10 = (f32[4,40,256]{2,1,0:T(8,128)S(1)}, f32[4,40,256]{2,1,0:T(8,128)S(1)}, u32[]{:S(2)}, u32[]{:S(2)}) collective-permute-start(f32[4,40,256]{2,1,0:T(8,128)S(1)} %pad_maximum_fusion.2), channel_id=1, source_target_pairs={{0,4},{4,0},{8,12},{12,8},{16,20},{20,16},{24,28},{28,24},{1,5},{5... | collective-permute-start | bytes 491528 | tf_op jit(solution)/shard_map/ppermute | solution.py:253
  41.3 4.6 %collective-permute-start.11 = (f32[2,40,256]{2,1,0:T(8,128)S(1)}, f32[2,40,256]{2,1,0:T(8,128)S(1)}, u32[]{:S(2)}, u32[]{:S(2)}) collective-permute-start(f32[2,40,256]{2,1,0:T(8,128)S(1)} %get-tuple-element.96), channel_id=1, source_target_pairs={{0,8},{4,12},{8,0},{12,4},{16,24},{20,28},{24,16},{28,20},{1,9},{5... | collective-permute-start | bytes 245768 | tf_op jit(solution)/shard_map/ppermute | solution.py:253
  42.8 5.3 %collective-permute-start.12 = (f32[2,40,256]{2,1,0:T(8,128)S(1)}, f32[2,40,256]{2,1,0:T(8,128)S(1)}, u32[]{:S(2)}, u32[]{:S(2)}) collective-permute-start(f32[2,40,256]{2,1,0:T(8,128)S(1)} %get-tuple-element.97), channel_id=1, source_target_pairs={{0,16},{4,20},{8,24},{12,28},{16,0},{20,4},{24,8},{28,12},{1,17},{... | collective-permute-start | bytes 245768 | tf_op jit(solution)/shard_map/ppermute | solution.py:253
  43.8 5.3 %collective-permute-start.13 = (f32[2,40,256]{2,1,0:T(8,128)S(1)}, f32[2,40,256]{2,1,0:T(8,128)S(1)}, u32[]{:S(2)}, u32[]{:S(2)}) collective-permute-start(f32[2,40,256]{2,1,0:T(8,128)S(1)} %get-tuple-element.98), channel_id=1, source_target_pairs={{0,24},{4,28},{8,16},{12,20},{16,8},{20,12},{24,0},{28,4},{1,25},{... | collective-permute-start | bytes 245768 | tf_op jit(solution)/shard_map/ppermute | solution.py:253
  49.1 1.5 %collective-permute-start.14 = (f32[4,40,256]{2,1,0:T(8,128)S(1)}, f32[4,40,256]{2,1,0:T(8,128)S(1)}, u32[]{:S(2)}, u32[]{:S(2)}) collective-permute-start(f32[4,40,256]{2,1,0:T(8,128)S(1)} %pad_maximum_fusion.3), channel_id=1, source_target_pairs={{0,4},{4,0},{8,12},{12,8},{16,20},{20,16},{24,28},{28,24},{1,5},{5... | collective-permute-start | bytes 491528 | tf_op jit(solution)/shard_map/ppermute | solution.py:253
  52.4 4.7 %collective-permute-start.15 = (f32[2,40,256]{2,1,0:T(8,128)S(1)}, f32[2,40,256]{2,1,0:T(8,128)S(1)}, u32[]{:S(2)}, u32[]{:S(2)}) collective-permute-start(f32[2,40,256]{2,1,0:T(8,128)S(1)} %get-tuple-element.107), channel_id=1, source_target_pairs={{0,8},{4,12},{8,0},{12,4},{16,24},{20,28},{24,16},{28,20},{1,9},{5... | collective-permute-start | bytes 245768 | tf_op jit(solution)/shard_map/ppermute | solution.py:253
  53.1 5.3 %collective-permute-start.16 = (f32[2,40,256]{2,1,0:T(8,128)S(1)}, f32[2,40,256]{2,1,0:T(8,128)S(1)}, u32[]{:S(2)}, u32[]{:S(2)}) collective-permute-start(f32[2,40,256]{2,1,0:T(8,128)S(1)} %get-tuple-element.108), channel_id=1, source_target_pairs={{0,16},{4,20},{8,24},{12,28},{16,0},{20,4},{24,8},{28,12},{1,17},{... | collective-permute-start | bytes 245768 | tf_op jit(solution)/shard_map/ppermute | solution.py:253
  54.0 5.3 %collective-permute-start.17 = (f32[2,40,256]{2,1,0:T(8,128)S(1)}, f32[2,40,256]{2,1,0:T(8,128)S(1)}, u32[]{:S(2)}, u32[]{:S(2)}) collective-permute-start(f32[2,40,256]{2,1,0:T(8,128)S(1)} %get-tuple-element.109), channel_id=1, source_target_pairs={{0,24},{4,28},{8,16},{12,20},{16,8},{20,12},{24,0},{28,4},{1,25},{... | collective-permute-start | bytes 245768 | tf_op jit(solution)/shard_map/ppermute | solution.py:253
  59.3 1.5 %collective-permute-start.18 = (f32[4,40,256]{2,1,0:T(8,128)S(1)}, f32[4,40,256]{2,1,0:T(8,128)S(1)}, u32[]{:S(2)}, u32[]{:S(2)}) collective-permute-start(f32[4,40,256]{2,1,0:T(8,128)S(1)} %pad_maximum_fusion.4), channel_id=1, source_target_pairs={{0,4},{4,0},{8,12},{12,8},{16,20},{20,16},{24,28},{28,24},{1,5},{5... | collective-permute-start | bytes 491528 | tf_op jit(solution)/shard_map/ppermute | solution.py:253

commit v3 on v2

--- a/solution.py
+++ b/solution.py
@@ -40,7 +40,7 @@
 
 def blocks_of(parts):
     if parts == 8:
-        return [0, 2, 4, 6, 1, 3, 5, 7]
+        return [0, 6, 2, 4, 1, 7, 3, 5]
     relative = [0]
     for offset in [*range(1, REACH + 1), *range(-REACH, 0), parts // 2]:
         if offset % parts not in relative:
@@ -49,6 +49,7 @@
 
 
 EARLY = 3
+NEAR_FIRST = 3
 
 
 def receiver_of(me, block, parts):
@@ -63,14 +64,17 @@
     return result
 
 
-def call(kernel, out_shape, cost, *args, scalars=0):
-    spaces = [pl.BlockSpec(memory_space=pltpu.SMEM if at < scalars else pltpu.VMEM) for at in range(len(args))]
-    outs = [pl.BlockSpec(memory_space=pltpu.VMEM)] * len(out_shape)
+def call(kernel, out_shape, cost, *args, scalars=0, remote=0, scratch=()):
+    held = slice(scalars, scalars + remote)
+    args = list(args)
+    args[held] = [pltpu.with_memory_space_constraint(arg, pltpu.HBM) for arg in args[held]]
+    spaces = [pltpu.SMEM] * scalars + [pltpu.HBM] * remote + [pltpu.VMEM] * (len(args) - scalars - remote)
     return pl.pallas_call(
         kernel,
         out_shape=[jax.ShapeDtypeStruct(shape, dtype) for shape, dtype in out_shape],
-        in_specs=spaces,
-        out_specs=outs,
+        in_specs=[pl.BlockSpec(memory_space=space) for space in spaces],
+        out_specs=[pl.BlockSpec(memory_space=pltpu.VMEM)] * len(out_shape),
+        scratch_shapes=scratch,
         compiler_params=pltpu.CompilerParams(vmem_limit_bytes=VMEM_LIMIT),
         cost_estimate=pl.CostEstimate(flops=cost[0], bytes_accessed=cost[1], transcendentals=0),
     )(*args)
@@ -104,9 +108,31 @@
             base = base + high_ref.shape[0]
 
 
-def plan_kernel(parts, capacity, me_ref, neighbours_ref, weights_ref, potential_ref, routes_ref, targets_ref, values_ref, diagonal_ref, select_ref, near_high, near_low):
+def plan_kernel(parts, paired, me_ref, *refs):
+    sources, refs = refs[:6], refs[6:]
+    targets_ref, values_ref, diagonal_ref, select_ref, near_high, near_low, field_ref, frozen_ref, late_ref, *refs = refs
+    early_refs, (routes_ref, neighbours_ref, weights_ref, potential_ref, arrival) = refs[:-5], refs[-5:]
+    arrays = [routes_ref, field_ref, neighbours_ref, weights_ref, potential_ref, frozen_ref]
+    copies = [
+        pltpu.make_async_copy(source, array, arrival.at[at])
+        for at, (source, array) in enumerate(zip(sources, arrays, strict=True))
+    ]
+    for copy in copies:
+        copy.start()
     count, points = neighbours_ref.shape
+    capacity = routes_ref.shape[2]
+    rows = field_ref.shape[0]
     me = me_ref[0]
+    copies[0].wait()
+    copies[1].wait()
+    row_id = lax.broadcasted_iota(jnp.int32, (points, capacity), 0)
+    for place, block in enumerate(blocks_of(parts)):
+        route = routes_ref[0, pl.ds(receiver_of(me, block, parts), 1), :]
+        select_ref[:, pl.ds(place * capacity, capacity)] = jnp.where(row_id == route, 1.0, 0.0).astype(BF16)
+    both, _ = stacked(field_ref[...])
+    pack(both, select_ref, early_refs, late_ref, paired)
+    for copy in copies[2:]:
+        copy.wait()
     named = neighbours_ref[...]
     ghost = jnp.maximum(named - points, 0)
     sender = ghost // capacity
@@ -124,10 +150,6 @@
     for k in range(count):
         targets_ref[k : k + 1] = targets[k]
         values_ref[k : k + 1] = values[k]
-    row_id = lax.broadcasted_iota(jnp.int32, (points, capacity), 0)
-    for place, block in enumerate(blocks_of(parts)):
-        route = routes_ref[pl.ds(receiver_of(me, block, parts), 1), :]
-        select_ref[:, pl.ds(place * capacity, capacity)] = jnp.where(row_id == route, 1.0, 0.0).astype(BF16)
     stencil_rows(targets, values, [(near_high, near_low)], 0)
 
 
@@ -170,47 +192,61 @@
     return product(both, high, wide_high, wide_low)
 
 
-def send(term, select_ref, turned_high, turned_low, early_refs, late_ref, partial_ref, paired):
-    rows = term.shape[0]
-    both, high = stacked(term)
-    partial = intersect(both, high, turned_high, turned_low)
-    partial_ref[...] = partial
+def slots_of(early_refs, late_ref, paired):
+    slots = [(ref, 0) for ref in early_refs]
+    if paired:
+        return slots + [(late_ref, 0)] + [(ref, 1) for ref in early_refs]
+    return slots + [(late_ref, at) for at in range(late_ref.shape[0])]
+
+
+def pack(both, select_ref, early_refs, late_ref, paired):
+    rows = both.shape[0] // 2
+    capacity = late_ref.shape[2]
+    for place, (ref, at) in enumerate(slots_of(early_refs, late_ref, paired)):
+        packed = dot(both, select_ref[:, pl.ds((place + 1) * capacity, capacity)])
+        ref[at, :rows, :] = packed[:rows] + packed[rows:]
+
+
+def spread(partial, early_refs, late_ref, paired):
     tall, width = partial.shape
     capacity = late_ref.shape[2]
     if width < capacity:
         partial = jnp.concatenate([partial, jnp.zeros((tall, capacity - width), F32)], axis=1)
-    late = late_ref.shape[0]
-    places = [(ref, 0) for ref in early_refs]
-    if paired:
-        places += [(late_ref, 0)] + [(ref, 1) for ref in early_refs]
-    else:
-        places += [(late_ref, at) for at in range(late)]
-    for place, (ref, at) in enumerate(places):
-        packed = dot(both, select_ref[:, pl.ds((place + 1) * capacity, capacity)])
-        ref[at, :rows, :] = packed[:rows] + packed[rows:]
-        ref[at, rows:, :] = partial
-
-
-def start_kernel(paired, frozen_ref, field_ref, select_ref, wide_high, wide_low, turned_high, turned_low, partial_ref, late_ref, *early_refs):
-    groups = frozen_ref.shape[0]
-    real = jnp.concatenate([frozen_ref[g, 0] for g in range(groups)], axis=0)
-    imag = jnp.concatenate([frozen_ref[g, 1] for g in range(groups)], axis=0)
+    for ref, at in slots_of(early_refs, late_ref, paired):
+        ref[at, -tall:, :] = partial
+
+
+def start_kernel(paired, groups, *refs):
+    pieces, (field_ref, late_in, *refs) = refs[:groups], refs[groups:]
+    early_in, (wide_high, wide_low, turned_high, turned_low, partial_ref, late_ref, *early_refs) = refs[:EARLY], refs[EARLY:]
+    rows = field_ref.shape[0]
+    pieces = [piece[...] for piece in pieces]
+    if pieces[0].ndim == 4:
+        pieces = [pieces[0][band] for band in range(pieces[0].shape[0])]
+    real = jnp.concatenate([piece[0] for piece in pieces], axis=0)
+    imag = jnp.concatenate([piece[1] for piece in pieces], axis=0)
     wide = jnp.concatenate([real, -imag, imag, real], axis=0)
     wide_high[...], wide_low[...] = split(wide)
-    high, low = split(wide.T)
-    turned_high[...] = high
-    turned_low[...] = low
-    send(field_ref[...], select_ref, high, low, early_refs, late_ref, partial_ref, paired)
-
-
-def near_kernel(term_ref, select_ref, near_high, near_low, diagonal_ref, base_ref):
+    turned_high[...], turned_low[...] = split(wide.T)
+    both, high = stacked(field_ref[...])
+    partial = intersect(both, high, turned_high[...], turned_low[...])
+    partial_ref[...] = partial
+    for source, target in zip([late_in, *early_in], [late_ref, *early_refs], strict=True):
+        target[:, :rows, :] = source[:, :rows, :]
+    spread(partial, early_refs, late_ref, paired)
+
+
+def near_kernel(term_ref, select_ref, first_high, first_low, rest_high, rest_low, diagonal_ref, base_ref):
     rows, points = term_ref.shape
     term = term_ref[...]
     both, high = stacked(term)
-    own = dot(both, select_ref[:, : near_high.shape[0] - points])
+    own = dot(both, select_ref[:, : first_high.shape[0] + rest_high.shape[0] - points])
     own_both, own_high = stacked(own[:rows] + own[rows:])
-    value = product(both, high, near_high[:points], near_low[:points])
-    value = value + product(own_both, own_high, near_high[points:], near_low[points:])
+    cut = first_high.shape[0]
+    value = product(both[:, :cut], high[:, :cut], first_high[...], first_low[...])
+    both = jnp.concatenate([both[:, cut:], own_both], axis=1)
+    high = jnp.concatenate([high[:, cut:], own_high], axis=1)
+    value = value + product(both, high, rest_high[...], rest_low[...])
     base_ref[...] = term * diagonal_ref[...] - value
 
 
@@ -246,7 +282,11 @@
         return
     _, term_ref, partial_ref, late_out, *early_outs = outs
     term_ref[...] = term
-    send(term, select_ref, turned_high[...], turned_low[...], early_outs, late_out, partial_ref, paired)
+    both, high = stacked(term)
+    partial = intersect(both, high, turned_high[...], turned_low[...])
+    partial_ref[...] = partial
+    pack(both, select_ref, early_outs, late_out, paired)
+    spread(partial, early_outs, late_out, paired)
 
 
 def swap(value, bits, parts):
@@ -260,11 +300,8 @@
 def gather_frozen(frozen):
     bands = lax.axis_size("band")
     if bands <= 4:
-        pieces = [frozen]
-        for step in range(1, bands):
-            pieces.append(lax.ppermute(frozen, "band", [(at, (at + step) % bands) for at in range(bands)]))
-        return jnp.stack(pieces)
-    return lax.all_gather(frozen, "band", axis=0, tiled=False)
+        return [lax.ppermute(frozen, "band", [(at, (at + step) % bands) for at in range(bands)]) for step in range(1, bands)]
+    return [lax.all_gather(frozen, "band", axis=0, tiled=False)]
 
 
 def body(states, frozen, weights, potential, send_list, neighbours):
@@ -277,58 +314,77 @@
     places = len(relations)
     paired = parts == 8
     me = lax.axis_index("mesh").astype(jnp.int32).reshape(1)
-    field = states.reshape(rows, points)
     count = neighbours.shape[0]
 
-    full_frozen = gather_frozen(frozen)
-    near_rows, early_rows, late_rows = points + capacity, EARLY * capacity, (places - 1 - EARLY) * capacity
-    targets, values, diagonal, select, near_high, near_low = call(
-        functools.partial(plan_kernel, parts, capacity),
-        [((count, points), jnp.int32), ((count, points), F32), ((1, points), F32), ((points, places * capacity), BF16)]
-        + [((near_rows, points), BF16)] * 2,
-        (6 * near_rows * points, 12 << 20),
-        me, neighbours, weights, potential.reshape(1, points), send_list[0], scalars=1,
-    )
-    vectors = full_frozen.shape[0] * full_frozen.shape[2]
-    columns = 2 * vectors
+    bands = lax.axis_size("band")
+    pieces = gather_frozen(frozen)
+    columns = 2 * bands * frozen.shape[1]
     sum_shape = (half, columns) if columns >= LANES else (half * columns // LANES, LANES)
     tall = rows + sum_shape[0]
-    outgoing = [(sum_shape, F32), ((1 if paired else places - 1 - EARLY, tall, capacity), F32)]
+    outgoing = [((1 if paired else places - 1 - EARLY, tall, capacity), F32)]
     outgoing += [((2 if paired else 1, tall, capacity), F32)] * EARLY
+    first_rows = NEAR_FIRST * TILE
+    rest_rows = points + capacity - first_rows
+    early_rows, late_rows = EARLY * capacity, (places - 1 - EARLY) * capacity
+    targets, values, diagonal, select, first_high, first_low, field, own_frozen, late, *early = call(
+        functools.partial(plan_kernel, parts, paired),
+        [((count, points), jnp.int32), ((count, points), F32), ((1, points), F32), ((points, places * capacity), BF16)]
+        + [((first_rows, points), BF16)] * 2
+        + [((rows, points), F32), (frozen.shape, F32)]
+        + outgoing,
+        (6 * first_rows * points, 12 << 20),
+        me, send_list, states.reshape(rows, points), neighbours, weights, potential.reshape(1, points), frozen,
+        scalars=1,
+        remote=6,
+        scratch=[
+            pltpu.VMEM(send_list.shape, jnp.int32),
+            pltpu.VMEM(neighbours.shape, jnp.int32),
+            pltpu.VMEM(weights.shape, F32),
+            pltpu.VMEM((1, points), F32),
+            pltpu.SemaphoreType.DMA((6,)),
+        ],
+    )
+    if len(pieces) == bands - 1:
+        pieces = [own_frozen, *pieces]
     wide_high, wide_low, turned_high, turned_low, partial, late, *early = call(
-        functools.partial(start_kernel, paired),
-        [((2 * columns, points), BF16)] * 2 + [((points, 2 * columns), BF16)] * 2 + outgoing,
-        (6 * rows * points * places * capacity, 4 << 20),
-        full_frozen, field, select,
+        functools.partial(start_kernel, paired, len(pieces)),
+        [((2 * columns, points), BF16)] * 2 + [((points, 2 * columns), BF16)] * 2 + [(sum_shape, F32)] + outgoing,
+        (6 * rows * points * 2 * columns, 4 << 20),
+        *pieces, field, late, *early,
     )
     total, term = field, field
-    ghost_matrices = None
     for order in range(1, TERMS + 1):
         if paired:
             early = [swap(block, bits, parts) for block, bits in zip(early, relations[1 : 1 + EARLY], strict=True)]
         else:
             early = [move(block, offset, parts) for block, offset in zip(early, relations[1:], strict=False)]
-        if ghost_matrices is None:
-            ghost_matrices = call(
-                functools.partial(ghost_kernel, near_rows),
-                [((early_rows, points), BF16)] * 2 + [((late_rows, points), BF16)] * 2,
-                (6 * (early_rows + late_rows) * points, 24 << 20),
+        if order == 1:
+            rest_high, rest_low, early_high, early_low = call(
+                functools.partial(ghost_kernel, first_rows),
+                [((rest_rows, points), BF16)] * 2 + [((early_rows, points), BF16)] * 2,
+                (6 * (rest_rows + early_rows) * points, 12 << 20),
                 targets, values,
             )
-            early_high, early_low, late_high, late_low = ghost_matrices
         (base,) = call(
             near_kernel,
             [((rows, points), F32)],
-            (6 * rows * points * near_rows, 16 << 20),
-            term, select, near_high, near_low, diagonal,
+            (6 * rows * points * (first_rows + rest_rows), 16 << 20),
+            term, select, first_high, first_low, rest_high, rest_low, diagonal,
         )
         if paired:
             late = jnp.concatenate([late] + [block[1:] for block in early], axis=0)
-            late, base = lax.optimization_barrier((late, base))
+            late, base, targets = lax.optimization_barrier((late, base, targets))
             late = swap(late, 1, parts)
         else:
             late = jnp.stack(
                 [move(late[at], offset, parts) for at, offset in enumerate(relations[1 + EARLY :])]
+            )
+        if order == 1:
+            late_high, late_low = call(
+                functools.partial(ghost_kernel, first_rows + rest_rows + early_rows),
+                [((late_rows, points), BF16)] * 2,
+                (6 * late_rows * points, 12 << 20),
+                targets, values,
             )
         base, sums = call(
             early_kernel,
@@ -339,7 +395,7 @@
         last = order == TERMS
         shapes = [((rows, points), F32)]
         if not last:
-            shapes += [((rows, points), F32)] + outgoing
+            shapes += [((rows, points), F32), (sum_shape, F32)] + outgoing
         outs = call(
             functools.partial(late_kernel, order, last, paired),
             shapes,

time: 62.8 us -> 56.7 us (0.903)
  local copies, waits for them, and re-layouts: 3.84 us -> 0.05 us
  waiting for transfers between devices: 13.8 us -> 11.8 us
  other arithmetic: 0.92 us -> 0.06 us
  Pallas kernels: 23.3 us -> 24 us
    unnamed x10 -> x0, local copies, waits for them, and re-layouts: 3.8 us -> none
    ppermute x16, waiting for transfers between devices: 13.8 us -> 10.6 us  [swap(): lax.ppermute(value, 'mesh', [(part, part ^ bits) for part in range(parts)])]
    ppermute x3, waiting for transfers between devices: 0.01 us -> 1.27 us  [gather_frozen(): lax.ppermute(frozen, 'band', [(at, (at + step) % bands) for at in range(b...]
    another operation x1 -> x0, other arithmetic: 0.86 us -> none  [gather_frozen(): return jnp.stack(pieces)]
    pallas_call x15 -> x16, Pallas kernels: 23.3 us -> 24 us  [call(): pl.pallas_call(kernel, out_shape=[jax.ShapeDtypeStruct(shape, dtype) for...]
  transfers between devices with their start and end apart: 19 -> 19, of which waited for: 13 -> 12; matrix products, arithmetic and copies ran while one was open for 0% -> 0% of each run, Pallas kernels for 25% -> 29%
where the time goes in v3:
time: 56.7 us; the launch traced here: 56.5 us
  Pallas kernels  24 us (42%)
  starting transfers between devices  20.4 us (36%)
  waiting for transfers between devices  11.8 us (21%)
    pallas_call x16, Pallas kernels, call(): pl.pallas_call(kernel, out_shape=[jax.ShapeDtypeStruct(shape, dtype) for...  24 us
    ppermute x16, starting transfers between devices, swap(): lax.ppermute(value, 'mesh', [(part, part ^ bits) for part in range(parts)])  14.3 us
    ppermute x16, waiting for transfers between devices, swap(): lax.ppermute(value, 'mesh', [(part, part ^ bits) for part in range(parts)])  10.6 us
    ppermute x3, starting transfers between devices, gather_frozen(): lax.ppermute(frozen, 'band', [(at, (at + step) % bands) for at in range(b...  6.06 us
    ppermute x3, waiting for transfers between devices, gather_frozen(): lax.ppermute(frozen, 'band', [(at, (at + step) % bands) for at in range(b...  1.27 us
  transfers between devices with their start and end apart: 19, of which 12 were waited for; matrix products, arithmetic and copies ran while one was open for 0% of the time, Pallas kernels for 29%

profile of v3, /device:TPU:0, one launch (start us, length us, event | category | flops | bytes accessed | tf_op | source)
XLA Modules:
  0.0 56.5 jit_solution(3996625789611179395)
XLA Ops:
  0.0 3.0 %collective-permute-start = (f32[2,8,1024]{2,1,0:T(8,128)}, f32[2,8,1024]{2,1,0:T(8,128)S(1)}, u32[]{:S(2)}, u32[]{:S(2)}) collective-permute-start(f32[2,8,1024]{2,1,0:T(8,128)} %refs_5_.1), channel_id=1, source_target_pairs={{0,1},{1,2},{2,3},{3,0},{4,5},{5,6},{6,7},{7,4},{8,9},{9,10},{10,1... | collective-permute-start | bytes 196616 | tf_op jit(solution)/shard_map/ppermute | solution.py:303
  3.0 2.0 %collective-permute-start.2 = (f32[2,8,1024]{2,1,0:T(8,128)}, f32[2,8,1024]{2,1,0:T(8,128)S(1)}, u32[]{:S(2)}, u32[]{:S(2)}) collective-permute-start(f32[2,8,1024]{2,1,0:T(8,128)} %refs_5_.1), channel_id=1, source_target_pairs={{0,3},{1,0},{2,1},{3,2},{4,7},{5,4},{6,5},{7,6},{8,11},{9,8},{10,9... | collective-permute-start | bytes 196616 | tf_op jit(solution)/shard_map/ppermute | solution.py:303
  5.1 1.0 %collective-permute-start.1 = (f32[2,8,1024]{2,1,0:T(8,128)}, f32[2,8,1024]{2,1,0:T(8,128)S(1)}, u32[]{:S(2)}, u32[]{:S(2)}) collective-permute-start(f32[2,8,1024]{2,1,0:T(8,128)} %refs_5_.1), channel_id=1, source_target_pairs={{0,2},{1,3},{2,0},{3,1},{4,6},{5,7},{6,4},{7,5},{8,10},{9,11},{10,... | collective-permute-start | bytes 196616 | tf_op jit(solution)/shard_map/ppermute | solution.py:303
  6.1 4.2 %shard_map.64 = (s32[8,1024]{1,0:T(8,128)S(1)}, f32[8,1024]{1,0:T(8,128)S(1)}, f32[1,1024]{1,0:T(1,128)S(1)}, bf16[1024,2048]{1,0:T(8,128)(2,1)S(1)}, bf16[768,1...) custom-call(s32[1]{0:T(128)} %bitcast.me_ref, ...), custom_call_target="tpu_custom_call" | custom-call | flops 4718592 | bytes 12582912 | tf_op jit(solution)/shard_map/pallas_call | solution.py:72
  10.3 0.0 collective-permute-done.refs_1_
  10.3 0.0 collective-permute-done.2.refs_3_
  10.3 1.3 %collective-permute-done.1.refs_2_ = f32[2,8,1024]{2,1,0:T(8,128)S(1)} collective-permute-done((f32[2,8,1024]{2,1,0:T(8,128)}, f32[2,8,1024]{2,1,0:T(8,128)S(1)}, u32[]{:S(2)}, u32[]{:S(2)}) %collective-permute-start.1) | collective-permute-done | bytes 65568 | tf_op jit(solution)/shard_map/ppermute | solution.py:303
  11.6 0.6 %shard_map.65 = (bf16[128,1024]{1,0:T(8,128)(2,1)S(1)}, bf16[128,1024]{1,0:T(8,128)(2,1)S(1)}, bf16[1024,128]{1,0:T(8,128)(2,1)S(1)}, bf16[1024,128]{1,0:T(8,128...) custom-call(f32[2,8,1024]{2,1,0:T(8,128)S(1)} %get-tuple-element.70., ...), custom_call_target="tpu_custom_call" | custom-call | flops 25165824 | bytes 4194304 | tf_op jit(solution)/shard_map/pallas_call | solution.py:72
  12.1 2.5 %collective-permute-start.3 = (f32[2,40,256]{2,1,0:T(8,128)S(1)}, f32[2,40,256]{2,1,0:T(8,128)S(1)}, u32[]{:S(2)}, u32[]{:S(2)}) collective-permute-start(f32[2,40,256]{2,1,0:T(8,128)S(1)} %get-tuple-element.77), channel_id=1, source_target_pairs={{0,24},{4,28},{8,16},{12,20},{16,8},{20,12},{24,0},{28,4},{1,25},{... | collective-permute-start | bytes 245768 | tf_op jit(solution)/shard_map/ppermute | solution.py:293
  14.6 0.5 collective-permute-start.4
  15.1 0.5 collective-permute-start.5
  15.6 2.9 %shard_map.66 = (bf16[512,1024]{1,0:T(8,128)(2,1)S(1)}, bf16[512,1024]{1,0:T(8,128)(2,1)S(1)}, bf16[768,1024]{1,0:T(8,128)(2,1)S(1)}, bf16[768,1024]{1,0:T(8,128)(2,1)S(1)}) custom-call(s32[8,1024]{1,0:T(8,128)S(1)} %get-tuple-element.95.targets_ref, f32[8,1024]{1,0:T(8,128)S(1)} %get-tuple-element.84.values_ref), custom_call_target="tpu_custom_call" | custom-call | flops 7864320 | bytes 12582912 | tf_op jit(solution)/shard_map/pallas_call | solution.py:72
  18.5 1.1 %shard_map.67.base_ref = f32[32,1024]{1,0:T(8,128)S(1)} custom-call(f32[32,1024]{1,0:T(8,128)S(1)} %get-tuple-element.71.refs_4_.term_ref.total_ref, bf16[1024,2048]{1,0:T(8,128)(2,1)S(1)} %get-tuple-element.80.select_ref, bf16[768,1024]{1,0:T(8,128)(2,1)S(1)} %get-tuple-element.81.first_high, bf16[768,1024]{1,0:T(8,128)(2,1)S(1)} %get-tuple-element.82.first_low, ...), custom_call_target="tpu_custom_call" | custom-call | flops 251658240 | bytes 16777216 | tf_op jit(solution)/shard_map/pallas_call | solution.py:72
  19.6 0.0 collective-permute-done.3.refs_0_
  19.6 0.0 collective-permute-done.4.refs_1_
  19.6 0.0 collective-permute-done.5.refs_2_
  19.7 0.1 collective-permute-start.6
  19.8 2.5 %shard_map.69 = (bf16[1024,1024]{1,0:T(8,128)(2,1)S(1)}, bf16[1024,1024]{1,0:T(8,128)(2,1)S(1)}) custom-call(s32[8,1024]{1,0:T(8,128)S(1)} %get-tuple-element.95.targets_ref, f32[8,1024]{1,0:T(8,128)S(1)} %get-tuple-element.84.values_ref), custom_call_target="tpu_custom_call" | custom-call | flops 6291456 | bytes 12582912 | tf_op jit(solution)/shard_map/pallas_call | solution.py:72
  22.3 0.6 %shard_map.68 = (f32[32,1024]{1,0:T(8,128)S(1)}, f32[8,128]{1,0:T(8,128)S(1)}) custom-call(f32[32,1024]{1,0:T(8,128)S(1)} %shard_map.67.base_ref, f32[8,128]{1,0:T(8,128)S(1)} %get-tuple-element.90.partial_ref, bf16[768,1024]{1,0:T(8,128)(2,1)S(1)} %get-tuple-element.91.early_high, bf16[768,1024]{1,0:T(8,128)(2,1)S(1)} %get-tuple-element.92.early_low, ...), custom_call_target="tpu_custom_call" | custom-call | flops 150994944 | bytes 4194304 | tf_op jit(solution)/shard_map/pallas_call | solution.py:72
  22.9 0.0 collective-permute-done.6.late_ref
  23.0 1.8 %shard_map.70 = (f32[32,1024]{1,0:T(8,128)S(1)}, f32[32,1024]{1,0:T(8,128)S(1)}, f32[8,128]{1,0:T(8,128)S(1)}, f32[1,40,256]{2,1,0:T(8,128)S(1)}, f32[2,40,256]{...) custom-call(f32[4,40,256]{2,1,0:T(8,128)S(1)} %collective-permute-done.6.late_ref, ...), custom_call_target="tpu_custom_call" | custom-call | flops 201326592 | bytes 12582912 | tf_op jit(solution)/shard_map/pallas_call | solution.py:72
  24.7 2.5 %collective-permute-start.7 = (f32[2,40,256]{2,1,0:T(8,128)S(1)}, f32[2,40,256]{2,1,0:T(8,128)S(1)}, u32[]{:S(2)}, u32[]{:S(2)}) collective-permute-start(f32[2,40,256]{2,1,0:T(8,128)S(1)} %get-tuple-element.103), channel_id=1, source_target_pairs={{0,24},{4,28},{8,16},{12,20},{16,8},{20,12},{24,0},{28,4},{1,25},{... | collective-permute-start | bytes 245768 | tf_op jit(solution)/shard_map/ppermute | solution.py:293
  27.2 0.5 collective-permute-start.8
  27.7 0.5 collective-permute-start.9
  28.3 1.1 %shard_map.71.base_ref = f32[32,1024]{1,0:T(8,128)S(1)} custom-call(f32[32,1024]{1,0:T(8,128)S(1)} %get-tuple-element.106.term_ref, bf16[1024,2048]{1,0:T(8,128)(2,1)S(1)} %get-tuple-element.80.select_ref, bf16[768,1024]{1,0:T(8,128)(2,1)S(1)} %get-tuple-element.81.first_high, bf16[768,1024]{1,0:T(8,128)(2,1)S(1)} %get-tuple-element.82.first_low, ...), custom_call_target="tpu_custom_call" | custom-call | flops 251658240 | bytes 16777216 | tf_op jit(solution)/shard_map/pallas_call | solution.py:72
  29.3 1.6 %collective-permute-done.7.refs_0_ = f32[2,40,256]{2,1,0:T(8,128)S(1)} collective-permute-done((f32[2,40,256]{2,1,0:T(8,128)S(1)}, f32[2,40,256]{2,1,0:T(8,128)S(1)}, u32[]{:S(2)}, u32[]{:S(2)}) %collective-permute-start.7) | collective-permute-done | bytes 81952 | tf_op jit(solution)/shard_map/ppermute | solution.py:293
  30.9 1.4 %collective-permute-done.8.refs_1_ = f32[2,40,256]{2,1,0:T(8,128)S(1)} collective-permute-done((f32[2,40,256]{2,1,0:T(8,128)S(1)}, f32[2,40,256]{2,1,0:T(8,128)S(1)}, u32[]{:S(2)}, u32[]{:S(2)}) %collective-permute-start.8) | collective-permute-done | bytes 81952 | tf_op jit(solution)/shard_map/ppermute | solution.py:293
  32.3 0.0 collective-permute-done.9.refs_2_
  32.4 0.1 collective-permute-start.10
  32.4 0.6 %shard_map.72 = (f32[32,1024]{1,0:T(8,128)S(1)}, f32[8,128]{1,0:T(8,128)S(1)}) custom-call(f32[32,1024]{1,0:T(8,128)S(1)} %shard_map.71.base_ref, f32[8,128]{1,0:T(8,128)S(1)} %get-tuple-element.109.partial_ref, bf16[768,1024]{1,0:T(8,128)(2,1)S(1)} %get-tuple-element.91.early_high, bf16[768,1024]{1,0:T(8,128)(2,1)S(1)} %get-tuple-element.92.early_low, ...), custom_call_target="tpu_custom_call" | custom-call | flops 150994944 | bytes 4194304 | tf_op jit(solution)/shard_map/pallas_call | solution.py:72
  33.1 0.7 %collective-permute-done.10.late_ref = f32[4,40,256]{2,1,0:T(8,128)S(1)} collective-permute-done((f32[4,40,256]{2,1,0:T(8,128)S(1)}, f32[4,40,256]{2,1,0:T(8,128)S(1)}, u32[]{:S(2)}, u32[]{:S(2)}) %collective-permute-start.10) | collective-permute-done | bytes 163872 | tf_op jit(solution)/shard_map/ppermute | solution.py:293
  33.8 1.8 %shard_map.73 = (f32[32,1024]{1,0:T(8,128)S(1)}, f32[32,1024]{1,0:T(8,128)S(1)}, f32[8,128]{1,0:T(8,128)S(1)}, f32[1,40,256]{2,1,0:T(8,128)S(1)}, f32[2,40,256]{...) custom-call(f32[4,40,256]{2,1,0:T(8,128)S(1)} %collective-permute-done.10.late_ref, ...), custom_call_target="tpu_custom_call" | custom-call | flops 201326592 | bytes 12582912 | tf_op jit(solution)/shard_map/pallas_call | solution.py:72
  35.6 2.4 %collective-permute-start.11 = (f32[2,40,256]{2,1,0:T(8,128)S(1)}, f32[2,40,256]{2,1,0:T(8,128)S(1)}, u32[]{:S(2)}, u32[]{:S(2)}) collective-permute-start(f32[2,40,256]{2,1,0:T(8,128)S(1)} %get-tuple-element.114), channel_id=1, source_target_pairs={{0,24},{4,28},{8,16},{12,20},{16,8},{20,12},{24,0},{28,4},{1,25},{... | collective-permute-start | bytes 245768 | tf_op jit(solution)/shard_map/ppermute | solution.py:293
  38.0 0.5 collective-permute-start.12
  38.5 0.6 %collective-permute-start.13 = (f32[2,40,256]{2,1,0:T(8,128)S(1)}, f32[2,40,256]{2,1,0:T(8,128)S(1)}, u32[]{:S(2)}, u32[]{:S(2)}) collective-permute-start(f32[2,40,256]{2,1,0:T(8,128)S(1)} %get-tuple-element.116), channel_id=1, source_target_pairs={{0,16},{4,20},{8,24},{12,28},{16,0},{20,4},{24,8},{28,12},{1,17},{... | collective-permute-start | bytes 245768 | tf_op jit(solution)/shard_map/ppermute | solution.py:293
  39.1 1.1 %shard_map.74.base_ref = f32[32,1024]{1,0:T(8,128)S(1)} custom-call(f32[32,1024]{1,0:T(8,128)S(1)} %get-tuple-element.117.term_ref, bf16[1024,2048]{1,0:T(8,128)(2,1)S(1)} %get-tuple-element.80.select_ref, bf16[768,1024]{1,0:T(8,128)(2,1)S(1)} %get-tuple-element.81.first_high, bf16[768,1024]{1,0:T(8,128)(2,1)S(1)} %get-tuple-element.82.first_low, ...), custom_call_target="tpu_custom_call" | custom-call | flops 251658240 | bytes 16777216 | tf_op jit(solution)/shard_map/pallas_call | solution.py:72
  40.2 1.4 %collective-permute-done.11.refs_0_ = f32[2,40,256]{2,1,0:T(8,128)S(1)} collective-permute-done((f32[2,40,256]{2,1,0:T(8,128)S(1)}, f32[2,40,256]{2,1,0:T(8,128)S(1)}, u32[]{:S(2)}, u32[]{:S(2)}) %collective-permute-start.11) | collective-permute-done | bytes 81952 | tf_op jit(solution)/shard_map/ppermute | solution.py:293
  41.6 1.2 %collective-permute-done.12.refs_1_ = f32[2,40,256]{2,1,0:T(8,128)S(1)} collective-permute-done((f32[2,40,256]{2,1,0:T(8,128)S(1)}, f32[2,40,256]{2,1,0:T(8,128)S(1)}, u32[]{:S(2)}, u32[]{:S(2)}) %collective-permute-start.12) | collective-permute-done | bytes 81952 | tf_op jit(solution)/shard_map/ppermute | solution.py:293
  42.7 0.2 collective-permute-done.13.refs_2_
  43.0 0.1 collective-permute-start.14
  43.1 0.6 %shard_map.75 = (f32[32,1024]{1,0:T(8,128)S(1)}, f32[8,128]{1,0:T(8,128)S(1)}) custom-call(f32[32,1024]{1,0:T(8,128)S(1)} %shard_map.74.base_ref, f32[8,128]{1,0:T(8,128)S(1)} %get-tuple-element.120.partial_ref, bf16[768,1024]{1,0:T(8,128)(2,1)S(1)} %get-tuple-element.91.early_high, bf16[768,1024]{1,0:T(8,128)(2,1)S(1)} %get-tuple-element.92.early_low, ...), custom_call_target="tpu_custom_call" | custom-call | flops 150994944 | bytes 4194304 | tf_op jit(solution)/shard_map/pallas_call | solution.py:72
  43.7 0.7 %collective-permute-done.14.late_ref = f32[4,40,256]{2,1,0:T(8,128)S(1)} collective-permute-done((f32[4,40,256]{2,1,0:T(8,128)S(1)}, f32[4,40,256]{2,1,0:T(8,128)S(1)}, u32[]{:S(2)}, u32[]{:S(2)}) %collective-permute-start.14) | collective-permute-done | bytes 163872 | tf_op jit(solution)/shard_map/ppermute | solution.py:293
  44.4 1.8 %shard_map.76 = (f32[32,1024]{1,0:T(8,128)S(1)}, f32[32,1024]{1,0:T(8,128)S(1)}, f32[8,128]{1,0:T(8,128)S(1)}, f32[1,40,256]{2,1,0:T(8,128)S(1)}, f32[2,40,256]{...) custom-call(f32[4,40,256]{2,1,0:T(8,128)S(1)} %collective-permute-done.14.late_ref, ...), custom_call_target="tpu_custom_call" | custom-call | flops 201326592 | bytes 12582912 | tf_op jit(solution)/shard_map/pallas_call | solution.py:72
  46.2 2.2 %collective-permute-start.15 = (f32[2,40,256]{2,1,0:T(8,128)S(1)}, f32[2,40,256]{2,1,0:T(8,128)S(1)}, u32[]{:S(2)}, u32[]{:S(2)}) collective-permute-start(f32[2,40,256]{2,1,0:T(8,128)S(1)} %get-tuple-element.125), channel_id=1, source_target_pairs={{0,24},{4,28},{8,16},{12,20},{16,8},{20,12},{24,0},{28,4},{1,25},{... | collective-permute-start | bytes 245768 | tf_op jit(solution)/shard_map/ppermute | solution.py:293
  48.4 0.5 collective-permute-start.16
  48.9 0.8 %collective-permute-start.17 = (f32[2,40,256]{2,1,0:T(8,128)S(1)}, f32[2,40,256]{2,1,0:T(8,128)S(1)}, u32[]{:S(2)}, u32[]{:S(2)}) collective-permute-start(f32[2,40,256]{2,1,0:T(8,128)S(1)} %get-tuple-element.127), channel_id=1, source_target_pairs={{0,16},{4,20},{8,24},{12,28},{16,0},{20,4},{24,8},{28,12},{1,17},{... | collective-permute-start | bytes 245768 | tf_op jit(solution)/shard_map/ppermute | solution.py:293
  49.7 1.1 %shard_map.77.base_ref = f32[32,1024]{1,0:T(8,128)S(1)} custom-call(f32[32,1024]{1,0:T(8,128)S(1)} %get-tuple-element.128.term_ref, bf16[1024,2048]{1,0:T(8,128)(2,1)S(1)} %get-tuple-element.80.select_ref, bf16[768,1024]{1,0:T(8,128)(2,1)S(1)} %get-tuple-element.81.first_high, bf16[768,1024]{1,0:T(8,128)(2,1)S(1)} %get-tuple-element.82.first_low, ...), custom_call_target="tpu_custom_call" | custom-call | flops 251658240 | bytes 16777216 | tf_op jit(solution)/shard_map/pallas_call | solution.py:72
  50.8 1.4 %collective-permute-done.15.refs_0_ = f32[2,40,256]{2,1,0:T(8,128)S(1)} collective-permute-done((f32[2,40,256]{2,1,0:T(8,128)S(1)}, f32[2,40,256]{2,1,0:T(8,128)S(1)}, u32[]{:S(2)}, u32[]{:S(2)}) %collective-permute-start.15) | collective-permute-done | bytes 81952 | tf_op jit(solution)/shard_map/ppermute | solution.py:293
  52.2 1.0 %collective-permute-done.16.refs_1_ = f32[2,40,256]{2,1,0:T(8,128)S(1)} collective-permute-done((f32[2,40,256]{2,1,0:T(8,128)S(1)}, f32[2,40,256]{2,1,0:T(8,128)S(1)}, u32[]{:S(2)}, u32[]{:S(2)}) %collective-permute-start.16) | collective-permute-done | bytes 81952 | tf_op jit(solution)/shard_map/ppermute | solution.py:293
  53.2 0.2 collective-permute-done.17.refs_2_
  53.4 0.1 collective-permute-start.18
  53.5 0.6 %shard_map.78 = (f32[32,1024]{1,0:T(8,128)S(1)}, f32[8,128]{1,0:T(8,128)S(1)}) custom-call(f32[32,1024]{1,0:T(8,128)S(1)} %shard_map.77.base_ref, f32[8,128]{1,0:T(8,128)S(1)} %get-tuple-element.131.partial_ref, bf16[768,1024]{1,0:T(8,128)(2,1)S(1)} %get-tuple-element.91.early_high, bf16[768,1024]{1,0:T(8,128)(2,1)S(1)} %get-tuple-element.92.early_low, ...), custom_call_target="tpu_custom_call" | custom-call | flops 150994944 | bytes 4194304 | tf_op jit(solution)/shard_map/pallas_call | solution.py:72
  54.1 0.7 %collective-permute-done.18.late_ref = f32[4,40,256]{2,1,0:T(8,128)S(1)} collective-permute-done((f32[4,40,256]{2,1,0:T(8,128)S(1)}, f32[4,40,256]{2,1,0:T(8,128)S(1)}, u32[]{:S(2)}, u32[]{:S(2)}) %collective-permute-start.18) | collective-permute-done | bytes 163872 | tf_op jit(solution)/shard_map/ppermute | solution.py:293
  54.9 1.6 %shard_map.79 = f32[32,1024]{1,0:T(8,128)} custom-call(f32[4,40,256]{2,1,0:T(8,128)S(1)} %collective-permute-done.18.late_ref, f32[32,1024]{1,0:T(8,128)S(1)} %get-tuple-element.132.base_ref, f32[8,128]{1,0:T(8,128)S(1)} %get-tuple-element.133.sums_ref, f32[32,1024]{1,0:T(8,128)S(1)} %get-tuple-element.134.total_ref, ...), custom_call_target="tpu_custom_call" | custom-call | flops 201326592 | bytes 12582912 | tf_op jit(solution)/shard_map/pallas_call | solution.py:72
  (16 shorter events, 0.1 us)
Async XLA Ops:
  0.0 10.3 %collective-permute-start = (f32[2,8,1024]{2,1,0:T(8,128)}, f32[2,8,1024]{2,1,0:T(8,128)S(1)}, u32[]{:S(2)}, u32[]{:S(2)}) collective-permute-start(f32[2,8,1024]{2,1,0:T(8,128)} %refs_5_.1), channel_id=1, source_target_pairs={{0,1},{1,2},{2,3},{3,0},{4,5},{5,6},{6,7},{7,4},{8,9},{9,10},{10,1... | collective-permute-start | bytes 196616 | tf_op jit(solution)/shard_map/ppermute | solution.py:303
  3.0 7.3 %collective-permute-start.2 = (f32[2,8,1024]{2,1,0:T(8,128)}, f32[2,8,1024]{2,1,0:T(8,128)S(1)}, u32[]{:S(2)}, u32[]{:S(2)}) collective-permute-start(f32[2,8,1024]{2,1,0:T(8,128)} %refs_5_.1), channel_id=1, source_target_pairs={{0,3},{1,0},{2,1},{3,2},{4,7},{5,4},{6,5},{7,6},{8,11},{9,8},{10,9... | collective-permute-start | bytes 196616 | tf_op jit(solution)/shard_map/ppermute | solution.py:303
  5.1 6.5 %collective-permute-start.1 = (f32[2,8,1024]{2,1,0:T(8,128)}, f32[2,8,1024]{2,1,0:T(8,128)S(1)}, u32[]{:S(2)}, u32[]{:S(2)}) collective-permute-start(f32[2,8,1024]{2,1,0:T(8,128)} %refs_5_.1), channel_id=1, source_target_pairs={{0,2},{1,3},{2,0},{3,1},{4,6},{5,7},{6,4},{7,5},{8,10},{9,11},{10,... | collective-permute-start | bytes 196616 | tf_op jit(solution)/shard_map/ppermute | solution.py:303
  12.1 7.5 %collective-permute-start.3 = (f32[2,40,256]{2,1,0:T(8,128)S(1)}, f32[2,40,256]{2,1,0:T(8,128)S(1)}, u32[]{:S(2)}, u32[]{:S(2)}) collective-permute-start(f32[2,40,256]{2,1,0:T(8,128)S(1)} %get-tuple-element.77), channel_id=1, source_target_pairs={{0,24},{4,28},{8,16},{12,20},{16,8},{20,12},{24,0},{28,4},{1,25},{... | collective-permute-start | bytes 245768 | tf_op jit(solution)/shard_map/ppermute | solution.py:293
  14.6 5.0 %collective-permute-start.4 = (f32[2,40,256]{2,1,0:T(8,128)S(1)}, f32[2,40,256]{2,1,0:T(8,128)S(1)}, u32[]{:S(2)}, u32[]{:S(2)}) collective-permute-start(f32[2,40,256]{2,1,0:T(8,128)S(1)} %get-tuple-element.78), channel_id=1, source_target_pairs={{0,8},{4,12},{8,0},{12,4},{16,24},{20,28},{24,16},{28,20},{1,9},{5... | collective-permute-start | bytes 245768 | tf_op jit(solution)/shard_map/ppermute | solution.py:293
  15.1 4.5 %collective-permute-start.5 = (f32[2,40,256]{2,1,0:T(8,128)S(1)}, f32[2,40,256]{2,1,0:T(8,128)S(1)}, u32[]{:S(2)}, u32[]{:S(2)}) collective-permute-start(f32[2,40,256]{2,1,0:T(8,128)S(1)} %get-tuple-element.79), channel_id=1, source_target_pairs={{0,16},{4,20},{8,24},{12,28},{16,0},{20,4},{24,8},{28,12},{1,17},{... | collective-permute-start | bytes 245768 | tf_op jit(solution)/shard_map/ppermute | solution.py:293
  19.7 3.3 %collective-permute-start.6 = (f32[4,40,256]{2,1,0:T(8,128)S(1)}, f32[4,40,256]{2,1,0:T(8,128)S(1)}, u32[]{:S(2)}, u32[]{:S(2)}) collective-permute-start(f32[4,40,256]{2,1,0:T(8,128)S(1)} %pad_maximum_fusion), channel_id=1, source_target_pairs={{0,4},{4,0},{8,12},{12,8},{16,20},{20,16},{24,28},{28,24},{1,5},{5... | collective-permute-start | bytes 491528 | tf_op jit(solution)/shard_map/ppermute | solution.py:293
  24.7 6.2 %collective-permute-start.7 = (f32[2,40,256]{2,1,0:T(8,128)S(1)}, f32[2,40,256]{2,1,0:T(8,128)S(1)}, u32[]{:S(2)}, u32[]{:S(2)}) collective-permute-start(f32[2,40,256]{2,1,0:T(8,128)S(1)} %get-tuple-element.103), channel_id=1, source_target_pairs={{0,24},{4,28},{8,16},{12,20},{16,8},{20,12},{24,0},{28,4},{1,25},{... | collective-permute-start | bytes 245768 | tf_op jit(solution)/shard_map/ppermute | solution.py:293
  27.2 5.1 %collective-permute-start.8 = (f32[2,40,256]{2,1,0:T(8,128)S(1)}, f32[2,40,256]{2,1,0:T(8,128)S(1)}, u32[]{:S(2)}, u32[]{:S(2)}) collective-permute-start(f32[2,40,256]{2,1,0:T(8,128)S(1)} %get-tuple-element.104), channel_id=1, source_target_pairs={{0,8},{4,12},{8,0},{12,4},{16,24},{20,28},{24,16},{28,20},{1,9},{5... | collective-permute-start | bytes 245768 | tf_op jit(solution)/shard_map/ppermute | solution.py:293
  27.7 4.6 %collective-permute-start.9 = (f32[2,40,256]{2,1,0:T(8,128)S(1)}, f32[2,40,256]{2,1,0:T(8,128)S(1)}, u32[]{:S(2)}, u32[]{:S(2)}) collective-permute-start(f32[2,40,256]{2,1,0:T(8,128)S(1)} %get-tuple-element.105), channel_id=1, source_target_pairs={{0,16},{4,20},{8,24},{12,28},{16,0},{20,4},{24,8},{28,12},{1,17},{... | collective-permute-start | bytes 245768 | tf_op jit(solution)/shard_map/ppermute | solution.py:293
  32.4 1.5 %collective-permute-start.10 = (f32[4,40,256]{2,1,0:T(8,128)S(1)}, f32[4,40,256]{2,1,0:T(8,128)S(1)}, u32[]{:S(2)}, u32[]{:S(2)}) collective-permute-start(f32[4,40,256]{2,1,0:T(8,128)S(1)} %pad_maximum_fusion.1), channel_id=1, source_target_pairs={{0,4},{4,0},{8,12},{12,8},{16,20},{20,16},{24,28},{28,24},{1,5},{5... | collective-permute-start | bytes 491528 | tf_op jit(solution)/shard_map/ppermute | solution.py:293
  35.6 6.0 %collective-permute-start.11 = (f32[2,40,256]{2,1,0:T(8,128)S(1)}, f32[2,40,256]{2,1,0:T(8,128)S(1)}, u32[]{:S(2)}, u32[]{:S(2)}) collective-permute-start(f32[2,40,256]{2,1,0:T(8,128)S(1)} %get-tuple-element.114), channel_id=1, source_target_pairs={{0,24},{4,28},{8,16},{12,20},{16,8},{20,12},{24,0},{28,4},{1,25},{... | collective-permute-start | bytes 245768 | tf_op jit(solution)/shard_map/ppermute | solution.py:293
  38.0 4.8 %collective-permute-start.12 = (f32[2,40,256]{2,1,0:T(8,128)S(1)}, f32[2,40,256]{2,1,0:T(8,128)S(1)}, u32[]{:S(2)}, u32[]{:S(2)}) collective-permute-start(f32[2,40,256]{2,1,0:T(8,128)S(1)} %get-tuple-element.115), channel_id=1, source_target_pairs={{0,8},{4,12},{8,0},{12,4},{16,24},{20,28},{24,16},{28,20},{1,9},{5... | collective-permute-start | bytes 245768 | tf_op jit(solution)/shard_map/ppermute | solution.py:293
  38.5 4.4 %collective-permute-start.13 = (f32[2,40,256]{2,1,0:T(8,128)S(1)}, f32[2,40,256]{2,1,0:T(8,128)S(1)}, u32[]{:S(2)}, u32[]{:S(2)}) collective-permute-start(f32[2,40,256]{2,1,0:T(8,128)S(1)} %get-tuple-element.116), channel_id=1, source_target_pairs={{0,16},{4,20},{8,24},{12,28},{16,0},{20,4},{24,8},{28,12},{1,17},{... | collective-permute-start | bytes 245768 | tf_op jit(solution)/shard_map/ppermute | solution.py:293
  43.0 1.5 %collective-permute-start.14 = (f32[4,40,256]{2,1,0:T(8,128)S(1)}, f32[4,40,256]{2,1,0:T(8,128)S(1)}, u32[]{:S(2)}, u32[]{:S(2)}) collective-permute-start(f32[4,40,256]{2,1,0:T(8,128)S(1)} %pad_maximum_fusion.2), channel_id=1, source_target_pairs={{0,4},{4,0},{8,12},{12,8},{16,20},{20,16},{24,28},{28,24},{1,5},{5... | collective-permute-start | bytes 491528 | tf_op jit(solution)/shard_map/ppermute | solution.py:293
  46.2 6.0 %collective-permute-start.15 = (f32[2,40,256]{2,1,0:T(8,128)S(1)}, f32[2,40,256]{2,1,0:T(8,128)S(1)}, u32[]{:S(2)}, u32[]{:S(2)}) collective-permute-start(f32[2,40,256]{2,1,0:T(8,128)S(1)} %get-tuple-element.125), channel_id=1, source_target_pairs={{0,24},{4,28},{8,16},{12,20},{16,8},{20,12},{24,0},{28,4},{1,25},{... | collective-permute-start | bytes 245768 | tf_op jit(solution)/shard_map/ppermute | solution.py:293
  48.4 4.8 %collective-permute-start.16 = (f32[2,40,256]{2,1,0:T(8,128)S(1)}, f32[2,40,256]{2,1,0:T(8,128)S(1)}, u32[]{:S(2)}, u32[]{:S(2)}) collective-permute-start(f32[2,40,256]{2,1,0:T(8,128)S(1)} %get-tuple-element.126), channel_id=1, source_target_pairs={{0,8},{4,12},{8,0},{12,4},{16,24},{20,28},{24,16},{28,20},{1,9},{5... | collective-permute-start | bytes 245768 | tf_op jit(solution)/shard_map/ppermute | solution.py:293
  48.9 4.4 %collective-permute-start.17 = (f32[2,40,256]{2,1,0:T(8,128)S(1)}, f32[2,40,256]{2,1,0:T(8,128)S(1)}, u32[]{:S(2)}, u32[]{:S(2)}) collective-permute-start(f32[2,40,256]{2,1,0:T(8,128)S(1)} %get-tuple-element.127), channel_id=1, source_target_pairs={{0,16},{4,20},{8,24},{12,28},{16,0},{20,4},{24,8},{28,12},{1,17},{... | collective-permute-start | bytes 245768 | tf_op jit(solution)/shard_map/ppermute | solution.py:293
  53.4 1.5 %collective-permute-start.18 = (f32[4,40,256]{2,1,0:T(8,128)S(1)}, f32[4,40,256]{2,1,0:T(8,128)S(1)}, u32[]{:S(2)}, u32[]{:S(2)}) collective-permute-start(f32[4,40,256]{2,1,0:T(8,128)S(1)} %pad_maximum_fusion.3), channel_id=1, source_target_pairs={{0,4},{4,0},{8,12},{12,8},{16,20},{20,16},{24,28},{28,24},{1,5},{5... | collective-permute-start | bytes 491528 | tf_op jit(solution)/shard_map/ppermute | solution.py:293

commit v4 on v3

--- a/solution.py
+++ b/solution.py
@@ -49,7 +49,7 @@
 
 
 EARLY = 3
-NEAR_FIRST = 3
+LATE_FIRST = 2
 
 
 def receiver_of(me, block, parts):
@@ -108,10 +108,10 @@
             base = base + high_ref.shape[0]
 
 
-def plan_kernel(parts, paired, me_ref, *refs):
+def plan_kernel(parts, me_ref, *refs):
     sources, refs = refs[:6], refs[6:]
-    targets_ref, values_ref, diagonal_ref, select_ref, near_high, near_low, field_ref, frozen_ref, late_ref, *refs = refs
-    early_refs, (routes_ref, neighbours_ref, weights_ref, potential_ref, arrival) = refs[:-5], refs[-5:]
+    targets_ref, values_ref, diagonal_ref, select_ref, near_high, near_low, field_ref, frozen_ref, *refs = refs
+    out, (routes_ref, neighbours_ref, weights_ref, potential_ref, arrival) = refs[:-5], refs[-5:]
     arrays = [routes_ref, field_ref, neighbours_ref, weights_ref, potential_ref, frozen_ref]
     copies = [
         pltpu.make_async_copy(source, array, arrival.at[at])
@@ -125,12 +125,17 @@
     me = me_ref[0]
     copies[0].wait()
     copies[1].wait()
-    row_id = lax.broadcasted_iota(jnp.int32, (points, capacity), 0)
+    tall = 16
+    row_id = lax.broadcasted_iota(jnp.int32, (tall, capacity), 0).astype(jnp.int16)
+    one, zero = jnp.ones((tall, capacity), BF16), jnp.zeros((tall, capacity), BF16)
     for place, block in enumerate(blocks_of(parts)):
         route = routes_ref[0, pl.ds(receiver_of(me, block, parts), 1), :]
-        select_ref[:, pl.ds(place * capacity, capacity)] = jnp.where(row_id == route, 1.0, 0.0).astype(BF16)
+        route = jnp.broadcast_to(route, (tall, capacity)).astype(jnp.int16)
+        for row in range(0, points, tall):
+            hit = route == row_id + jnp.int16(row)
+            select_ref[row : row + tall, pl.ds(place * capacity, capacity)] = jnp.where(hit, one, zero)
     both, _ = stacked(field_ref[...])
-    pack(both, select_ref, early_refs, late_ref, paired)
+    pack(both, select_ref, out[:-1], out[-1])
     for copy in copies[2:]:
         copy.wait()
     named = neighbours_ref[...]
@@ -192,33 +197,37 @@
     return product(both, high, wide_high, wide_low)
 
 
-def slots_of(early_refs, late_ref, paired):
+def slots_of(rows, tall, early_refs, late_ref):
     slots = [(ref, 0) for ref in early_refs]
-    if paired:
-        return slots + [(late_ref, 0)] + [(ref, 1) for ref in early_refs]
-    return slots + [(late_ref, at) for at in range(late_ref.shape[0])]
-
-
-def pack(both, select_ref, early_refs, late_ref, paired):
+    slots += [(late_ref.at[at], tall) for at in range(late_ref.shape[0])]
+    if early_refs[0].shape[0] > rows + tall:
+        slots += [(ref, rows + tall) for ref in early_refs]
+    return slots
+
+
+def pack(both, select_ref, early_refs, late_ref):
     rows = both.shape[0] // 2
-    capacity = late_ref.shape[2]
-    for place, (ref, at) in enumerate(slots_of(early_refs, late_ref, paired)):
+    capacity = early_refs[0].shape[1]
+    tall = late_ref.shape[1] - rows
+    for place, (ref, start) in enumerate(slots_of(rows, tall, early_refs, late_ref)):
         packed = dot(both, select_ref[:, pl.ds((place + 1) * capacity, capacity)])
-        ref[at, :rows, :] = packed[:rows] + packed[rows:]
-
-
-def spread(partial, early_refs, late_ref, paired):
+        ref[start : start + rows, :] = packed[:rows] + packed[rows:]
+
+
+def spread(partial, rows, early_refs, late_ref):
     tall, width = partial.shape
-    capacity = late_ref.shape[2]
+    capacity = early_refs[0].shape[1]
     if width < capacity:
         partial = jnp.concatenate([partial, jnp.zeros((tall, capacity - width), F32)], axis=1)
-    for ref, at in slots_of(early_refs, late_ref, paired):
-        ref[at, -tall:, :] = partial
-
-
-def start_kernel(paired, groups, *refs):
-    pieces, (field_ref, late_in, *refs) = refs[:groups], refs[groups:]
-    early_in, (wide_high, wide_low, turned_high, turned_low, partial_ref, late_ref, *early_refs) = refs[:EARLY], refs[EARLY:]
+    for ref in early_refs:
+        ref[rows : rows + tall, :] = partial
+    for at in range(late_ref.shape[0]):
+        late_ref[at, :tall, :] = partial
+
+
+def start_kernel(groups, *refs):
+    pieces, (field_ref, *refs) = refs[:groups], refs[groups:]
+    ready, (wide_high, wide_low, turned_high, turned_low, partial_ref, *out) = refs[: EARLY + 1], refs[EARLY + 1 :]
     rows = field_ref.shape[0]
     pieces = [piece[...] for piece in pieces]
     if pieces[0].ndim == 4:
@@ -231,23 +240,28 @@
     both, high = stacked(field_ref[...])
     partial = intersect(both, high, turned_high[...], turned_low[...])
     partial_ref[...] = partial
-    for source, target in zip([late_in, *early_in], [late_ref, *early_refs], strict=True):
-        target[:, :rows, :] = source[:, :rows, :]
-    spread(partial, early_refs, late_ref, paired)
-
-
-def near_kernel(term_ref, select_ref, first_high, first_low, rest_high, rest_low, diagonal_ref, base_ref):
+    tall = partial.shape[0]
+    (*early_in, late_in), (*early_refs, late_ref) = ready, out
+    slots_in = slots_of(rows, tall, early_in, late_in)
+    for (source, start), (target, _) in zip(slots_in, slots_of(rows, tall, early_refs, late_ref), strict=True):
+        target[start : start + rows, :] = source[start : start + rows, :]
+    spread(partial, rows, early_refs, late_ref)
+
+
+def near_kernel(first, term_ref, select_ref, near_high, near_low, diagonal_ref, *refs):
+    if first is not None:
+        targets_ref, values_ref, base_ref, *outs = refs
+        ghost_kernel(first, targets_ref, values_ref, *outs)
+    else:
+        (base_ref,) = refs
     rows, points = term_ref.shape
     term = term_ref[...]
     both, high = stacked(term)
-    own = dot(both, select_ref[:, : first_high.shape[0] + rest_high.shape[0] - points])
+    own = dot(both, select_ref[:, : near_high.shape[0] - points])
     own_both, own_high = stacked(own[:rows] + own[rows:])
-    cut = first_high.shape[0]
-    value = product(both[:, :cut], high[:, :cut], first_high[...], first_low[...])
-    both = jnp.concatenate([both[:, cut:], own_both], axis=1)
-    high = jnp.concatenate([high[:, cut:], own_high], axis=1)
-    value = value + product(both, high, rest_high[...], rest_low[...])
-    base_ref[...] = term * diagonal_ref[...] - value
+    both = jnp.concatenate([both, own_both], axis=1)
+    high = jnp.concatenate([high, own_high], axis=1)
+    base_ref[...] = term * diagonal_ref[...] - product(both, high, near_high[...], near_low[...])
 
 
 def ghost_values(blocks, high, low):
@@ -260,33 +274,37 @@
     early_refs, (base_out, sums_out) = refs[:-2], refs[-2:]
     rows = base_ref.shape[0]
     sums = partial_ref[...]
+    tall, width = sums.shape
     for ref in early_refs:
-        sums = sums + ref[0, rows:, : sums.shape[1]]
+        sums = sums + ref[rows : rows + tall, :width]
     sums_out[...] = sums
-    base_out[...] = base_ref[...] - ghost_values([ref[0, :rows, :] for ref in early_refs], early_high[...], early_low[...])
-
-
-def late_kernel(order, last, paired, late_ref, base_ref, sums_ref, total_ref, select_ref, late_high, late_low, wide_high, wide_low, turned_high, turned_low, *outs):
-    rows = base_ref.shape[0]
-    half = rows // 2
-    blocks = late_ref.shape[0]
+    base_out[...] = base_ref[...] - ghost_values([ref[:rows, :] for ref in early_refs], early_high[...], early_low[...])
+
+
+def late_kernel(order, last, late_ref, base_ref, sums_ref, total_ref, select_ref, first_high, first_low, rest_high, rest_low, wide_high, wide_low, turned_high, turned_low, *outs):
+    half = base_ref.shape[0] // 2
+    blocks = range(late_ref.shape[0])
     sums = sums_ref[...]
-    for block in range(blocks):
-        sums = sums + late_ref[block, rows:, : sums.shape[1]]
+    tall, width = sums.shape
+    for block in blocks:
+        sums = sums + late_ref[block, :tall, :width]
+    ghosts = [late_ref[block, tall:, :] for block in blocks]
+    cut = first_high.shape[0] // late_ref.shape[2]
     image = base_ref[...] - exchange_term(sums, half, wide_high[...], wide_low[...])
-    image = image - ghost_values([late_ref[block, :rows, :] for block in range(blocks)], late_high[...], late_low[...])
+    image = image - ghost_values(ghosts[:cut], first_high[...], first_low[...])
+    image = image - ghost_values(ghosts[cut:], rest_high[...], rest_low[...])
     scale = time_step / order
     term = jnp.concatenate([scale * image[half:], -scale * image[:half]], axis=0)
     outs[0][...] = total_ref[...] + term
     if last:
         return
-    _, term_ref, partial_ref, late_out, *early_outs = outs
+    _, term_ref, partial_ref, *out = outs
     term_ref[...] = term
     both, high = stacked(term)
     partial = intersect(both, high, turned_high[...], turned_low[...])
     partial_ref[...] = partial
-    pack(both, select_ref, early_outs, late_out, paired)
-    spread(partial, early_outs, late_out, paired)
+    pack(both, select_ref, out[:-1], out[-1])
+    spread(partial, term.shape[0], out[:-1], out[-1])
 
 
 def swap(value, bits, parts):
@@ -321,18 +339,19 @@
     columns = 2 * bands * frozen.shape[1]
     sum_shape = (half, columns) if columns >= LANES else (half * columns // LANES, LANES)
     tall = rows + sum_shape[0]
-    outgoing = [((1 if paired else places - 1 - EARLY, tall, capacity), F32)]
-    outgoing += [((2 if paired else 1, tall, capacity), F32)] * EARLY
-    first_rows = NEAR_FIRST * TILE
-    rest_rows = points + capacity - first_rows
-    early_rows, late_rows = EARLY * capacity, (places - 1 - EARLY) * capacity
-    targets, values, diagonal, select, first_high, first_low, field, own_frozen, late, *early = call(
-        functools.partial(plan_kernel, parts, paired),
+    late_blocks = places - 1 - EARLY
+    outgoing = [((tall + rows if paired else tall, capacity), F32)] * EARLY
+    outgoing += [((late_blocks - EARLY if paired else late_blocks, tall, capacity), F32)]
+    near_rows, early_rows = points + capacity, EARLY * capacity
+    first_rows = LATE_FIRST * capacity
+    rest_rows = late_blocks * capacity - first_rows
+    targets, values, diagonal, select, near_high, near_low, field, own_frozen, *sent = call(
+        functools.partial(plan_kernel, parts),
         [((count, points), jnp.int32), ((count, points), F32), ((1, points), F32), ((points, places * capacity), BF16)]
-        + [((first_rows, points), BF16)] * 2
+        + [((near_rows, points), BF16)] * 2
         + [((rows, points), F32), (frozen.shape, F32)]
         + outgoing,
-        (6 * first_rows * points, 12 << 20),
+        (6 * near_rows * points, 12 << 20),
         me, send_list, states.reshape(rows, points), neighbours, weights, potential.reshape(1, points), frozen,
         scalars=1,
         remote=6,
@@ -346,44 +365,46 @@
     )
     if len(pieces) == bands - 1:
         pieces = [own_frozen, *pieces]
-    wide_high, wide_low, turned_high, turned_low, partial, late, *early = call(
-        functools.partial(start_kernel, paired, len(pieces)),
+    wide_high, wide_low, turned_high, turned_low, partial, *sent = call(
+        functools.partial(start_kernel, len(pieces)),
         [((2 * columns, points), BF16)] * 2 + [((points, 2 * columns), BF16)] * 2 + [(sum_shape, F32)] + outgoing,
         (6 * rows * points * 2 * columns, 4 << 20),
-        *pieces, field, late, *early,
+        *pieces, field, *sent,
     )
+    sent[0], field, diagonal, targets = lax.optimization_barrier((sent[0], field, diagonal, targets))
     total, term = field, field
     for order in range(1, TERMS + 1):
+        *early, late = sent
         if paired:
-            early = [swap(block, bits, parts) for block, bits in zip(early, relations[1 : 1 + EARLY], strict=True)]
+            early = [swap(block, bits, parts) for block, bits in zip(early, relations[1:], strict=False)]
         else:
             early = [move(block, offset, parts) for block, offset in zip(early, relations[1:], strict=False)]
+        near = [term, select, near_high, near_low, diagonal]
         if order == 1:
-            rest_high, rest_low, early_high, early_low = call(
-                functools.partial(ghost_kernel, first_rows),
-                [((rest_rows, points), BF16)] * 2 + [((early_rows, points), BF16)] * 2,
-                (6 * (rest_rows + early_rows) * points, 12 << 20),
-                targets, values,
+            base, early_high, early_low, first_high, first_low = call(
+                functools.partial(near_kernel, near_rows),
+                [((rows, points), F32)] + [((early_rows, points), BF16)] * 2 + [((first_rows, points), BF16)] * 2,
+                (6 * rows * points * near_rows, 16 << 20),
+                *near, targets, values,
             )
-        (base,) = call(
-            near_kernel,
-            [((rows, points), F32)],
-            (6 * rows * points * (first_rows + rest_rows), 16 << 20),
-            term, select, first_high, first_low, rest_high, rest_low, diagonal,
-        )
+        else:
+            (base,) = call(
+                functools.partial(near_kernel, None),
+                [((rows, points), F32)],
+                (6 * rows * points * near_rows, 16 << 20),
+                *near,
+            )
         if paired:
-            late = jnp.concatenate([late] + [block[1:] for block in early], axis=0)
+            late = jnp.concatenate([late] + [block[None, rows:] for block in early], axis=0)
             late, base, targets = lax.optimization_barrier((late, base, targets))
             late = swap(late, 1, parts)
         else:
-            late = jnp.stack(
-                [move(late[at], offset, parts) for at, offset in enumerate(relations[1 + EARLY :])]
-            )
+            late = jnp.stack([move(late[at], offset, parts) for at, offset in enumerate(relations[1 + EARLY :])])
         if order == 1:
-            late_high, late_low = call(
-                functools.partial(ghost_kernel, first_rows + rest_rows + early_rows),
-                [((late_rows, points), BF16)] * 2,
-                (6 * late_rows * points, 12 << 20),
+            rest_high, rest_low = call(
+                functools.partial(ghost_kernel, near_rows + early_rows + first_rows),
+                [((rest_rows, points), BF16)] * 2,
+                (6 * rest_rows * points, 12 << 20),
                 targets, values,
             )
         base, sums = call(
@@ -397,14 +418,15 @@
         if not last:
             shapes += [((rows, points), F32), (sum_shape, F32)] + outgoing
         outs = call(
-            functools.partial(late_kernel, order, last, paired),
+            functools.partial(late_kernel, order, last),
             shapes,
-            (6 * rows * points * late_rows, 12 << 20),
-            late, base, sums, total, select, late_high, late_low, wide_high, wide_low, turned_high, turned_low,
+            (6 * rows * points * (first_rows + rest_rows), 12 << 20),
+            late, base, sums, total, select, first_high, first_low, rest_high, rest_low,
+            wide_high, wide_low, turned_high, turned_low,
         )
         total = outs[0]
         if not last:
-            _, term, partial, late, *early = outs
+            _, term, partial, *sent = outs
     return total.reshape(states.shape)
 
 

time: 56.7 us -> 54.8 us (0.966)
  waiting for transfers between devices: 11.8 us -> 10.3 us
    ppermute x3, waiting for transfers between devices: 1.27 us -> 0.5 us  [gather_frozen(): lax.ppermute(frozen, 'band', [(at, (at + step) % bands) for at in range(b...]
    ppermute x16, waiting for transfers between devices: 10.6 us -> 9.79 us  [swap(): lax.ppermute(value, 'mesh', [(part, part ^ bits) for part in range(parts)])]
    pallas_call x16 -> x15, Pallas kernels: 24 us -> 23.6 us  [call(): pl.pallas_call(kernel, out_shape=[jax.ShapeDtypeStruct(shape, dtype) for...]
  transfers between devices with their start and end apart: 19 -> 19, of which waited for: 12 -> 13; matrix products, arithmetic and copies ran while one was open for 0% -> 0% of each run, Pallas kernels for 29% -> 30%
where the time goes in v4:
time: 54.8 us; the launch traced here: 54.6 us
  Pallas kernels  23.6 us (43%)
  starting transfers between devices  20.4 us (37%)
  waiting for transfers between devices  10.3 us (19%)
    pallas_call x15, Pallas kernels, call(): pl.pallas_call(kernel, out_shape=[jax.ShapeDtypeStruct(shape, dtype) for...  23.6 us
    ppermute x16, starting transfers between devices, swap(): lax.ppermute(value, 'mesh', [(part, part ^ bits) for part in range(parts)])  14.3 us
    ppermute x16, waiting for transfers between devices, swap(): lax.ppermute(value, 'mesh', [(part, part ^ bits) for part in range(parts)])  9.79 us
    ppermute x3, starting transfers between devices, gather_frozen(): lax.ppermute(frozen, 'band', [(at, (at + step) % bands) for at in range(b...  6.06 us
  transfers between devices with their start and end apart: 19, of which 13 were waited for; matrix products, arithmetic and copies ran while one was open for 0% of the time, Pallas kernels for 30%

profile of v4, /device:TPU:0, one launch (start us, length us, event | category | flops | bytes accessed | tf_op | source)
XLA Modules:
  0.0 54.6 jit_solution(13242651348320150032)
XLA Ops:
  0.0 3.0 %collective-permute-start = (f32[2,8,1024]{2,1,0:T(8,128)}, f32[2,8,1024]{2,1,0:T(8,128)S(1)}, u32[]{:S(2)}, u32[]{:S(2)}) collective-permute-start(f32[2,8,1024]{2,1,0:T(8,128)} %refs_5_.1), channel_id=1, source_target_pairs={{0,1},{1,2},{2,3},{3,0},{4,5},{5,6},{6,7},{7,4},{8,9},{9,10},{10,1... | collective-permute-start | bytes 196616 | tf_op jit(solution)/shard_map/ppermute | solution.py:321
  3.0 2.0 %collective-permute-start.2 = (f32[2,8,1024]{2,1,0:T(8,128)}, f32[2,8,1024]{2,1,0:T(8,128)S(1)}, u32[]{:S(2)}, u32[]{:S(2)}) collective-permute-start(f32[2,8,1024]{2,1,0:T(8,128)} %refs_5_.1), channel_id=1, source_target_pairs={{0,3},{1,0},{2,1},{3,2},{4,7},{5,4},{6,5},{7,6},{8,11},{9,8},{10,9... | collective-permute-start | bytes 196616 | tf_op jit(solution)/shard_map/ppermute | solution.py:321
  5.1 1.0 %collective-permute-start.1 = (f32[2,8,1024]{2,1,0:T(8,128)}, f32[2,8,1024]{2,1,0:T(8,128)S(1)}, u32[]{:S(2)}, u32[]{:S(2)}) collective-permute-start(f32[2,8,1024]{2,1,0:T(8,128)} %refs_5_.1), channel_id=1, source_target_pairs={{0,2},{1,3},{2,0},{3,1},{4,6},{5,7},{6,4},{7,5},{8,10},{9,11},{10,... | collective-permute-start | bytes 196616 | tf_op jit(solution)/shard_map/ppermute | solution.py:321
  6.1 5.0 %shard_map.64 = (s32[8,1024]{1,0:T(8,128)S(1)}, f32[8,1024]{1,0:T(8,128)S(1)}, f32[1,1024]{1,0:T(1,128)S(1)}, bf16[1024,2048]{1,0:T(8,128)(2,1)S(1)}, bf16[1280,...) custom-call(s32[1]{0:T(128)} %bitcast.me_ref, ...), custom_call_target="tpu_custom_call" | custom-call | flops 7864320 | bytes 12582912 | tf_op jit(solution)/shard_map/pallas_call | solution.py:72
  11.0 0.0 collective-permute-done.refs_1_
  11.1 0.0 collective-permute-done.2.refs_3_
  11.1 0.5 collective-permute-done.1.refs_2_
  11.6 0.6 %shard_map.65 = (bf16[128,1024]{1,0:T(8,128)(2,1)S(1)}, bf16[128,1024]{1,0:T(8,128)(2,1)S(1)}, bf16[1024,128]{1,0:T(8,128)(2,1)S(1)}, bf16[1024,128]{1,0:T(8,128...) custom-call(f32[2,8,1024]{2,1,0:T(8,128)S(1)} %get-tuple-element.75., ...), custom_call_target="tpu_custom_call" | custom-call | flops 25165824 | bytes 4194304 | tf_op jit(solution)/shard_map/pallas_call | solution.py:72
  12.1 2.5 %collective-permute-start.3 = (f32[72,256]{1,0:T(8,128)S(1)}, f32[72,256]{1,0:T(8,128)S(1)}, u32[]{:S(2)}, u32[]{:S(2)}) collective-permute-start(f32[72,256]{1,0:T(8,128)S(1)} %get-tuple-element.85), channel_id=1, source_target_pairs={{0,24},{4,28},{8,16},{12,20},{16,8},{20,12},{24,0},{28,4},{1,25},{... | collective-permute-start | bytes 221192 | tf_op jit(solution)/shard_map/ppermute | solution.py:311
  14.6 0.5 collective-permute-start.4
  15.1 0.5 collective-permute-start.5
  15.6 4.0 %shard_map.66 = (f32[32,1024]{1,0:T(8,128)S(1)}, bf16[768,1024]{1,0:T(8,128)(2,1)S(1)}, bf16[768,1024]{1,0:T(8,128)(2,1)S(1)}, bf16[512,1024]{1,0:T(8,128)(2,1)S(1)}, bf16[512,1024]{1,0:T(8,128)(2,1)S(1)}) custom-call(f32[32,1024]{1,0:T(8,128)S(1)} %get-tuple-element.88.refs_4_.term_ref.total_ref, bf16[1024,2048]{1,0:T(8,128)(2,1)S(1)} %get-tuple-element.89.select_ref, ...), custom_call_target="tpu_custom_call" | custom-call | flops 251658240 | bytes 16777216 | tf_op jit(solution)/shard_map/pallas_call | solution.py:72
  19.6 0.0 collective-permute-done.3.refs_0_
  19.6 0.0 collective-permute-done.4.refs_1_
  19.6 0.0 collective-permute-done.5.refs_2_
  19.7 0.1 collective-permute-start.6
  19.8 1.4 %shard_map.68 = (bf16[512,1024]{1,0:T(8,128)(2,1)S(1)}, bf16[512,1024]{1,0:T(8,128)(2,1)S(1)}) custom-call(s32[8,1024]{1,0:T(8,128)S(1)} %get-tuple-element.105.refs_0_.targets_ref, f32[8,1024]{1,0:T(8,128)S(1)} %get-tuple-element.94.refs_1_.values_ref), custom_call_target="tpu_custom_call" | custom-call | flops 3145728 | bytes 12582912 | tf_op jit(solution)/shard_map/pallas_call | solution.py:72
  21.1 0.6 %shard_map.67 = (f32[32,1024]{1,0:T(8,128)S(1)}, f32[8,128]{1,0:T(8,128)S(1)}) custom-call(f32[32,1024]{1,0:T(8,128)S(1)} %get-tuple-element.97.base_ref, f32[8,128]{1,0:T(8,128)S(1)} %get-tuple-element.98.partial_ref, bf16[768,1024]{1,0:T(8,128)(2,1)S(1)} %get-tuple-element.99.early_high, bf16[768,1024]{1,0:T(8,128)(2,1)S(1)} %get-tuple-element.100.early_low, ...), custom_call_target="tpu_custom_call" | custom-call | flops 150994944 | bytes 4194304 | tf_op jit(solution)/shard_map/pallas_call | solution.py:72
  21.8 0.0 collective-permute-done.6.late_ref
  21.8 1.8 %shard_map.69 = (f32[32,1024]{1,0:T(8,128)S(1)}, f32[32,1024]{1,0:T(8,128)S(1)}, f32[8,128]{1,0:T(8,128)S(1)}, f32[72,256]{1,0:T(8,128)S(1)}, f32[72,256]{1,0:T(...) custom-call(f32[4,40,256]{2,1,0:T(8,128)S(1)} %collective-permute-done.6.late_ref, ...), custom_call_target="tpu_custom_call" | custom-call | flops 201326592 | bytes 12582912 | tf_op jit(solution)/shard_map/pallas_call | solution.py:72
  23.6 2.5 %collective-permute-start.7 = (f32[72,256]{1,0:T(8,128)S(1)}, f32[72,256]{1,0:T(8,128)S(1)}, u32[]{:S(2)}, u32[]{:S(2)}) collective-permute-start(f32[72,256]{1,0:T(8,128)S(1)} %get-tuple-element.113), channel_id=1, source_target_pairs={{0,24},{4,28},{8,16},{12,20},{16,8},{20,12},{24,0},{28,4},{1,25},{... | collective-permute-start | bytes 221192 | tf_op jit(solution)/shard_map/ppermute | solution.py:311
  26.0 0.5 collective-permute-start.8
  26.6 0.5 collective-permute-start.9
  27.1 1.1 %shard_map.70.base_ref = f32[32,1024]{1,0:T(8,128)S(1)} custom-call(f32[32,1024]{1,0:T(8,128)S(1)} %get-tuple-element.116.term_ref, bf16[1024,2048]{1,0:T(8,128)(2,1)S(1)} %get-tuple-element.89.select_ref, bf16[1280,1024]{1,0:T(8,128)(2,1)S(1)} %get-tuple-element.90.near_high, bf16[1280,1024]{1,0:T(8,128)(2,1)S(1)} %get-tuple-element.91.near_low, ...), custom_call_target="tpu_custom_call" | custom-call | flops 251658240 | bytes 16777216 | tf_op jit(solution)/shard_map/pallas_call | solution.py:72
  28.2 1.4 %collective-permute-done.7.refs_0_ = f32[72,256]{1,0:T(8,128)S(1)} collective-permute-done((f32[72,256]{1,0:T(8,128)S(1)}, f32[72,256]{1,0:T(8,128)S(1)}, u32[]{:S(2)}, u32[]{:S(2)}) %collective-permute-start.7) | collective-permute-done | bytes 73760 | tf_op jit(solution)/shard_map/ppermute | solution.py:311
  29.6 1.2 %collective-permute-done.8.refs_1_ = f32[72,256]{1,0:T(8,128)S(1)} collective-permute-done((f32[72,256]{1,0:T(8,128)S(1)}, f32[72,256]{1,0:T(8,128)S(1)}, u32[]{:S(2)}, u32[]{:S(2)}) %collective-permute-start.8) | collective-permute-done | bytes 73760 | tf_op jit(solution)/shard_map/ppermute | solution.py:311
  30.8 0.1 collective-permute-done.9.refs_2_
  31.0 0.1 collective-permute-start.10
  31.0 0.6 %shard_map.71 = (f32[32,1024]{1,0:T(8,128)S(1)}, f32[8,128]{1,0:T(8,128)S(1)}) custom-call(f32[32,1024]{1,0:T(8,128)S(1)} %shard_map.70.base_ref, f32[8,128]{1,0:T(8,128)S(1)} %get-tuple-element.119.partial_ref, bf16[768,1024]{1,0:T(8,128)(2,1)S(1)} %get-tuple-element.99.early_high, bf16[768,1024]{1,0:T(8,128)(2,1)S(1)} %get-tuple-element.100.early_low, ...), custom_call_target="tpu_custom_call" | custom-call | flops 150994944 | bytes 4194304 | tf_op jit(solution)/shard_map/pallas_call | solution.py:72
  31.7 0.7 %collective-permute-done.10.late_ref = f32[4,40,256]{2,1,0:T(8,128)S(1)} collective-permute-done((f32[4,40,256]{2,1,0:T(8,128)S(1)}, f32[4,40,256]{2,1,0:T(8,128)S(1)}, u32[]{:S(2)}, u32[]{:S(2)}) %collective-permute-start.10) | collective-permute-done | bytes 163872 | tf_op jit(solution)/shard_map/ppermute | solution.py:311
  32.4 1.8 %shard_map.72 = (f32[32,1024]{1,0:T(8,128)S(1)}, f32[32,1024]{1,0:T(8,128)S(1)}, f32[8,128]{1,0:T(8,128)S(1)}, f32[72,256]{1,0:T(8,128)S(1)}, f32[72,256]{1,0:T(...) custom-call(f32[4,40,256]{2,1,0:T(8,128)S(1)} %collective-permute-done.10.late_ref, ...), custom_call_target="tpu_custom_call" | custom-call | flops 201326592 | bytes 12582912 | tf_op jit(solution)/shard_map/pallas_call | solution.py:72
  34.2 2.3 %collective-permute-start.11 = (f32[72,256]{1,0:T(8,128)S(1)}, f32[72,256]{1,0:T(8,128)S(1)}, u32[]{:S(2)}, u32[]{:S(2)}) collective-permute-start(f32[72,256]{1,0:T(8,128)S(1)} %get-tuple-element.124), channel_id=1, source_target_pairs={{0,24},{4,28},{8,16},{12,20},{16,8},{20,12},{24,0},{28,4},{1,25},{... | collective-permute-start | bytes 221192 | tf_op jit(solution)/shard_map/ppermute | solution.py:311
  36.5 0.5 collective-permute-start.12
  37.0 0.7 %collective-permute-start.13 = (f32[72,256]{1,0:T(8,128)S(1)}, f32[72,256]{1,0:T(8,128)S(1)}, u32[]{:S(2)}, u32[]{:S(2)}) collective-permute-start(f32[72,256]{1,0:T(8,128)S(1)} %get-tuple-element.126), channel_id=1, source_target_pairs={{0,16},{4,20},{8,24},{12,28},{16,0},{20,4},{24,8},{28,12},{1,17},{... | collective-permute-start | bytes 221192 | tf_op jit(solution)/shard_map/ppermute | solution.py:311
  37.7 1.1 %shard_map.73.base_ref = f32[32,1024]{1,0:T(8,128)S(1)} custom-call(f32[32,1024]{1,0:T(8,128)S(1)} %get-tuple-element.127.term_ref, bf16[1024,2048]{1,0:T(8,128)(2,1)S(1)} %get-tuple-element.89.select_ref, bf16[1280,1024]{1,0:T(8,128)(2,1)S(1)} %get-tuple-element.90.near_high, bf16[1280,1024]{1,0:T(8,128)(2,1)S(1)} %get-tuple-element.91.near_low, ...), custom_call_target="tpu_custom_call" | custom-call | flops 251658240 | bytes 16777216 | tf_op jit(solution)/shard_map/pallas_call | solution.py:72
  38.8 1.2 %collective-permute-done.11.refs_0_ = f32[72,256]{1,0:T(8,128)S(1)} collective-permute-done((f32[72,256]{1,0:T(8,128)S(1)}, f32[72,256]{1,0:T(8,128)S(1)}, u32[]{:S(2)}, u32[]{:S(2)}) %collective-permute-start.11) | collective-permute-done | bytes 73760 | tf_op jit(solution)/shard_map/ppermute | solution.py:311
  39.9 0.9 %collective-permute-done.12.refs_1_ = f32[72,256]{1,0:T(8,128)S(1)} collective-permute-done((f32[72,256]{1,0:T(8,128)S(1)}, f32[72,256]{1,0:T(8,128)S(1)}, u32[]{:S(2)}, u32[]{:S(2)}) %collective-permute-start.12) | collective-permute-done | bytes 73760 | tf_op jit(solution)/shard_map/ppermute | solution.py:311
  40.9 0.4 collective-permute-done.13.refs_2_
  41.4 0.1 collective-permute-start.14
  41.4 0.6 %shard_map.74 = (f32[32,1024]{1,0:T(8,128)S(1)}, f32[8,128]{1,0:T(8,128)S(1)}) custom-call(f32[32,1024]{1,0:T(8,128)S(1)} %shard_map.73.base_ref, f32[8,128]{1,0:T(8,128)S(1)} %get-tuple-element.130.partial_ref, bf16[768,1024]{1,0:T(8,128)(2,1)S(1)} %get-tuple-element.99.early_high, bf16[768,1024]{1,0:T(8,128)(2,1)S(1)} %get-tuple-element.100.early_low, ...), custom_call_target="tpu_custom_call" | custom-call | flops 150994944 | bytes 4194304 | tf_op jit(solution)/shard_map/pallas_call | solution.py:72
  42.1 0.7 %collective-permute-done.14.late_ref = f32[4,40,256]{2,1,0:T(8,128)S(1)} collective-permute-done((f32[4,40,256]{2,1,0:T(8,128)S(1)}, f32[4,40,256]{2,1,0:T(8,128)S(1)}, u32[]{:S(2)}, u32[]{:S(2)}) %collective-permute-start.14) | collective-permute-done | bytes 163872 | tf_op jit(solution)/shard_map/ppermute | solution.py:311
  42.8 1.8 %shard_map.75 = (f32[32,1024]{1,0:T(8,128)S(1)}, f32[32,1024]{1,0:T(8,128)S(1)}, f32[8,128]{1,0:T(8,128)S(1)}, f32[72,256]{1,0:T(8,128)S(1)}, f32[72,256]{1,0:T(...) custom-call(f32[4,40,256]{2,1,0:T(8,128)S(1)} %collective-permute-done.14.late_ref, ...), custom_call_target="tpu_custom_call" | custom-call | flops 201326592 | bytes 12582912 | tf_op jit(solution)/shard_map/pallas_call | solution.py:72
  44.6 1.9 %collective-permute-start.15 = (f32[72,256]{1,0:T(8,128)S(1)}, f32[72,256]{1,0:T(8,128)S(1)}, u32[]{:S(2)}, u32[]{:S(2)}) collective-permute-start(f32[72,256]{1,0:T(8,128)S(1)} %get-tuple-element.135), channel_id=1, source_target_pairs={{0,24},{4,28},{8,16},{12,20},{16,8},{20,12},{24,0},{28,4},{1,25},{... | collective-permute-start | bytes 221192 | tf_op jit(solution)/shard_map/ppermute | solution.py:311
  46.5 0.5 collective-permute-start.16
  47.0 1.0 %collective-permute-start.17 = (f32[72,256]{1,0:T(8,128)S(1)}, f32[72,256]{1,0:T(8,128)S(1)}, u32[]{:S(2)}, u32[]{:S(2)}) collective-permute-start(f32[72,256]{1,0:T(8,128)S(1)} %get-tuple-element.137), channel_id=1, source_target_pairs={{0,16},{4,20},{8,24},{12,28},{16,0},{20,4},{24,8},{28,12},{1,17},{... | collective-permute-start | bytes 221192 | tf_op jit(solution)/shard_map/ppermute | solution.py:311
  48.1 1.1 %shard_map.76.base_ref = f32[32,1024]{1,0:T(8,128)S(1)} custom-call(f32[32,1024]{1,0:T(8,128)S(1)} %get-tuple-element.138.term_ref, bf16[1024,2048]{1,0:T(8,128)(2,1)S(1)} %get-tuple-element.89.select_ref, bf16[1280,1024]{1,0:T(8,128)(2,1)S(1)} %get-tuple-element.90.near_high, bf16[1280,1024]{1,0:T(8,128)(2,1)S(1)} %get-tuple-element.91.near_low, ...), custom_call_target="tpu_custom_call" | custom-call | flops 251658240 | bytes 16777216 | tf_op jit(solution)/shard_map/pallas_call | solution.py:72
  49.2 1.2 %collective-permute-done.15.refs_0_ = f32[72,256]{1,0:T(8,128)S(1)} collective-permute-done((f32[72,256]{1,0:T(8,128)S(1)}, f32[72,256]{1,0:T(8,128)S(1)}, u32[]{:S(2)}, u32[]{:S(2)}) %collective-permute-start.15) | collective-permute-done | bytes 73760 | tf_op jit(solution)/shard_map/ppermute | solution.py:311
  50.3 0.6 %collective-permute-done.16.refs_1_ = f32[72,256]{1,0:T(8,128)S(1)} collective-permute-done((f32[72,256]{1,0:T(8,128)S(1)}, f32[72,256]{1,0:T(8,128)S(1)}, u32[]{:S(2)}, u32[]{:S(2)}) %collective-permute-start.16) | collective-permute-done | bytes 73760 | tf_op jit(solution)/shard_map/ppermute | solution.py:311
  51.0 0.5 collective-permute-done.17.refs_2_
  51.5 0.1 collective-permute-start.18
  51.5 0.6 %shard_map.77 = (f32[32,1024]{1,0:T(8,128)S(1)}, f32[8,128]{1,0:T(8,128)S(1)}) custom-call(f32[32,1024]{1,0:T(8,128)S(1)} %shard_map.76.base_ref, f32[8,128]{1,0:T(8,128)S(1)} %get-tuple-element.141.partial_ref, bf16[768,1024]{1,0:T(8,128)(2,1)S(1)} %get-tuple-element.99.early_high, bf16[768,1024]{1,0:T(8,128)(2,1)S(1)} %get-tuple-element.100.early_low, ...), custom_call_target="tpu_custom_call" | custom-call | flops 150994944 | bytes 4194304 | tf_op jit(solution)/shard_map/pallas_call | solution.py:72
  52.2 0.7 %collective-permute-done.18.late_ref = f32[4,40,256]{2,1,0:T(8,128)S(1)} collective-permute-done((f32[4,40,256]{2,1,0:T(8,128)S(1)}, f32[4,40,256]{2,1,0:T(8,128)S(1)}, u32[]{:S(2)}, u32[]{:S(2)}) %collective-permute-start.18) | collective-permute-done | bytes 163872 | tf_op jit(solution)/shard_map/ppermute | solution.py:311
  52.9 1.6 %shard_map.78 = f32[32,1024]{1,0:T(8,128)} custom-call(f32[4,40,256]{2,1,0:T(8,128)S(1)} %collective-permute-done.18.late_ref, f32[32,1024]{1,0:T(8,128)S(1)} %get-tuple-element.142.base_ref, f32[8,128]{1,0:T(8,128)S(1)} %get-tuple-element.143.sums_ref, f32[32,1024]{1,0:T(8,128)S(1)} %get-tuple-element.144.total_ref, ...), custom_call_target="tpu_custom_call" | custom-call | flops 201326592 | bytes 12582912 | tf_op jit(solution)/shard_map/pallas_call | solution.py:72
  (16 shorter events, 0.1 us)
Async XLA Ops:
  0.0 11.0 %collective-permute-start = (f32[2,8,1024]{2,1,0:T(8,128)}, f32[2,8,1024]{2,1,0:T(8,128)S(1)}, u32[]{:S(2)}, u32[]{:S(2)}) collective-permute-start(f32[2,8,1024]{2,1,0:T(8,128)} %refs_5_.1), channel_id=1, source_target_pairs={{0,1},{1,2},{2,3},{3,0},{4,5},{5,6},{6,7},{7,4},{8,9},{9,10},{10,1... | collective-permute-start | bytes 196616 | tf_op jit(solution)/shard_map/ppermute | solution.py:321
  3.0 8.0 %collective-permute-start.2 = (f32[2,8,1024]{2,1,0:T(8,128)}, f32[2,8,1024]{2,1,0:T(8,128)S(1)}, u32[]{:S(2)}, u32[]{:S(2)}) collective-permute-start(f32[2,8,1024]{2,1,0:T(8,128)} %refs_5_.1), channel_id=1, source_target_pairs={{0,3},{1,0},{2,1},{3,2},{4,7},{5,4},{6,5},{7,6},{8,11},{9,8},{10,9... | collective-permute-start | bytes 196616 | tf_op jit(solution)/shard_map/ppermute | solution.py:321
  5.1 6.5 %collective-permute-start.1 = (f32[2,8,1024]{2,1,0:T(8,128)}, f32[2,8,1024]{2,1,0:T(8,128)S(1)}, u32[]{:S(2)}, u32[]{:S(2)}) collective-permute-start(f32[2,8,1024]{2,1,0:T(8,128)} %refs_5_.1), channel_id=1, source_target_pairs={{0,2},{1,3},{2,0},{3,1},{4,6},{5,7},{6,4},{7,5},{8,10},{9,11},{10,... | collective-permute-start | bytes 196616 | tf_op jit(solution)/shard_map/ppermute | solution.py:321
  12.1 7.5 %collective-permute-start.3 = (f32[72,256]{1,0:T(8,128)S(1)}, f32[72,256]{1,0:T(8,128)S(1)}, u32[]{:S(2)}, u32[]{:S(2)}) collective-permute-start(f32[72,256]{1,0:T(8,128)S(1)} %get-tuple-element.85), channel_id=1, source_target_pairs={{0,24},{4,28},{8,16},{12,20},{16,8},{20,12},{24,0},{28,4},{1,25},{... | collective-permute-start | bytes 221192 | tf_op jit(solution)/shard_map/ppermute | solution.py:311
  14.6 5.0 %collective-permute-start.4 = (f32[72,256]{1,0:T(8,128)S(1)}, f32[72,256]{1,0:T(8,128)S(1)}, u32[]{:S(2)}, u32[]{:S(2)}) collective-permute-start(f32[72,256]{1,0:T(8,128)S(1)} %get-tuple-element.86), channel_id=1, source_target_pairs={{0,8},{4,12},{8,0},{12,4},{16,24},{20,28},{24,16},{28,20},{1,9},{5... | collective-permute-start | bytes 221192 | tf_op jit(solution)/shard_map/ppermute | solution.py:311
  15.1 4.5 %collective-permute-start.5 = (f32[72,256]{1,0:T(8,128)S(1)}, f32[72,256]{1,0:T(8,128)S(1)}, u32[]{:S(2)}, u32[]{:S(2)}) collective-permute-start(f32[72,256]{1,0:T(8,128)S(1)} %get-tuple-element.87), channel_id=1, source_target_pairs={{0,16},{4,20},{8,24},{12,28},{16,0},{20,4},{24,8},{28,12},{1,17},{... | collective-permute-start | bytes 221192 | tf_op jit(solution)/shard_map/ppermute | solution.py:311
  19.7 2.1 %collective-permute-start.6 = (f32[4,40,256]{2,1,0:T(8,128)S(1)}, f32[4,40,256]{2,1,0:T(8,128)S(1)}, u32[]{:S(2)}, u32[]{:S(2)}) collective-permute-start(f32[4,40,256]{2,1,0:T(8,128)S(1)} %pad_maximum_fusion), channel_id=1, source_target_pairs={{0,4},{4,0},{8,12},{12,8},{16,20},{20,16},{24,28},{28,24},{1,5},{5... | collective-permute-start | bytes 491528 | tf_op jit(solution)/shard_map/ppermute | solution.py:311
  23.6 6.0 %collective-permute-start.7 = (f32[72,256]{1,0:T(8,128)S(1)}, f32[72,256]{1,0:T(8,128)S(1)}, u32[]{:S(2)}, u32[]{:S(2)}) collective-permute-start(f32[72,256]{1,0:T(8,128)S(1)} %get-tuple-element.113), channel_id=1, source_target_pairs={{0,24},{4,28},{8,16},{12,20},{16,8},{20,12},{24,0},{28,4},{1,25},{... | collective-permute-start | bytes 221192 | tf_op jit(solution)/shard_map/ppermute | solution.py:311
  26.0 4.8 %collective-permute-start.8 = (f32[72,256]{1,0:T(8,128)S(1)}, f32[72,256]{1,0:T(8,128)S(1)}, u32[]{:S(2)}, u32[]{:S(2)}) collective-permute-start(f32[72,256]{1,0:T(8,128)S(1)} %get-tuple-element.114), channel_id=1, source_target_pairs={{0,8},{4,12},{8,0},{12,4},{16,24},{20,28},{24,16},{28,20},{1,9},{5... | collective-permute-start | bytes 221192 | tf_op jit(solution)/shard_map/ppermute | solution.py:311
  26.6 4.4 %collective-permute-start.9 = (f32[72,256]{1,0:T(8,128)S(1)}, f32[72,256]{1,0:T(8,128)S(1)}, u32[]{:S(2)}, u32[]{:S(2)}) collective-permute-start(f32[72,256]{1,0:T(8,128)S(1)} %get-tuple-element.115), channel_id=1, source_target_pairs={{0,16},{4,20},{8,24},{12,28},{16,0},{20,4},{24,8},{28,12},{1,17},{... | collective-permute-start | bytes 221192 | tf_op jit(solution)/shard_map/ppermute | solution.py:311
  31.0 1.5 %collective-permute-start.10 = (f32[4,40,256]{2,1,0:T(8,128)S(1)}, f32[4,40,256]{2,1,0:T(8,128)S(1)}, u32[]{:S(2)}, u32[]{:S(2)}) collective-permute-start(f32[4,40,256]{2,1,0:T(8,128)S(1)} %pad_maximum_fusion.1), channel_id=1, source_target_pairs={{0,4},{4,0},{8,12},{12,8},{16,20},{20,16},{24,28},{28,24},{1,5},{5... | collective-permute-start | bytes 491528 | tf_op jit(solution)/shard_map/ppermute | solution.py:311
  34.2 5.8 %collective-permute-start.11 = (f32[72,256]{1,0:T(8,128)S(1)}, f32[72,256]{1,0:T(8,128)S(1)}, u32[]{:S(2)}, u32[]{:S(2)}) collective-permute-start(f32[72,256]{1,0:T(8,128)S(1)} %get-tuple-element.124), channel_id=1, source_target_pairs={{0,24},{4,28},{8,16},{12,20},{16,8},{20,12},{24,0},{28,4},{1,25},{... | collective-permute-start | bytes 221192 | tf_op jit(solution)/shard_map/ppermute | solution.py:311
  36.5 4.4 %collective-permute-start.12 = (f32[72,256]{1,0:T(8,128)S(1)}, f32[72,256]{1,0:T(8,128)S(1)}, u32[]{:S(2)}, u32[]{:S(2)}) collective-permute-start(f32[72,256]{1,0:T(8,128)S(1)} %get-tuple-element.125), channel_id=1, source_target_pairs={{0,8},{4,12},{8,0},{12,4},{16,24},{20,28},{24,16},{28,20},{1,9},{5... | collective-permute-start | bytes 221192 | tf_op jit(solution)/shard_map/ppermute | solution.py:311
  37.0 4.4 %collective-permute-start.13 = (f32[72,256]{1,0:T(8,128)S(1)}, f32[72,256]{1,0:T(8,128)S(1)}, u32[]{:S(2)}, u32[]{:S(2)}) collective-permute-start(f32[72,256]{1,0:T(8,128)S(1)} %get-tuple-element.126), channel_id=1, source_target_pairs={{0,16},{4,20},{8,24},{12,28},{16,0},{20,4},{24,8},{28,12},{1,17},{... | collective-permute-start | bytes 221192 | tf_op jit(solution)/shard_map/ppermute | solution.py:311
  41.4 1.5 %collective-permute-start.14 = (f32[4,40,256]{2,1,0:T(8,128)S(1)}, f32[4,40,256]{2,1,0:T(8,128)S(1)}, u32[]{:S(2)}, u32[]{:S(2)}) collective-permute-start(f32[4,40,256]{2,1,0:T(8,128)S(1)} %pad_maximum_fusion.2), channel_id=1, source_target_pairs={{0,4},{4,0},{8,12},{12,8},{16,20},{20,16},{24,28},{28,24},{1,5},{5... | collective-permute-start | bytes 491528 | tf_op jit(solution)/shard_map/ppermute | solution.py:311
  44.6 5.8 %collective-permute-start.15 = (f32[72,256]{1,0:T(8,128)S(1)}, f32[72,256]{1,0:T(8,128)S(1)}, u32[]{:S(2)}, u32[]{:S(2)}) collective-permute-start(f32[72,256]{1,0:T(8,128)S(1)} %get-tuple-element.135), channel_id=1, source_target_pairs={{0,24},{4,28},{8,16},{12,20},{16,8},{20,12},{24,0},{28,4},{1,25},{... | collective-permute-start | bytes 221192 | tf_op jit(solution)/shard_map/ppermute | solution.py:311
  46.5 4.4 %collective-permute-start.16 = (f32[72,256]{1,0:T(8,128)S(1)}, f32[72,256]{1,0:T(8,128)S(1)}, u32[]{:S(2)}, u32[]{:S(2)}) collective-permute-start(f32[72,256]{1,0:T(8,128)S(1)} %get-tuple-element.136), channel_id=1, source_target_pairs={{0,8},{4,12},{8,0},{12,4},{16,24},{20,28},{24,16},{28,20},{1,9},{5... | collective-permute-start | bytes 221192 | tf_op jit(solution)/shard_map/ppermute | solution.py:311
  47.0 4.4 %collective-permute-start.17 = (f32[72,256]{1,0:T(8,128)S(1)}, f32[72,256]{1,0:T(8,128)S(1)}, u32[]{:S(2)}, u32[]{:S(2)}) collective-permute-start(f32[72,256]{1,0:T(8,128)S(1)} %get-tuple-element.137), channel_id=1, source_target_pairs={{0,16},{4,20},{8,24},{12,28},{16,0},{20,4},{24,8},{28,12},{1,17},{... | collective-permute-start | bytes 221192 | tf_op jit(solution)/shard_map/ppermute | solution.py:311
  51.5 1.5 %collective-permute-start.18 = (f32[4,40,256]{2,1,0:T(8,128)S(1)}, f32[4,40,256]{2,1,0:T(8,128)S(1)}, u32[]{:S(2)}, u32[]{:S(2)}) collective-permute-start(f32[4,40,256]{2,1,0:T(8,128)S(1)} %pad_maximum_fusion.3), channel_id=1, source_target_pairs={{0,4},{4,0},{8,12},{12,8},{16,20},{20,16},{24,28},{28,24},{1,5},{5... | collective-permute-start | bytes 491528 | tf_op jit(solution)/shard_map/ppermute | solution.py:311

commit v5 on v4

--- a/solution.py
+++ b/solution.py
@@ -40,7 +40,7 @@
 
 def blocks_of(parts):
     if parts == 8:
-        return [0, 6, 2, 4, 1, 7, 3, 5]
+        return [0, 1, 6, 4, 2, 7, 5, 3]
     relative = [0]
     for offset in [*range(1, REACH + 1), *range(-REACH, 0), parts // 2]:
         if offset % parts not in relative:
@@ -48,8 +48,8 @@
     return relative
 
 
-EARLY = 3
-LATE_FIRST = 2
+EARLY = 4
+LATE_FIRST = 1
 
 
 def receiver_of(me, block, parts):
@@ -81,19 +81,20 @@
 
 
 def stencil_rows(targets, values, outs, first):
-    tall = 16
+    tall, chunk = 16, 2 * LANES
     points = targets[0].shape[1]
-    row_id = lax.broadcasted_iota(jnp.int32, (tall, LANES), 0).astype(jnp.int16)
-    zero = jnp.zeros((tall, LANES), BF16)
-    for lane in range(0, points, LANES):
-        at = [jnp.broadcast_to(t[:, lane : lane + LANES], (tall, LANES)) for t in targets]
-        pieces = [split(jnp.broadcast_to(v[:, lane : lane + LANES], (tall, LANES))) for v in values]
+    row_id = lax.broadcasted_iota(jnp.int32, (tall, chunk), 0).astype(jnp.int16)
+    zero = jnp.zeros((tall, chunk), BF16)
+    for lane in range(0, points, chunk):
+        at = [jnp.broadcast_to(t[:, lane : lane + chunk], (tall, chunk)).astype(jnp.int16) for t in targets]
+        pieces = [split(jnp.broadcast_to(v[:, lane : lane + chunk], (tall, chunk))) for v in values]
         base = first
         for high_ref, low_ref in outs:
 
             @pl.loop(0, high_ref.shape[0] // TILE)
             def _(tile, base=base, high_ref=high_ref, low_ref=low_ref):
-                local = [(a - (base + tile * TILE)).astype(jnp.int16) for a in at]
+                start = (base + tile * TILE).astype(jnp.int16)
+                local = [a - start for a in at]
                 for row in range(0, TILE, tall):
                     here = row_id + jnp.int16(row)
                     high, low = zero, zero
@@ -101,14 +102,14 @@
                         hit = target == here
                         high = jnp.where(hit, value_high, high)
                         low = jnp.where(hit, value_low, low)
-                    start = pl.multiple_of(tile * TILE + row, tall)
-                    high_ref[pl.ds(start, tall), lane : lane + LANES] = high
-                    low_ref[pl.ds(start, tall), lane : lane + LANES] = low
+                    place = pl.multiple_of(tile * TILE + row, tall)
+                    high_ref[pl.ds(place, tall), lane : lane + chunk] = high
+                    low_ref[pl.ds(place, tall), lane : lane + chunk] = low
 
             base = base + high_ref.shape[0]
 
 
-def plan_kernel(parts, me_ref, *refs):
+def plan_kernel(parts, tall, me_ref, *refs):
     sources, refs = refs[:6], refs[6:]
     targets_ref, values_ref, diagonal_ref, select_ref, near_high, near_low, field_ref, frozen_ref, *refs = refs
     out, (routes_ref, neighbours_ref, weights_ref, potential_ref, arrival) = refs[:-5], refs[-5:]
@@ -125,17 +126,17 @@
     me = me_ref[0]
     copies[0].wait()
     copies[1].wait()
-    tall = 16
-    row_id = lax.broadcasted_iota(jnp.int32, (tall, capacity), 0).astype(jnp.int16)
-    one, zero = jnp.ones((tall, capacity), BF16), jnp.zeros((tall, capacity), BF16)
+    step = 16
+    row_id = lax.broadcasted_iota(jnp.int32, (step, capacity), 0).astype(jnp.int16)
+    one, zero = jnp.ones((step, capacity), BF16), jnp.zeros((step, capacity), BF16)
     for place, block in enumerate(blocks_of(parts)):
         route = routes_ref[0, pl.ds(receiver_of(me, block, parts), 1), :]
-        route = jnp.broadcast_to(route, (tall, capacity)).astype(jnp.int16)
-        for row in range(0, points, tall):
+        route = jnp.broadcast_to(route, (step, capacity)).astype(jnp.int16)
+        for row in range(0, points, step):
             hit = route == row_id + jnp.int16(row)
-            select_ref[row : row + tall, pl.ds(place * capacity, capacity)] = jnp.where(hit, one, zero)
+            select_ref[row : row + step, pl.ds(place * capacity, capacity)] = jnp.where(hit, one, zero)
     both, _ = stacked(field_ref[...])
-    pack(both, select_ref, out[:-1], out[-1])
+    pack(both, select_ref, tall, out)
     for copy in copies[2:]:
         copy.wait()
     named = neighbours_ref[...]
@@ -165,10 +166,12 @@
     stencil_rows(targets, values, list(zip(outs[::2], outs[1::2], strict=True)), first)
 
 
-def intersect(both, high, turned_high, turned_low):
-    half = high.shape[0] // 2
-    columns = turned_high.shape[1] // 2
-    result = product(both, high, turned_high, turned_low)
+def intersect(both, turned):
+    rows = both.shape[0] // 2
+    half = rows // 2
+    columns = turned.shape[1] // 4
+    result = dot(both, turned)
+    result = result[:rows, : 2 * columns] + result[rows:, : 2 * columns] + result[:rows, 2 * columns :]
     if columns >= LANES:
         return result[:half, :columns] + result[half:, columns:]
     result = result[:half] + pltpu.roll(result[half:], columns, 1)
@@ -176,8 +179,8 @@
     return jnp.where(lane < columns, result[: half // 2], pltpu.roll(result[half // 2 :], columns, 1))
 
 
-def exchange_term(sums, half, wide_high, wide_low):
-    columns = wide_high.shape[0] // 2
+def exchange_term(sums, wide):
+    columns = wide.shape[0] // 4
     if columns >= LANES:
         zero = jnp.zeros_like(sums)
         left = jnp.concatenate([jnp.concatenate([sums, zero], axis=1), jnp.concatenate([zero, sums], axis=1)], axis=0)
@@ -193,41 +196,54 @@
             ],
             axis=0,
         )
-    both, high = stacked(left)
-    return product(both, high, wide_high, wide_low)
-
-
-def slots_of(rows, tall, early_refs, late_ref):
-    slots = [(ref, 0) for ref in early_refs]
-    slots += [(late_ref.at[at], tall) for at in range(late_ref.shape[0])]
-    if early_refs[0].shape[0] > rows + tall:
-        slots += [(ref, rows + tall) for ref in early_refs]
-    return slots
-
-
-def pack(both, select_ref, early_refs, late_ref):
+    rows = left.shape[0]
+    high, low = split(left)
+    upper = jnp.concatenate([high, high], axis=1)
+    lower = jnp.concatenate([low, jnp.zeros_like(low)], axis=1)
+    result = dot(jnp.concatenate([upper, lower], axis=0), wide)
+    return result[:rows] + result[rows:]
+
+
+def slots_of(rows, tall, refs):
+    slots = [(ref, 0) for ref in refs[: EARLY - 1]]
+    if refs[0].shape[0] > rows + tall:
+        return slots + [(ref, rows + tall) for ref in refs[: EARLY - 1]]
+    return slots + [(refs[-1].at[at], tall) for at in range(refs[-1].shape[0])]
+
+
+def packed(both, select_ref, place):
     rows = both.shape[0] // 2
-    capacity = early_refs[0].shape[1]
-    tall = late_ref.shape[1] - rows
-    for place, (ref, start) in enumerate(slots_of(rows, tall, early_refs, late_ref)):
-        packed = dot(both, select_ref[:, pl.ds((place + 1) * capacity, capacity)])
-        ref[start : start + rows, :] = packed[:rows] + packed[rows:]
-
-
-def spread(partial, rows, early_refs, late_ref):
+    result = dot(both, select_ref[:, pl.ds(place * TILE, TILE)])
+    return result[:rows] + result[rows:]
+
+
+def pack(both, select_ref, tall, refs):
+    rows = both.shape[0] // 2
+    for place, (ref, start) in enumerate(slots_of(rows, tall, refs)):
+        ref[start : start + rows, :] = packed(both, select_ref, place + 2)
+
+
+def widened(partial, capacity):
     tall, width = partial.shape
-    capacity = early_refs[0].shape[1]
-    if width < capacity:
-        partial = jnp.concatenate([partial, jnp.zeros((tall, capacity - width), F32)], axis=1)
-    for ref in early_refs:
+    if width == capacity:
+        return partial
+    return jnp.concatenate([partial, jnp.zeros((tall, capacity - width), F32)], axis=1)
+
+
+def spread(partial, rows, refs):
+    tall = partial.shape[0]
+    partial = widened(partial, refs[0].shape[1])
+    for ref in refs[: EARLY - 1]:
         ref[rows : rows + tall, :] = partial
-    for at in range(late_ref.shape[0]):
-        late_ref[at, :tall, :] = partial
+    for late_ref in refs[EARLY - 1 :]:
+        for at in range(late_ref.shape[0]):
+            late_ref[at, :tall, :] = partial
 
 
 def start_kernel(groups, *refs):
     pieces, (field_ref, *refs) = refs[:groups], refs[groups:]
-    ready, (wide_high, wide_low, turned_high, turned_low, partial_ref, *out) = refs[: EARLY + 1], refs[EARLY + 1 :]
+    sent = (len(refs) - 3) // 2
+    ready, (wide_ref, turned_ref, partial_ref, *out) = refs[:sent], refs[sent:]
     rows = field_ref.shape[0]
     pieces = [piece[...] for piece in pieces]
     if pieces[0].ndim == 4:
@@ -235,30 +251,29 @@
     real = jnp.concatenate([piece[0] for piece in pieces], axis=0)
     imag = jnp.concatenate([piece[1] for piece in pieces], axis=0)
     wide = jnp.concatenate([real, -imag, imag, real], axis=0)
-    wide_high[...], wide_low[...] = split(wide)
-    turned_high[...], turned_low[...] = split(wide.T)
-    both, high = stacked(field_ref[...])
-    partial = intersect(both, high, turned_high[...], turned_low[...])
+    wide_ref[...] = jnp.concatenate(split(wide), axis=0)
+    turned_ref[...] = jnp.concatenate(split(wide.T), axis=1)
+    both, _ = stacked(field_ref[...])
+    partial = intersect(both, turned_ref[...])
     partial_ref[...] = partial
     tall = partial.shape[0]
-    (*early_in, late_in), (*early_refs, late_ref) = ready, out
-    slots_in = slots_of(rows, tall, early_in, late_in)
-    for (source, start), (target, _) in zip(slots_in, slots_of(rows, tall, early_refs, late_ref), strict=True):
+    for (source, start), (target, _) in zip(slots_of(rows, tall, ready), slots_of(rows, tall, out), strict=True):
         target[start : start + rows, :] = source[start : start + rows, :]
-    spread(partial, rows, early_refs, late_ref)
-
-
-def near_kernel(first, term_ref, select_ref, near_high, near_low, diagonal_ref, *refs):
+    spread(partial, rows, out)
+
+
+def near_kernel(first, term_ref, partial_ref, select_ref, near_high, near_low, diagonal_ref, *refs):
     if first is not None:
-        targets_ref, values_ref, base_ref, *outs = refs
+        targets_ref, values_ref, base_ref, message_ref, *outs = refs
         ghost_kernel(first, targets_ref, values_ref, *outs)
     else:
-        (base_ref,) = refs
+        base_ref, message_ref = refs
     rows, points = term_ref.shape
     term = term_ref[...]
     both, high = stacked(term)
-    own = dot(both, select_ref[:, : near_high.shape[0] - points])
-    own_both, own_high = stacked(own[:rows] + own[rows:])
+    message_ref[:rows, :] = packed(both, select_ref, 1)
+    message_ref[rows:, :] = widened(partial_ref[...], message_ref.shape[1])
+    own_both, own_high = stacked(packed(both, select_ref, 0))
     both = jnp.concatenate([both, own_both], axis=1)
     high = jnp.concatenate([high, own_high], axis=1)
     base_ref[...] = term * diagonal_ref[...] - product(both, high, near_high[...], near_low[...])
@@ -281,7 +296,7 @@
     base_out[...] = base_ref[...] - ghost_values([ref[:rows, :] for ref in early_refs], early_high[...], early_low[...])
 
 
-def late_kernel(order, last, late_ref, base_ref, sums_ref, total_ref, select_ref, first_high, first_low, rest_high, rest_low, wide_high, wide_low, turned_high, turned_low, *outs):
+def late_kernel(order, last, late_ref, base_ref, sums_ref, total_ref, select_ref, first_high, first_low, rest_high, rest_low, wide_ref, turned_ref, *outs):
     half = base_ref.shape[0] // 2
     blocks = range(late_ref.shape[0])
     sums = sums_ref[...]
@@ -290,7 +305,7 @@
         sums = sums + late_ref[block, :tall, :width]
     ghosts = [late_ref[block, tall:, :] for block in blocks]
     cut = first_high.shape[0] // late_ref.shape[2]
-    image = base_ref[...] - exchange_term(sums, half, wide_high[...], wide_low[...])
+    image = base_ref[...] - exchange_term(sums, wide_ref[...])
     image = image - ghost_values(ghosts[:cut], first_high[...], first_low[...])
     image = image - ghost_values(ghosts[cut:], rest_high[...], rest_low[...])
     scale = time_step / order
@@ -300,11 +315,11 @@
         return
     _, term_ref, partial_ref, *out = outs
     term_ref[...] = term
-    both, high = stacked(term)
-    partial = intersect(both, high, turned_high[...], turned_low[...])
+    both, _ = stacked(term)
+    partial = intersect(both, turned_ref[...])
     partial_ref[...] = partial
-    pack(both, select_ref, out[:-1], out[-1])
-    spread(partial, term.shape[0], out[:-1], out[-1])
+    pack(both, select_ref, tall, out)
+    spread(partial, term.shape[0], out)
 
 
 def swap(value, bits, parts):
@@ -340,13 +355,14 @@
     sum_shape = (half, columns) if columns >= LANES else (half * columns // LANES, LANES)
     tall = rows + sum_shape[0]
     late_blocks = places - 1 - EARLY
-    outgoing = [((tall + rows if paired else tall, capacity), F32)] * EARLY
-    outgoing += [((late_blocks - EARLY if paired else late_blocks, tall, capacity), F32)]
+    outgoing = [((tall + rows if paired else tall, capacity), F32)] * (EARLY - 1)
+    if not paired:
+        outgoing += [((late_blocks, tall, capacity), F32)]
     near_rows, early_rows = points + capacity, EARLY * capacity
     first_rows = LATE_FIRST * capacity
     rest_rows = late_blocks * capacity - first_rows
     targets, values, diagonal, select, near_high, near_low, field, own_frozen, *sent = call(
-        functools.partial(plan_kernel, parts),
+        functools.partial(plan_kernel, parts, sum_shape[0]),
         [((count, points), jnp.int32), ((count, points), F32), ((1, points), F32), ((points, places * capacity), BF16)]
         + [((near_rows, points), BF16)] * 2
         + [((rows, points), F32), (frozen.shape, F32)]
@@ -365,41 +381,47 @@
     )
     if len(pieces) == bands - 1:
         pieces = [own_frozen, *pieces]
-    wide_high, wide_low, turned_high, turned_low, partial, *sent = call(
+    wide, turned, partial, *sent = call(
         functools.partial(start_kernel, len(pieces)),
-        [((2 * columns, points), BF16)] * 2 + [((points, 2 * columns), BF16)] * 2 + [(sum_shape, F32)] + outgoing,
+        [((4 * columns, points), BF16), ((points, 4 * columns), BF16), (sum_shape, F32)] + outgoing,
         (6 * rows * points * 2 * columns, 4 << 20),
         *pieces, field, *sent,
     )
     sent[0], field, diagonal, targets = lax.optimization_barrier((sent[0], field, diagonal, targets))
     total, term = field, field
     for order in range(1, TERMS + 1):
-        *early, late = sent
         if paired:
-            early = [swap(block, bits, parts) for block, bits in zip(early, relations[1:], strict=False)]
+            early = [swap(block, bits, parts) for block, bits in zip(sent, relations[2:], strict=False)]
         else:
-            early = [move(block, offset, parts) for block, offset in zip(early, relations[1:], strict=False)]
-        near = [term, select, near_high, near_low, diagonal]
+            early = [move(block, offset, parts) for block, offset in zip(sent[: EARLY - 1], relations[2:], strict=False)]
+        near = [term, partial, select, near_high, near_low, diagonal]
         if order == 1:
-            base, early_high, early_low, first_high, first_low = call(
+            base, message, early_high, early_low, first_high, first_low = call(
                 functools.partial(near_kernel, near_rows),
-                [((rows, points), F32)] + [((early_rows, points), BF16)] * 2 + [((first_rows, points), BF16)] * 2,
+                [((rows, points), F32), ((tall, capacity), F32)] + [((early_rows, points), BF16)] * 2 + [((first_rows, points), BF16)] * 2,
                 (6 * rows * points * near_rows, 16 << 20),
                 *near, targets, values,
             )
         else:
-            (base,) = call(
+            base, message = call(
                 functools.partial(near_kernel, None),
-                [((rows, points), F32)],
+                [((rows, points), F32), ((tall, capacity), F32)],
                 (6 * rows * points * near_rows, 16 << 20),
                 *near,
             )
         if paired:
-            late = jnp.concatenate([late] + [block[None, rows:] for block in early], axis=0)
-            late, base, targets = lax.optimization_barrier((late, base, targets))
+            message = swap(message, 1, parts)
+            late = jnp.stack([block[rows:] for block in early])
+            if order == 1:
+                late, base, targets = lax.optimization_barrier((late, base, targets))
+            else:
+                late, message, base, near_high, near_low, diagonal = lax.optimization_barrier(
+                    (late, message, base, near_high, near_low, diagonal)
+                )
             late = swap(late, 1, parts)
         else:
-            late = jnp.stack([move(late[at], offset, parts) for at, offset in enumerate(relations[1 + EARLY :])])
+            message = move(message, relations[1], parts)
+            late = jnp.stack([move(sent[-1][at], offset, parts) for at, offset in enumerate(relations[1 + EARLY :])])
         if order == 1:
             rest_high, rest_low = call(
                 functools.partial(ghost_kernel, near_rows + early_rows + first_rows),
@@ -411,7 +433,7 @@
             early_kernel,
             [((rows, points), F32), (sum_shape, F32)],
             (6 * rows * points * early_rows, 4 << 20),
-            base, partial, early_high, early_low, *early,
+            base, partial, early_high, early_low, message, *early,
         )
         last = order == TERMS
         shapes = [((rows, points), F32)]
@@ -422,7 +444,7 @@
             shapes,
             (6 * rows * points * (first_rows + rest_rows), 12 << 20),
             late, base, sums, total, select, first_high, first_low, rest_high, rest_low,
-            wide_high, wide_low, turned_high, turned_low,
+            wide, turned,
         )
         total = outs[0]
         if not last:

time: 54.8 us -> 53.2 us (0.971)
  Pallas kernels: 23.6 us -> 22.5 us
  waiting for transfers between devices: 10.3 us -> 9.29 us
    ppermute x16 -> x20, waiting for transfers between devices: 9.79 us -> 8.36 us  [swap(): lax.ppermute(value, 'mesh', [(part, part ^ bits) for part in range(parts)])]
    pallas_call x15, Pallas kernels: 23.6 us -> 22.5 us  [call(): pl.pallas_call(kernel, out_shape=[jax.ShapeDtypeStruct(shape, dtype) for...]
    ppermute x16 -> x20, starting transfers between devices: 14.3 us -> 14.9 us  [swap(): lax.ppermute(value, 'mesh', [(part, part ^ bits) for part in range(parts)])]
  transfers between devices with their start and end apart: 19 -> 23, of which waited for: 13 -> 12; matrix products, arithmetic and copies ran while one was open for 0% -> 0% of each run, Pallas kernels for 30% -> 31%
where the time goes in v5:
time: 53.2 us; the launch traced here: 53 us
  Pallas kernels  22.5 us (42%)
  starting transfers between devices  20.9 us (39%)
  waiting for transfers between devices  9.29 us (17%)
    pallas_call x15, Pallas kernels, call(): pl.pallas_call(kernel, out_shape=[jax.ShapeDtypeStruct(shape, dtype) for...  22.5 us
    ppermute x20, starting transfers between devices, swap(): lax.ppermute(value, 'mesh', [(part, part ^ bits) for part in range(parts)])  14.9 us
    ppermute x20, waiting for transfers between devices, swap(): lax.ppermute(value, 'mesh', [(part, part ^ bits) for part in range(parts)])  8.36 us
    ppermute x3, starting transfers between devices, gather_frozen(): lax.ppermute(frozen, 'band', [(at, (at + step) % bands) for at in range(b...  6.06 us
  transfers between devices with their start and end apart: 23, of which 12 were waited for; matrix products, arithmetic and copies ran while one was open for 0% of the time, Pallas kernels for 31%

profile of v5, /device:TPU:0, one launch (start us, length us, event | category | flops | bytes accessed | tf_op | source)
XLA Modules:
  0.0 53.0 jit_solution(15877914598854038793)
XLA Ops:
  0.0 3.0 %collective-permute-start = (f32[2,8,1024]{2,1,0:T(8,128)}, f32[2,8,1024]{2,1,0:T(8,128)S(1)}, u32[]{:S(2)}, u32[]{:S(2)}) collective-permute-start(f32[2,8,1024]{2,1,0:T(8,128)} %refs_5_.1), channel_id=1, source_target_pairs={{0,1},{1,2},{2,3},{3,0},{4,5},{5,6},{6,7},{7,4},{8,9},{9,10},{10,1... | collective-permute-start | bytes 196616 | tf_op jit(solution)/shard_map/ppermute | solution.py:336
  3.0 2.0 %collective-permute-start.2 = (f32[2,8,1024]{2,1,0:T(8,128)}, f32[2,8,1024]{2,1,0:T(8,128)S(1)}, u32[]{:S(2)}, u32[]{:S(2)}) collective-permute-start(f32[2,8,1024]{2,1,0:T(8,128)} %refs_5_.1), channel_id=1, source_target_pairs={{0,3},{1,0},{2,1},{3,2},{4,7},{5,4},{6,5},{7,6},{8,11},{9,8},{10,9... | collective-permute-start | bytes 196616 | tf_op jit(solution)/shard_map/ppermute | solution.py:336
  5.1 1.0 %collective-permute-start.1 = (f32[2,8,1024]{2,1,0:T(8,128)}, f32[2,8,1024]{2,1,0:T(8,128)S(1)}, u32[]{:S(2)}, u32[]{:S(2)}) collective-permute-start(f32[2,8,1024]{2,1,0:T(8,128)} %refs_5_.1), channel_id=1, source_target_pairs={{0,2},{1,3},{2,0},{3,1},{4,6},{5,7},{6,4},{7,5},{8,10},{9,11},{10,... | collective-permute-start | bytes 196616 | tf_op jit(solution)/shard_map/ppermute | solution.py:336
  6.1 4.6 %shard_map.64 = (s32[8,1024]{1,0:T(8,128)S(1)}, f32[8,1024]{1,0:T(8,128)S(1)}, f32[1,1024]{1,0:T(1,128)S(1)}, bf16[1024,2048]{1,0:T(8,128)(2,1)S(1)}, bf16[1280,...) custom-call(s32[1]{0:T(128)} %bitcast.me_ref, ...), custom_call_target="tpu_custom_call" | custom-call | flops 7864320 | bytes 12582912 | tf_op jit(solution)/shard_map/pallas_call | solution.py:72
  10.6 0.0 collective-permute-done.refs_1_
  10.6 0.0 collective-permute-done.2.refs_3_
  10.6 0.9 %collective-permute-done.1.refs_2_ = f32[2,8,1024]{2,1,0:T(8,128)S(1)} collective-permute-done((f32[2,8,1024]{2,1,0:T(8,128)}, f32[2,8,1024]{2,1,0:T(8,128)S(1)}, u32[]{:S(2)}, u32[]{:S(2)}) %collective-permute-start.1) | collective-permute-done | bytes 65568 | tf_op jit(solution)/shard_map/ppermute | solution.py:336
  11.6 0.5 shard_map.65
  12.1 2.5 %collective-permute-start.3 = (f32[72,256]{1,0:T(8,128)S(1)}, f32[72,256]{1,0:T(8,128)S(1)}, u32[]{:S(2)}, u32[]{:S(2)}) collective-permute-start(f32[72,256]{1,0:T(8,128)S(1)} %get-tuple-element.92), channel_id=1, source_target_pairs={{0,24},{4,28},{8,16},{12,20},{16,8},{20,12},{24,0},{28,4},{1,25},{... | collective-permute-start | bytes 221192 | tf_op jit(solution)/shard_map/ppermute | solution.py:326
  14.5 0.5 collective-permute-start.4
  15.0 0.5 %collective-permute-start.5 = (f32[72,256]{1,0:T(8,128)S(1)}, f32[72,256]{1,0:T(8,128)S(1)}, u32[]{:S(2)}, u32[]{:S(2)}) collective-permute-start(f32[72,256]{1,0:T(8,128)S(1)} %get-tuple-element.94), channel_id=1, source_target_pairs={{0,8},{4,12},{8,0},{12,4},{16,24},{20,28},{24,16},{28,20},{1,9},{5... | collective-permute-start | bytes 221192 | tf_op jit(solution)/shard_map/ppermute | solution.py:326
  15.6 3.7 %shard_map.66 = (f32[32,1024]{1,0:T(8,128)S(1)}, f32[40,256]{1,0:T(8,128)S(1)}, bf16[1024,1024]{1,0:T(8,128)(2,1)S(1)}, bf16[1024,1024]{1,0:T(8,128)(2,1)S(1)}, ...) custom-call(f32[32,1024]{1,0:T(8,128)S(1)} %get-tuple-element.95.refs_4_.term_ref.total_ref, ...), custom_call_target="tpu_custom_call" | custom-call | flops 251658240 | bytes 16777216 | tf_op jit(solution)/shard_map/pallas_call | solution.py:72
  19.3 0.0 collective-permute-done.3.refs_1_
  19.3 0.0 collective-permute-done.4.refs_2_
  19.3 0.0 collective-permute-done.5.refs_3_
  19.4 0.1 collective-permute-start.6
  19.5 0.5 collective-permute-start.7
  20.0 1.2 %shard_map.68 = (bf16[512,1024]{1,0:T(8,128)(2,1)S(1)}, bf16[512,1024]{1,0:T(8,128)(2,1)S(1)}) custom-call(s32[8,1024]{1,0:T(8,128)S(1)} %get-tuple-element.113.refs_0_.targets_ref, f32[8,1024]{1,0:T(8,128)S(1)} %get-tuple-element.102.refs_1_.values_ref), custom_call_target="tpu_custom_call" | custom-call | flops 3145728 | bytes 12582912 | tf_op jit(solution)/shard_map/pallas_call | solution.py:72
  21.2 0.0 collective-permute-done.7.refs_0_
  21.2 0.8 %shard_map.67 = (f32[32,1024]{1,0:T(8,128)S(1)}, f32[8,128]{1,0:T(8,128)S(1)}) custom-call(f32[32,1024]{1,0:T(8,128)S(1)} %get-tuple-element.105.base_ref, f32[8,128]{1,0:T(8,128)S(1)} %get-tuple-element.96.partial_ref, bf16[1024,1024]{1,0:T(8,128)(2,1)S(1)} %get-tuple-element.106.early_high, bf16[1024,1024]{1,0:T(8,128)(2,1)S(1)} %get-tuple-element.107.early_low, ...), custom_call_target="tpu_custom_call" | custom-call | flops 201326592 | bytes 4194304 | tf_op jit(solution)/shard_map/pallas_call | solution.py:72
  22.1 0.0 collective-permute-done.6.late_ref
  22.1 1.4 %shard_map.69 = (f32[32,1024]{1,0:T(8,128)S(1)}, f32[32,1024]{1,0:T(8,128)S(1)}, f32[8,128]{1,0:T(8,128)S(1)}, f32[72,256]{1,0:T(8,128)S(1)}, f32[72,256]{1,0:T(8,128)S(1)}, /*index=5*/f32[72,256]{1,0:T(8,128)S(1)}) custom-call(f32[3,40,256]{2,1,0:T(8,128)S(1)} %collective-permute-done.6.late_ref, f32[32,1024]{1,0:T(8,128)S(1)} %get-tuple-element.109.base_ref, ...), custom_call_target="tpu_custom_call" | custom-call | flops 150994944 | bytes 12582912 | tf_op jit(solution)/shard_map/pallas_call | solution.py:72
  23.5 2.4 %collective-permute-start.8 = (f32[72,256]{1,0:T(8,128)S(1)}, f32[72,256]{1,0:T(8,128)S(1)}, u32[]{:S(2)}, u32[]{:S(2)}) collective-permute-start(f32[72,256]{1,0:T(8,128)S(1)} %get-tuple-element.118), channel_id=1, source_target_pairs={{0,24},{4,28},{8,16},{12,20},{16,8},{20,12},{24,0},{28,4},{1,25},{... | collective-permute-start | bytes 221192 | tf_op jit(solution)/shard_map/ppermute | solution.py:326
  25.9 0.5 collective-permute-start.9
  26.4 0.5 %collective-permute-start.10 = (f32[72,256]{1,0:T(8,128)S(1)}, f32[72,256]{1,0:T(8,128)S(1)}, u32[]{:S(2)}, u32[]{:S(2)}) collective-permute-start(f32[72,256]{1,0:T(8,128)S(1)} %get-tuple-element.120), channel_id=1, source_target_pairs={{0,8},{4,12},{8,0},{12,4},{16,24},{20,28},{24,16},{28,20},{1,9},{5... | collective-permute-start | bytes 221192 | tf_op jit(solution)/shard_map/ppermute | solution.py:326
  27.0 1.2 %shard_map.70 = (f32[32,1024]{1,0:T(8,128)S(1)}, f32[40,256]{1,0:T(8,128)S(1)}) custom-call(f32[32,1024]{1,0:T(8,128)S(1)} %get-tuple-element.121.term_ref, f32[8,128]{1,0:T(8,128)S(1)} %get-tuple-element.122.partial_ref, bf16[1024,2048]{1,0:T(8,128)(2,1)S(1)} %get-tuple-element.97.select_ref, bf16[1280,1024]{1,0:T(8,128)(2,1)S(1)} %get-tuple-element.152.near_high, ...), custom_call_target="tpu_custom_call" | custom-call | flops 251658240 | bytes 16777216 | tf_op jit(solution)/shard_map/pallas_call | solution.py:72
  28.2 0.0 collective-permute-start.11
  28.2 0.6 %collective-permute-done.8.refs_1_ = f32[72,256]{1,0:T(8,128)S(1)} collective-permute-done((f32[72,256]{1,0:T(8,128)S(1)}, f32[72,256]{1,0:T(8,128)S(1)}, u32[]{:S(2)}, u32[]{:S(2)}) %collective-permute-start.8) | collective-permute-done | bytes 73760 | tf_op jit(solution)/shard_map/ppermute | solution.py:326
  28.8 1.5 %collective-permute-done.9.refs_2_ = f32[72,256]{1,0:T(8,128)S(1)} collective-permute-done((f32[72,256]{1,0:T(8,128)S(1)}, f32[72,256]{1,0:T(8,128)S(1)}, u32[]{:S(2)}, u32[]{:S(2)}) %collective-permute-start.9) | collective-permute-done | bytes 73760 | tf_op jit(solution)/shard_map/ppermute | solution.py:326
  30.3 0.5 collective-permute-done.10.refs_3_
  30.8 0.0 collective-permute-done.11.refs_0_
  30.8 0.1 collective-permute-start.12
  30.9 0.8 %shard_map.71 = (f32[32,1024]{1,0:T(8,128)S(1)}, f32[8,128]{1,0:T(8,128)S(1)}) custom-call(f32[32,1024]{1,0:T(8,128)S(1)} %get-tuple-element.126.base_ref, f32[8,128]{1,0:T(8,128)S(1)} %get-tuple-element.122.partial_ref, bf16[1024,1024]{1,0:T(8,128)(2,1)S(1)} %get-tuple-element.106.early_high, bf16[1024,1024]{1,0:T(8,128)(2,1)S(1)} %get-tuple-element.107.early_low, ...), custom_call_target="tpu_custom_call" | custom-call | flops 201326592 | bytes 4194304 | tf_op jit(solution)/shard_map/pallas_call | solution.py:72
  31.7 0.5 collective-permute-done.12.late_ref
  32.2 1.4 %shard_map.72 = (f32[32,1024]{1,0:T(8,128)S(1)}, f32[32,1024]{1,0:T(8,128)S(1)}, f32[8,128]{1,0:T(8,128)S(1)}, f32[72,256]{1,0:T(8,128)S(1)}, f32[72,256]{1,0:T(8,128)S(1)}, /*index=5*/f32[72,256]{1,0:T(8,128)S(1)}) custom-call(f32[3,40,256]{2,1,0:T(8,128)S(1)} %collective-permute-done.12.late_ref, f32[32,1024]{1,0:T(8,128)S(1)} %get-tuple-element.128.base_ref, ...), custom_call_target="tpu_custom_call" | custom-call | flops 150994944 | bytes 12582912 | tf_op jit(solution)/shard_map/pallas_call | solution.py:72
  33.6 1.5 %collective-permute-start.13 = (f32[72,256]{1,0:T(8,128)S(1)}, f32[72,256]{1,0:T(8,128)S(1)}, u32[]{:S(2)}, u32[]{:S(2)}) collective-permute-start(f32[72,256]{1,0:T(8,128)S(1)} %get-tuple-element.131), channel_id=1, source_target_pairs={{0,24},{4,28},{8,16},{12,20},{16,8},{20,12},{24,0},{28,4},{1,25},{... | collective-permute-start | bytes 221192 | tf_op jit(solution)/shard_map/ppermute | solution.py:326
  35.1 0.9 %collective-permute-start.14 = (f32[72,256]{1,0:T(8,128)S(1)}, f32[72,256]{1,0:T(8,128)S(1)}, u32[]{:S(2)}, u32[]{:S(2)}) collective-permute-start(f32[72,256]{1,0:T(8,128)S(1)} %get-tuple-element.132), channel_id=1, source_target_pairs={{0,16},{4,20},{8,24},{12,28},{16,0},{20,4},{24,8},{28,12},{1,17},{... | collective-permute-start | bytes 221192 | tf_op jit(solution)/shard_map/ppermute | solution.py:326
  36.0 1.1 %collective-permute-start.15 = (f32[72,256]{1,0:T(8,128)S(1)}, f32[72,256]{1,0:T(8,128)S(1)}, u32[]{:S(2)}, u32[]{:S(2)}) collective-permute-start(f32[72,256]{1,0:T(8,128)S(1)} %get-tuple-element.133), channel_id=1, source_target_pairs={{0,8},{4,12},{8,0},{12,4},{16,24},{20,28},{24,16},{28,20},{1,9},{5... | collective-permute-start | bytes 221192 | tf_op jit(solution)/shard_map/ppermute | solution.py:326
  37.1 1.2 %shard_map.73 = (f32[32,1024]{1,0:T(8,128)S(1)}, f32[40,256]{1,0:T(8,128)S(1)}) custom-call(f32[32,1024]{1,0:T(8,128)S(1)} %get-tuple-element.134.term_ref, f32[8,128]{1,0:T(8,128)S(1)} %get-tuple-element.135.partial_ref, bf16[1024,2048]{1,0:T(8,128)(2,1)S(1)} %get-tuple-element.97.select_ref, bf16[1280,1024]{1,0:T(8,128)(2,1)S(1)} %get-tuple-element.152.near_high, ...), custom_call_target="tpu_custom_call" | custom-call | flops 251658240 | bytes 16777216 | tf_op jit(solution)/shard_map/pallas_call | solution.py:72
  38.3 0.0 collective-permute-start.16
  38.3 0.7 %collective-permute-done.13.refs_1_ = f32[72,256]{1,0:T(8,128)S(1)} collective-permute-done((f32[72,256]{1,0:T(8,128)S(1)}, f32[72,256]{1,0:T(8,128)S(1)}, u32[]{:S(2)}, u32[]{:S(2)}) %collective-permute-start.13) | collective-permute-done | bytes 73760 | tf_op jit(solution)/shard_map/ppermute | solution.py:326
  39.0 1.4 %collective-permute-done.14.refs_2_ = f32[72,256]{1,0:T(8,128)S(1)} collective-permute-done((f32[72,256]{1,0:T(8,128)S(1)}, f32[72,256]{1,0:T(8,128)S(1)}, u32[]{:S(2)}, u32[]{:S(2)}) %collective-permute-start.14) | collective-permute-done | bytes 73760 | tf_op jit(solution)/shard_map/ppermute | solution.py:326
  40.4 0.1 collective-permute-done.15.refs_3_
  40.5 0.0 collective-permute-done.16.refs_0_
  40.5 0.1 collective-permute-start.17
  40.6 0.8 %shard_map.74 = (f32[32,1024]{1,0:T(8,128)S(1)}, f32[8,128]{1,0:T(8,128)S(1)}) custom-call(f32[32,1024]{1,0:T(8,128)S(1)} %get-tuple-element.142.base_ref, f32[8,128]{1,0:T(8,128)S(1)} %get-tuple-element.135.partial_ref, bf16[1024,1024]{1,0:T(8,128)(2,1)S(1)} %get-tuple-element.106.early_high, bf16[1024,1024]{1,0:T(8,128)(2,1)S(1)} %get-tuple-element.107.early_low, ...), custom_call_target="tpu_custom_call" | custom-call | flops 201326592 | bytes 4194304 | tf_op jit(solution)/shard_map/pallas_call | solution.py:72
  41.4 0.5 collective-permute-done.17.late_ref
  41.9 1.4 %shard_map.75 = (f32[32,1024]{1,0:T(8,128)S(1)}, f32[32,1024]{1,0:T(8,128)S(1)}, f32[8,128]{1,0:T(8,128)S(1)}, f32[72,256]{1,0:T(8,128)S(1)}, f32[72,256]{1,0:T(8,128)S(1)}, /*index=5*/f32[72,256]{1,0:T(8,128)S(1)}) custom-call(f32[3,40,256]{2,1,0:T(8,128)S(1)} %collective-permute-done.17.late_ref, f32[32,1024]{1,0:T(8,128)S(1)} %get-tuple-element.144.base_ref, ...), custom_call_target="tpu_custom_call" | custom-call | flops 150994944 | bytes 12582912 | tf_op jit(solution)/shard_map/pallas_call | solution.py:72
  43.3 1.9 %collective-permute-start.18 = (f32[72,256]{1,0:T(8,128)S(1)}, f32[72,256]{1,0:T(8,128)S(1)}, u32[]{:S(2)}, u32[]{:S(2)}) collective-permute-start(f32[72,256]{1,0:T(8,128)S(1)} %get-tuple-element.147), channel_id=1, source_target_pairs={{0,24},{4,28},{8,16},{12,20},{16,8},{20,12},{24,0},{28,4},{1,25},{... | collective-permute-start | bytes 221192 | tf_op jit(solution)/shard_map/ppermute | solution.py:326
  45.2 0.5 collective-permute-start.19
  45.7 1.1 %collective-permute-start.20 = (f32[72,256]{1,0:T(8,128)S(1)}, f32[72,256]{1,0:T(8,128)S(1)}, u32[]{:S(2)}, u32[]{:S(2)}) collective-permute-start(f32[72,256]{1,0:T(8,128)S(1)} %get-tuple-element.149), channel_id=1, source_target_pairs={{0,8},{4,12},{8,0},{12,4},{16,24},{20,28},{24,16},{28,20},{1,9},{5... | collective-permute-start | bytes 221192 | tf_op jit(solution)/shard_map/ppermute | solution.py:326
  46.8 1.2 %shard_map.76 = (f32[32,1024]{1,0:T(8,128)S(1)}, f32[40,256]{1,0:T(8,128)S(1)}) custom-call(f32[32,1024]{1,0:T(8,128)S(1)} %get-tuple-element.150.term_ref, f32[8,128]{1,0:T(8,128)S(1)} %get-tuple-element.151.partial_ref, bf16[1024,2048]{1,0:T(8,128)(2,1)S(1)} %get-tuple-element.97.select_ref, bf16[1280,1024]{1,0:T(8,128)(2,1)S(1)} %get-tuple-element.152.near_high, ...), custom_call_target="tpu_custom_call" | custom-call | flops 251658240 | bytes 16777216 | tf_op jit(solution)/shard_map/pallas_call | solution.py:72
  48.0 0.0 collective-permute-start.21
  48.0 0.6 %collective-permute-done.18.refs_1_ = f32[72,256]{1,0:T(8,128)S(1)} collective-permute-done((f32[72,256]{1,0:T(8,128)S(1)}, f32[72,256]{1,0:T(8,128)S(1)}, u32[]{:S(2)}, u32[]{:S(2)}) %collective-permute-start.18) | collective-permute-done | bytes 73760 | tf_op jit(solution)/shard_map/ppermute | solution.py:326
  48.6 1.5 %collective-permute-done.19.refs_2_ = f32[72,256]{1,0:T(8,128)S(1)} collective-permute-done((f32[72,256]{1,0:T(8,128)S(1)}, f32[72,256]{1,0:T(8,128)S(1)}, u32[]{:S(2)}, u32[]{:S(2)}) %collective-permute-start.19) | collective-permute-done | bytes 73760 | tf_op jit(solution)/shard_map/ppermute | solution.py:326
  50.1 0.0 collective-permute-done.20.refs_3_
  50.1 0.0 collective-permute-done.21.refs_0_
  50.1 0.1 collective-permute-start.22
  50.2 0.8 %shard_map.77 = (f32[32,1024]{1,0:T(8,128)S(1)}, f32[8,128]{1,0:T(8,128)S(1)}) custom-call(f32[32,1024]{1,0:T(8,128)S(1)} %get-tuple-element.158.base_ref, f32[8,128]{1,0:T(8,128)S(1)} %get-tuple-element.151.partial_ref, bf16[1024,1024]{1,0:T(8,128)(2,1)S(1)} %get-tuple-element.106.early_high, bf16[1024,1024]{1,0:T(8,128)(2,1)S(1)} %get-tuple-element.107.early_low, ...), custom_call_target="tpu_custom_call" | custom-call | flops 201326592 | bytes 4194304 | tf_op jit(solution)/shard_map/pallas_call | solution.py:72
  51.0 0.5 collective-permute-done.22.late_ref
  51.5 1.4 %shard_map.78 = f32[32,1024]{1,0:T(8,128)} custom-call(f32[3,40,256]{2,1,0:T(8,128)S(1)} %collective-permute-done.22.late_ref, f32[32,1024]{1,0:T(8,128)S(1)} %get-tuple-element.160.base_ref, f32[8,128]{1,0:T(8,128)S(1)} %get-tuple-element.161.sums_ref, f32[32,1024]{1,0:T(8,128)S(1)} %get-tuple-element.162.total_ref, ...), custom_call_target="tpu_custom_call" | custom-call | flops 150994944 | bytes 12582912 | tf_op jit(solution)/shard_map/pallas_call | solution.py:72
  (16 shorter events, 0.1 us)
Async XLA Ops:
  0.0 10.6 %collective-permute-start = (f32[2,8,1024]{2,1,0:T(8,128)}, f32[2,8,1024]{2,1,0:T(8,128)S(1)}, u32[]{:S(2)}, u32[]{:S(2)}) collective-permute-start(f32[2,8,1024]{2,1,0:T(8,128)} %refs_5_.1), channel_id=1, source_target_pairs={{0,1},{1,2},{2,3},{3,0},{4,5},{5,6},{6,7},{7,4},{8,9},{9,10},{10,1... | collective-permute-start | bytes 196616 | tf_op jit(solution)/shard_map/ppermute | solution.py:336
  3.0 7.6 %collective-permute-start.2 = (f32[2,8,1024]{2,1,0:T(8,128)}, f32[2,8,1024]{2,1,0:T(8,128)S(1)}, u32[]{:S(2)}, u32[]{:S(2)}) collective-permute-start(f32[2,8,1024]{2,1,0:T(8,128)} %refs_5_.1), channel_id=1, source_target_pairs={{0,3},{1,0},{2,1},{3,2},{4,7},{5,4},{6,5},{7,6},{8,11},{9,8},{10,9... | collective-permute-start | bytes 196616 | tf_op jit(solution)/shard_map/ppermute | solution.py:336
  5.1 6.5 %collective-permute-start.1 = (f32[2,8,1024]{2,1,0:T(8,128)}, f32[2,8,1024]{2,1,0:T(8,128)S(1)}, u32[]{:S(2)}, u32[]{:S(2)}) collective-permute-start(f32[2,8,1024]{2,1,0:T(8,128)} %refs_5_.1), channel_id=1, source_target_pairs={{0,2},{1,3},{2,0},{3,1},{4,6},{5,7},{6,4},{7,5},{8,10},{9,11},{10,... | collective-permute-start | bytes 196616 | tf_op jit(solution)/shard_map/ppermute | solution.py:336
  12.1 7.2 %collective-permute-start.3 = (f32[72,256]{1,0:T(8,128)S(1)}, f32[72,256]{1,0:T(8,128)S(1)}, u32[]{:S(2)}, u32[]{:S(2)}) collective-permute-start(f32[72,256]{1,0:T(8,128)S(1)} %get-tuple-element.92), channel_id=1, source_target_pairs={{0,24},{4,28},{8,16},{12,20},{16,8},{20,12},{24,0},{28,4},{1,25},{... | collective-permute-start | bytes 221192 | tf_op jit(solution)/shard_map/ppermute | solution.py:326
  14.5 4.8 %collective-permute-start.4 = (f32[72,256]{1,0:T(8,128)S(1)}, f32[72,256]{1,0:T(8,128)S(1)}, u32[]{:S(2)}, u32[]{:S(2)}) collective-permute-start(f32[72,256]{1,0:T(8,128)S(1)} %get-tuple-element.93), channel_id=1, source_target_pairs={{0,16},{4,20},{8,24},{12,28},{16,0},{20,4},{24,8},{28,12},{1,17},{... | collective-permute-start | bytes 221192 | tf_op jit(solution)/shard_map/ppermute | solution.py:326
  15.0 4.4 %collective-permute-start.5 = (f32[72,256]{1,0:T(8,128)S(1)}, f32[72,256]{1,0:T(8,128)S(1)}, u32[]{:S(2)}, u32[]{:S(2)}) collective-permute-start(f32[72,256]{1,0:T(8,128)S(1)} %get-tuple-element.94), channel_id=1, source_target_pairs={{0,8},{4,12},{8,0},{12,4},{16,24},{20,28},{24,16},{28,20},{1,9},{5... | collective-permute-start | bytes 221192 | tf_op jit(solution)/shard_map/ppermute | solution.py:326
  19.4 2.7 %collective-permute-start.6 = (f32[3,40,256]{2,1,0:T(8,128)S(1)}, f32[3,40,256]{2,1,0:T(8,128)S(1)}, u32[]{:S(2)}, u32[]{:S(2)}) collective-permute-start(f32[3,40,256]{2,1,0:T(8,128)S(1)} %pad_maximum_fusion), channel_id=1, source_target_pairs={{0,4},{4,0},{8,12},{12,8},{16,20},{20,16},{24,28},{28,24},{1,5},{5... | collective-permute-start | bytes 368648 | tf_op jit(solution)/shard_map/ppermute | solution.py:326
  19.5 1.7 %collective-permute-start.7 = (f32[40,256]{1,0:T(8,128)S(1)}, f32[40,256]{1,0:T(8,128)S(1)}, u32[]{:S(2)}, u32[]{:S(2)}) collective-permute-start(f32[40,256]{1,0:T(8,128)S(1)} %get-tuple-element.108), channel_id=1, source_target_pairs={{0,4},{4,0},{8,12},{12,8},{16,20},{20,16},{24,28},{28,24},{1,5},{5... | collective-permute-start | bytes 122888 | tf_op jit(solution)/shard_map/ppermute | solution.py:326
  23.5 5.3 %collective-permute-start.8 = (f32[72,256]{1,0:T(8,128)S(1)}, f32[72,256]{1,0:T(8,128)S(1)}, u32[]{:S(2)}, u32[]{:S(2)}) collective-permute-start(f32[72,256]{1,0:T(8,128)S(1)} %get-tuple-element.118), channel_id=1, source_target_pairs={{0,24},{4,28},{8,16},{12,20},{16,8},{20,12},{24,0},{28,4},{1,25},{... | collective-permute-start | bytes 221192 | tf_op jit(solution)/shard_map/ppermute | solution.py:326
  25.9 4.4 %collective-permute-start.9 = (f32[72,256]{1,0:T(8,128)S(1)}, f32[72,256]{1,0:T(8,128)S(1)}, u32[]{:S(2)}, u32[]{:S(2)}) collective-permute-start(f32[72,256]{1,0:T(8,128)S(1)} %get-tuple-element.119), channel_id=1, source_target_pairs={{0,16},{4,20},{8,24},{12,28},{16,0},{20,4},{24,8},{28,12},{1,17},{... | collective-permute-start | bytes 221192 | tf_op jit(solution)/shard_map/ppermute | solution.py:326
  26.4 4.4 %collective-permute-start.10 = (f32[72,256]{1,0:T(8,128)S(1)}, f32[72,256]{1,0:T(8,128)S(1)}, u32[]{:S(2)}, u32[]{:S(2)}) collective-permute-start(f32[72,256]{1,0:T(8,128)S(1)} %get-tuple-element.120), channel_id=1, source_target_pairs={{0,8},{4,12},{8,0},{12,4},{16,24},{20,28},{24,16},{28,20},{1,9},{5... | collective-permute-start | bytes 221192 | tf_op jit(solution)/shard_map/ppermute | solution.py:326
  28.2 2.6 %collective-permute-start.11 = (f32[40,256]{1,0:T(8,128)S(1)}, f32[40,256]{1,0:T(8,128)S(1)}, u32[]{:S(2)}, u32[]{:S(2)}) collective-permute-start(f32[40,256]{1,0:T(8,128)S(1)} %get-tuple-element.123), channel_id=1, source_target_pairs={{0,4},{4,0},{8,12},{12,8},{16,20},{20,16},{24,28},{28,24},{1,5},{5... | collective-permute-start | bytes 122888 | tf_op jit(solution)/shard_map/ppermute | solution.py:326
  30.8 1.4 %collective-permute-start.12 = (f32[3,40,256]{2,1,0:T(8,128)S(1)}, f32[3,40,256]{2,1,0:T(8,128)S(1)}, u32[]{:S(2)}, u32[]{:S(2)}) collective-permute-start(f32[3,40,256]{2,1,0:T(8,128)S(1)} %pad_maximum_fusion.1), channel_id=1, source_target_pairs={{0,4},{4,0},{8,12},{12,8},{16,20},{20,16},{24,28},{28,24},{1,5},{5... | collective-permute-start | bytes 368648 | tf_op jit(solution)/shard_map/ppermute | solution.py:326
  33.6 5.4 %collective-permute-start.13 = (f32[72,256]{1,0:T(8,128)S(1)}, f32[72,256]{1,0:T(8,128)S(1)}, u32[]{:S(2)}, u32[]{:S(2)}) collective-permute-start(f32[72,256]{1,0:T(8,128)S(1)} %get-tuple-element.131), channel_id=1, source_target_pairs={{0,24},{4,28},{8,16},{12,20},{16,8},{20,12},{24,0},{28,4},{1,25},{... | collective-permute-start | bytes 221192 | tf_op jit(solution)/shard_map/ppermute | solution.py:326
  35.1 5.3 %collective-permute-start.14 = (f32[72,256]{1,0:T(8,128)S(1)}, f32[72,256]{1,0:T(8,128)S(1)}, u32[]{:S(2)}, u32[]{:S(2)}) collective-permute-start(f32[72,256]{1,0:T(8,128)S(1)} %get-tuple-element.132), channel_id=1, source_target_pairs={{0,16},{4,20},{8,24},{12,28},{16,0},{20,4},{24,8},{28,12},{1,17},{... | collective-permute-start | bytes 221192 | tf_op jit(solution)/shard_map/ppermute | solution.py:326
  36.0 4.5 %collective-permute-start.15 = (f32[72,256]{1,0:T(8,128)S(1)}, f32[72,256]{1,0:T(8,128)S(1)}, u32[]{:S(2)}, u32[]{:S(2)}) collective-permute-start(f32[72,256]{1,0:T(8,128)S(1)} %get-tuple-element.133), channel_id=1, source_target_pairs={{0,8},{4,12},{8,0},{12,4},{16,24},{20,28},{24,16},{28,20},{1,9},{5... | collective-permute-start | bytes 221192 | tf_op jit(solution)/shard_map/ppermute | solution.py:326
  38.3 2.2 %collective-permute-start.16 = (f32[40,256]{1,0:T(8,128)S(1)}, f32[40,256]{1,0:T(8,128)S(1)}, u32[]{:S(2)}, u32[]{:S(2)}) collective-permute-start(f32[40,256]{1,0:T(8,128)S(1)} %get-tuple-element.139), channel_id=1, source_target_pairs={{0,4},{4,0},{8,12},{12,8},{16,20},{20,16},{24,28},{28,24},{1,5},{5... | collective-permute-start | bytes 122888 | tf_op jit(solution)/shard_map/ppermute | solution.py:326
  40.5 1.4 %collective-permute-start.17 = (f32[3,40,256]{2,1,0:T(8,128)S(1)}, f32[3,40,256]{2,1,0:T(8,128)S(1)}, u32[]{:S(2)}, u32[]{:S(2)}) collective-permute-start(f32[3,40,256]{2,1,0:T(8,128)S(1)} %pad_maximum_fusion.2), channel_id=1, source_target_pairs={{0,4},{4,0},{8,12},{12,8},{16,20},{20,16},{24,28},{28,24},{1,5},{5... | collective-permute-start | bytes 368648 | tf_op jit(solution)/shard_map/ppermute | solution.py:326
  43.3 5.3 %collective-permute-start.18 = (f32[72,256]{1,0:T(8,128)S(1)}, f32[72,256]{1,0:T(8,128)S(1)}, u32[]{:S(2)}, u32[]{:S(2)}) collective-permute-start(f32[72,256]{1,0:T(8,128)S(1)} %get-tuple-element.147), channel_id=1, source_target_pairs={{0,24},{4,28},{8,16},{12,20},{16,8},{20,12},{24,0},{28,4},{1,25},{... | collective-permute-start | bytes 221192 | tf_op jit(solution)/shard_map/ppermute | solution.py:326
  45.2 4.9 %collective-permute-start.19 = (f32[72,256]{1,0:T(8,128)S(1)}, f32[72,256]{1,0:T(8,128)S(1)}, u32[]{:S(2)}, u32[]{:S(2)}) collective-permute-start(f32[72,256]{1,0:T(8,128)S(1)} %get-tuple-element.148), channel_id=1, source_target_pairs={{0,16},{4,20},{8,24},{12,28},{16,0},{20,4},{24,8},{28,12},{1,17},{... | collective-permute-start | bytes 221192 | tf_op jit(solution)/shard_map/ppermute | solution.py:326
  45.7 4.4 %collective-permute-start.20 = (f32[72,256]{1,0:T(8,128)S(1)}, f32[72,256]{1,0:T(8,128)S(1)}, u32[]{:S(2)}, u32[]{:S(2)}) collective-permute-start(f32[72,256]{1,0:T(8,128)S(1)} %get-tuple-element.149), channel_id=1, source_target_pairs={{0,8},{4,12},{8,0},{12,4},{16,24},{20,28},{24,16},{28,20},{1,9},{5... | collective-permute-start | bytes 221192 | tf_op jit(solution)/shard_map/ppermute | solution.py:326
  48.0 2.2 %collective-permute-start.21 = (f32[40,256]{1,0:T(8,128)S(1)}, f32[40,256]{1,0:T(8,128)S(1)}, u32[]{:S(2)}, u32[]{:S(2)}) collective-permute-start(f32[40,256]{1,0:T(8,128)S(1)} %get-tuple-element.155), channel_id=1, source_target_pairs={{0,4},{4,0},{8,12},{12,8},{16,20},{20,16},{24,28},{28,24},{1,5},{5... | collective-permute-start | bytes 122888 | tf_op jit(solution)/shard_map/ppermute | solution.py:326
  50.1 1.4 %collective-permute-start.22 = (f32[3,40,256]{2,1,0:T(8,128)S(1)}, f32[3,40,256]{2,1,0:T(8,128)S(1)}, u32[]{:S(2)}, u32[]{:S(2)}) collective-permute-start(f32[3,40,256]{2,1,0:T(8,128)S(1)} %pad_maximum_fusion.3), channel_id=1, source_target_pairs={{0,4},{4,0},{8,12},{12,8},{16,20},{20,16},{24,28},{28,24},{1,5},{5... | collective-permute-start | bytes 368648 | tf_op jit(solution)/shard_map/ppermute | solution.py:326

commit v6 on v5

--- a/solution.py
+++ b/solution.py
@@ -332,8 +332,8 @@
 
 def gather_frozen(frozen):
     bands = lax.axis_size("band")
-    if bands <= 4:
-        return [lax.ppermute(frozen, "band", [(at, (at + step) % bands) for at in range(bands)]) for step in range(1, bands)]
+    if bands == 4:
+        return [lax.ppermute(frozen, "band", [(at, at ^ step) for at in range(bands)]) for step in (2, 1, 3)]
     return [lax.all_gather(frozen, "band", axis=0, tiled=False)]
 
 

time: 53.2 us -> 52.2 us (0.981)
    ppermute x3, waiting for transfers between devices: 0.92 us -> 0.38 us  [gather_frozen(): lax.ppermute(frozen, 'band', [(at, at ^ step) for at in range(bands)])]
  transfers between devices with their start and end apart: 23 -> 23, of which waited for: 12 -> 13; matrix products, arithmetic and copies ran while one was open for 0% -> 0% of each run, Pallas kernels for 31% -> 32%
where the time goes in v6:
time: 52.2 us; the launch traced here: 52 us
  Pallas kernels  22.5 us (43%)
  starting transfers between devices  20.5 us (39%)
  waiting for transfers between devices  8.77 us (17%)
    pallas_call x15, Pallas kernels, call(): pl.pallas_call(kernel, out_shape=[jax.ShapeDtypeStruct(shape, dtype) for...  22.5 us
    ppermute x20, starting transfers between devices, swap(): lax.ppermute(value, 'mesh', [(part, part ^ bits) for part in range(parts)])  14.9 us
    ppermute x20, waiting for transfers between devices, swap(): lax.ppermute(value, 'mesh', [(part, part ^ bits) for part in range(parts)])  8.39 us
    ppermute x3, starting transfers between devices, gather_frozen(): lax.ppermute(frozen, 'band', [(at, at ^ step) for at in range(bands)])  5.62 us
  transfers between devices with their start and end apart: 23, of which 13 were waited for; matrix products, arithmetic and copies ran while one was open for 0% of the time, Pallas kernels for 32%

profile of v6, /device:TPU:0, one launch (start us, length us, event | category | flops | bytes accessed | tf_op | source)
XLA Modules:
  0.0 52.0 jit_solution(9409527431810596880)
XLA Ops:
  0.0 4.0 %collective-permute-start = (f32[2,8,1024]{2,1,0:T(8,128)}, f32[2,8,1024]{2,1,0:T(8,128)S(1)}, u32[]{:S(2)}, u32[]{:S(2)}) collective-permute-start(f32[2,8,1024]{2,1,0:T(8,128)} %refs_5_.1), channel_id=1, source_target_pairs={{0,2},{1,3},{2,0},{3,1},{4,6},{5,7},{6,4},{7,5},{8,10},{9,11},{10,... | collective-permute-start | bytes 196616 | tf_op jit(solution)/shard_map/ppermute | solution.py:336
  4.0 1.3 %collective-permute-start.2 = (f32[2,8,1024]{2,1,0:T(8,128)}, f32[2,8,1024]{2,1,0:T(8,128)S(1)}, u32[]{:S(2)}, u32[]{:S(2)}) collective-permute-start(f32[2,8,1024]{2,1,0:T(8,128)} %refs_5_.1), channel_id=1, source_target_pairs={{0,3},{1,2},{2,1},{3,0},{4,7},{5,6},{6,5},{7,4},{8,11},{9,10},{10,... | collective-permute-start | bytes 196616 | tf_op jit(solution)/shard_map/ppermute | solution.py:336
  5.4 0.2 collective-permute-start.1
  5.6 4.6 %shard_map.64 = (s32[8,1024]{1,0:T(8,128)S(1)}, f32[8,1024]{1,0:T(8,128)S(1)}, f32[1,1024]{1,0:T(1,128)S(1)}, bf16[1024,2048]{1,0:T(8,128)(2,1)S(1)}, bf16[1280,...) custom-call(s32[1]{0:T(128)} %bitcast.me_ref, ...), custom_call_target="tpu_custom_call" | custom-call | flops 7864320 | bytes 12582912 | tf_op jit(solution)/shard_map/pallas_call | solution.py:72
  10.2 0.0 collective-permute-done.refs_1_
  10.2 0.3 collective-permute-done.2.refs_3_
  10.5 0.1 collective-permute-done.1.refs_2_
  10.6 0.5 shard_map.65
  11.1 2.5 %collective-permute-start.3 = (f32[72,256]{1,0:T(8,128)S(1)}, f32[72,256]{1,0:T(8,128)S(1)}, u32[]{:S(2)}, u32[]{:S(2)}) collective-permute-start(f32[72,256]{1,0:T(8,128)S(1)} %get-tuple-element.92), channel_id=1, source_target_pairs={{0,24},{4,28},{8,16},{12,20},{16,8},{20,12},{24,0},{28,4},{1,25},{... | collective-permute-start | bytes 221192 | tf_op jit(solution)/shard_map/ppermute | solution.py:326
  13.5 0.5 collective-permute-start.4
  14.0 0.5 %collective-permute-start.5 = (f32[72,256]{1,0:T(8,128)S(1)}, f32[72,256]{1,0:T(8,128)S(1)}, u32[]{:S(2)}, u32[]{:S(2)}) collective-permute-start(f32[72,256]{1,0:T(8,128)S(1)} %get-tuple-element.94), channel_id=1, source_target_pairs={{0,8},{4,12},{8,0},{12,4},{16,24},{20,28},{24,16},{28,20},{1,9},{5... | collective-permute-start | bytes 221192 | tf_op jit(solution)/shard_map/ppermute | solution.py:326
  14.6 3.7 %shard_map.66 = (f32[32,1024]{1,0:T(8,128)S(1)}, f32[40,256]{1,0:T(8,128)S(1)}, bf16[1024,1024]{1,0:T(8,128)(2,1)S(1)}, bf16[1024,1024]{1,0:T(8,128)(2,1)S(1)}, ...) custom-call(f32[32,1024]{1,0:T(8,128)S(1)} %get-tuple-element.95.refs_4_.term_ref.total_ref, ...), custom_call_target="tpu_custom_call" | custom-call | flops 251658240 | bytes 16777216 | tf_op jit(solution)/shard_map/pallas_call | solution.py:72
  18.3 0.0 collective-permute-done.3.refs_1_
  18.3 0.0 collective-permute-done.4.refs_2_
  18.3 0.0 collective-permute-done.5.refs_3_
  18.4 0.1 collective-permute-start.6
  18.5 0.5 collective-permute-start.7
  19.0 1.2 %shard_map.68 = (bf16[512,1024]{1,0:T(8,128)(2,1)S(1)}, bf16[512,1024]{1,0:T(8,128)(2,1)S(1)}) custom-call(s32[8,1024]{1,0:T(8,128)S(1)} %get-tuple-element.113.refs_0_.targets_ref, f32[8,1024]{1,0:T(8,128)S(1)} %get-tuple-element.102.refs_1_.values_ref), custom_call_target="tpu_custom_call" | custom-call | flops 3145728 | bytes 12582912 | tf_op jit(solution)/shard_map/pallas_call | solution.py:72
  20.2 0.0 collective-permute-done.7.refs_0_
  20.2 0.8 %shard_map.67 = (f32[32,1024]{1,0:T(8,128)S(1)}, f32[8,128]{1,0:T(8,128)S(1)}) custom-call(f32[32,1024]{1,0:T(8,128)S(1)} %get-tuple-element.105.base_ref, f32[8,128]{1,0:T(8,128)S(1)} %get-tuple-element.96.partial_ref, bf16[1024,1024]{1,0:T(8,128)(2,1)S(1)} %get-tuple-element.106.early_high, bf16[1024,1024]{1,0:T(8,128)(2,1)S(1)} %get-tuple-element.107.early_low, ...), custom_call_target="tpu_custom_call" | custom-call | flops 201326592 | bytes 4194304 | tf_op jit(solution)/shard_map/pallas_call | solution.py:72
  21.1 0.0 collective-permute-done.6.late_ref
  21.1 1.4 %shard_map.69 = (f32[32,1024]{1,0:T(8,128)S(1)}, f32[32,1024]{1,0:T(8,128)S(1)}, f32[8,128]{1,0:T(8,128)S(1)}, f32[72,256]{1,0:T(8,128)S(1)}, f32[72,256]{1,0:T(8,128)S(1)}, /*index=5*/f32[72,256]{1,0:T(8,128)S(1)}) custom-call(f32[3,40,256]{2,1,0:T(8,128)S(1)} %collective-permute-done.6.late_ref, f32[32,1024]{1,0:T(8,128)S(1)} %get-tuple-element.109.base_ref, ...), custom_call_target="tpu_custom_call" | custom-call | flops 150994944 | bytes 12582912 | tf_op jit(solution)/shard_map/pallas_call | solution.py:72
  22.5 2.5 %collective-permute-start.8 = (f32[72,256]{1,0:T(8,128)S(1)}, f32[72,256]{1,0:T(8,128)S(1)}, u32[]{:S(2)}, u32[]{:S(2)}) collective-permute-start(f32[72,256]{1,0:T(8,128)S(1)} %get-tuple-element.118), channel_id=1, source_target_pairs={{0,24},{4,28},{8,16},{12,20},{16,8},{20,12},{24,0},{28,4},{1,25},{... | collective-permute-start | bytes 221192 | tf_op jit(solution)/shard_map/ppermute | solution.py:326
  24.9 0.5 collective-permute-start.9
  25.4 0.5 %collective-permute-start.10 = (f32[72,256]{1,0:T(8,128)S(1)}, f32[72,256]{1,0:T(8,128)S(1)}, u32[]{:S(2)}, u32[]{:S(2)}) collective-permute-start(f32[72,256]{1,0:T(8,128)S(1)} %get-tuple-element.120), channel_id=1, source_target_pairs={{0,8},{4,12},{8,0},{12,4},{16,24},{20,28},{24,16},{28,20},{1,9},{5... | collective-permute-start | bytes 221192 | tf_op jit(solution)/shard_map/ppermute | solution.py:326
  26.0 1.2 %shard_map.70 = (f32[32,1024]{1,0:T(8,128)S(1)}, f32[40,256]{1,0:T(8,128)S(1)}) custom-call(f32[32,1024]{1,0:T(8,128)S(1)} %get-tuple-element.121.term_ref, f32[8,128]{1,0:T(8,128)S(1)} %get-tuple-element.122.partial_ref, bf16[1024,2048]{1,0:T(8,128)(2,1)S(1)} %get-tuple-element.97.select_ref, bf16[1280,1024]{1,0:T(8,128)(2,1)S(1)} %get-tuple-element.152.near_high, ...), custom_call_target="tpu_custom_call" | custom-call | flops 251658240 | bytes 16777216 | tf_op jit(solution)/shard_map/pallas_call | solution.py:72
  27.2 0.0 collective-permute-start.11
  27.2 0.6 %collective-permute-done.8.refs_1_ = f32[72,256]{1,0:T(8,128)S(1)} collective-permute-done((f32[72,256]{1,0:T(8,128)S(1)}, f32[72,256]{1,0:T(8,128)S(1)}, u32[]{:S(2)}, u32[]{:S(2)}) %collective-permute-start.8) | collective-permute-done | bytes 73760 | tf_op jit(solution)/shard_map/ppermute | solution.py:326
  27.8 1.5 %collective-permute-done.9.refs_2_ = f32[72,256]{1,0:T(8,128)S(1)} collective-permute-done((f32[72,256]{1,0:T(8,128)S(1)}, f32[72,256]{1,0:T(8,128)S(1)}, u32[]{:S(2)}, u32[]{:S(2)}) %collective-permute-start.9) | collective-permute-done | bytes 73760 | tf_op jit(solution)/shard_map/ppermute | solution.py:326
  29.3 0.5 collective-permute-done.10.refs_3_
  29.8 0.0 collective-permute-done.11.refs_0_
  29.8 0.1 collective-permute-start.12
  29.9 0.8 %shard_map.71 = (f32[32,1024]{1,0:T(8,128)S(1)}, f32[8,128]{1,0:T(8,128)S(1)}) custom-call(f32[32,1024]{1,0:T(8,128)S(1)} %get-tuple-element.126.base_ref, f32[8,128]{1,0:T(8,128)S(1)} %get-tuple-element.122.partial_ref, bf16[1024,1024]{1,0:T(8,128)(2,1)S(1)} %get-tuple-element.106.early_high, bf16[1024,1024]{1,0:T(8,128)(2,1)S(1)} %get-tuple-element.107.early_low, ...), custom_call_target="tpu_custom_call" | custom-call | flops 201326592 | bytes 4194304 | tf_op jit(solution)/shard_map/pallas_call | solution.py:72
  30.7 0.5 collective-permute-done.12.late_ref
  31.2 1.4 %shard_map.72 = (f32[32,1024]{1,0:T(8,128)S(1)}, f32[32,1024]{1,0:T(8,128)S(1)}, f32[8,128]{1,0:T(8,128)S(1)}, f32[72,256]{1,0:T(8,128)S(1)}, f32[72,256]{1,0:T(8,128)S(1)}, /*index=5*/f32[72,256]{1,0:T(8,128)S(1)}) custom-call(f32[3,40,256]{2,1,0:T(8,128)S(1)} %collective-permute-done.12.late_ref, f32[32,1024]{1,0:T(8,128)S(1)} %get-tuple-element.128.base_ref, ...), custom_call_target="tpu_custom_call" | custom-call | flops 150994944 | bytes 12582912 | tf_op jit(solution)/shard_map/pallas_call | solution.py:72
  32.6 1.5 %collective-permute-start.13 = (f32[72,256]{1,0:T(8,128)S(1)}, f32[72,256]{1,0:T(8,128)S(1)}, u32[]{:S(2)}, u32[]{:S(2)}) collective-permute-start(f32[72,256]{1,0:T(8,128)S(1)} %get-tuple-element.131), channel_id=1, source_target_pairs={{0,24},{4,28},{8,16},{12,20},{16,8},{20,12},{24,0},{28,4},{1,25},{... | collective-permute-start | bytes 221192 | tf_op jit(solution)/shard_map/ppermute | solution.py:326
  34.1 0.9 %collective-permute-start.14 = (f32[72,256]{1,0:T(8,128)S(1)}, f32[72,256]{1,0:T(8,128)S(1)}, u32[]{:S(2)}, u32[]{:S(2)}) collective-permute-start(f32[72,256]{1,0:T(8,128)S(1)} %get-tuple-element.132), channel_id=1, source_target_pairs={{0,16},{4,20},{8,24},{12,28},{16,0},{20,4},{24,8},{28,12},{1,17},{... | collective-permute-start | bytes 221192 | tf_op jit(solution)/shard_map/ppermute | solution.py:326
  35.0 1.1 %collective-permute-start.15 = (f32[72,256]{1,0:T(8,128)S(1)}, f32[72,256]{1,0:T(8,128)S(1)}, u32[]{:S(2)}, u32[]{:S(2)}) collective-permute-start(f32[72,256]{1,0:T(8,128)S(1)} %get-tuple-element.133), channel_id=1, source_target_pairs={{0,8},{4,12},{8,0},{12,4},{16,24},{20,28},{24,16},{28,20},{1,9},{5... | collective-permute-start | bytes 221192 | tf_op jit(solution)/shard_map/ppermute | solution.py:326
  36.1 1.2 %shard_map.73 = (f32[32,1024]{1,0:T(8,128)S(1)}, f32[40,256]{1,0:T(8,128)S(1)}) custom-call(f32[32,1024]{1,0:T(8,128)S(1)} %get-tuple-element.134.term_ref, f32[8,128]{1,0:T(8,128)S(1)} %get-tuple-element.135.partial_ref, bf16[1024,2048]{1,0:T(8,128)(2,1)S(1)} %get-tuple-element.97.select_ref, bf16[1280,1024]{1,0:T(8,128)(2,1)S(1)} %get-tuple-element.152.near_high, ...), custom_call_target="tpu_custom_call" | custom-call | flops 251658240 | bytes 16777216 | tf_op jit(solution)/shard_map/pallas_call | solution.py:72
  37.3 0.0 collective-permute-start.16
  37.3 0.7 %collective-permute-done.13.refs_1_ = f32[72,256]{1,0:T(8,128)S(1)} collective-permute-done((f32[72,256]{1,0:T(8,128)S(1)}, f32[72,256]{1,0:T(8,128)S(1)}, u32[]{:S(2)}, u32[]{:S(2)}) %collective-permute-start.13) | collective-permute-done | bytes 73760 | tf_op jit(solution)/shard_map/ppermute | solution.py:326
  38.0 1.4 %collective-permute-done.14.refs_2_ = f32[72,256]{1,0:T(8,128)S(1)} collective-permute-done((f32[72,256]{1,0:T(8,128)S(1)}, f32[72,256]{1,0:T(8,128)S(1)}, u32[]{:S(2)}, u32[]{:S(2)}) %collective-permute-start.14) | collective-permute-done | bytes 73760 | tf_op jit(solution)/shard_map/ppermute | solution.py:326
  39.4 0.1 collective-permute-done.15.refs_3_
  39.5 0.0 collective-permute-done.16.refs_0_
  39.5 0.1 collective-permute-start.17
  39.6 0.8 %shard_map.74 = (f32[32,1024]{1,0:T(8,128)S(1)}, f32[8,128]{1,0:T(8,128)S(1)}) custom-call(f32[32,1024]{1,0:T(8,128)S(1)} %get-tuple-element.142.base_ref, f32[8,128]{1,0:T(8,128)S(1)} %get-tuple-element.135.partial_ref, bf16[1024,1024]{1,0:T(8,128)(2,1)S(1)} %get-tuple-element.106.early_high, bf16[1024,1024]{1,0:T(8,128)(2,1)S(1)} %get-tuple-element.107.early_low, ...), custom_call_target="tpu_custom_call" | custom-call | flops 201326592 | bytes 4194304 | tf_op jit(solution)/shard_map/pallas_call | solution.py:72
  40.4 0.5 collective-permute-done.17.late_ref
  40.9 1.4 %shard_map.75 = (f32[32,1024]{1,0:T(8,128)S(1)}, f32[32,1024]{1,0:T(8,128)S(1)}, f32[8,128]{1,0:T(8,128)S(1)}, f32[72,256]{1,0:T(8,128)S(1)}, f32[72,256]{1,0:T(8,128)S(1)}, /*index=5*/f32[72,256]{1,0:T(8,128)S(1)}) custom-call(f32[3,40,256]{2,1,0:T(8,128)S(1)} %collective-permute-done.17.late_ref, f32[32,1024]{1,0:T(8,128)S(1)} %get-tuple-element.144.base_ref, ...), custom_call_target="tpu_custom_call" | custom-call | flops 150994944 | bytes 12582912 | tf_op jit(solution)/shard_map/pallas_call | solution.py:72
  42.3 1.9 %collective-permute-start.18 = (f32[72,256]{1,0:T(8,128)S(1)}, f32[72,256]{1,0:T(8,128)S(1)}, u32[]{:S(2)}, u32[]{:S(2)}) collective-permute-start(f32[72,256]{1,0:T(8,128)S(1)} %get-tuple-element.147), channel_id=1, source_target_pairs={{0,24},{4,28},{8,16},{12,20},{16,8},{20,12},{24,0},{28,4},{1,25},{... | collective-permute-start | bytes 221192 | tf_op jit(solution)/shard_map/ppermute | solution.py:326
  44.2 0.5 collective-permute-start.19
  44.7 1.1 %collective-permute-start.20 = (f32[72,256]{1,0:T(8,128)S(1)}, f32[72,256]{1,0:T(8,128)S(1)}, u32[]{:S(2)}, u32[]{:S(2)}) collective-permute-start(f32[72,256]{1,0:T(8,128)S(1)} %get-tuple-element.149), channel_id=1, source_target_pairs={{0,8},{4,12},{8,0},{12,4},{16,24},{20,28},{24,16},{28,20},{1,9},{5... | collective-permute-start | bytes 221192 | tf_op jit(solution)/shard_map/ppermute | solution.py:326
  45.8 1.2 %shard_map.76 = (f32[32,1024]{1,0:T(8,128)S(1)}, f32[40,256]{1,0:T(8,128)S(1)}) custom-call(f32[32,1024]{1,0:T(8,128)S(1)} %get-tuple-element.150.term_ref, f32[8,128]{1,0:T(8,128)S(1)} %get-tuple-element.151.partial_ref, bf16[1024,2048]{1,0:T(8,128)(2,1)S(1)} %get-tuple-element.97.select_ref, bf16[1280,1024]{1,0:T(8,128)(2,1)S(1)} %get-tuple-element.152.near_high, ...), custom_call_target="tpu_custom_call" | custom-call | flops 251658240 | bytes 16777216 | tf_op jit(solution)/shard_map/pallas_call | solution.py:72
  47.0 0.0 collective-permute-start.21
  47.0 0.6 %collective-permute-done.18.refs_1_ = f32[72,256]{1,0:T(8,128)S(1)} collective-permute-done((f32[72,256]{1,0:T(8,128)S(1)}, f32[72,256]{1,0:T(8,128)S(1)}, u32[]{:S(2)}, u32[]{:S(2)}) %collective-permute-start.18) | collective-permute-done | bytes 73760 | tf_op jit(solution)/shard_map/ppermute | solution.py:326
  47.6 1.5 %collective-permute-done.19.refs_2_ = f32[72,256]{1,0:T(8,128)S(1)} collective-permute-done((f32[72,256]{1,0:T(8,128)S(1)}, f32[72,256]{1,0:T(8,128)S(1)}, u32[]{:S(2)}, u32[]{:S(2)}) %collective-permute-start.19) | collective-permute-done | bytes 73760 | tf_op jit(solution)/shard_map/ppermute | solution.py:326
  49.1 0.0 collective-permute-done.20.refs_3_
  49.1 0.0 collective-permute-done.21.refs_0_
  49.1 0.1 collective-permute-start.22
  49.2 0.8 %shard_map.77 = (f32[32,1024]{1,0:T(8,128)S(1)}, f32[8,128]{1,0:T(8,128)S(1)}) custom-call(f32[32,1024]{1,0:T(8,128)S(1)} %get-tuple-element.158.base_ref, f32[8,128]{1,0:T(8,128)S(1)} %get-tuple-element.151.partial_ref, bf16[1024,1024]{1,0:T(8,128)(2,1)S(1)} %get-tuple-element.106.early_high, bf16[1024,1024]{1,0:T(8,128)(2,1)S(1)} %get-tuple-element.107.early_low, ...), custom_call_target="tpu_custom_call" | custom-call | flops 201326592 | bytes 4194304 | tf_op jit(solution)/shard_map/pallas_call | solution.py:72
  50.0 0.5 collective-permute-done.22.late_ref
  50.5 1.4 %shard_map.78 = f32[32,1024]{1,0:T(8,128)} custom-call(f32[3,40,256]{2,1,0:T(8,128)S(1)} %collective-permute-done.22.late_ref, f32[32,1024]{1,0:T(8,128)S(1)} %get-tuple-element.160.base_ref, f32[8,128]{1,0:T(8,128)S(1)} %get-tuple-element.161.sums_ref, f32[32,1024]{1,0:T(8,128)S(1)} %get-tuple-element.162.total_ref, ...), custom_call_target="tpu_custom_call" | custom-call | flops 150994944 | bytes 12582912 | tf_op jit(solution)/shard_map/pallas_call | solution.py:72
  (16 shorter events, 0.1 us)
Async XLA Ops:
  0.0 10.2 %collective-permute-start = (f32[2,8,1024]{2,1,0:T(8,128)}, f32[2,8,1024]{2,1,0:T(8,128)S(1)}, u32[]{:S(2)}, u32[]{:S(2)}) collective-permute-start(f32[2,8,1024]{2,1,0:T(8,128)} %refs_5_.1), channel_id=1, source_target_pairs={{0,2},{1,3},{2,0},{3,1},{4,6},{5,7},{6,4},{7,5},{8,10},{9,11},{10,... | collective-permute-start | bytes 196616 | tf_op jit(solution)/shard_map/ppermute | solution.py:336
  4.0 6.4 %collective-permute-start.2 = (f32[2,8,1024]{2,1,0:T(8,128)}, f32[2,8,1024]{2,1,0:T(8,128)S(1)}, u32[]{:S(2)}, u32[]{:S(2)}) collective-permute-start(f32[2,8,1024]{2,1,0:T(8,128)} %refs_5_.1), channel_id=1, source_target_pairs={{0,3},{1,2},{2,1},{3,0},{4,7},{5,6},{6,5},{7,4},{8,11},{9,10},{10,... | collective-permute-start | bytes 196616 | tf_op jit(solution)/shard_map/ppermute | solution.py:336
  5.4 5.2 %collective-permute-start.1 = (f32[2,8,1024]{2,1,0:T(8,128)}, f32[2,8,1024]{2,1,0:T(8,128)S(1)}, u32[]{:S(2)}, u32[]{:S(2)}) collective-permute-start(f32[2,8,1024]{2,1,0:T(8,128)} %refs_5_.1), channel_id=1, source_target_pairs={{0,1},{1,0},{2,3},{3,2},{4,5},{5,4},{6,7},{7,6},{8,9},{9,8},{10,11... | collective-permute-start | bytes 196616 | tf_op jit(solution)/shard_map/ppermute | solution.py:336
  11.1 7.2 %collective-permute-start.3 = (f32[72,256]{1,0:T(8,128)S(1)}, f32[72,256]{1,0:T(8,128)S(1)}, u32[]{:S(2)}, u32[]{:S(2)}) collective-permute-start(f32[72,256]{1,0:T(8,128)S(1)} %get-tuple-element.92), channel_id=1, source_target_pairs={{0,24},{4,28},{8,16},{12,20},{16,8},{20,12},{24,0},{28,4},{1,25},{... | collective-permute-start | bytes 221192 | tf_op jit(solution)/shard_map/ppermute | solution.py:326
  13.5 4.8 %collective-permute-start.4 = (f32[72,256]{1,0:T(8,128)S(1)}, f32[72,256]{1,0:T(8,128)S(1)}, u32[]{:S(2)}, u32[]{:S(2)}) collective-permute-start(f32[72,256]{1,0:T(8,128)S(1)} %get-tuple-element.93), channel_id=1, source_target_pairs={{0,16},{4,20},{8,24},{12,28},{16,0},{20,4},{24,8},{28,12},{1,17},{... | collective-permute-start | bytes 221192 | tf_op jit(solution)/shard_map/ppermute | solution.py:326
  14.0 4.4 %collective-permute-start.5 = (f32[72,256]{1,0:T(8,128)S(1)}, f32[72,256]{1,0:T(8,128)S(1)}, u32[]{:S(2)}, u32[]{:S(2)}) collective-permute-start(f32[72,256]{1,0:T(8,128)S(1)} %get-tuple-element.94), channel_id=1, source_target_pairs={{0,8},{4,12},{8,0},{12,4},{16,24},{20,28},{24,16},{28,20},{1,9},{5... | collective-permute-start | bytes 221192 | tf_op jit(solution)/shard_map/ppermute | solution.py:326
  18.4 2.7 %collective-permute-start.6 = (f32[3,40,256]{2,1,0:T(8,128)S(1)}, f32[3,40,256]{2,1,0:T(8,128)S(1)}, u32[]{:S(2)}, u32[]{:S(2)}) collective-permute-start(f32[3,40,256]{2,1,0:T(8,128)S(1)} %pad_maximum_fusion), channel_id=1, source_target_pairs={{0,4},{4,0},{8,12},{12,8},{16,20},{20,16},{24,28},{28,24},{1,5},{5... | collective-permute-start | bytes 368648 | tf_op jit(solution)/shard_map/ppermute | solution.py:326
  18.5 1.7 %collective-permute-start.7 = (f32[40,256]{1,0:T(8,128)S(1)}, f32[40,256]{1,0:T(8,128)S(1)}, u32[]{:S(2)}, u32[]{:S(2)}) collective-permute-start(f32[40,256]{1,0:T(8,128)S(1)} %get-tuple-element.108), channel_id=1, source_target_pairs={{0,4},{4,0},{8,12},{12,8},{16,20},{20,16},{24,28},{28,24},{1,5},{5... | collective-permute-start | bytes 122888 | tf_op jit(solution)/shard_map/ppermute | solution.py:326
  22.5 5.3 %collective-permute-start.8 = (f32[72,256]{1,0:T(8,128)S(1)}, f32[72,256]{1,0:T(8,128)S(1)}, u32[]{:S(2)}, u32[]{:S(2)}) collective-permute-start(f32[72,256]{1,0:T(8,128)S(1)} %get-tuple-element.118), channel_id=1, source_target_pairs={{0,24},{4,28},{8,16},{12,20},{16,8},{20,12},{24,0},{28,4},{1,25},{... | collective-permute-start | bytes 221192 | tf_op jit(solution)/shard_map/ppermute | solution.py:326
  24.9 4.4 %collective-permute-start.9 = (f32[72,256]{1,0:T(8,128)S(1)}, f32[72,256]{1,0:T(8,128)S(1)}, u32[]{:S(2)}, u32[]{:S(2)}) collective-permute-start(f32[72,256]{1,0:T(8,128)S(1)} %get-tuple-element.119), channel_id=1, source_target_pairs={{0,16},{4,20},{8,24},{12,28},{16,0},{20,4},{24,8},{28,12},{1,17},{... | collective-permute-start | bytes 221192 | tf_op jit(solution)/shard_map/ppermute | solution.py:326
  25.4 4.4 %collective-permute-start.10 = (f32[72,256]{1,0:T(8,128)S(1)}, f32[72,256]{1,0:T(8,128)S(1)}, u32[]{:S(2)}, u32[]{:S(2)}) collective-permute-start(f32[72,256]{1,0:T(8,128)S(1)} %get-tuple-element.120), channel_id=1, source_target_pairs={{0,8},{4,12},{8,0},{12,4},{16,24},{20,28},{24,16},{28,20},{1,9},{5... | collective-permute-start | bytes 221192 | tf_op jit(solution)/shard_map/ppermute | solution.py:326
  27.2 2.6 %collective-permute-start.11 = (f32[40,256]{1,0:T(8,128)S(1)}, f32[40,256]{1,0:T(8,128)S(1)}, u32[]{:S(2)}, u32[]{:S(2)}) collective-permute-start(f32[40,256]{1,0:T(8,128)S(1)} %get-tuple-element.123), channel_id=1, source_target_pairs={{0,4},{4,0},{8,12},{12,8},{16,20},{20,16},{24,28},{28,24},{1,5},{5... | collective-permute-start | bytes 122888 | tf_op jit(solution)/shard_map/ppermute | solution.py:326
  29.8 1.4 %collective-permute-start.12 = (f32[3,40,256]{2,1,0:T(8,128)S(1)}, f32[3,40,256]{2,1,0:T(8,128)S(1)}, u32[]{:S(2)}, u32[]{:S(2)}) collective-permute-start(f32[3,40,256]{2,1,0:T(8,128)S(1)} %pad_maximum_fusion.1), channel_id=1, source_target_pairs={{0,4},{4,0},{8,12},{12,8},{16,20},{20,16},{24,28},{28,24},{1,5},{5... | collective-permute-start | bytes 368648 | tf_op jit(solution)/shard_map/ppermute | solution.py:326
  32.6 5.4 %collective-permute-start.13 = (f32[72,256]{1,0:T(8,128)S(1)}, f32[72,256]{1,0:T(8,128)S(1)}, u32[]{:S(2)}, u32[]{:S(2)}) collective-permute-start(f32[72,256]{1,0:T(8,128)S(1)} %get-tuple-element.131), channel_id=1, source_target_pairs={{0,24},{4,28},{8,16},{12,20},{16,8},{20,12},{24,0},{28,4},{1,25},{... | collective-permute-start | bytes 221192 | tf_op jit(solution)/shard_map/ppermute | solution.py:326
  34.1 5.3 %collective-permute-start.14 = (f32[72,256]{1,0:T(8,128)S(1)}, f32[72,256]{1,0:T(8,128)S(1)}, u32[]{:S(2)}, u32[]{:S(2)}) collective-permute-start(f32[72,256]{1,0:T(8,128)S(1)} %get-tuple-element.132), channel_id=1, source_target_pairs={{0,16},{4,20},{8,24},{12,28},{16,0},{20,4},{24,8},{28,12},{1,17},{... | collective-permute-start | bytes 221192 | tf_op jit(solution)/shard_map/ppermute | solution.py:326
  35.0 4.5 %collective-permute-start.15 = (f32[72,256]{1,0:T(8,128)S(1)}, f32[72,256]{1,0:T(8,128)S(1)}, u32[]{:S(2)}, u32[]{:S(2)}) collective-permute-start(f32[72,256]{1,0:T(8,128)S(1)} %get-tuple-element.133), channel_id=1, source_target_pairs={{0,8},{4,12},{8,0},{12,4},{16,24},{20,28},{24,16},{28,20},{1,9},{5... | collective-permute-start | bytes 221192 | tf_op jit(solution)/shard_map/ppermute | solution.py:326
  37.3 2.2 %collective-permute-start.16 = (f32[40,256]{1,0:T(8,128)S(1)}, f32[40,256]{1,0:T(8,128)S(1)}, u32[]{:S(2)}, u32[]{:S(2)}) collective-permute-start(f32[40,256]{1,0:T(8,128)S(1)} %get-tuple-element.139), channel_id=1, source_target_pairs={{0,4},{4,0},{8,12},{12,8},{16,20},{20,16},{24,28},{28,24},{1,5},{5... | collective-permute-start | bytes 122888 | tf_op jit(solution)/shard_map/ppermute | solution.py:326
  39.5 1.4 %collective-permute-start.17 = (f32[3,40,256]{2,1,0:T(8,128)S(1)}, f32[3,40,256]{2,1,0:T(8,128)S(1)}, u32[]{:S(2)}, u32[]{:S(2)}) collective-permute-start(f32[3,40,256]{2,1,0:T(8,128)S(1)} %pad_maximum_fusion.2), channel_id=1, source_target_pairs={{0,4},{4,0},{8,12},{12,8},{16,20},{20,16},{24,28},{28,24},{1,5},{5... | collective-permute-start | bytes 368648 | tf_op jit(solution)/shard_map/ppermute | solution.py:326
  42.3 5.3 %collective-permute-start.18 = (f32[72,256]{1,0:T(8,128)S(1)}, f32[72,256]{1,0:T(8,128)S(1)}, u32[]{:S(2)}, u32[]{:S(2)}) collective-permute-start(f32[72,256]{1,0:T(8,128)S(1)} %get-tuple-element.147), channel_id=1, source_target_pairs={{0,24},{4,28},{8,16},{12,20},{16,8},{20,12},{24,0},{28,4},{1,25},{... | collective-permute-start | bytes 221192 | tf_op jit(solution)/shard_map/ppermute | solution.py:326
  44.2 4.9 %collective-permute-start.19 = (f32[72,256]{1,0:T(8,128)S(1)}, f32[72,256]{1,0:T(8,128)S(1)}, u32[]{:S(2)}, u32[]{:S(2)}) collective-permute-start(f32[72,256]{1,0:T(8,128)S(1)} %get-tuple-element.148), channel_id=1, source_target_pairs={{0,16},{4,20},{8,24},{12,28},{16,0},{20,4},{24,8},{28,12},{1,17},{... | collective-permute-start | bytes 221192 | tf_op jit(solution)/shard_map/ppermute | solution.py:326
  44.7 4.4 %collective-permute-start.20 = (f32[72,256]{1,0:T(8,128)S(1)}, f32[72,256]{1,0:T(8,128)S(1)}, u32[]{:S(2)}, u32[]{:S(2)}) collective-permute-start(f32[72,256]{1,0:T(8,128)S(1)} %get-tuple-element.149), channel_id=1, source_target_pairs={{0,8},{4,12},{8,0},{12,4},{16,24},{20,28},{24,16},{28,20},{1,9},{5... | collective-permute-start | bytes 221192 | tf_op jit(solution)/shard_map/ppermute | solution.py:326
  47.0 2.2 %collective-permute-start.21 = (f32[40,256]{1,0:T(8,128)S(1)}, f32[40,256]{1,0:T(8,128)S(1)}, u32[]{:S(2)}, u32[]{:S(2)}) collective-permute-start(f32[40,256]{1,0:T(8,128)S(1)} %get-tuple-element.155), channel_id=1, source_target_pairs={{0,4},{4,0},{8,12},{12,8},{16,20},{20,16},{24,28},{28,24},{1,5},{5... | collective-permute-start | bytes 122888 | tf_op jit(solution)/shard_map/ppermute | solution.py:326
  49.1 1.4 %collective-permute-start.22 = (f32[3,40,256]{2,1,0:T(8,128)S(1)}, f32[3,40,256]{2,1,0:T(8,128)S(1)}, u32[]{:S(2)}, u32[]{:S(2)}) collective-permute-start(f32[3,40,256]{2,1,0:T(8,128)S(1)} %pad_maximum_fusion.3), channel_id=1, source_target_pairs={{0,4},{4,0},{8,12},{12,8},{16,20},{20,16},{24,28},{28,24},{1,5},{5... | collective-permute-start | bytes 368648 | tf_op jit(solution)/shard_map/ppermute | solution.py:326

commit v7 on v6

--- a/solution.py
+++ b/solution.py
@@ -136,7 +136,9 @@
             hit = route == row_id + jnp.int16(row)
             select_ref[row : row + step, pl.ds(place * capacity, capacity)] = jnp.where(hit, one, zero)
     both, _ = stacked(field_ref[...])
+    *out, message_ref = out
     pack(both, select_ref, tall, out)
+    message_ref[: field_ref.shape[0], :] = packed(both, select_ref, 1)
     for copy in copies[2:]:
         copy.wait()
     named = neighbours_ref[...]
@@ -243,7 +245,7 @@
 def start_kernel(groups, *refs):
     pieces, (field_ref, *refs) = refs[:groups], refs[groups:]
     sent = (len(refs) - 3) // 2
-    ready, (wide_ref, turned_ref, partial_ref, *out) = refs[:sent], refs[sent:]
+    (*ready, message_in), (wide_ref, turned_ref, partial_ref, *out, message_ref) = refs[:sent], refs[sent:]
     rows = field_ref.shape[0]
     pieces = [piece[...] for piece in pieces]
     if pieces[0].ndim == 4:
@@ -260,23 +262,30 @@
     for (source, start), (target, _) in zip(slots_of(rows, tall, ready), slots_of(rows, tall, out), strict=True):
         target[start : start + rows, :] = source[start : start + rows, :]
     spread(partial, rows, out)
-
-
-def near_kernel(first, term_ref, partial_ref, select_ref, near_high, near_low, diagonal_ref, *refs):
-    if first is not None:
-        targets_ref, values_ref, base_ref, message_ref, *outs = refs
-        ghost_kernel(first, targets_ref, values_ref, *outs)
-    else:
-        base_ref, message_ref = refs
-    rows, points = term_ref.shape
+    message_ref[:rows, :] = message_in[:rows, :]
+    message_ref[rows:, :] = widened(partial, message_ref.shape[1])
+
+
+def near_values(both, high, select_ref, near_high, near_low):
+    own_both, own_high = stacked(packed(both, select_ref, 0))
+    both = jnp.concatenate([both, own_both], axis=1)
+    return product(both, jnp.concatenate([high, own_high], axis=1), near_high[...], near_low[...])
+
+
+def near_kernel(term_ref, partial_ref, select_ref, near_high, near_low, diagonal_ref, base_ref, message_ref):
+    rows = term_ref.shape[0]
     term = term_ref[...]
     both, high = stacked(term)
     message_ref[:rows, :] = packed(both, select_ref, 1)
     message_ref[rows:, :] = widened(partial_ref[...], message_ref.shape[1])
-    own_both, own_high = stacked(packed(both, select_ref, 0))
-    both = jnp.concatenate([both, own_both], axis=1)
-    high = jnp.concatenate([high, own_high], axis=1)
-    base_ref[...] = term * diagonal_ref[...] - product(both, high, near_high[...], near_low[...])
+    base_ref[...] = term * diagonal_ref[...] - near_values(both, high, select_ref, near_high, near_low)
+
+
+def first_near_kernel(first, term_ref, select_ref, near_high, near_low, diagonal_ref, targets_ref, values_ref, base_ref, *outs):
+    ghost_kernel(first, targets_ref, values_ref, *outs)
+    term = term_ref[...]
+    both, high = stacked(term)
+    base_ref[...] = term * diagonal_ref[...] - near_values(both, high, select_ref, near_high, near_low)
 
 
 def ghost_values(blocks, high, low):
@@ -366,7 +375,8 @@
         [((count, points), jnp.int32), ((count, points), F32), ((1, points), F32), ((points, places * capacity), BF16)]
         + [((near_rows, points), BF16)] * 2
         + [((rows, points), F32), (frozen.shape, F32)]
-        + outgoing,
+        + outgoing
+        + [((tall, capacity), F32)],
         (6 * near_rows * points, 12 << 20),
         me, send_list, states.reshape(rows, points), neighbours, weights, potential.reshape(1, points), frozen,
         scalars=1,
@@ -381,9 +391,9 @@
     )
     if len(pieces) == bands - 1:
         pieces = [own_frozen, *pieces]
-    wide, turned, partial, *sent = call(
+    wide, turned, partial, *sent, message = call(
         functools.partial(start_kernel, len(pieces)),
-        [((4 * columns, points), BF16), ((points, 4 * columns), BF16), (sum_shape, F32)] + outgoing,
+        [((4 * columns, points), BF16), ((points, 4 * columns), BF16), (sum_shape, F32)] + outgoing + [((tall, capacity), F32)],
         (6 * rows * points * 2 * columns, 4 << 20),
         *pieces, field, *sent,
     )
@@ -394,30 +404,26 @@
             early = [swap(block, bits, parts) for block, bits in zip(sent, relations[2:], strict=False)]
         else:
             early = [move(block, offset, parts) for block, offset in zip(sent[: EARLY - 1], relations[2:], strict=False)]
-        near = [term, partial, select, near_high, near_low, diagonal]
         if order == 1:
-            base, message, early_high, early_low, first_high, first_low = call(
-                functools.partial(near_kernel, near_rows),
-                [((rows, points), F32), ((tall, capacity), F32)] + [((early_rows, points), BF16)] * 2 + [((first_rows, points), BF16)] * 2,
+            base, early_high, early_low, first_high, first_low = call(
+                functools.partial(first_near_kernel, near_rows),
+                [((rows, points), F32)] + [((early_rows, points), BF16)] * 2 + [((first_rows, points), BF16)] * 2,
                 (6 * rows * points * near_rows, 16 << 20),
-                *near, targets, values,
+                term, select, near_high, near_low, diagonal, targets, values,
             )
         else:
             base, message = call(
-                functools.partial(near_kernel, None),
+                near_kernel,
                 [((rows, points), F32), ((tall, capacity), F32)],
                 (6 * rows * points * near_rows, 16 << 20),
-                *near,
+                term, partial, select, near_high, near_low, diagonal,
             )
         if paired:
             message = swap(message, 1, parts)
             late = jnp.stack([block[rows:] for block in early])
-            if order == 1:
-                late, base, targets = lax.optimization_barrier((late, base, targets))
-            else:
-                late, message, base, near_high, near_low, diagonal = lax.optimization_barrier(
-                    (late, message, base, near_high, near_low, diagonal)
-                )
+            late, message, base, near_high, near_low, diagonal, targets = lax.optimization_barrier(
+                (late, message, base, near_high, near_low, diagonal, targets)
+            )
             late = swap(late, 1, parts)
         else:
             message = move(message, relations[1], parts)

time: 52.2 us -> 52 us (level)
  transfers between devices with their start and end apart: 23 -> 23, of which waited for: 13 -> 14; matrix products, arithmetic and copies ran while one was open for 0% -> 0% of each run, Pallas kernels for 32% -> 32%
where the time goes in v7:
time: 52 us; the launch traced here: 51.8 us
  Pallas kernels  22.4 us (43%)
  starting transfers between devices  20 us (38%)
  waiting for transfers between devices  9.06 us (17%)
    pallas_call x15, Pallas kernels, call(): pl.pallas_call(kernel, out_shape=[jax.ShapeDtypeStruct(shape, dtype) for...  22.4 us
    ppermute x20, starting transfers between devices, swap(): lax.ppermute(value, 'mesh', [(part, part ^ bits) for part in range(parts)])  14.4 us
    ppermute x20, waiting for transfers between devices, swap(): lax.ppermute(value, 'mesh', [(part, part ^ bits) for part in range(parts)])  8.74 us
    ppermute x3, starting transfers between devices, gather_frozen(): lax.ppermute(frozen, 'band', [(at, at ^ step) for at in range(bands)])  5.62 us
  transfers between devices with their start and end apart: 23, of which 14 were waited for; matrix products, arithmetic and copies ran while one was open for 0% of the time, Pallas kernels for 32%

profile of v7, /device:TPU:0, one launch (start us, length us, event | category | flops | bytes accessed | tf_op | source)
XLA Modules:
  0.0 51.8 jit_solution(8692368122822426971)
XLA Ops:
  0.0 4.0 %collective-permute-start = (f32[2,8,1024]{2,1,0:T(8,128)}, f32[2,8,1024]{2,1,0:T(8,128)S(1)}, u32[]{:S(2)}, u32[]{:S(2)}) collective-permute-start(f32[2,8,1024]{2,1,0:T(8,128)} %refs_5_.1), channel_id=1, source_target_pairs={{0,2},{1,3},{2,0},{3,1},{4,6},{5,7},{6,4},{7,5},{8,10},{9,11},{10,... | collective-permute-start | bytes 196616 | tf_op jit(solution)/shard_map/ppermute | solution.py:345
  4.0 1.3 %collective-permute-start.2 = (f32[2,8,1024]{2,1,0:T(8,128)}, f32[2,8,1024]{2,1,0:T(8,128)S(1)}, u32[]{:S(2)}, u32[]{:S(2)}) collective-permute-start(f32[2,8,1024]{2,1,0:T(8,128)} %refs_5_.1), channel_id=1, source_target_pairs={{0,3},{1,2},{2,1},{3,0},{4,7},{5,6},{6,5},{7,4},{8,11},{9,10},{10,... | collective-permute-start | bytes 196616 | tf_op jit(solution)/shard_map/ppermute | solution.py:345
  5.4 0.2 collective-permute-start.1
  5.6 4.6 %shard_map.64 = (s32[8,1024]{1,0:T(8,128)S(1)}, f32[8,1024]{1,0:T(8,128)S(1)}, f32[1,1024]{1,0:T(1,128)S(1)}, bf16[1024,2048]{1,0:T(8,128)(2,1)S(1)}, bf16[1280,...) custom-call(s32[1]{0:T(128)} %bitcast.me_ref, ...), custom_call_target="tpu_custom_call" | custom-call | flops 7864320 | bytes 12582912 | tf_op jit(solution)/shard_map/pallas_call | solution.py:72
  10.2 0.0 collective-permute-done.refs_1_
  10.3 0.2 collective-permute-done.2.refs_3_
  10.5 0.1 collective-permute-done.1.refs_2_
  10.6 0.5 shard_map.65
  11.1 2.5 %collective-permute-start.3 = (f32[72,256]{1,0:T(8,128)S(1)}, f32[72,256]{1,0:T(8,128)S(1)}, u32[]{:S(2)}, u32[]{:S(2)}) collective-permute-start(f32[72,256]{1,0:T(8,128)S(1)} %get-tuple-element.98), channel_id=1, source_target_pairs={{0,24},{4,28},{8,16},{12,20},{16,8},{20,12},{24,0},{28,4},{1,25},{... | collective-permute-start | bytes 221192 | tf_op jit(solution)/shard_map/ppermute | solution.py:335
  13.5 0.0 collective-permute-start.6
  13.5 0.5 collective-permute-start.4
  14.0 0.5 %collective-permute-start.5 = (f32[72,256]{1,0:T(8,128)S(1)}, f32[72,256]{1,0:T(8,128)S(1)}, u32[]{:S(2)}, u32[]{:S(2)}) collective-permute-start(f32[72,256]{1,0:T(8,128)S(1)} %get-tuple-element.100), channel_id=1, source_target_pairs={{0,8},{4,12},{8,0},{12,4},{16,24},{20,28},{24,16},{28,20},{1,9},{5... | collective-permute-start | bytes 221192 | tf_op jit(solution)/shard_map/ppermute | solution.py:335
  14.6 3.6 %shard_map.66 = (f32[32,1024]{1,0:T(8,128)S(1)}, bf16[1024,1024]{1,0:T(8,128)(2,1)S(1)}, bf16[1024,1024]{1,0:T(8,128)(2,1)S(1)}, bf16[256,1024]{1,0:T(8,128)(2,1)S(1)}, bf16[256,1024]{1,0:T(8,128)(2,1)S(1)}) custom-call(f32[32,1024]{1,0:T(8,128)S(1)} %get-tuple-element.102.refs_4_.term_ref.total_ref, bf16[1024,2048]{1,0:T(8,128)(2,1)S(1)} %get-tuple-element.103.select_ref, ...), custom_call_target="tpu_custom_call" | custom-call | flops 251658240 | bytes 16777216 | tf_op jit(solution)/shard_map/pallas_call | solution.py:72
  18.2 0.0 collective-permute-done.3.refs_1_
  18.2 0.0 collective-permute-done.4.refs_2_
  18.3 0.2 collective-permute-done.5.refs_3_
  18.4 0.0 collective-permute-done.6.refs_0_
  18.5 0.1 collective-permute-start.7
  18.5 1.3 %shard_map.68 = (bf16[512,1024]{1,0:T(8,128)(2,1)S(1)}, bf16[512,1024]{1,0:T(8,128)(2,1)S(1)}) custom-call(s32[8,1024]{1,0:T(8,128)S(1)} %get-tuple-element.120.targets_ref, f32[8,1024]{1,0:T(8,128)S(1)} %get-tuple-element.108.values_ref), custom_call_target="tpu_custom_call" | custom-call | flops 3145728 | bytes 12582912 | tf_op jit(solution)/shard_map/pallas_call | solution.py:72
  19.8 0.8 %shard_map.67 = (f32[32,1024]{1,0:T(8,128)S(1)}, f32[8,128]{1,0:T(8,128)S(1)}) custom-call(f32[32,1024]{1,0:T(8,128)S(1)} %get-tuple-element.111.base_ref, f32[8,128]{1,0:T(8,128)S(1)} %get-tuple-element.112.partial_ref, bf16[1024,1024]{1,0:T(8,128)(2,1)S(1)} %get-tuple-element.113.early_high, bf16[1024,1024]{1,0:T(8,128)(2,1)S(1)} %get-tuple-element.114.early_low, ...), custom_call_target="tpu_custom_call" | custom-call | flops 201326592 | bytes 4194304 | tf_op jit(solution)/shard_map/pallas_call | solution.py:72
  20.6 0.0 collective-permute-done.7.late_ref
  20.7 1.4 %shard_map.69 = (f32[32,1024]{1,0:T(8,128)S(1)}, f32[32,1024]{1,0:T(8,128)S(1)}, f32[8,128]{1,0:T(8,128)S(1)}, f32[72,256]{1,0:T(8,128)S(1)}, f32[72,256]{1,0:T(8,128)S(1)}, /*index=5*/f32[72,256]{1,0:T(8,128)S(1)}) custom-call(f32[3,40,256]{2,1,0:T(8,128)S(1)} %collective-permute-done.7.late_ref, f32[32,1024]{1,0:T(8,128)S(1)} %get-tuple-element.116.base_ref, ...), custom_call_target="tpu_custom_call" | custom-call | flops 150994944 | bytes 12582912 | tf_op jit(solution)/shard_map/pallas_call | solution.py:72
  22.0 2.3 %collective-permute-start.8 = (f32[72,256]{1,0:T(8,128)S(1)}, f32[72,256]{1,0:T(8,128)S(1)}, u32[]{:S(2)}, u32[]{:S(2)}) collective-permute-start(f32[72,256]{1,0:T(8,128)S(1)} %get-tuple-element.125), channel_id=1, source_target_pairs={{0,24},{4,28},{8,16},{12,20},{16,8},{20,12},{24,0},{28,4},{1,25},{... | collective-permute-start | bytes 221192 | tf_op jit(solution)/shard_map/ppermute | solution.py:335
  24.3 0.5 collective-permute-start.9
  24.8 0.7 %collective-permute-start.10 = (f32[72,256]{1,0:T(8,128)S(1)}, f32[72,256]{1,0:T(8,128)S(1)}, u32[]{:S(2)}, u32[]{:S(2)}) collective-permute-start(f32[72,256]{1,0:T(8,128)S(1)} %get-tuple-element.127), channel_id=1, source_target_pairs={{0,8},{4,12},{8,0},{12,4},{16,24},{20,28},{24,16},{28,20},{1,9},{5... | collective-permute-start | bytes 221192 | tf_op jit(solution)/shard_map/ppermute | solution.py:335
  25.5 1.2 %shard_map.70 = (f32[32,1024]{1,0:T(8,128)S(1)}, f32[40,256]{1,0:T(8,128)S(1)}) custom-call(f32[32,1024]{1,0:T(8,128)S(1)} %get-tuple-element.128.term_ref, f32[8,128]{1,0:T(8,128)S(1)} %get-tuple-element.129.partial_ref, bf16[1024,2048]{1,0:T(8,128)(2,1)S(1)} %get-tuple-element.103.select_ref, bf16[1280,1024]{1,0:T(8,128)(2,1)S(1)} %get-tuple-element.162.near_high, ...), custom_call_target="tpu_custom_call" | custom-call | flops 251658240 | bytes 16777216 | tf_op jit(solution)/shard_map/pallas_call | solution.py:72
  26.7 0.0 collective-permute-start.11
  26.8 0.9 %collective-permute-done.8.refs_1_ = f32[72,256]{1,0:T(8,128)S(1)} collective-permute-done((f32[72,256]{1,0:T(8,128)S(1)}, f32[72,256]{1,0:T(8,128)S(1)}, u32[]{:S(2)}, u32[]{:S(2)}) %collective-permute-start.8) | collective-permute-done | bytes 73760 | tf_op jit(solution)/shard_map/ppermute | solution.py:335
  27.7 1.5 %collective-permute-done.9.refs_2_ = f32[72,256]{1,0:T(8,128)S(1)} collective-permute-done((f32[72,256]{1,0:T(8,128)S(1)}, f32[72,256]{1,0:T(8,128)S(1)}, u32[]{:S(2)}, u32[]{:S(2)}) %collective-permute-start.9) | collective-permute-done | bytes 73760 | tf_op jit(solution)/shard_map/ppermute | solution.py:335
  29.2 0.1 collective-permute-done.10.refs_3_
  29.3 0.0 collective-permute-done.11.refs_0_
  29.3 0.1 collective-permute-start.12
  29.3 0.8 %shard_map.71 = (f32[32,1024]{1,0:T(8,128)S(1)}, f32[8,128]{1,0:T(8,128)S(1)}) custom-call(f32[32,1024]{1,0:T(8,128)S(1)} %get-tuple-element.136.base_ref, f32[8,128]{1,0:T(8,128)S(1)} %get-tuple-element.129.partial_ref, bf16[1024,1024]{1,0:T(8,128)(2,1)S(1)} %get-tuple-element.113.early_high, bf16[1024,1024]{1,0:T(8,128)(2,1)S(1)} %get-tuple-element.114.early_low, ...), custom_call_target="tpu_custom_call" | custom-call | flops 201326592 | bytes 4194304 | tf_op jit(solution)/shard_map/pallas_call | solution.py:72
  30.2 0.5 collective-permute-done.12.late_ref
  30.7 1.4 %shard_map.72 = (f32[32,1024]{1,0:T(8,128)S(1)}, f32[32,1024]{1,0:T(8,128)S(1)}, f32[8,128]{1,0:T(8,128)S(1)}, f32[72,256]{1,0:T(8,128)S(1)}, f32[72,256]{1,0:T(8,128)S(1)}, /*index=5*/f32[72,256]{1,0:T(8,128)S(1)}) custom-call(f32[3,40,256]{2,1,0:T(8,128)S(1)} %collective-permute-done.12.late_ref, f32[32,1024]{1,0:T(8,128)S(1)} %get-tuple-element.138.base_ref, ...), custom_call_target="tpu_custom_call" | custom-call | flops 150994944 | bytes 12582912 | tf_op jit(solution)/shard_map/pallas_call | solution.py:72
  32.0 1.7 %collective-permute-start.13 = (f32[72,256]{1,0:T(8,128)S(1)}, f32[72,256]{1,0:T(8,128)S(1)}, u32[]{:S(2)}, u32[]{:S(2)}) collective-permute-start(f32[72,256]{1,0:T(8,128)S(1)} %get-tuple-element.141), channel_id=1, source_target_pairs={{0,24},{4,28},{8,16},{12,20},{16,8},{20,12},{24,0},{28,4},{1,25},{... | collective-permute-start | bytes 221192 | tf_op jit(solution)/shard_map/ppermute | solution.py:335
  33.8 1.2 %collective-permute-start.14 = (f32[72,256]{1,0:T(8,128)S(1)}, f32[72,256]{1,0:T(8,128)S(1)}, u32[]{:S(2)}, u32[]{:S(2)}) collective-permute-start(f32[72,256]{1,0:T(8,128)S(1)} %get-tuple-element.142), channel_id=1, source_target_pairs={{0,16},{4,20},{8,24},{12,28},{16,0},{20,4},{24,8},{28,12},{1,17},{... | collective-permute-start | bytes 221192 | tf_op jit(solution)/shard_map/ppermute | solution.py:335
  34.9 0.6 %collective-permute-start.15 = (f32[72,256]{1,0:T(8,128)S(1)}, f32[72,256]{1,0:T(8,128)S(1)}, u32[]{:S(2)}, u32[]{:S(2)}) collective-permute-start(f32[72,256]{1,0:T(8,128)S(1)} %get-tuple-element.143), channel_id=1, source_target_pairs={{0,8},{4,12},{8,0},{12,4},{16,24},{20,28},{24,16},{28,20},{1,9},{5... | collective-permute-start | bytes 221192 | tf_op jit(solution)/shard_map/ppermute | solution.py:335
  35.5 1.2 %shard_map.73 = (f32[32,1024]{1,0:T(8,128)S(1)}, f32[40,256]{1,0:T(8,128)S(1)}) custom-call(f32[32,1024]{1,0:T(8,128)S(1)} %get-tuple-element.144.term_ref, f32[8,128]{1,0:T(8,128)S(1)} %get-tuple-element.145.partial_ref, bf16[1024,2048]{1,0:T(8,128)(2,1)S(1)} %get-tuple-element.103.select_ref, bf16[1280,1024]{1,0:T(8,128)(2,1)S(1)} %get-tuple-element.162.near_high, ...), custom_call_target="tpu_custom_call" | custom-call | flops 251658240 | bytes 16777216 | tf_op jit(solution)/shard_map/pallas_call | solution.py:72
  36.7 0.0 collective-permute-start.16
  36.8 0.6 %collective-permute-done.13.refs_1_ = f32[72,256]{1,0:T(8,128)S(1)} collective-permute-done((f32[72,256]{1,0:T(8,128)S(1)}, f32[72,256]{1,0:T(8,128)S(1)}, u32[]{:S(2)}, u32[]{:S(2)}) %collective-permute-start.13) | collective-permute-done | bytes 73760 | tf_op jit(solution)/shard_map/ppermute | solution.py:335
  37.4 1.5 %collective-permute-done.14.refs_2_ = f32[72,256]{1,0:T(8,128)S(1)} collective-permute-done((f32[72,256]{1,0:T(8,128)S(1)}, f32[72,256]{1,0:T(8,128)S(1)}, u32[]{:S(2)}, u32[]{:S(2)}) %collective-permute-start.14) | collective-permute-done | bytes 73760 | tf_op jit(solution)/shard_map/ppermute | solution.py:335
  38.9 0.4 collective-permute-done.15.refs_3_
  39.3 0.0 collective-permute-done.16.refs_0_
  39.3 0.1 collective-permute-start.17
  39.4 0.8 %shard_map.74 = (f32[32,1024]{1,0:T(8,128)S(1)}, f32[8,128]{1,0:T(8,128)S(1)}) custom-call(f32[32,1024]{1,0:T(8,128)S(1)} %get-tuple-element.152.base_ref, f32[8,128]{1,0:T(8,128)S(1)} %get-tuple-element.145.partial_ref, bf16[1024,1024]{1,0:T(8,128)(2,1)S(1)} %get-tuple-element.113.early_high, bf16[1024,1024]{1,0:T(8,128)(2,1)S(1)} %get-tuple-element.114.early_low, ...), custom_call_target="tpu_custom_call" | custom-call | flops 201326592 | bytes 4194304 | tf_op jit(solution)/shard_map/pallas_call | solution.py:72
  40.2 0.5 collective-permute-done.17.late_ref
  40.7 1.4 %shard_map.75 = (f32[32,1024]{1,0:T(8,128)S(1)}, f32[32,1024]{1,0:T(8,128)S(1)}, f32[8,128]{1,0:T(8,128)S(1)}, f32[72,256]{1,0:T(8,128)S(1)}, f32[72,256]{1,0:T(8,128)S(1)}, /*index=5*/f32[72,256]{1,0:T(8,128)S(1)}) custom-call(f32[3,40,256]{2,1,0:T(8,128)S(1)} %collective-permute-done.17.late_ref, f32[32,1024]{1,0:T(8,128)S(1)} %get-tuple-element.154.base_ref, ...), custom_call_target="tpu_custom_call" | custom-call | flops 150994944 | bytes 12582912 | tf_op jit(solution)/shard_map/pallas_call | solution.py:72
  42.1 1.6 %collective-permute-start.18 = (f32[72,256]{1,0:T(8,128)S(1)}, f32[72,256]{1,0:T(8,128)S(1)}, u32[]{:S(2)}, u32[]{:S(2)}) collective-permute-start(f32[72,256]{1,0:T(8,128)S(1)} %get-tuple-element.157), channel_id=1, source_target_pairs={{0,24},{4,28},{8,16},{12,20},{16,8},{20,12},{24,0},{28,4},{1,25},{... | collective-permute-start | bytes 221192 | tf_op jit(solution)/shard_map/ppermute | solution.py:335
  43.6 0.9 %collective-permute-start.19 = (f32[72,256]{1,0:T(8,128)S(1)}, f32[72,256]{1,0:T(8,128)S(1)}, u32[]{:S(2)}, u32[]{:S(2)}) collective-permute-start(f32[72,256]{1,0:T(8,128)S(1)} %get-tuple-element.158), channel_id=1, source_target_pairs={{0,16},{4,20},{8,24},{12,28},{16,0},{20,4},{24,8},{28,12},{1,17},{... | collective-permute-start | bytes 221192 | tf_op jit(solution)/shard_map/ppermute | solution.py:335
  44.5 1.0 %collective-permute-start.20 = (f32[72,256]{1,0:T(8,128)S(1)}, f32[72,256]{1,0:T(8,128)S(1)}, u32[]{:S(2)}, u32[]{:S(2)}) collective-permute-start(f32[72,256]{1,0:T(8,128)S(1)} %get-tuple-element.159), channel_id=1, source_target_pairs={{0,8},{4,12},{8,0},{12,4},{16,24},{20,28},{24,16},{28,20},{1,9},{5... | collective-permute-start | bytes 221192 | tf_op jit(solution)/shard_map/ppermute | solution.py:335
  45.6 1.2 %shard_map.76 = (f32[32,1024]{1,0:T(8,128)S(1)}, f32[40,256]{1,0:T(8,128)S(1)}) custom-call(f32[32,1024]{1,0:T(8,128)S(1)} %get-tuple-element.160.term_ref, f32[8,128]{1,0:T(8,128)S(1)} %get-tuple-element.161.partial_ref, bf16[1024,2048]{1,0:T(8,128)(2,1)S(1)} %get-tuple-element.103.select_ref, bf16[1280,1024]{1,0:T(8,128)(2,1)S(1)} %get-tuple-element.162.near_high, ...), custom_call_target="tpu_custom_call" | custom-call | flops 251658240 | bytes 16777216 | tf_op jit(solution)/shard_map/pallas_call | solution.py:72
  46.8 0.0 collective-permute-start.21
  46.8 0.6 %collective-permute-done.18.refs_1_ = f32[72,256]{1,0:T(8,128)S(1)} collective-permute-done((f32[72,256]{1,0:T(8,128)S(1)}, f32[72,256]{1,0:T(8,128)S(1)}, u32[]{:S(2)}, u32[]{:S(2)}) %collective-permute-start.18) | collective-permute-done | bytes 73760 | tf_op jit(solution)/shard_map/ppermute | solution.py:335
  47.4 1.4 %collective-permute-done.19.refs_2_ = f32[72,256]{1,0:T(8,128)S(1)} collective-permute-done((f32[72,256]{1,0:T(8,128)S(1)}, f32[72,256]{1,0:T(8,128)S(1)}, u32[]{:S(2)}, u32[]{:S(2)}) %collective-permute-start.19) | collective-permute-done | bytes 73760 | tf_op jit(solution)/shard_map/ppermute | solution.py:335
  48.9 0.0 collective-permute-done.20.refs_3_
  48.9 0.0 collective-permute-done.21.refs_0_
  48.9 0.1 collective-permute-start.22
  49.0 0.8 %shard_map.77 = (f32[32,1024]{1,0:T(8,128)S(1)}, f32[8,128]{1,0:T(8,128)S(1)}) custom-call(f32[32,1024]{1,0:T(8,128)S(1)} %get-tuple-element.168.base_ref, f32[8,128]{1,0:T(8,128)S(1)} %get-tuple-element.161.partial_ref, bf16[1024,1024]{1,0:T(8,128)(2,1)S(1)} %get-tuple-element.113.early_high, bf16[1024,1024]{1,0:T(8,128)(2,1)S(1)} %get-tuple-element.114.early_low, ...), custom_call_target="tpu_custom_call" | custom-call | flops 201326592 | bytes 4194304 | tf_op jit(solution)/shard_map/pallas_call | solution.py:72
  49.8 0.5 collective-permute-done.22.late_ref
  50.3 1.4 %shard_map.78 = f32[32,1024]{1,0:T(8,128)} custom-call(f32[3,40,256]{2,1,0:T(8,128)S(1)} %collective-permute-done.22.late_ref, f32[32,1024]{1,0:T(8,128)S(1)} %get-tuple-element.170.base_ref, f32[8,128]{1,0:T(8,128)S(1)} %get-tuple-element.171.sums_ref, f32[32,1024]{1,0:T(8,128)S(1)} %get-tuple-element.172.total_ref, ...), custom_call_target="tpu_custom_call" | custom-call | flops 150994944 | bytes 12582912 | tf_op jit(solution)/shard_map/pallas_call | solution.py:72
  (16 shorter events, 0.1 us)
Async XLA Ops:
  0.0 10.2 %collective-permute-start = (f32[2,8,1024]{2,1,0:T(8,128)}, f32[2,8,1024]{2,1,0:T(8,128)S(1)}, u32[]{:S(2)}, u32[]{:S(2)}) collective-permute-start(f32[2,8,1024]{2,1,0:T(8,128)} %refs_5_.1), channel_id=1, source_target_pairs={{0,2},{1,3},{2,0},{3,1},{4,6},{5,7},{6,4},{7,5},{8,10},{9,11},{10,... | collective-permute-start | bytes 196616 | tf_op jit(solution)/shard_map/ppermute | solution.py:345
  4.0 6.4 %collective-permute-start.2 = (f32[2,8,1024]{2,1,0:T(8,128)}, f32[2,8,1024]{2,1,0:T(8,128)S(1)}, u32[]{:S(2)}, u32[]{:S(2)}) collective-permute-start(f32[2,8,1024]{2,1,0:T(8,128)} %refs_5_.1), channel_id=1, source_target_pairs={{0,3},{1,2},{2,1},{3,0},{4,7},{5,6},{6,5},{7,4},{8,11},{9,10},{10,... | collective-permute-start | bytes 196616 | tf_op jit(solution)/shard_map/ppermute | solution.py:345
  5.4 5.2 %collective-permute-start.1 = (f32[2,8,1024]{2,1,0:T(8,128)}, f32[2,8,1024]{2,1,0:T(8,128)S(1)}, u32[]{:S(2)}, u32[]{:S(2)}) collective-permute-start(f32[2,8,1024]{2,1,0:T(8,128)} %refs_5_.1), channel_id=1, source_target_pairs={{0,1},{1,0},{2,3},{3,2},{4,5},{5,4},{6,7},{7,6},{8,9},{9,8},{10,11... | collective-permute-start | bytes 196616 | tf_op jit(solution)/shard_map/ppermute | solution.py:345
  11.1 7.2 %collective-permute-start.3 = (f32[72,256]{1,0:T(8,128)S(1)}, f32[72,256]{1,0:T(8,128)S(1)}, u32[]{:S(2)}, u32[]{:S(2)}) collective-permute-start(f32[72,256]{1,0:T(8,128)S(1)} %get-tuple-element.98), channel_id=1, source_target_pairs={{0,24},{4,28},{8,16},{12,20},{16,8},{20,12},{24,0},{28,4},{1,25},{... | collective-permute-start | bytes 221192 | tf_op jit(solution)/shard_map/ppermute | solution.py:335
  13.5 4.9 %collective-permute-start.6 = (f32[40,256]{1,0:T(8,128)S(1)}, f32[40,256]{1,0:T(8,128)S(1)}, u32[]{:S(2)}, u32[]{:S(2)}) collective-permute-start(f32[40,256]{1,0:T(8,128)S(1)} %get-tuple-element.101), channel_id=1, source_target_pairs={{0,4},{4,0},{8,12},{12,8},{16,20},{20,16},{24,28},{28,24},{1,5},{5... | collective-permute-start | bytes 122888 | tf_op jit(solution)/shard_map/ppermute | solution.py:335
  13.5 4.7 %collective-permute-start.4 = (f32[72,256]{1,0:T(8,128)S(1)}, f32[72,256]{1,0:T(8,128)S(1)}, u32[]{:S(2)}, u32[]{:S(2)}) collective-permute-start(f32[72,256]{1,0:T(8,128)S(1)} %get-tuple-element.99), channel_id=1, source_target_pairs={{0,16},{4,20},{8,24},{12,28},{16,0},{20,4},{24,8},{28,12},{1,17},{... | collective-permute-start | bytes 221192 | tf_op jit(solution)/shard_map/ppermute | solution.py:335
  14.0 4.4 %collective-permute-start.5 = (f32[72,256]{1,0:T(8,128)S(1)}, f32[72,256]{1,0:T(8,128)S(1)}, u32[]{:S(2)}, u32[]{:S(2)}) collective-permute-start(f32[72,256]{1,0:T(8,128)S(1)} %get-tuple-element.100), channel_id=1, source_target_pairs={{0,8},{4,12},{8,0},{12,4},{16,24},{20,28},{24,16},{28,20},{1,9},{5... | collective-permute-start | bytes 221192 | tf_op jit(solution)/shard_map/ppermute | solution.py:335
  18.5 2.2 %collective-permute-start.7 = (f32[3,40,256]{2,1,0:T(8,128)S(1)}, f32[3,40,256]{2,1,0:T(8,128)S(1)}, u32[]{:S(2)}, u32[]{:S(2)}) collective-permute-start(f32[3,40,256]{2,1,0:T(8,128)S(1)} %pad_maximum_fusion), channel_id=1, source_target_pairs={{0,4},{4,0},{8,12},{12,8},{16,20},{20,16},{24,28},{28,24},{1,5},{5... | collective-permute-start | bytes 368648 | tf_op jit(solution)/shard_map/ppermute | solution.py:335
  22.0 5.6 %collective-permute-start.8 = (f32[72,256]{1,0:T(8,128)S(1)}, f32[72,256]{1,0:T(8,128)S(1)}, u32[]{:S(2)}, u32[]{:S(2)}) collective-permute-start(f32[72,256]{1,0:T(8,128)S(1)} %get-tuple-element.125), channel_id=1, source_target_pairs={{0,24},{4,28},{8,16},{12,20},{16,8},{20,12},{24,0},{28,4},{1,25},{... | collective-permute-start | bytes 221192 | tf_op jit(solution)/shard_map/ppermute | solution.py:335
  24.3 4.8 %collective-permute-start.9 = (f32[72,256]{1,0:T(8,128)S(1)}, f32[72,256]{1,0:T(8,128)S(1)}, u32[]{:S(2)}, u32[]{:S(2)}) collective-permute-start(f32[72,256]{1,0:T(8,128)S(1)} %get-tuple-element.126), channel_id=1, source_target_pairs={{0,16},{4,20},{8,24},{12,28},{16,0},{20,4},{24,8},{28,12},{1,17},{... | collective-permute-start | bytes 221192 | tf_op jit(solution)/shard_map/ppermute | solution.py:335
  24.8 4.4 %collective-permute-start.10 = (f32[72,256]{1,0:T(8,128)S(1)}, f32[72,256]{1,0:T(8,128)S(1)}, u32[]{:S(2)}, u32[]{:S(2)}) collective-permute-start(f32[72,256]{1,0:T(8,128)S(1)} %get-tuple-element.127), channel_id=1, source_target_pairs={{0,8},{4,12},{8,0},{12,4},{16,24},{20,28},{24,16},{28,20},{1,9},{5... | collective-permute-start | bytes 221192 | tf_op jit(solution)/shard_map/ppermute | solution.py:335
  26.7 2.5 %collective-permute-start.11 = (f32[40,256]{1,0:T(8,128)S(1)}, f32[40,256]{1,0:T(8,128)S(1)}, u32[]{:S(2)}, u32[]{:S(2)}) collective-permute-start(f32[40,256]{1,0:T(8,128)S(1)} %get-tuple-element.133), channel_id=1, source_target_pairs={{0,4},{4,0},{8,12},{12,8},{16,20},{20,16},{24,28},{28,24},{1,5},{5... | collective-permute-start | bytes 122888 | tf_op jit(solution)/shard_map/ppermute | solution.py:335
  29.3 1.4 %collective-permute-start.12 = (f32[3,40,256]{2,1,0:T(8,128)S(1)}, f32[3,40,256]{2,1,0:T(8,128)S(1)}, u32[]{:S(2)}, u32[]{:S(2)}) collective-permute-start(f32[3,40,256]{2,1,0:T(8,128)S(1)} %pad_maximum_fusion.1), channel_id=1, source_target_pairs={{0,4},{4,0},{8,12},{12,8},{16,20},{20,16},{24,28},{28,24},{1,5},{5... | collective-permute-start | bytes 368648 | tf_op jit(solution)/shard_map/ppermute | solution.py:335
  32.0 5.3 %collective-permute-start.13 = (f32[72,256]{1,0:T(8,128)S(1)}, f32[72,256]{1,0:T(8,128)S(1)}, u32[]{:S(2)}, u32[]{:S(2)}) collective-permute-start(f32[72,256]{1,0:T(8,128)S(1)} %get-tuple-element.141), channel_id=1, source_target_pairs={{0,24},{4,28},{8,16},{12,20},{16,8},{20,12},{24,0},{28,4},{1,25},{... | collective-permute-start | bytes 221192 | tf_op jit(solution)/shard_map/ppermute | solution.py:335
  33.8 5.1 %collective-permute-start.14 = (f32[72,256]{1,0:T(8,128)S(1)}, f32[72,256]{1,0:T(8,128)S(1)}, u32[]{:S(2)}, u32[]{:S(2)}) collective-permute-start(f32[72,256]{1,0:T(8,128)S(1)} %get-tuple-element.142), channel_id=1, source_target_pairs={{0,16},{4,20},{8,24},{12,28},{16,0},{20,4},{24,8},{28,12},{1,17},{... | collective-permute-start | bytes 221192 | tf_op jit(solution)/shard_map/ppermute | solution.py:335
  34.9 4.4 %collective-permute-start.15 = (f32[72,256]{1,0:T(8,128)S(1)}, f32[72,256]{1,0:T(8,128)S(1)}, u32[]{:S(2)}, u32[]{:S(2)}) collective-permute-start(f32[72,256]{1,0:T(8,128)S(1)} %get-tuple-element.143), channel_id=1, source_target_pairs={{0,8},{4,12},{8,0},{12,4},{16,24},{20,28},{24,16},{28,20},{1,9},{5... | collective-permute-start | bytes 221192 | tf_op jit(solution)/shard_map/ppermute | solution.py:335
  36.7 2.5 %collective-permute-start.16 = (f32[40,256]{1,0:T(8,128)S(1)}, f32[40,256]{1,0:T(8,128)S(1)}, u32[]{:S(2)}, u32[]{:S(2)}) collective-permute-start(f32[40,256]{1,0:T(8,128)S(1)} %get-tuple-element.149), channel_id=1, source_target_pairs={{0,4},{4,0},{8,12},{12,8},{16,20},{20,16},{24,28},{28,24},{1,5},{5... | collective-permute-start | bytes 122888 | tf_op jit(solution)/shard_map/ppermute | solution.py:335
  39.3 1.4 %collective-permute-start.17 = (f32[3,40,256]{2,1,0:T(8,128)S(1)}, f32[3,40,256]{2,1,0:T(8,128)S(1)}, u32[]{:S(2)}, u32[]{:S(2)}) collective-permute-start(f32[3,40,256]{2,1,0:T(8,128)S(1)} %pad_maximum_fusion.2), channel_id=1, source_target_pairs={{0,4},{4,0},{8,12},{12,8},{16,20},{20,16},{24,28},{28,24},{1,5},{5... | collective-permute-start | bytes 368648 | tf_op jit(solution)/shard_map/ppermute | solution.py:335
  42.1 5.4 %collective-permute-start.18 = (f32[72,256]{1,0:T(8,128)S(1)}, f32[72,256]{1,0:T(8,128)S(1)}, u32[]{:S(2)}, u32[]{:S(2)}) collective-permute-start(f32[72,256]{1,0:T(8,128)S(1)} %get-tuple-element.157), channel_id=1, source_target_pairs={{0,24},{4,28},{8,16},{12,20},{16,8},{20,12},{24,0},{28,4},{1,25},{... | collective-permute-start | bytes 221192 | tf_op jit(solution)/shard_map/ppermute | solution.py:335
  43.6 5.3 %collective-permute-start.19 = (f32[72,256]{1,0:T(8,128)S(1)}, f32[72,256]{1,0:T(8,128)S(1)}, u32[]{:S(2)}, u32[]{:S(2)}) collective-permute-start(f32[72,256]{1,0:T(8,128)S(1)} %get-tuple-element.158), channel_id=1, source_target_pairs={{0,16},{4,20},{8,24},{12,28},{16,0},{20,4},{24,8},{28,12},{1,17},{... | collective-permute-start | bytes 221192 | tf_op jit(solution)/shard_map/ppermute | solution.py:335
  44.5 4.4 %collective-permute-start.20 = (f32[72,256]{1,0:T(8,128)S(1)}, f32[72,256]{1,0:T(8,128)S(1)}, u32[]{:S(2)}, u32[]{:S(2)}) collective-permute-start(f32[72,256]{1,0:T(8,128)S(1)} %get-tuple-element.159), channel_id=1, source_target_pairs={{0,8},{4,12},{8,0},{12,4},{16,24},{20,28},{24,16},{28,20},{1,9},{5... | collective-permute-start | bytes 221192 | tf_op jit(solution)/shard_map/ppermute | solution.py:335
  46.8 2.2 %collective-permute-start.21 = (f32[40,256]{1,0:T(8,128)S(1)}, f32[40,256]{1,0:T(8,128)S(1)}, u32[]{:S(2)}, u32[]{:S(2)}) collective-permute-start(f32[40,256]{1,0:T(8,128)S(1)} %get-tuple-element.165), channel_id=1, source_target_pairs={{0,4},{4,0},{8,12},{12,8},{16,20},{20,16},{24,28},{28,24},{1,5},{5... | collective-permute-start | bytes 122888 | tf_op jit(solution)/shard_map/ppermute | solution.py:335
  48.9 1.4 %collective-permute-start.22 = (f32[3,40,256]{2,1,0:T(8,128)S(1)}, f32[3,40,256]{2,1,0:T(8,128)S(1)}, u32[]{:S(2)}, u32[]{:S(2)}) collective-permute-start(f32[3,40,256]{2,1,0:T(8,128)S(1)} %pad_maximum_fusion.3), channel_id=1, source_target_pairs={{0,4},{4,0},{8,12},{12,8},{16,20},{20,16},{24,28},{28,24},{1,5},{5... | collective-permute-start | bytes 368648 | tf_op jit(solution)/shard_map/ppermute | solution.py:335

commit v8 on v7

--- a/solution.py
+++ b/solution.py
@@ -272,9 +272,10 @@
     return product(both, jnp.concatenate([high, own_high], axis=1), near_high[...], near_low[...])
 
 
-def near_kernel(term_ref, partial_ref, select_ref, near_high, near_low, diagonal_ref, base_ref, message_ref):
+def near_kernel(term_ref, total_ref, partial_ref, select_ref, near_high, near_low, diagonal_ref, base_ref, message_ref, total_out):
     rows = term_ref.shape[0]
     term = term_ref[...]
+    total_out[...] = total_ref[...] + term
     both, high = stacked(term)
     message_ref[:rows, :] = packed(both, select_ref, 1)
     message_ref[rows:, :] = widened(partial_ref[...], message_ref.shape[1])
@@ -319,10 +320,10 @@
     image = image - ghost_values(ghosts[cut:], rest_high[...], rest_low[...])
     scale = time_step / order
     term = jnp.concatenate([scale * image[half:], -scale * image[:half]], axis=0)
-    outs[0][...] = total_ref[...] + term
     if last:
+        outs[0][...] = total_ref[...] + term
         return
-    _, term_ref, partial_ref, *out = outs
+    term_ref, partial_ref, *out = outs
     term_ref[...] = term
     both, _ = stacked(term)
     partial = intersect(both, turned_ref[...])
@@ -404,6 +405,7 @@
             early = [swap(block, bits, parts) for block, bits in zip(sent, relations[2:], strict=False)]
         else:
             early = [move(block, offset, parts) for block, offset in zip(sent[: EARLY - 1], relations[2:], strict=False)]
+        before = total
         if order == 1:
             base, early_high, early_low, first_high, first_low = call(
                 functools.partial(first_near_kernel, near_rows),
@@ -412,17 +414,17 @@
                 term, select, near_high, near_low, diagonal, targets, values,
             )
         else:
-            base, message = call(
+            base, message, total = call(
                 near_kernel,
-                [((rows, points), F32), ((tall, capacity), F32)],
+                [((rows, points), F32), ((tall, capacity), F32), ((rows, points), F32)],
                 (6 * rows * points * near_rows, 16 << 20),
-                term, partial, select, near_high, near_low, diagonal,
+                term, total, partial, select, near_high, near_low, diagonal,
             )
         if paired:
             message = swap(message, 1, parts)
             late = jnp.stack([block[rows:] for block in early])
-            late, message, base, near_high, near_low, diagonal, targets = lax.optimization_barrier(
-                (late, message, base, near_high, near_low, diagonal, targets)
+            late, message, base, near_high, near_low, diagonal, targets, _, _ = lax.optimization_barrier(
+                (late, message, base, near_high, near_low, diagonal, targets, before, term)
             )
             late = swap(late, 1, parts)
         else:
@@ -444,7 +446,7 @@
         last = order == TERMS
         shapes = [((rows, points), F32)]
         if not last:
-            shapes += [((rows, points), F32), (sum_shape, F32)] + outgoing
+            shapes += [(sum_shape, F32)] + outgoing
         outs = call(
             functools.partial(late_kernel, order, last),
             shapes,
@@ -452,10 +454,9 @@
             late, base, sums, total, select, first_high, first_low, rest_high, rest_low,
             wide, turned,
         )
-        total = outs[0]
         if not last:
-            _, term, partial, *sent = outs
-    return total.reshape(states.shape)
+            term, partial, *sent = outs
+    return outs[0].reshape(states.shape)
 
 
 def solution(mesh):

time: 52 us -> 51.8 us (level)
  no operation moved by 1% of the time
where the time goes in v8:
time: 51.8 us; the launch traced here: 51.6 us
  Pallas kernels  22.3 us (43%)
  starting transfers between devices  20 us (39%)
  waiting for transfers between devices  9.07 us (18%)
    pallas_call x15, Pallas kernels, call(): pl.pallas_call(kernel, out_shape=[jax.ShapeDtypeStruct(shape, dtype) for...  22.3 us
    ppermute x20, starting transfers between devices, swap(): lax.ppermute(value, 'mesh', [(part, part ^ bits) for part in range(parts)])  14.4 us
    ppermute x20, waiting for transfers between devices, swap(): lax.ppermute(value, 'mesh', [(part, part ^ bits) for part in range(parts)])  8.75 us
    ppermute x3, starting transfers between devices, gather_frozen(): lax.ppermute(frozen, 'band', [(at, at ^ step) for at in range(bands)])  5.62 us
  transfers between devices with their start and end apart: 23, of which 14 were waited for; matrix products, arithmetic and copies ran while one was open for 0% of the time, Pallas kernels for 32%

profile of v8, /device:TPU:0, one launch (start us, length us, event | category | flops | bytes accessed | tf_op | source)
XLA Modules:
  0.0 51.6 jit_solution(6078262062908300985)
XLA Ops:
  0.0 4.0 %collective-permute-start = (f32[2,8,1024]{2,1,0:T(8,128)}, f32[2,8,1024]{2,1,0:T(8,128)S(1)}, u32[]{:S(2)}, u32[]{:S(2)}) collective-permute-start(f32[2,8,1024]{2,1,0:T(8,128)} %refs_5_.1), channel_id=1, source_target_pairs={{0,2},{1,3},{2,0},{3,1},{4,6},{5,7},{6,4},{7,5},{8,10},{9,11},{10,... | collective-permute-start | bytes 196616 | tf_op jit(solution)/shard_map/ppermute | solution.py:346
  4.0 1.3 %collective-permute-start.2 = (f32[2,8,1024]{2,1,0:T(8,128)}, f32[2,8,1024]{2,1,0:T(8,128)S(1)}, u32[]{:S(2)}, u32[]{:S(2)}) collective-permute-start(f32[2,8,1024]{2,1,0:T(8,128)} %refs_5_.1), channel_id=1, source_target_pairs={{0,3},{1,2},{2,1},{3,0},{4,7},{5,6},{6,5},{7,4},{8,11},{9,10},{10,... | collective-permute-start | bytes 196616 | tf_op jit(solution)/shard_map/ppermute | solution.py:346
  5.4 0.2 collective-permute-start.1
  5.6 4.6 %shard_map.64 = (s32[8,1024]{1,0:T(8,128)S(1)}, f32[8,1024]{1,0:T(8,128)S(1)}, f32[1,1024]{1,0:T(1,128)S(1)}, bf16[1024,2048]{1,0:T(8,128)(2,1)S(1)}, bf16[1280,...) custom-call(s32[1]{0:T(128)} %bitcast.me_ref, ...), custom_call_target="tpu_custom_call" | custom-call | flops 7864320 | bytes 12582912 | tf_op jit(solution)/shard_map/pallas_call | solution.py:72
  10.2 0.0 collective-permute-done.refs_1_
  10.3 0.2 collective-permute-done.2.refs_3_
  10.5 0.1 collective-permute-done.1.refs_2_
  10.6 0.5 shard_map.65
  11.1 2.5 %collective-permute-start.3 = (f32[72,256]{1,0:T(8,128)S(1)}, f32[72,256]{1,0:T(8,128)S(1)}, u32[]{:S(2)}, u32[]{:S(2)}) collective-permute-start(f32[72,256]{1,0:T(8,128)S(1)} %get-tuple-element.98), channel_id=1, source_target_pairs={{0,24},{4,28},{8,16},{12,20},{16,8},{20,12},{24,0},{28,4},{1,25},{... | collective-permute-start | bytes 221192 | tf_op jit(solution)/shard_map/ppermute | solution.py:336
  13.5 0.0 collective-permute-start.6
  13.5 0.5 collective-permute-start.4
  14.0 0.5 %collective-permute-start.5 = (f32[72,256]{1,0:T(8,128)S(1)}, f32[72,256]{1,0:T(8,128)S(1)}, u32[]{:S(2)}, u32[]{:S(2)}) collective-permute-start(f32[72,256]{1,0:T(8,128)S(1)} %get-tuple-element.100), channel_id=1, source_target_pairs={{0,8},{4,12},{8,0},{12,4},{16,24},{20,28},{24,16},{28,20},{1,9},{5... | collective-permute-start | bytes 221192 | tf_op jit(solution)/shard_map/ppermute | solution.py:336
  14.6 3.6 %shard_map.66 = (f32[32,1024]{1,0:T(8,128)S(1)}, bf16[1024,1024]{1,0:T(8,128)(2,1)S(1)}, bf16[1024,1024]{1,0:T(8,128)(2,1)S(1)}, bf16[256,1024]{1,0:T(8,128)(2,1)S(1)}, bf16[256,1024]{1,0:T(8,128)(2,1)S(1)}) custom-call(f32[32,1024]{1,0:T(8,128)S(1)} %get-tuple-element.102.refs_4_.term_ref.total_ref, bf16[1024,2048]{1,0:T(8,128)(2,1)S(1)} %get-tuple-element.103.select_ref, ...), custom_call_target="tpu_custom_call" | custom-call | flops 251658240 | bytes 16777216 | tf_op jit(solution)/shard_map/pallas_call | solution.py:72
  18.2 0.0 collective-permute-done.3.refs_1_
  18.2 0.0 collective-permute-done.4.refs_2_
  18.2 0.2 collective-permute-done.5.refs_3_
  18.4 0.0 collective-permute-done.6.refs_0_
  18.5 0.1 collective-permute-start.7
  18.5 1.2 %shard_map.68 = (bf16[512,1024]{1,0:T(8,128)(2,1)S(1)}, bf16[512,1024]{1,0:T(8,128)(2,1)S(1)}) custom-call(s32[8,1024]{1,0:T(8,128)S(1)} %get-tuple-element.120.targets_ref, f32[8,1024]{1,0:T(8,128)S(1)} %get-tuple-element.108.values_ref), custom_call_target="tpu_custom_call" | custom-call | flops 3145728 | bytes 12582912 | tf_op jit(solution)/shard_map/pallas_call | solution.py:72
  19.8 0.8 %shard_map.67 = (f32[32,1024]{1,0:T(8,128)S(1)}, f32[8,128]{1,0:T(8,128)S(1)}) custom-call(f32[32,1024]{1,0:T(8,128)S(1)} %get-tuple-element.111.base_ref, f32[8,128]{1,0:T(8,128)S(1)} %get-tuple-element.112.partial_ref, bf16[1024,1024]{1,0:T(8,128)(2,1)S(1)} %get-tuple-element.113.early_high, bf16[1024,1024]{1,0:T(8,128)(2,1)S(1)} %get-tuple-element.114.early_low, ...), custom_call_target="tpu_custom_call" | custom-call | flops 201326592 | bytes 4194304 | tf_op jit(solution)/shard_map/pallas_call | solution.py:72
  20.6 0.0 collective-permute-done.7.late_ref
  20.6 1.3 %shard_map.69 = (f32[32,1024]{1,0:T(8,128)S(1)}, f32[8,128]{1,0:T(8,128)S(1)}, f32[72,256]{1,0:T(8,128)S(1)}, f32[72,256]{1,0:T(8,128)S(1)}, f32[72,256]{1,0:T(8,128)S(1)}) custom-call(f32[3,40,256]{2,1,0:T(8,128)S(1)} %collective-permute-done.7.late_ref, f32[32,1024]{1,0:T(8,128)S(1)} %get-tuple-element.116.base_ref, ...), custom_call_target="tpu_custom_call" | custom-call | flops 150994944 | bytes 12582912 | tf_op jit(solution)/shard_map/pallas_call | solution.py:72
  22.0 2.3 %collective-permute-start.8 = (f32[72,256]{1,0:T(8,128)S(1)}, f32[72,256]{1,0:T(8,128)S(1)}, u32[]{:S(2)}, u32[]{:S(2)}) collective-permute-start(f32[72,256]{1,0:T(8,128)S(1)} %get-tuple-element.125), channel_id=1, source_target_pairs={{0,24},{4,28},{8,16},{12,20},{16,8},{20,12},{24,0},{28,4},{1,25},{... | collective-permute-start | bytes 221192 | tf_op jit(solution)/shard_map/ppermute | solution.py:336
  24.3 0.5 collective-permute-start.9
  24.8 0.7 %collective-permute-start.10 = (f32[72,256]{1,0:T(8,128)S(1)}, f32[72,256]{1,0:T(8,128)S(1)}, u32[]{:S(2)}, u32[]{:S(2)}) collective-permute-start(f32[72,256]{1,0:T(8,128)S(1)} %get-tuple-element.127), channel_id=1, source_target_pairs={{0,8},{4,12},{8,0},{12,4},{16,24},{20,28},{24,16},{28,20},{1,9},{5... | collective-permute-start | bytes 221192 | tf_op jit(solution)/shard_map/ppermute | solution.py:336
  25.5 1.2 %shard_map.70 = (f32[32,1024]{1,0:T(8,128)S(1)}, f32[40,256]{1,0:T(8,128)S(1)}, f32[32,1024]{1,0:T(8,128)S(1)}) custom-call(f32[32,1024]{1,0:T(8,128)S(1)} %get-tuple-element.128.term_ref, f32[32,1024]{1,0:T(8,128)S(1)} %get-tuple-element.102.refs_4_.term_ref.total_ref, f32[8,128]{1,0:T(8,128)S(1)} %get-tuple-element.129.partial_ref, ...), custom_call_target="tpu_custom_call" | custom-call | flops 251658240 | bytes 16777216 | tf_op jit(solution)/shard_map/pallas_call | solution.py:72
  26.7 0.0 collective-permute-start.11
  26.7 0.9 %collective-permute-done.8.refs_1_ = f32[72,256]{1,0:T(8,128)S(1)} collective-permute-done((f32[72,256]{1,0:T(8,128)S(1)}, f32[72,256]{1,0:T(8,128)S(1)}, u32[]{:S(2)}, u32[]{:S(2)}) %collective-permute-start.8) | collective-permute-done | bytes 73760 | tf_op jit(solution)/shard_map/ppermute | solution.py:336
  27.6 1.5 %collective-permute-done.9.refs_2_ = f32[72,256]{1,0:T(8,128)S(1)} collective-permute-done((f32[72,256]{1,0:T(8,128)S(1)}, f32[72,256]{1,0:T(8,128)S(1)}, u32[]{:S(2)}, u32[]{:S(2)}) %collective-permute-start.9) | collective-permute-done | bytes 73760 | tf_op jit(solution)/shard_map/ppermute | solution.py:336
  29.1 0.1 collective-permute-done.10.refs_3_
  29.2 0.0 collective-permute-done.11.refs_0_
  29.2 0.1 collective-permute-start.12
  29.3 0.8 %shard_map.71 = (f32[32,1024]{1,0:T(8,128)S(1)}, f32[8,128]{1,0:T(8,128)S(1)}) custom-call(f32[32,1024]{1,0:T(8,128)S(1)} %get-tuple-element.136.base_ref, f32[8,128]{1,0:T(8,128)S(1)} %get-tuple-element.129.partial_ref, bf16[1024,1024]{1,0:T(8,128)(2,1)S(1)} %get-tuple-element.113.early_high, bf16[1024,1024]{1,0:T(8,128)(2,1)S(1)} %get-tuple-element.114.early_low, ...), custom_call_target="tpu_custom_call" | custom-call | flops 201326592 | bytes 4194304 | tf_op jit(solution)/shard_map/pallas_call | solution.py:72
  30.1 0.5 collective-permute-done.12.late_ref
  30.6 1.3 %shard_map.72 = (f32[32,1024]{1,0:T(8,128)S(1)}, f32[8,128]{1,0:T(8,128)S(1)}, f32[72,256]{1,0:T(8,128)S(1)}, f32[72,256]{1,0:T(8,128)S(1)}, f32[72,256]{1,0:T(8,128)S(1)}) custom-call(f32[3,40,256]{2,1,0:T(8,128)S(1)} %collective-permute-done.12.late_ref, f32[32,1024]{1,0:T(8,128)S(1)} %get-tuple-element.138.base_ref, ...), custom_call_target="tpu_custom_call" | custom-call | flops 150994944 | bytes 12582912 | tf_op jit(solution)/shard_map/pallas_call | solution.py:72
  32.0 1.7 %collective-permute-start.13 = (f32[72,256]{1,0:T(8,128)S(1)}, f32[72,256]{1,0:T(8,128)S(1)}, u32[]{:S(2)}, u32[]{:S(2)}) collective-permute-start(f32[72,256]{1,0:T(8,128)S(1)} %get-tuple-element.141), channel_id=1, source_target_pairs={{0,24},{4,28},{8,16},{12,20},{16,8},{20,12},{24,0},{28,4},{1,25},{... | collective-permute-start | bytes 221192 | tf_op jit(solution)/shard_map/ppermute | solution.py:336
  33.7 1.1 %collective-permute-start.14 = (f32[72,256]{1,0:T(8,128)S(1)}, f32[72,256]{1,0:T(8,128)S(1)}, u32[]{:S(2)}, u32[]{:S(2)}) collective-permute-start(f32[72,256]{1,0:T(8,128)S(1)} %get-tuple-element.142), channel_id=1, source_target_pairs={{0,16},{4,20},{8,24},{12,28},{16,0},{20,4},{24,8},{28,12},{1,17},{... | collective-permute-start | bytes 221192 | tf_op jit(solution)/shard_map/ppermute | solution.py:336
  34.8 0.7 %collective-permute-start.15 = (f32[72,256]{1,0:T(8,128)S(1)}, f32[72,256]{1,0:T(8,128)S(1)}, u32[]{:S(2)}, u32[]{:S(2)}) collective-permute-start(f32[72,256]{1,0:T(8,128)S(1)} %get-tuple-element.143), channel_id=1, source_target_pairs={{0,8},{4,12},{8,0},{12,4},{16,24},{20,28},{24,16},{28,20},{1,9},{5... | collective-permute-start | bytes 221192 | tf_op jit(solution)/shard_map/ppermute | solution.py:336
  35.5 1.2 %shard_map.73 = (f32[32,1024]{1,0:T(8,128)S(1)}, f32[40,256]{1,0:T(8,128)S(1)}, f32[32,1024]{1,0:T(8,128)S(1)}) custom-call(f32[32,1024]{1,0:T(8,128)S(1)} %get-tuple-element.144.term_ref, f32[32,1024]{1,0:T(8,128)S(1)} %get-tuple-element.140.total_ref, f32[8,128]{1,0:T(8,128)S(1)} %get-tuple-element.145.partial_ref, ...), custom_call_target="tpu_custom_call" | custom-call | flops 251658240 | bytes 16777216 | tf_op jit(solution)/shard_map/pallas_call | solution.py:72
  36.7 0.0 collective-permute-start.16
  36.7 0.6 %collective-permute-done.13.refs_1_ = f32[72,256]{1,0:T(8,128)S(1)} collective-permute-done((f32[72,256]{1,0:T(8,128)S(1)}, f32[72,256]{1,0:T(8,128)S(1)}, u32[]{:S(2)}, u32[]{:S(2)}) %collective-permute-start.13) | collective-permute-done | bytes 73760 | tf_op jit(solution)/shard_map/ppermute | solution.py:336
  37.3 1.5 %collective-permute-done.14.refs_2_ = f32[72,256]{1,0:T(8,128)S(1)} collective-permute-done((f32[72,256]{1,0:T(8,128)S(1)}, f32[72,256]{1,0:T(8,128)S(1)}, u32[]{:S(2)}, u32[]{:S(2)}) %collective-permute-start.14) | collective-permute-done | bytes 73760 | tf_op jit(solution)/shard_map/ppermute | solution.py:336
  38.8 0.4 collective-permute-done.15.refs_3_
  39.2 0.0 collective-permute-done.16.refs_0_
  39.2 0.1 collective-permute-start.17
  39.3 0.8 %shard_map.74 = (f32[32,1024]{1,0:T(8,128)S(1)}, f32[8,128]{1,0:T(8,128)S(1)}) custom-call(f32[32,1024]{1,0:T(8,128)S(1)} %get-tuple-element.152.base_ref, f32[8,128]{1,0:T(8,128)S(1)} %get-tuple-element.145.partial_ref, bf16[1024,1024]{1,0:T(8,128)(2,1)S(1)} %get-tuple-element.113.early_high, bf16[1024,1024]{1,0:T(8,128)(2,1)S(1)} %get-tuple-element.114.early_low, ...), custom_call_target="tpu_custom_call" | custom-call | flops 201326592 | bytes 4194304 | tf_op jit(solution)/shard_map/pallas_call | solution.py:72
  40.1 0.5 collective-permute-done.17.late_ref
  40.6 1.3 %shard_map.75 = (f32[32,1024]{1,0:T(8,128)S(1)}, f32[8,128]{1,0:T(8,128)S(1)}, f32[72,256]{1,0:T(8,128)S(1)}, f32[72,256]{1,0:T(8,128)S(1)}, f32[72,256]{1,0:T(8,128)S(1)}) custom-call(f32[3,40,256]{2,1,0:T(8,128)S(1)} %collective-permute-done.17.late_ref, f32[32,1024]{1,0:T(8,128)S(1)} %get-tuple-element.154.base_ref, ...), custom_call_target="tpu_custom_call" | custom-call | flops 150994944 | bytes 12582912 | tf_op jit(solution)/shard_map/pallas_call | solution.py:72
  41.9 1.6 %collective-permute-start.18 = (f32[72,256]{1,0:T(8,128)S(1)}, f32[72,256]{1,0:T(8,128)S(1)}, u32[]{:S(2)}, u32[]{:S(2)}) collective-permute-start(f32[72,256]{1,0:T(8,128)S(1)} %get-tuple-element.157), channel_id=1, source_target_pairs={{0,24},{4,28},{8,16},{12,20},{16,8},{20,12},{24,0},{28,4},{1,25},{... | collective-permute-start | bytes 221192 | tf_op jit(solution)/shard_map/ppermute | solution.py:336
  43.5 0.9 %collective-permute-start.19 = (f32[72,256]{1,0:T(8,128)S(1)}, f32[72,256]{1,0:T(8,128)S(1)}, u32[]{:S(2)}, u32[]{:S(2)}) collective-permute-start(f32[72,256]{1,0:T(8,128)S(1)} %get-tuple-element.158), channel_id=1, source_target_pairs={{0,16},{4,20},{8,24},{12,28},{16,0},{20,4},{24,8},{28,12},{1,17},{... | collective-permute-start | bytes 221192 | tf_op jit(solution)/shard_map/ppermute | solution.py:336
  44.4 1.0 %collective-permute-start.20 = (f32[72,256]{1,0:T(8,128)S(1)}, f32[72,256]{1,0:T(8,128)S(1)}, u32[]{:S(2)}, u32[]{:S(2)}) collective-permute-start(f32[72,256]{1,0:T(8,128)S(1)} %get-tuple-element.159), channel_id=1, source_target_pairs={{0,8},{4,12},{8,0},{12,4},{16,24},{20,28},{24,16},{28,20},{1,9},{5... | collective-permute-start | bytes 221192 | tf_op jit(solution)/shard_map/ppermute | solution.py:336
  45.4 1.2 %shard_map.76 = (f32[32,1024]{1,0:T(8,128)S(1)}, f32[40,256]{1,0:T(8,128)S(1)}, f32[32,1024]{1,0:T(8,128)S(1)}) custom-call(f32[32,1024]{1,0:T(8,128)S(1)} %get-tuple-element.160.term_ref, f32[32,1024]{1,0:T(8,128)S(1)} %get-tuple-element.156.total_ref, f32[8,128]{1,0:T(8,128)S(1)} %get-tuple-element.161.partial_ref, ...), custom_call_target="tpu_custom_call" | custom-call | flops 251658240 | bytes 16777216 | tf_op jit(solution)/shard_map/pallas_call | solution.py:72
  46.6 0.0 collective-permute-start.21
  46.7 0.6 %collective-permute-done.18.refs_1_ = f32[72,256]{1,0:T(8,128)S(1)} collective-permute-done((f32[72,256]{1,0:T(8,128)S(1)}, f32[72,256]{1,0:T(8,128)S(1)}, u32[]{:S(2)}, u32[]{:S(2)}) %collective-permute-start.18) | collective-permute-done | bytes 73760 | tf_op jit(solution)/shard_map/ppermute | solution.py:336
  47.3 1.5 %collective-permute-done.19.refs_2_ = f32[72,256]{1,0:T(8,128)S(1)} collective-permute-done((f32[72,256]{1,0:T(8,128)S(1)}, f32[72,256]{1,0:T(8,128)S(1)}, u32[]{:S(2)}, u32[]{:S(2)}) %collective-permute-start.19) | collective-permute-done | bytes 73760 | tf_op jit(solution)/shard_map/ppermute | solution.py:336
  48.8 0.0 collective-permute-done.20.refs_3_
  48.8 0.0 collective-permute-done.21.refs_0_
  48.8 0.1 collective-permute-start.22
  48.9 0.8 %shard_map.77 = (f32[32,1024]{1,0:T(8,128)S(1)}, f32[8,128]{1,0:T(8,128)S(1)}) custom-call(f32[32,1024]{1,0:T(8,128)S(1)} %get-tuple-element.168.base_ref, f32[8,128]{1,0:T(8,128)S(1)} %get-tuple-element.161.partial_ref, bf16[1024,1024]{1,0:T(8,128)(2,1)S(1)} %get-tuple-element.113.early_high, bf16[1024,1024]{1,0:T(8,128)(2,1)S(1)} %get-tuple-element.114.early_low, ...), custom_call_target="tpu_custom_call" | custom-call | flops 201326592 | bytes 4194304 | tf_op jit(solution)/shard_map/pallas_call | solution.py:72
  49.7 0.5 collective-permute-done.22.late_ref
  50.2 1.4 %shard_map.78 = f32[32,1024]{1,0:T(8,128)} custom-call(f32[3,40,256]{2,1,0:T(8,128)S(1)} %collective-permute-done.22.late_ref, f32[32,1024]{1,0:T(8,128)S(1)} %get-tuple-element.170.base_ref, f32[8,128]{1,0:T(8,128)S(1)} %get-tuple-element.171.sums_ref, f32[32,1024]{1,0:T(8,128)S(1)} %get-tuple-element.172.total_ref, ...), custom_call_target="tpu_custom_call" | custom-call | flops 150994944 | bytes 12582912 | tf_op jit(solution)/shard_map/pallas_call | solution.py:72
  (16 shorter events, 0.1 us)
Async XLA Ops:
  0.0 10.2 %collective-permute-start = (f32[2,8,1024]{2,1,0:T(8,128)}, f32[2,8,1024]{2,1,0:T(8,128)S(1)}, u32[]{:S(2)}, u32[]{:S(2)}) collective-permute-start(f32[2,8,1024]{2,1,0:T(8,128)} %refs_5_.1), channel_id=1, source_target_pairs={{0,2},{1,3},{2,0},{3,1},{4,6},{5,7},{6,4},{7,5},{8,10},{9,11},{10,... | collective-permute-start | bytes 196616 | tf_op jit(solution)/shard_map/ppermute | solution.py:346
  4.0 6.4 %collective-permute-start.2 = (f32[2,8,1024]{2,1,0:T(8,128)}, f32[2,8,1024]{2,1,0:T(8,128)S(1)}, u32[]{:S(2)}, u32[]{:S(2)}) collective-permute-start(f32[2,8,1024]{2,1,0:T(8,128)} %refs_5_.1), channel_id=1, source_target_pairs={{0,3},{1,2},{2,1},{3,0},{4,7},{5,6},{6,5},{7,4},{8,11},{9,10},{10,... | collective-permute-start | bytes 196616 | tf_op jit(solution)/shard_map/ppermute | solution.py:346
  5.4 5.2 %collective-permute-start.1 = (f32[2,8,1024]{2,1,0:T(8,128)}, f32[2,8,1024]{2,1,0:T(8,128)S(1)}, u32[]{:S(2)}, u32[]{:S(2)}) collective-permute-start(f32[2,8,1024]{2,1,0:T(8,128)} %refs_5_.1), channel_id=1, source_target_pairs={{0,1},{1,0},{2,3},{3,2},{4,5},{5,4},{6,7},{7,6},{8,9},{9,8},{10,11... | collective-permute-start | bytes 196616 | tf_op jit(solution)/shard_map/ppermute | solution.py:346
  11.1 7.1 %collective-permute-start.3 = (f32[72,256]{1,0:T(8,128)S(1)}, f32[72,256]{1,0:T(8,128)S(1)}, u32[]{:S(2)}, u32[]{:S(2)}) collective-permute-start(f32[72,256]{1,0:T(8,128)S(1)} %get-tuple-element.98), channel_id=1, source_target_pairs={{0,24},{4,28},{8,16},{12,20},{16,8},{20,12},{24,0},{28,4},{1,25},{... | collective-permute-start | bytes 221192 | tf_op jit(solution)/shard_map/ppermute | solution.py:336
  13.5 4.9 %collective-permute-start.6 = (f32[40,256]{1,0:T(8,128)S(1)}, f32[40,256]{1,0:T(8,128)S(1)}, u32[]{:S(2)}, u32[]{:S(2)}) collective-permute-start(f32[40,256]{1,0:T(8,128)S(1)} %get-tuple-element.101), channel_id=1, source_target_pairs={{0,4},{4,0},{8,12},{12,8},{16,20},{20,16},{24,28},{28,24},{1,5},{5... | collective-permute-start | bytes 122888 | tf_op jit(solution)/shard_map/ppermute | solution.py:336
  13.5 4.7 %collective-permute-start.4 = (f32[72,256]{1,0:T(8,128)S(1)}, f32[72,256]{1,0:T(8,128)S(1)}, u32[]{:S(2)}, u32[]{:S(2)}) collective-permute-start(f32[72,256]{1,0:T(8,128)S(1)} %get-tuple-element.99), channel_id=1, source_target_pairs={{0,16},{4,20},{8,24},{12,28},{16,0},{20,4},{24,8},{28,12},{1,17},{... | collective-permute-start | bytes 221192 | tf_op jit(solution)/shard_map/ppermute | solution.py:336
  14.0 4.4 %collective-permute-start.5 = (f32[72,256]{1,0:T(8,128)S(1)}, f32[72,256]{1,0:T(8,128)S(1)}, u32[]{:S(2)}, u32[]{:S(2)}) collective-permute-start(f32[72,256]{1,0:T(8,128)S(1)} %get-tuple-element.100), channel_id=1, source_target_pairs={{0,8},{4,12},{8,0},{12,4},{16,24},{20,28},{24,16},{28,20},{1,9},{5... | collective-permute-start | bytes 221192 | tf_op jit(solution)/shard_map/ppermute | solution.py:336
  18.5 2.2 %collective-permute-start.7 = (f32[3,40,256]{2,1,0:T(8,128)S(1)}, f32[3,40,256]{2,1,0:T(8,128)S(1)}, u32[]{:S(2)}, u32[]{:S(2)}) collective-permute-start(f32[3,40,256]{2,1,0:T(8,128)S(1)} %pad_maximum_fusion), channel_id=1, source_target_pairs={{0,4},{4,0},{8,12},{12,8},{16,20},{20,16},{24,28},{28,24},{1,5},{5... | collective-permute-start | bytes 368648 | tf_op jit(solution)/shard_map/ppermute | solution.py:336
  22.0 5.6 %collective-permute-start.8 = (f32[72,256]{1,0:T(8,128)S(1)}, f32[72,256]{1,0:T(8,128)S(1)}, u32[]{:S(2)}, u32[]{:S(2)}) collective-permute-start(f32[72,256]{1,0:T(8,128)S(1)} %get-tuple-element.125), channel_id=1, source_target_pairs={{0,24},{4,28},{8,16},{12,20},{16,8},{20,12},{24,0},{28,4},{1,25},{... | collective-permute-start | bytes 221192 | tf_op jit(solution)/shard_map/ppermute | solution.py:336
  24.3 4.9 %collective-permute-start.9 = (f32[72,256]{1,0:T(8,128)S(1)}, f32[72,256]{1,0:T(8,128)S(1)}, u32[]{:S(2)}, u32[]{:S(2)}) collective-permute-start(f32[72,256]{1,0:T(8,128)S(1)} %get-tuple-element.126), channel_id=1, source_target_pairs={{0,16},{4,20},{8,24},{12,28},{16,0},{20,4},{24,8},{28,12},{1,17},{... | collective-permute-start | bytes 221192 | tf_op jit(solution)/shard_map/ppermute | solution.py:336
  24.8 4.4 %collective-permute-start.10 = (f32[72,256]{1,0:T(8,128)S(1)}, f32[72,256]{1,0:T(8,128)S(1)}, u32[]{:S(2)}, u32[]{:S(2)}) collective-permute-start(f32[72,256]{1,0:T(8,128)S(1)} %get-tuple-element.127), channel_id=1, source_target_pairs={{0,8},{4,12},{8,0},{12,4},{16,24},{20,28},{24,16},{28,20},{1,9},{5... | collective-permute-start | bytes 221192 | tf_op jit(solution)/shard_map/ppermute | solution.py:336
  26.7 2.5 %collective-permute-start.11 = (f32[40,256]{1,0:T(8,128)S(1)}, f32[40,256]{1,0:T(8,128)S(1)}, u32[]{:S(2)}, u32[]{:S(2)}) collective-permute-start(f32[40,256]{1,0:T(8,128)S(1)} %get-tuple-element.133), channel_id=1, source_target_pairs={{0,4},{4,0},{8,12},{12,8},{16,20},{20,16},{24,28},{28,24},{1,5},{5... | collective-permute-start | bytes 122888 | tf_op jit(solution)/shard_map/ppermute | solution.py:336
  29.2 1.4 %collective-permute-start.12 = (f32[3,40,256]{2,1,0:T(8,128)S(1)}, f32[3,40,256]{2,1,0:T(8,128)S(1)}, u32[]{:S(2)}, u32[]{:S(2)}) collective-permute-start(f32[3,40,256]{2,1,0:T(8,128)S(1)} %pad_maximum_fusion.1), channel_id=1, source_target_pairs={{0,4},{4,0},{8,12},{12,8},{16,20},{20,16},{24,28},{28,24},{1,5},{5... | collective-permute-start | bytes 368648 | tf_op jit(solution)/shard_map/ppermute | solution.py:336
  32.0 5.3 %collective-permute-start.13 = (f32[72,256]{1,0:T(8,128)S(1)}, f32[72,256]{1,0:T(8,128)S(1)}, u32[]{:S(2)}, u32[]{:S(2)}) collective-permute-start(f32[72,256]{1,0:T(8,128)S(1)} %get-tuple-element.141), channel_id=1, source_target_pairs={{0,24},{4,28},{8,16},{12,20},{16,8},{20,12},{24,0},{28,4},{1,25},{... | collective-permute-start | bytes 221192 | tf_op jit(solution)/shard_map/ppermute | solution.py:336
  33.7 5.1 %collective-permute-start.14 = (f32[72,256]{1,0:T(8,128)S(1)}, f32[72,256]{1,0:T(8,128)S(1)}, u32[]{:S(2)}, u32[]{:S(2)}) collective-permute-start(f32[72,256]{1,0:T(8,128)S(1)} %get-tuple-element.142), channel_id=1, source_target_pairs={{0,16},{4,20},{8,24},{12,28},{16,0},{20,4},{24,8},{28,12},{1,17},{... | collective-permute-start | bytes 221192 | tf_op jit(solution)/shard_map/ppermute | solution.py:336
  34.8 4.4 %collective-permute-start.15 = (f32[72,256]{1,0:T(8,128)S(1)}, f32[72,256]{1,0:T(8,128)S(1)}, u32[]{:S(2)}, u32[]{:S(2)}) collective-permute-start(f32[72,256]{1,0:T(8,128)S(1)} %get-tuple-element.143), channel_id=1, source_target_pairs={{0,8},{4,12},{8,0},{12,4},{16,24},{20,28},{24,16},{28,20},{1,9},{5... | collective-permute-start | bytes 221192 | tf_op jit(solution)/shard_map/ppermute | solution.py:336
  36.7 2.5 %collective-permute-start.16 = (f32[40,256]{1,0:T(8,128)S(1)}, f32[40,256]{1,0:T(8,128)S(1)}, u32[]{:S(2)}, u32[]{:S(2)}) collective-permute-start(f32[40,256]{1,0:T(8,128)S(1)} %get-tuple-element.149), channel_id=1, source_target_pairs={{0,4},{4,0},{8,12},{12,8},{16,20},{20,16},{24,28},{28,24},{1,5},{5... | collective-permute-start | bytes 122888 | tf_op jit(solution)/shard_map/ppermute | solution.py:336
  39.2 1.4 %collective-permute-start.17 = (f32[3,40,256]{2,1,0:T(8,128)S(1)}, f32[3,40,256]{2,1,0:T(8,128)S(1)}, u32[]{:S(2)}, u32[]{:S(2)}) collective-permute-start(f32[3,40,256]{2,1,0:T(8,128)S(1)} %pad_maximum_fusion.2), channel_id=1, source_target_pairs={{0,4},{4,0},{8,12},{12,8},{16,20},{20,16},{24,28},{28,24},{1,5},{5... | collective-permute-start | bytes 368648 | tf_op jit(solution)/shard_map/ppermute | solution.py:336
  41.9 5.3 %collective-permute-start.18 = (f32[72,256]{1,0:T(8,128)S(1)}, f32[72,256]{1,0:T(8,128)S(1)}, u32[]{:S(2)}, u32[]{:S(2)}) collective-permute-start(f32[72,256]{1,0:T(8,128)S(1)} %get-tuple-element.157), channel_id=1, source_target_pairs={{0,24},{4,28},{8,16},{12,20},{16,8},{20,12},{24,0},{28,4},{1,25},{... | collective-permute-start | bytes 221192 | tf_op jit(solution)/shard_map/ppermute | solution.py:336
  43.5 5.2 %collective-permute-start.19 = (f32[72,256]{1,0:T(8,128)S(1)}, f32[72,256]{1,0:T(8,128)S(1)}, u32[]{:S(2)}, u32[]{:S(2)}) collective-permute-start(f32[72,256]{1,0:T(8,128)S(1)} %get-tuple-element.158), channel_id=1, source_target_pairs={{0,16},{4,20},{8,24},{12,28},{16,0},{20,4},{24,8},{28,12},{1,17},{... | collective-permute-start | bytes 221192 | tf_op jit(solution)/shard_map/ppermute | solution.py:336
  44.4 4.4 %collective-permute-start.20 = (f32[72,256]{1,0:T(8,128)S(1)}, f32[72,256]{1,0:T(8,128)S(1)}, u32[]{:S(2)}, u32[]{:S(2)}) collective-permute-start(f32[72,256]{1,0:T(8,128)S(1)} %get-tuple-element.159), channel_id=1, source_target_pairs={{0,8},{4,12},{8,0},{12,4},{16,24},{20,28},{24,16},{28,20},{1,9},{5... | collective-permute-start | bytes 221192 | tf_op jit(solution)/shard_map/ppermute | solution.py:336
  46.6 2.2 %collective-permute-start.21 = (f32[40,256]{1,0:T(8,128)S(1)}, f32[40,256]{1,0:T(8,128)S(1)}, u32[]{:S(2)}, u32[]{:S(2)}) collective-permute-start(f32[40,256]{1,0:T(8,128)S(1)} %get-tuple-element.165), channel_id=1, source_target_pairs={{0,4},{4,0},{8,12},{12,8},{16,20},{20,16},{24,28},{28,24},{1,5},{5... | collective-permute-start | bytes 122888 | tf_op jit(solution)/shard_map/ppermute | solution.py:336
  48.8 1.4 %collective-permute-start.22 = (f32[3,40,256]{2,1,0:T(8,128)S(1)}, f32[3,40,256]{2,1,0:T(8,128)S(1)}, u32[]{:S(2)}, u32[]{:S(2)}) collective-permute-start(f32[3,40,256]{2,1,0:T(8,128)S(1)} %pad_maximum_fusion.3), channel_id=1, source_target_pairs={{0,4},{4,0},{8,12},{12,8},{16,20},{20,16},{24,28},{28,24},{1,5},{5... | collective-permute-start | bytes 368648 | tf_op jit(solution)/shard_map/ppermute | solution.py:336
